TPU v7x, 256 devices: a whole 4x4x8 slice. The times are simulated.
256 devices in a mesh: section: 2 (over y_hi), segment: 8 (over x, core), fsdp: 16 (over z, y_lo).
Axes of the slice: x: 4, y: 4 (y_hi: 2, y_lo: 2; y = y_hi * 2 + y_lo), z: 8, core: 2. Of those that a mesh axis runs over, the one named last changes fastest.
Arguments:
- out_grad: bfloat16 [2, 16, 256, 6144], P(None, 'fsdp'), may hold values from -48 to 48
- queries: bfloat16 [2, 16, 256, 6144], P(None, 'fsdp', None, 'segment'), may hold values from -40 to 40
- enc_keys: bfloat16 [2, 16, 256, 6144], P(None, 'fsdp', None, 'segment'), may hold values from -4 to 4
- enc_values: bfloat16 [2, 16, 256, 6144], P(None, 'fsdp', None, 'segment'), may hold values from -6 to 6
- key_mask: int32 [2, 16, 256], P(None, 'fsdp'), may hold values from 0 to 1, as said below
- weights: bfloat16 [2, 2, 6144, 6144], P('section', None, 'fsdp', 'segment'), may hold values from -0.078125 to 0.078125
Outputs:
- grads: bfloat16 [2, 2, 16, 256, 6144], P('section', None, 'fsdp', None, 'segment')
Inputs may be any that keep to these rules, and one draw needn't show every extreme that they name: `key_mask`: each row is 1 on a prefix of 128 or more positions and 0 after it; the first reaction of every microbatch has no padding.
All inputs are finite; a program needn't handle non-finite values.
Results may differ from a plain program's by a relative error of at most 0.014.
Values may be sent and summed in bfloat16 or wider, within the bound.
No kernel may reach another device: no remote copies, remote signals or barrier semaphores. Data moves between devices by JAX's collectives and lax.ppermute only.
A program may use at most 128 MiB of HBM per device.

v0:
```python
import jax
import jax.numpy as jnp
from jax import lax
from jax.sharding import PartitionSpec as P

HDIM = 128


def passed_along(value, axis, by):
    peers = lax.axis_size(axis)
    pairs = [(i, i + by) for i in range(peers) if 0 <= i + by < peers]
    return lax.ppermute(value, axis, pairs)


def attend(grad_rows, first_weight, queries, enc_keys, enc_values, key_mask):
    reaction_count, seq_length, local_width = queries.shape
    head_count = local_width // HDIM
    score_scale = HDIM ** (-0.5)
    ctx_grad = jnp.dot(grad_rows, first_weight, preferred_element_type=jnp.float32).astype(
        jnp.bfloat16
    )
    shaped = (reaction_count, seq_length, head_count, HDIM)
    grad_heads = ctx_grad.reshape(shaped)
    query_heads = queries.reshape(shaped)
    key_heads = enc_keys.reshape(shaped)
    value_heads = enc_values.reshape(shaped)
    scores = (
        jnp.einsum("bihc,bjhc->bhij", query_heads, key_heads, preferred_element_type=jnp.float32)
        * score_scale
    )
    scores = jnp.where(key_mask[:, None, None, :] > 0, scores, -jnp.inf)
    row_top = jnp.max(scores, axis=-1, keepdims=True)
    exp_scores = jnp.exp(scores - row_top)
    probabilities = exp_scores / jnp.sum(exp_scores, axis=-1, keepdims=True)
    probs_half = probabilities.astype(jnp.bfloat16)
    prob_grad = jnp.einsum(
        "bihc,bjhc->bhij", grad_heads, value_heads, preferred_element_type=jnp.float32
    )
    center = jnp.sum(probabilities * prob_grad, axis=-1, keepdims=True)
    score_grad = (probabilities * (prob_grad - center)).astype(jnp.bfloat16)
    query_grad = (
        jnp.einsum("bhij,bjhc->bihc", score_grad, key_heads, preferred_element_type=jnp.float32)
        * score_scale
    ).astype(jnp.bfloat16)
    key_grad = (
        jnp.einsum("bhij,bihc->bjhc", score_grad, query_heads, preferred_element_type=jnp.float32)
        * score_scale
    ).astype(jnp.bfloat16)
    value_grad = jnp.einsum(
        "bhij,bihc->bjhc", probs_half, grad_heads, preferred_element_type=jnp.float32
    ).astype(jnp.bfloat16)
    flat = (reaction_count * seq_length, local_width)
    return (query_grad.reshape(flat), key_grad.reshape(flat), value_grad.reshape(flat))


def project(grad_rows, weight_cols):
    return lax.dot_general(
        grad_rows, weight_cols, (((1,), (1,)), ((), ())), preferred_element_type=jnp.float32
    )


def per_device(out_grad, queries, enc_keys, enc_values, key_mask, weights):
    decoder = lax.axis_index("section") == 1
    gathered = lax.all_gather(weights, "fsdp", axis=2, tiled=True)
    first_weight = gathered[0, 0]
    second_weight = gathered[0, 1]
    micro_count, reaction_count, seq_length, feature_width = out_grad.shape
    local_width = queries.shape[3]
    row_count = micro_count * reaction_count * seq_length
    flat = (micro_count * reaction_count, seq_length, local_width)

    def decoder_work():
        return attend(
            out_grad.reshape(row_count, feature_width),
            first_weight,
            queries.reshape(flat),
            enc_keys.reshape(flat),
            enc_values.reshape(flat),
            key_mask.reshape(micro_count * reaction_count, seq_length),
        )

    def encoder_work():
        blank_grads = jnp.zeros((row_count, local_width), jnp.bfloat16)
        return (blank_grads, blank_grads, blank_grads)

    query_grad, key_grad, value_grad = lax.cond(decoder, decoder_work, encoder_work)
    got_keys, got_values = passed_along((key_grad, value_grad), "section", -1)
    partial_sum = lax.cond(
        decoder,
        lambda: project(query_grad, second_weight),
        lambda: project(got_keys, first_weight) + project(got_values, second_weight),
    )
    summed = lax.psum_scatter(
        partial_sum.astype(jnp.bfloat16), "segment", scatter_dimension=1, tiled=True
    ).astype(jnp.float32)
    result = summed.astype(jnp.bfloat16).reshape(
        1, micro_count, reaction_count, seq_length, summed.shape[1]
    )
    return result


def solution(mesh):
    return jax.shard_map(
        per_device,
        mesh=mesh,
        in_specs=(
            P(None, "fsdp", None, None),
            P(None, "fsdp", None, "segment"),
            P(None, "fsdp", None, "segment"),
            P(None, "fsdp", None, "segment"),
            P(None, "fsdp", None),
            P("section", None, "fsdp", "segment"),
        ),
        out_specs=P("section", None, "fsdp", None, "segment"),
        check_vma=False,
    )
```

profile of v0, /device:TPU:1, one launch (start us, length us, event | category | flops | bytes accessed | tf_op | source)
XLA Modules:
  0.0 565.3 jit_solution(8359995170980936187)
XLA Ops:
  6.5 0.0 all-gather.2.cloned.1.call-start
  6.5 0.7 all-gather.2.cloned.1.call-update
  7.3 0.0 reduce-scatter.2.cloned.1.call-start
  7.3 0.0 copy-start.3
  7.3 0.0 copy-start.5
  7.3 398.5 %all-gather.2.cloned.1.call-done = bf16[1,2,6144,768]{3,2,1,0:T(8,128)(2,1)} async-done(((bf16[1,2,384,768]{3,2,1,0:T(8,128)(2,1)}), bf16[1,2,6144,768]{3,2,1,0:T(8,128)(2,1)}) %all-gather.2.cloned.1.call-update) | async-done | bytes 18874384 | tf_op jit(solution)/shard_map/all_gather | solution.py:64
  405.9 14.6 %slice_bitcast_fusion = (bf16[6144,768]{1,0:T(8,128)(2,1)}, bf16[6144,768]{1,0:T(8,128)(2,1)}) fusion(bf16[1,2,6144,768]{3,2,1,0:T(8,128)(2,1)} %all-gather.2.cloned.1.call-done), kind=kLoop, calls=%fused_computation.24 | loop fusion | bytes 37748736 | tf_op jit(solution)/shard_map/squeeze | solution.py:66
  420.5 0.0 copy-done.3
  420.5 0.0 copy-done.5
  420.5 1.1 conditional.2
  420.5 0.1 broadcast.21.clone.1
  420.5 0.1 broadcast.21.clone
  420.6 0.9 broadcast.21
  421.5 0.3 copy.39
  421.8 0.3 copy.40
  422.1 1.3 collective-permute-start.1
  423.4 1.3 collective-permute-start
  424.7 43.1 %collective-permute-done.1 = bf16[512,768]{1,0:T(8,128)(2,1)S(1)} collective-permute-done((bf16[512,768]{1,0:T(8,128)(2,1)S(1)}, bf16[512,768]{1,0:T(8,128)(2,1)S(1)}, u32[]{:S(2)}, u32[]{:S(2)}) %collective-permute-start.1) | collective-permute-done | bytes 786464 | tf_op jit(solution)/shard_map/ppermute | solution.py:12
  467.8 16.9 %collective-permute-done = bf16[512,768]{1,0:T(8,128)(2,1)S(1)} collective-permute-done((bf16[512,768]{1,0:T(8,128)(2,1)S(1)}, bf16[512,768]{1,0:T(8,128)(2,1)S(1)}, u32[]{:S(2)}, u32[]{:S(2)}) %collective-permute-start) | collective-permute-done | bytes 786464 | tf_op jit(solution)/shard_map/ppermute | solution.py:12
  484.6 24.2 %conditional.3 = (bf16[512,6144]{1,0:T(8,128)(2,1)}) conditional(s32[]{:T(128)} %convert_element_type.36, (bf16[512,768]{1,0:T(8,128)(2,1)S(1)}, bf16[6144,768]{1,0:T(8,128)(2,1)}, bf16[512,768]{1,0:T(8,128)(2,1)S(1)}, bf16[6144,768]{1,0:T(8,128)(2,1)}) %tuple.21, (bf16[512,768]{0,1:T(8,128)(2,1)}, bf16[6144,768]{1,0:T(8,128)(2,1)}) %tuple.22), branch_computations={%region_5.6_spmd, %region_6.7_spmd} | conditional | flops 9669967872 | bytes 51904520 | solution.py:88
  484.6 11.6 %fusion.21 = f32[512,6144]{1,0:T(8,128)} fusion(bf16[512,768]{1,0:T(8,128)(2,1)S(1)} %get-tuple-element.38, bf16[6144,768]{1,0:T(8,128)(2,1)} %get-tuple-element.39), kind=kOutput, calls=%fused_computation.28 | convolution fusion | flops 4831838208 | bytes 22806528 | tf_op jit(solution)/shard_map/cond/branch_0_fun/dot_general | solution.py:57
  496.2 12.6 %convolution_add_fusion = bf16[512,6144]{1,0:T(8,128)(2,1)} fusion(f32[512,6144]{1,0:T(8,128)} %fusion.21, bf16[512,768]{1,0:T(8,128)(2,1)S(1)} %get-tuple-element.40, bf16[6144,768]{1,0:T(8,128)(2,1)} %get-tuple-element.41), kind=kOutput, calls=%fused_computation.23 | convolution fusion | flops 4838129664 | bytes 29097984 | tf_op jit(solution)/shard_map/cond/branch_0_fun/dot_general | solution.py:57
  508.8 0.0 reduce-scatter.2.cloned.1.call-update
  508.9 49.6 %reduce-scatter.2.cloned.1.call-done = bf16[512,768]{1,0:T(8,128)(2,1)} async-done(((bf16[512,6144]{1,0:T(8,128)(2,1)}), bf16[512,768]{1,0:T(8,128)(2,1)}) %reduce-scatter.2.cloned.1.call-update) | async-done | bytes 786448 | tf_op jit(solution)/shard_map/reduce_scatter | solution.py:93
Async XLA Ops:
  6.5 399.3 %all-gather.2.cloned.1.call-start = ((), (), s32[]{:S(2)}) async-start(), calls=%async_computation.1 | async-start | bytes 20054016 | tf_op jit(solution)/shard_map/all_gather | solution.py:64
  7.3 551.2 %reduce-scatter.2.cloned.1.call-start = ((), (), s32[]{:S(2)}) async-start(), calls=%async_computation.2 | async-start | bytes 7077888 | tf_op jit(solution)/shard_map/reduce_scatter | solution.py:93
  7.3 413.2 %copy-start.3 = (bf16[2,1,256,768]{3,2,1,0:T(8,128)(2,1)S(1)}, bf16[2,1,256,768]{3,2,1,0:T(8,128)(2,1)}, u32[]{:S(2)}) copy-start(bf16[2,1,256,768]{3,2,1,0:T(8,128)(2,1)} %param.13) | copy-start | bytes 2359300
  7.3 413.1 %copy-start.5 = (s32[2,1,256]{2,1,0:T(1,128)S(1)}, s32[2,1,256]{2,1,0:T(1,128)}, u32[]{:S(2)}) copy-start(s32[2,1,256]{2,1,0:T(1,128)} %param.14) | copy-start | bytes 6148
  422.1 45.7 %collective-permute-start.1 = (bf16[512,768]{1,0:T(8,128)(2,1)S(1)}, bf16[512,768]{1,0:T(8,128)(2,1)S(1)}, u32[]{:S(2)}, u32[]{:S(2)}) collective-permute-start(bf16[512,768]{1,0:T(8,128)(2,1)S(1)} %copy.40), channel_id=1, source_target_pairs={{128,0},{129,1},{130,2},{131,3},{132,4},{133,5},{134,6},{135,7},{1... | collective-permute-start | bytes 2359304 | tf_op jit(solution)/shard_map/ppermute | solution.py:12
  423.4 61.2 %collective-permute-start = (bf16[512,768]{1,0:T(8,128)(2,1)S(1)}, bf16[512,768]{1,0:T(8,128)(2,1)S(1)}, u32[]{:S(2)}, u32[]{:S(2)}) collective-permute-start(bf16[512,768]{1,0:T(8,128)(2,1)S(1)} %copy.39), channel_id=1, source_target_pairs={{128,0},{129,1},{130,2},{131,3},{132,4},{133,5},{134,6},{135,7},{1... | collective-permute-start | bytes 2359304 | tf_op jit(solution)/shard_map/ppermute | solution.py:12
Sparse Core Ops, SparseCore 0:
  9.1 396.7 all-gather.1
  509.0 49.4 reduce-scatter.1
where the time goes:
time: 565 us
  waiting for transfers between devices  509 us (90%)
  matrix products  24.2 us (4%)
  local copies, waits for them, and re-layouts  16.2 us (3%)
  between operations  13.5 us (2%)
    all_gather x1, waiting for transfers between devices, per_device(): gathered = lax.all_gather(weights, 'fsdp', axis=2, tiled=True)  399 us
    ppermute x2, waiting for transfers between devices, passed_along(): return lax.ppermute(value, axis, pairs)  59.9 us
    reduce_scatter x1, waiting for transfers between devices, per_device(): lax.psum_scatter(partial_sum.astype(jnp.bfloat16), 'segment', scatter_dim...  49.6 us
    dot_general x2, matrix products, project(): lax.dot_general(grad_rows, weight_cols, (((1,), (1,)), ((), ())), preferr...  24.2 us
    squeeze x1, local copies, waits for them, and re-layouts, per_device(): second_weight = gathered[0, 1]  14.6 us
  transfers between devices with their start and end apart: 4, of which 4 were waited for; matrix products, arithmetic and copies ran while one was open for 0% of the time, Pallas kernels for 0%

commit v1 on v0

v1 whole, which is shorter than its diff:
```python
import functools

import jax
import jax.numpy as jnp
from jax import lax
from jax.experimental import pallas as pl
from jax.experimental.pallas import tpu as pltpu
from jax.sharding import PartitionSpec as P


HDIM = 128

Z_LINES = [[2 * z + half for z in range(8)] for half in range(2)]
DEC_SWAP = [(16 + f, 16 + (f ^ 1)) for f in range(16)]
ENC_SWAP = [(f, f ^ 1) for f in range(16)]
DEC_TO_ENC = [(16 + f, f ^ 1) for f in range(16)]
HALF_SWAP = [(f, f ^ 1) for f in range(16)]
CORE_SWAP = [(g, g ^ 1) for g in range(8)]
BOTH = ("section", "fsdp")
STEPS = (2, 1, 3, 0)
F32 = jnp.float32
BF16 = jnp.bfloat16
NT = (((1,), (1,)), ((), ()))
TN = (((0,), (0,)), ((), ()))
NN = (((1,), (0,)), ((), ()))


def mm(left, right, dims):
    return lax.dot_general(left, right, dims, preferred_element_type=F32)


def cost(flops, bytes_accessed):
    return pl.CostEstimate(flops=flops, bytes_accessed=bytes_accessed, transcendentals=0)


def pick_kernel(where, source, target):
    target[...] = source[...]


def picked(source, columns, width):
    rows = source.shape[0]
    count = columns.shape[0]
    return pl.pallas_call(
        pick_kernel,
        grid_spec=pltpu.PrefetchScalarGridSpec(
            num_scalar_prefetch=1,
            grid=(count,),
            in_specs=[pl.BlockSpec((rows, width), lambda i, at: (0, at[i]))],
            out_specs=pl.BlockSpec((rows, width), lambda i, at: (0, i)),
        ),
        out_shape=jax.ShapeDtypeStruct((rows, count * width), source.dtype),
        cost_estimate=cost(0, 2 * rows * count * width * 2),
        name="pick",
    )(columns, source)


def far_kernel(core, came, twin, weight, out, acc):
    step = pl.program_id(0)

    @pl.when(step == 0)
    def _():
        acc[...] = jnp.zeros_like(acc)

    rows = jnp.where(core[0] == step // 2, came[...], twin[...])
    acc[...] += mm(rows, weight[...], NN)

    @pl.when(step == pl.num_programs(0) - 1)
    def _():
        out[...] = acc[...].astype(BF16)


def far_partial(core, came, twin, weight, micro, seq_length):
    depth, width = weight.shape
    piece = depth // 4
    rows = pl.BlockSpec((seq_length, piece), lambda j, core: (micro, j % 2))
    return pl.pallas_call(
        far_kernel,
        grid_spec=pltpu.PrefetchScalarGridSpec(
            num_scalar_prefetch=1,
            grid=(4,),
            in_specs=[rows, rows, pl.BlockSpec((piece, width), lambda j, core: (j, 0))],
            out_specs=pl.BlockSpec((seq_length, width), lambda j, core: (0, 0)),
            scratch_shapes=[pltpu.VMEM((seq_length, width), F32)],
        ),
        out_shape=jax.ShapeDtypeStruct((seq_length, width), BF16),
        cost_estimate=cost(2 * seq_length * depth * width, 2 * depth * width),
        name="far",
    )(core, came, twin, weight)


def near_kernel(half, low, high, weight, *outs):
    part = mm(jnp.concatenate([low[...], high[...]], axis=1), weight[...], NN)
    rows = part.shape[0] // len(outs)
    for micro, out in enumerate(outs):
        cut = part[micro * rows : (micro + 1) * rows]

        @pl.when(pl.program_id(0) == 0)
        def _():
            out[...] = cut

        @pl.when(pl.program_id(0) > 0)
        def _():
            out[...] += cut


def near_partial(half, grads, weight):
    row_count = grads.shape[0]
    depth, width = weight.shape
    piece = depth // 4
    return pl.pallas_call(
        near_kernel,
        grid_spec=pltpu.PrefetchScalarGridSpec(
            num_scalar_prefetch=1,
            grid=(4,),
            in_specs=[
                pl.BlockSpec((row_count, piece // 2), lambda j, half: (0, 4 * j + half[0])),
                pl.BlockSpec((row_count, piece // 2), lambda j, half: (0, 4 * j + 2 + half[0])),
                pl.BlockSpec((piece, width), lambda j, half: (j, 0)),
            ],
            out_specs=[pl.BlockSpec((row_count // 2, width), lambda j, half: (0, 0))] * 2,
        ),
        out_shape=[jax.ShapeDtypeStruct((row_count // 2, width), F32)] * 2,
        cost_estimate=cost(2 * row_count * depth * width, 2 * depth * width),
        name="near",
    )(half, grads, grads, weight)


def attend_kernel(heads, flags, held, sent, query, key, value, mask, dq, dk, dv):
    scale = HDIM ** (-0.5)
    here = mask[0] > 0

    @pl.when(flags[0] + flags[1] > 0)
    def _():
        for head in range(heads):
            cut = slice(head * HDIM, (head + 1) * HDIM)
            grad = jnp.where(flags[2] > 0, held[:, cut], sent[:, cut])
            q, k, v = query[:, cut], key[:, cut], value[:, cut]
            scores = jnp.where(here, mm(q, k, NT) * scale, -jnp.inf)
            raised = jnp.exp(scores - jnp.max(scores, axis=-1, keepdims=True))
            probs = raised * (1.0 / jnp.sum(raised, axis=-1, keepdims=True))
            prob_grad = mm(grad, v, NT)
            center = jnp.sum(probs * prob_grad, axis=-1, keepdims=True)
            score_grad = (probs * (prob_grad - center)).astype(BF16)

            @pl.when(flags[0] > 0)
            def _():
                dq[:, cut] = (mm(score_grad, k, NN) * scale).astype(BF16)

            @pl.when(flags[1] > 0)
            def _():
                dk[:, cut] = (mm(score_grad, q, TN) * scale).astype(BF16)
                dv[:, cut] = mm(probs.astype(BF16), grad, TN).astype(BF16)


def attend(flags, held, sent, query, key, value, mask, micro):
    seq_length, width = held.shape
    heads = 2
    wide = heads * HDIM
    one = pl.BlockSpec((seq_length, wide), lambda h, flags: (0, h))
    row = pl.BlockSpec((None, seq_length, wide), lambda h, flags: (micro, 0, h))
    out = jax.ShapeDtypeStruct((seq_length, width), BF16)
    return pl.pallas_call(
        functools.partial(attend_kernel, heads),
        grid_spec=pltpu.PrefetchScalarGridSpec(
            num_scalar_prefetch=1,
            grid=(width // wide,),
            in_specs=[
                one,
                one,
                row,
                row,
                row,
                pl.BlockSpec((1, 1, seq_length), lambda h, flags: (micro, 0, 0)),
            ],
            out_specs=[one, one, one],
        ),
        out_shape=[out, out, out],
        cost_estimate=cost(
            10 * seq_length * seq_length * width, 16 * seq_length * width
        ),
        name="attend",
    )(flags, held, sent, query, key, value, mask)


def products(flags, grads, first, second, put):
    dq, dk, dv = grads
    for micro in range(2):

        @pl.when(flags[0] > 0)
        def _():
            put(micro, mm(dq[micro][...], second[...], NT))

        @pl.when(flags[0] == 0)
        def _():
            put(micro, mm(dk[micro][...], first[...], NT) + mm(dv[micro][...], second[...], NT))


def give_kernel(at, flags, q0, q1, k0, k1, v0, v1, first, second, out):
    rows = q0.shape[0]

    def put(micro, value):
        out[micro * rows : (micro + 1) * rows, :] = value.astype(BF16)

    products(flags, ((q0, q1), (k0, k1), (v0, v1)), first, second, put)


def keep_kernel(at, flags, q0, q1, k0, k1, v0, v1, first, second, other, *outs):
    rows = q0.shape[0]

    def put(micro, value):
        cut = slice(micro * rows, (micro + 1) * rows)
        total = value + other[cut, :].astype(F32)
        for i, out in enumerate(outs):

            @pl.when(pl.program_id(0) == i)
            def _():
                out[cut, :] = total.astype(out.dtype)

    products(flags, ((q0, q1), (k0, k1), (v0, v1)), first, second, put)


def projected(at, flags, grads, first, second, other=None):
    rows, width = grads[0].shape
    shard = first.shape[1]
    whole = pl.BlockSpec((rows, width), lambda i, at, flags: (0, 0))
    weight = pl.BlockSpec((None, shard, width), lambda i, at, flags: (at[i], 0, 0))
    moving = pl.BlockSpec((None, 2 * rows, shard), lambda i, at, flags: (i, 0, 0))
    fixed = pl.BlockSpec((2 * rows, shard), lambda i, at, flags: (0, 0))
    if other is None:
        kernel, extra = give_kernel, ()
        out_specs = moving
        out_shape = jax.ShapeDtypeStruct((4, 2 * rows, shard), BF16)
    else:
        kernel, extra = keep_kernel, (other,)
        out_specs = [fixed] * 4
        out_shape = [jax.ShapeDtypeStruct((2 * rows, shard), t) for t in (BF16, BF16, BF16, F32)]
    return pl.pallas_call(
        kernel,
        grid_spec=pltpu.PrefetchScalarGridSpec(
            num_scalar_prefetch=2,
            grid=(4,),
            in_specs=[whole] * 6 + [weight] * 2 + [moving] * len(extra),
            out_specs=out_specs,
        ),
        out_shape=out_shape,
        cost_estimate=cost(2 * 2 * rows * 2 * width * 4 * shard, 2 * 2 * 4 * shard * width),
    )(at, flags, *grads, first, second, *extra)


def per_device(out_grad, queries, enc_keys, enc_values, key_mask, weights):
    decoder = lax.axis_index("section") == 1
    half = lax.axis_index("fsdp") % 2
    segment = lax.axis_index("segment")
    core = segment % 2
    chip = segment // 2
    micro_count, reaction_count, seq_length, feature_width = out_grad.shape
    local_width = queries.shape[3]
    shard_rows = weights.shape[2]
    row_count = micro_count * reaction_count * seq_length
    flat = (micro_count, seq_length, local_width)
    micros = range(micro_count)
    dec = decoder.astype(jnp.int32)

    def gathered(shard):
        return lax.all_gather(shard, "fsdp", axis=0, axis_index_groups=Z_LINES)

    grads = out_grad.reshape(row_count, feature_width)
    columns = 2 * (4 * core + jnp.arange(4, dtype=jnp.int32)) + 1 - half
    came = lax.ppermute(picked(grads, columns, shard_rows), BOTH, DEC_SWAP)
    twin = lax.ppermute(came, "segment", CORE_SWAP)

    own = (
        queries.reshape(flat),
        enc_keys.reshape(flat),
        enc_values.reshape(flat),
        key_mask.reshape(micro_count, 1, seq_length),
    )
    came_near = tuple(lax.ppermute(value, BOTH, ENC_SWAP) for value in own)

    first = gathered(weights[0, 0])
    first, second_shard, came_near, came, twin = lax.optimization_barrier(
        (first, weights[0, 1], came_near, came, twin)
    )
    second = gathered(second_shard)
    near = [jnp.where(decoder, mine, other) for mine, other in zip(own, came_near)]

    first_rows = first.reshape(8 * shard_rows, local_width)
    far = [
        lax.ppermute(
            far_partial(core[None], came, twin, first_rows, micro, seq_length), BOTH, DEC_SWAP
        )
        for micro in micros
    ]
    own_partial = near_partial(half[None], grads, first_rows)
    ctx, ctx_near, ctx_own = [], [], []
    for micro in micros:
        part = far[micro]
        if micro > 0:
            part, ctx[-1] = lax.optimization_barrier((part, ctx[-1]))
        ctx.append((own_partial[micro] + part.astype(F32)).astype(BF16))
        ctx_near.append(lax.ppermute(ctx[micro], BOTH, DEC_TO_ENC))
        ctx_own.append(lax.ppermute(ctx_near[micro], BOTH, ENC_SWAP))

    near_flags = jnp.stack([dec, 1 - dec, dec])
    own_flags = jnp.stack([0 * dec, 1 - dec, 0 * dec])

    def attended(flags, held, sent, operands):
        grads = []
        for micro in micros:
            came = sent[micro]
            if micro > 0:
                came, grads[-1] = lax.optimization_barrier((came, grads[-1]))
            grads.append(attend(flags, held[micro], came, *operands, micro))
        return zip(*grads)

    dq, dk, dv = attended(near_flags, ctx, ctx_near, near)
    far_dq = []
    for micro in micros:
        far_dq.append(lax.ppermute(dq[micro], BOTH, DEC_SWAP))
    _, own_dk, own_dv = attended(own_flags, ctx, ctx_own, own)

    places = 2 * ((chip + jnp.array(STEPS, jnp.int32)) % 4)
    keep_at, give_at = places + core, places + 1 - core

    second, own_dk, own_dv = lax.optimization_barrier((second, own_dk, own_dv))

    def chip_sums(grads):
        give = projected(give_at, dec[None], grads, first, second)
        other = lax.ppermute(give, "segment", CORE_SWAP)
        return projected(keep_at, dec[None], grads, first, second, other)

    def reduced(blocks, result):
        for step, block in zip(STEPS, blocks):
            pairs = [(2 * x + k, 2 * ((x + step) % 4) + k) for x in range(4) for k in range(2)]
            other = lax.ppermute(block, "segment", pairs)
            result = result + other.astype(F32)
        return result.astype(BF16)

    *blocks, block = chip_sums((*far_dq, *dk, *dv))
    own_grads, blocks = lax.optimization_barrier(((*dq, *own_dk, *own_dv), blocks))
    from_partner = lax.ppermute(reduced(blocks, block), "fsdp", HALF_SWAP)
    *blocks, block = chip_sums(own_grads)
    own_out = reduced(blocks, block)
    result = jnp.where(
        half == 0,
        jnp.concatenate([own_out, from_partner], axis=1),
        jnp.concatenate([from_partner, own_out], axis=1),
    )
    return result.reshape(1, micro_count, reaction_count, seq_length, 2 * shard_rows)


def solution(mesh):
    return jax.shard_map(
        per_device,
        mesh=mesh,
        in_specs=(
            P(None, "fsdp", None, None),
            P(None, "fsdp", None, "segment"),
            P(None, "fsdp", None, "segment"),
            P(None, "fsdp", None, "segment"),
            P(None, "fsdp", None),
            P("section", None, "fsdp", "segment"),
        ),
        out_specs=P("section", None, "fsdp", None, "segment"),
        check_vma=False,
    )
```

time: 565 us -> 235 us (0.42)
  waiting for transfers between devices: 509 us -> 73.4 us
  Pallas kernels: 0 us -> 87.3 us
  starting transfers between devices: 2.62 us -> 39.4 us
  matrix products: 24.2 us -> 0 us
  other arithmetic: 0 us -> 11.6 us
  local copies, waits for them, and re-layouts: 16.2 us -> 8.79 us
    all_gather x1 -> x2, waiting for transfers between devices: 399 us -> 0.01 us  [gathered(): return lax.all_gather(shard, 'fsdp', axis=0, axis_index_groups=Z_LINES)]
    pallas_call x0 -> x12, Pallas kernels: none -> 87.3 us  [the longest x4 35.8 us: projected(): pl.pallas_call(kernel, grid_spec=pltpu.PrefetchScalarGridSpec(num_scalar_...]
    reduce_scatter x1 -> x0, waiting for transfers between devices: 49.6 us -> none  [per_device(): lax.psum_scatter(partial_sum.astype(jnp.bfloat16), 'segment', scatter_dim...]
    ppermute x2 -> x23, starting transfers between devices: 2.58 us -> 39.4 us  [the longest x4 10.6 us: per_device(): came_near = tuple((lax.ppermute(value, BOTH, ENC_SWAP) for value in own))]
    dot_general x2 -> x0, matrix products: 24.2 us -> none  [project(): lax.dot_general(grad_rows, weight_cols, (((1,), (1,)), ((), ())), preferr...]
    ppermute x2 -> x23, waiting for transfers between devices: 59.9 us -> 73.3 us  [the longest x4 44.1 us: per_device(): came_near = tuple((lax.ppermute(value, BOTH, ENC_SWAP) for value in own))]
    squeeze x1, local copies, waits for them, and re-layouts: 14.6 us -> 2.32 us  [per_device(): weights[0, 1]]
    unnamed x4 -> x46, local copies, waits for them, and re-layouts: 0.01 us -> 6.48 us
  transfers between devices with their start and end apart: 4 -> 25, of which waited for: 4 -> 6; matrix products, arithmetic and copies ran while one was open for 0% -> 4% of each run, Pallas kernels for 0% -> 26%
where the time goes in v1:
time: 235 us; the launch traced here: 234 us
  Pallas kernels  87.3 us (37%)
  waiting for transfers between devices  73.4 us (31%)
  starting transfers between devices  39.4 us (17%)
  between operations  13.8 us (6%)
  other arithmetic  11.6 us (5%)
  local copies, waits for them, and re-layouts  8.79 us (4%)
    ppermute x4, waiting for transfers between devices, per_device(): came_near = tuple((lax.ppermute(value, BOTH, ENC_SWAP) for value in own))  44.1 us
    pallas_call x4, Pallas kernels, projected(): pl.pallas_call(kernel, grid_spec=pltpu.PrefetchScalarGridSpec(num_scalar_...  35.8 us
    pallas_call x4, Pallas kernels, attend(): pl.pallas_call(functools.partial(attend_kernel, heads), grid_spec=pltpu.P...  28.7 us
    ppermute x6, waiting for transfers between devices, reduced(): other = lax.ppermute(block, 'segment', pairs)  17.8 us
    pallas_call x2, Pallas kernels, far_partial(): pl.pallas_call(far_kernel, grid_spec=pltpu.PrefetchScalarGridSpec(num_sca...  11.1 us
    ppermute x4, starting transfers between devices, per_device(): came_near = tuple((lax.ppermute(value, BOTH, ENC_SWAP) for value in own))  10.6 us
    ppermute x2, waiting for transfers between devices, per_device(): ctx_near.append(lax.ppermute(ctx[micro], BOTH, DEC_TO_ENC))  8.72 us
    ppermute x6, starting transfers between devices, reduced(): other = lax.ppermute(block, 'segment', pairs)  8.63 us
  transfers between devices with their start and end apart: 25, of which 6 were waited for; matrix products, arithmetic and copies ran while one was open for 4% of the time, Pallas kernels for 26%

profile of v1, /device:TPU:1, one launch (start us, length us, event | category | flops | bytes accessed | tf_op | source)
XLA Modules:
  0.0 234.3 jit_solution(13541333102814727885)
XLA Ops:
  6.5 2.3 slice_bitcast_fusion
  9.5 4.5 %pick.1 = bf16[512,1536]{1,0:T(8,128)(2,1)} custom-call(s32[4]{0:T(128)} %add_subtract_fusion.1.where, bf16[512,6144]{1,0:T(8,128)(2,1)} %bitcast.33), custom_call_target="tpu_custom_call" | custom-call | bytes 3145728 | tf_op jit(solution)/shard_map/pick/pallas_call | solution.py:43
  14.0 0.7 collective-permute-start.4
  14.8 3.3 %collective-permute-start.5 = (bf16[512,1536]{1,0:T(8,128)(2,1)S(1)}, bf16[512,1536]{1,0:T(8,128)(2,1)}, u32[]{:S(2)}, u32[]{:S(2)}) collective-permute-start(bf16[512,1536]{1,0:T(8,128)(2,1)S(1)} %collective-permute-done.4.came), channel_id=1, source_target_pairs={{0,16},{16,0},{32,48},{48,32},{64,80},{80,64},{96,112},{112,96},{1... | collective-permute-start | bytes 4718600 | tf_op jit(solution)/shard_map/ppermute | solution.py:270
  18.1 1.9 collective-permute-start
  20.0 3.4 %collective-permute-start.1 = (bf16[2,256,768]{2,1,0:T(8,128)(2,1)S(1)}, bf16[2,256,768]{2,1,0:T(8,128)(2,1)S(1)}, u32[]{:S(2)}, u32[]{:S(2)}) collective-permute-start(bf16[2,256,768]{2,1,0:T(8,128)(2,1)S(1)} %bitcast.44), channel_id=1, source_target_pairs={{0,1},{1,0},{2,3},{3,2},{4,5},{5,4},{6,7},{7,6},{8,9},{9,8},{10,11... | collective-permute-start | bytes 2359304 | tf_op jit(solution)/shard_map/ppermute | solution.py:278
  23.4 1.9 collective-permute-start.2
  25.3 3.4 %collective-permute-start.3 = (s32[2,1,256]{2,1,0:T(1,128)S(1)}, s32[2,1,256]{2,1,0:T(1,128)S(1)}, u32[]{:S(2)}, u32[]{:S(2)}) collective-permute-start(s32[2,1,256]{2,1,0:T(1,128)S(1)} %copy-done.21), channel_id=1, source_target_pairs={{0,1},{1,0},{2,3},{3,2},{4,5},{5,4},{6,7},{7,6},{8,9},{9,8},{10,11... | collective-permute-start | bytes 6152 | tf_op jit(solution)/shard_map/ppermute | solution.py:278
  28.7 44.1 %collective-permute-done.3 = s32[2,1,256]{2,1,0:T(1,128)S(1)} collective-permute-done((s32[2,1,256]{2,1,0:T(1,128)S(1)}, s32[2,1,256]{2,1,0:T(1,128)S(1)}, u32[]{:S(2)}, u32[]{:S(2)}) %collective-permute-start.3) | collective-permute-done | bytes 2080 | tf_op jit(solution)/shard_map/ppermute | solution.py:278
  72.8 0.9 copy-done.13
  73.7 0.9 copy-done.11
  75.3 5.6 %far.2 = bf16[256,768]{1,0:T(8,128)(2,1)} custom-call(s32[1]{0:T(128)} %bitcast.9.core, bf16[512,1536]{1,0:T(8,128)(2,1)} %copy-done.3, bf16[512,1536]{1,0:T(8,128)(2,1)} %collective-permute-done.5.twin, bf16[3072,768]{1,0:T(8,128)(2,1)} %bitcast.22), custom_call_target="tpu_custom_call" | custom-call | flops 1207959552 | bytes 4718592 | tf_op jit(solution)/shard_map/far/pallas_call | solution.py:76
  81.5 5.6 %far.3 = bf16[256,768]{1,0:T(8,128)(2,1)} custom-call(s32[1]{0:T(128)} %bitcast.9.core, bf16[512,1536]{1,0:T(8,128)(2,1)} %copy-done.3, bf16[512,1536]{1,0:T(8,128)(2,1)} %collective-permute-done.5.twin, bf16[3072,768]{1,0:T(8,128)(2,1)} %bitcast.23), custom_call_target="tpu_custom_call" | custom-call | flops 1207959552 | bytes 4718592 | tf_op jit(solution)/shard_map/far/pallas_call | solution.py:76
  87.1 1.4 collective-permute-start.7
  88.5 2.1 broadcast_select_fusion.2.query
  90.6 7.1 %near.1 = (f32[256,768]{1,0:T(8,128)}, f32[256,768]{1,0:T(8,128)}) custom-call(s32[1]{0:T(128)} %bitcast.1.half, bf16[512,6144]{1,0:T(8,128)(2,1)} %bitcast.34, bf16[512,6144]{1,0:T(8,128)(2,1)} %bitcast.35, bf16[3072,768]{1,0:T(8,128)(2,1)} %bitcast.24), custom_call_target="tpu_custom_call" | custom-call | flops 2415919104 | bytes 4718592 | tf_op jit(solution)/shard_map/near/pallas_call | solution.py:110
  97.7 1.4 add_convert_fusion.3.held
  99.1 1.3 collective-permute-start.9
  100.6 1.3 collective-permute-start.8
  102.4 1.3 broadcast_select_fusion
  103.7 8.7 %collective-permute-done.9.sent = bf16[256,768]{1,0:T(8,128)(2,1)S(1)} collective-permute-done((bf16[256,768]{1,0:T(8,128)(2,1)S(1)}, bf16[256,768]{1,0:T(8,128)(2,1)S(1)}, u32[]{:S(2)}, u32[]{:S(2)}) %collective-permute-start.9) | collective-permute-done | bytes 393248 | tf_op jit(solution)/shard_map/ppermute | solution.py:301
  112.4 1.9 collective-permute-start.11
  114.4 7.2 %attend.4 = (bf16[256,768]{1,0:T(8,128)(2,1)}, bf16[256,768]{1,0:T(8,128)(2,1)}, bf16[256,768]{1,0:T(8,128)(2,1)}) custom-call(s32[3]{0:T(128)} %pad_add_fusion.flags, bf16[256,768]{1,0:T(8,128)(2,1)} %copy-done.4, bf16[256,768]{1,0:T(8,128)(2,1)} %copy-done.17, bf16[2,256,768]{2,1,0:T(8,128)(2,1)} %broadcast_select_fusion.2.query, ...), custom_call_target="tpu_custom_call" | custom-call | flops 503316480 | bytes 3145728 | tf_op jit(solution)/shard_map/attend/pallas_call | solution.py:162
  121.6 3.5 %collective-permute-start.10 = (bf16[256,768]{1,0:T(8,128)(2,1)S(1)}, bf16[256,768]{1,0:T(8,128)(2,1)S(1)}, u32[]{:S(2)}, u32[]{:S(2)}) collective-permute-start(bf16[256,768]{1,0:T(8,128)(2,1)S(1)} %collective-permute-done.8.sent), channel_id=1, source_target_pairs={{0,1},{1,0},{2,3},{3,2},{4,5},{5,4},{6,7},{7,6},{8,9},{9,8},{10,11... | collective-permute-start | bytes 1179656 | tf_op jit(solution)/shard_map/ppermute | solution.py:302
  125.1 7.2 %attend.5 = (bf16[256,768]{1,0:T(8,128)(2,1)}, bf16[256,768]{1,0:T(8,128)(2,1)}, bf16[256,768]{1,0:T(8,128)(2,1)}) custom-call(s32[3]{0:T(128)} %pad_add_fusion.flags, bf16[256,768]{1,0:T(8,128)(2,1)} %copy-done.5, bf16[256,768]{1,0:T(8,128)(2,1)} %copy-done.18, bf16[2,256,768]{2,1,0:T(8,128)(2,1)} %broadcast_select_fusion.2.query, ...), custom_call_target="tpu_custom_call" | custom-call | flops 503316480 | bytes 3145728 | tf_op jit(solution)/shard_map/attend/pallas_call | solution.py:162
  133.0 0.7 collective-permute-start.12
  134.9 0.7 copy-done.19
  135.7 7.1 %attend.6 = (bf16[256,768]{1,0:T(8,128)(2,1)}, bf16[256,768]{1,0:T(8,128)(2,1)}, bf16[256,768]{1,0:T(8,128)(2,1)}) custom-call(s32[3]{0:T(128)} %pad_add_fusion.1.flags, bf16[256,768]{1,0:T(8,128)(2,1)} %copy-done.4, bf16[256,768]{1,0:T(8,128)(2,1)} %copy-done.19, bf16[2,256,768]{2,1,0:T(8,128)(2,1)} %bitcast.36, bf16[2,256,768]{2,1,0:T(8,128)(2,1)} %bitcast.42, ...), custom_call_target="tpu_custom_call" | custom-call | flops 503316480 | bytes 3145728 | tf_op jit(solution)/shard_map/attend/pallas_call | solution.py:162
  142.8 0.7 copy-done.20
  143.6 7.1 %attend.7 = (bf16[256,768]{1,0:T(8,128)(2,1)}, bf16[256,768]{1,0:T(8,128)(2,1)}, bf16[256,768]{1,0:T(8,128)(2,1)}) custom-call(s32[3]{0:T(128)} %pad_add_fusion.1.flags, bf16[256,768]{1,0:T(8,128)(2,1)} %copy-done.5, bf16[256,768]{1,0:T(8,128)(2,1)} %copy-done.20, bf16[2,256,768]{2,1,0:T(8,128)(2,1)} %bitcast.37, bf16[2,256,768]{2,1,0:T(8,128)(2,1)} %bitcast.43, ...), custom_call_target="tpu_custom_call" | custom-call | flops 503316480 | bytes 3145728 | tf_op jit(solution)/shard_map/attend/pallas_call | solution.py:162
  150.7 0.7 copy-done.9
  151.6 8.4 %shard_map.73 = bf16[4,512,384]{2,1,0:T(8,128)(2,1)} custom-call(s32[4]{0:T(128)} %get-tuple-element.107.at, s32[1]{0:T(128)} %bitcast.flags, bf16[256,768]{1,0:T(8,128)(2,1)} %copy-done.10, bf16[256,768]{1,0:T(8,128)(2,1)} %copy-done.9, bf16[256,768]{1,0:T(8,128)(2,1)} %get-tuple-element.85.k0, bf16[256,768]{1,0:T(8,128)(2,1)} %get-tuple-element.86.k1, ...), custom_call_target="tpu_custom_call" | custom-call | flops 2415919104 | bytes 4718592 | tf_op jit(solution)/shard_map/pallas_call | solution.py:237
  160.1 4.4 %collective-permute-start.14 = (bf16[4,512,384]{2,1,0:T(8,128)(2,1)}, bf16[4,512,384]{2,1,0:T(8,128)(2,1)S(1)}, u32[]{:S(2)}, u32[]{:S(2)}) collective-permute-start(bf16[4,512,384]{2,1,0:T(8,128)(2,1)} %shard_map.73), channel_id=1, source_target_pairs={{0,16},{16,0},{32,48},{48,32},{64,80},{80,64},{96,112},{112,96},{1... | collective-permute-start | bytes 4718600 | tf_op jit(solution)/shard_map/ppermute | solution.py:329
  165.0 2.7 %collective-permute-done.14.other = bf16[4,512,384]{2,1,0:T(8,128)(2,1)S(1)} collective-permute-done((bf16[4,512,384]{2,1,0:T(8,128)(2,1)}, bf16[4,512,384]{2,1,0:T(8,128)(2,1)S(1)}, u32[]{:S(2)}, u32[]{:S(2)}) %collective-permute-start.14) | collective-permute-done | bytes 1572896 | tf_op jit(solution)/shard_map/ppermute | solution.py:329
  167.7 1.1 copy-done.7
  168.9 9.5 %shard_map.74 = (bf16[512,384]{1,0:T(8,128)(2,1)}, bf16[512,384]{1,0:T(8,128)(2,1)}, bf16[512,384]{1,0:T(8,128)(2,1)}, f32[512,384]{1,0:T(8,128)}) custom-call(s32[4]{0:T(128)} %broadcast_add_fusion.at, s32[1]{0:T(128)} %bitcast.flags, bf16[256,768]{1,0:T(8,128)(2,1)} %copy-done.10, bf16[256,768]{1,0:T(8,128)(2,1)} %copy-done.9, ...), custom_call_target="tpu_custom_call" | custom-call | flops 2415919104 | bytes 4718592 | tf_op jit(solution)/shard_map/pallas_call | solution.py:237
  178.3 8.4 %shard_map.75 = bf16[4,512,384]{2,1,0:T(8,128)(2,1)} custom-call(s32[4]{0:T(128)} %get-tuple-element.107.at, s32[1]{0:T(128)} %bitcast.flags, bf16[256,768]{1,0:T(8,128)(2,1)} %get-tuple-element.93.q0, bf16[256,768]{1,0:T(8,128)(2,1)} %get-tuple-element.94.q1, bf16[256,768]{1,0:T(8,128)(2,1)} %get-tuple-element.95.k0, ...), custom_call_target="tpu_custom_call" | custom-call | flops 2415919104 | bytes 4718592 | tf_op jit(solution)/shard_map/pallas_call | solution.py:237
  187.1 2.7 %collective-permute-start.19 = (bf16[512,384]{1,0:T(8,128)(2,1)}, bf16[512,384]{1,0:T(8,128)(2,1)S(1)}, u32[]{:S(2)}, u32[]{:S(2)}) collective-permute-start(bf16[512,384]{1,0:T(8,128)(2,1)} %get-tuple-element.104), channel_id=1, source_target_pairs={{0,64},{16,80},{32,96},{48,112},{64,0},{80,16},{96,32},{112,48},{1... | collective-permute-start | bytes 1179656 | tf_op jit(solution)/shard_map/ppermute | solution.py:335
  190.1 2.4 %collective-permute-start.21 = (bf16[512,384]{1,0:T(8,128)(2,1)}, bf16[512,384]{1,0:T(8,128)(2,1)S(1)}, u32[]{:S(2)}, u32[]{:S(2)}) collective-permute-start(bf16[512,384]{1,0:T(8,128)(2,1)} %get-tuple-element.106), channel_id=1, source_target_pairs={{0,96},{16,112},{32,0},{48,16},{64,32},{80,48},{96,64},{112,80},{1... | collective-permute-start | bytes 1179656 | tf_op jit(solution)/shard_map/ppermute | solution.py:335
  192.5 1.1 copy-done.6
  193.7 9.5 %shard_map.76 = (bf16[512,384]{1,0:T(8,128)(2,1)}, bf16[512,384]{1,0:T(8,128)(2,1)}, bf16[512,384]{1,0:T(8,128)(2,1)}, f32[512,384]{1,0:T(8,128)}) custom-call(s32[4]{0:T(128)} %broadcast_add_fusion.at, s32[1]{0:T(128)} %bitcast.flags, bf16[256,768]{1,0:T(8,128)(2,1)} %get-tuple-element.93.q0, bf16[256,768]{1,0:T(8,128)(2,1)} %get-tuple-element.94.q1, ...), custom_call_target="tpu_custom_call" | custom-call | flops 2415919104 | bytes 4718592 | tf_op jit(solution)/shard_map/pallas_call | solution.py:237
  204.0 2.4 %collective-permute-start.18 = (bf16[512,384]{1,0:T(8,128)(2,1)}, bf16[512,384]{1,0:T(8,128)(2,1)}, u32[]{:S(2)}, u32[]{:S(2)}) collective-permute-start(bf16[512,384]{1,0:T(8,128)(2,1)} %get-tuple-element.102), channel_id=1, source_target_pairs={{0,96},{16,112},{32,0},{48,16},{64,32},{80,48},{96,64},{112,80},{1... | collective-permute-start | bytes 1179656 | tf_op jit(solution)/shard_map/ppermute | solution.py:335
  206.4 2.4 %collective-permute-done.20 = bf16[512,384]{1,0:T(8,128)(2,1)S(1)} collective-permute-done((bf16[512,384]{1,0:T(8,128)(2,1)}, bf16[512,384]{1,0:T(8,128)(2,1)S(1)}, u32[]{:S(2)}, u32[]{:S(2)}) %collective-permute-start.20) | collective-permute-done | bytes 393248 | tf_op jit(solution)/shard_map/ppermute | solution.py:335
  208.8 0.9 add_convert_fusion
  209.7 6.6 %collective-permute-done.16 = bf16[512,384]{1,0:T(8,128)(2,1)S(1)} collective-permute-done((bf16[512,384]{1,0:T(8,128)(2,1)}, bf16[512,384]{1,0:T(8,128)(2,1)S(1)}, u32[]{:S(2)}, u32[]{:S(2)}) %collective-permute-start.16) | collective-permute-done | bytes 393248 | tf_op jit(solution)/shard_map/ppermute | solution.py:335
  216.3 8.9 %collective-permute-done.17 = bf16[512,384]{1,0:T(8,128)(2,1)S(1)} collective-permute-done((bf16[512,384]{1,0:T(8,128)(2,1)}, bf16[512,384]{1,0:T(8,128)(2,1)S(1)}, u32[]{:S(2)}, u32[]{:S(2)}) %collective-permute-start.17) | collective-permute-done | bytes 393248 | tf_op jit(solution)/shard_map/ppermute | solution.py:335
  225.2 1.2 add_convert_fusion.1
  226.4 1.1 maximum_select_fusion
  (76 shorter events, 6.8 us)
Async XLA Ops:
  6.5 68.0 %all-gather.5.cloned.1.call-start = ((), (), s32[]{:S(2)}) async-start(), calls=%async_computation | async-start | bytes 5308416 | tf_op jit(solution)/shard_map/all_gather | solution.py:265
  8.9 141.8 %all-gather.7.cloned.1.call-start = ((), (), s32[]{:S(2)}) async-start(), calls=%async_computation.1 | async-start | bytes 5308416 | tf_op jit(solution)/shard_map/all_gather | solution.py:265
  9.5 8.6 %copy-start = (bf16[2,1,256,768]{3,2,1,0:T(8,128)(2,1)S(1)}, bf16[2,1,256,768]{3,2,1,0:T(8,128)(2,1)}, u32[]{:S(2)}) copy-start(bf16[2,1,256,768]{3,2,1,0:T(8,128)(2,1)} %param.8) | copy-start | bytes 2359300
  9.5 10.5 %copy-start.2 = (bf16[2,1,256,768]{3,2,1,0:T(8,128)(2,1)S(1)}, bf16[2,1,256,768]{3,2,1,0:T(8,128)(2,1)}, u32[]{:S(2)}) copy-start(bf16[2,1,256,768]{3,2,1,0:T(8,128)(2,1)} %param.9) | copy-start | bytes 2359300
  9.5 13.9 %copy-start.1 = (bf16[2,1,256,768]{3,2,1,0:T(8,128)(2,1)S(1)}, bf16[2,1,256,768]{3,2,1,0:T(8,128)(2,1)}, u32[]{:S(2)}) copy-start(bf16[2,1,256,768]{3,2,1,0:T(8,128)(2,1)} %param.10) | copy-start | bytes 2359300
  9.5 15.9 %copy-start.21 = (s32[2,1,256]{2,1,0:T(1,128)S(1)}, s32[2,1,256]{2,1,0:T(1,128)}, u32[]{:S(2)}) copy-start(s32[2,1,256]{2,1,0:T(1,128)} %mask.3) | copy-start | bytes 6148
  14.0 0.8 collective-permute-start.4
  14.8 58.0 %copy-start.3 = (bf16[512,1536]{1,0:T(8,128)(2,1)}, bf16[512,1536]{1,0:T(8,128)(2,1)S(1)}, u32[]{:S(2)}) copy-start(bf16[512,1536]{1,0:T(8,128)(2,1)S(1)} %collective-permute-done.4.came) | copy-start | bytes 4718596
  14.8 59.8 %collective-permute-start.5 = (bf16[512,1536]{1,0:T(8,128)(2,1)S(1)}, bf16[512,1536]{1,0:T(8,128)(2,1)}, u32[]{:S(2)}, u32[]{:S(2)}) collective-permute-start(bf16[512,1536]{1,0:T(8,128)(2,1)S(1)} %collective-permute-done.4.came), channel_id=1, source_target_pairs={{0,16},{16,0},{32,48},{48,32},{64,80},{80,64},{96,112},{112,96},{1... | collective-permute-start | bytes 4718600 | tf_op jit(solution)/shard_map/ppermute | solution.py:270
  18.1 54.7 %collective-permute-start = (bf16[2,256,768]{2,1,0:T(8,128)(2,1)S(1)}, bf16[2,256,768]{2,1,0:T(8,128)(2,1)S(1)}, u32[]{:S(2)}, u32[]{:S(2)}) collective-permute-start(bf16[2,256,768]{2,1,0:T(8,128)(2,1)S(1)} %bitcast.38), channel_id=1, source_target_pairs={{0,1},{1,0},{2,3},{3,2},{4,5},{5,4},{6,7},{7,6},{8,9},{9,8},{10,11... | collective-permute-start | bytes 2359304 | tf_op jit(solution)/shard_map/ppermute | solution.py:278
  20.0 52.8 %collective-permute-start.1 = (bf16[2,256,768]{2,1,0:T(8,128)(2,1)S(1)}, bf16[2,256,768]{2,1,0:T(8,128)(2,1)S(1)}, u32[]{:S(2)}, u32[]{:S(2)}) collective-permute-start(bf16[2,256,768]{2,1,0:T(8,128)(2,1)S(1)} %bitcast.44), channel_id=1, source_target_pairs={{0,1},{1,0},{2,3},{3,2},{4,5},{5,4},{6,7},{7,6},{8,9},{9,8},{10,11... | collective-permute-start | bytes 2359304 | tf_op jit(solution)/shard_map/ppermute | solution.py:278
  23.4 49.4 %collective-permute-start.2 = (bf16[2,256,768]{2,1,0:T(8,128)(2,1)S(1)}, bf16[2,256,768]{2,1,0:T(8,128)(2,1)S(1)}, u32[]{:S(2)}, u32[]{:S(2)}) collective-permute-start(bf16[2,256,768]{2,1,0:T(8,128)(2,1)S(1)} %bitcast.41), channel_id=1, source_target_pairs={{0,1},{1,0},{2,3},{3,2},{4,5},{5,4},{6,7},{7,6},{8,9},{9,8},{10,11... | collective-permute-start | bytes 2359304 | tf_op jit(solution)/shard_map/ppermute | solution.py:278
  25.3 47.5 %collective-permute-start.3 = (s32[2,1,256]{2,1,0:T(1,128)S(1)}, s32[2,1,256]{2,1,0:T(1,128)S(1)}, u32[]{:S(2)}, u32[]{:S(2)}) collective-permute-start(s32[2,1,256]{2,1,0:T(1,128)S(1)} %copy-done.21), channel_id=1, source_target_pairs={{0,1},{1,0},{2,3},{3,2},{4,5},{5,4},{6,7},{7,6},{8,9},{9,8},{10,11... | collective-permute-start | bytes 6152 | tf_op jit(solution)/shard_map/ppermute | solution.py:278
  72.8 0.9 copy-start.13
  73.7 0.9 copy-start.11
  80.8 19.6 %collective-permute-start.6 = (bf16[256,768]{1,0:T(8,128)(2,1)}, bf16[256,768]{1,0:T(8,128)(2,1)S(1)}, u32[]{:S(2)}, u32[]{:S(2)}) collective-permute-start(bf16[256,768]{1,0:T(8,128)(2,1)} %far.2), channel_id=1, source_target_pairs={{128,129},{129,128},{130,131},{131,130},{132,133},{133,132},{134,1... | collective-permute-start | bytes 1179656 | tf_op jit(solution)/shard_map/ppermute | solution.py:289
  87.1 10.6 %collective-permute-start.7 = (bf16[256,768]{1,0:T(8,128)(2,1)}, bf16[256,768]{1,0:T(8,128)(2,1)}, u32[]{:S(2)}, u32[]{:S(2)}) collective-permute-start(bf16[256,768]{1,0:T(8,128)(2,1)} %far.3), channel_id=1, source_target_pairs={{128,129},{129,128},{130,131},{131,130},{132,133},{133,132},{134,1... | collective-permute-start | bytes 1179656 | tf_op jit(solution)/shard_map/ppermute | solution.py:289
  97.7 2.8 %copy-start.14 = (f32[256,768]{1,0:T(8,128)S(1)}, f32[256,768]{1,0:T(8,128)}, u32[]{:S(2)}) copy-start(f32[256,768]{1,0:T(8,128)} %get-tuple-element.57) | copy-start | bytes 2359300
  97.7 4.8 %copy-start.12 = (bf16[2,256,768]{2,1,0:T(8,128)(2,1)S(1)}, bf16[2,256,768]{2,1,0:T(8,128)(2,1)}, u32[]{:S(2)}) copy-start(bf16[2,256,768]{2,1,0:T(8,128)(2,1)} %copy-done.11) | copy-start | bytes 2359300
  99.1 4.6 %copy-start.4 = (bf16[256,768]{1,0:T(8,128)(2,1)}, bf16[256,768]{1,0:T(8,128)(2,1)S(1)}, u32[]{:S(2)}) copy-start(bf16[256,768]{1,0:T(8,128)(2,1)S(1)} %add_convert_fusion.3.held) | copy-start | bytes 1179652
  99.1 13.3 %collective-permute-start.9 = (bf16[256,768]{1,0:T(8,128)(2,1)S(1)}, bf16[256,768]{1,0:T(8,128)(2,1)S(1)}, u32[]{:S(2)}, u32[]{:S(2)}) collective-permute-start(bf16[256,768]{1,0:T(8,128)(2,1)S(1)} %add_convert_fusion.3.held), channel_id=1, source_target_pairs={{128,1},{129,0},{130,3},{131,2},{132,5},{133,4},{134,7},{135,6},{1... | collective-permute-start | bytes 1179656 | tf_op jit(solution)/shard_map/ppermute | solution.py:301
  100.5 3.2 %copy-start.5 = (bf16[256,768]{1,0:T(8,128)(2,1)}, bf16[256,768]{1,0:T(8,128)(2,1)S(1)}, u32[]{:S(2)}) copy-start(bf16[256,768]{1,0:T(8,128)(2,1)S(1)} %add_convert_fusion.2.held) | copy-start | bytes 1179652
  100.6 21.0 %collective-permute-start.8 = (bf16[256,768]{1,0:T(8,128)(2,1)S(1)}, bf16[256,768]{1,0:T(8,128)(2,1)S(1)}, u32[]{:S(2)}, u32[]{:S(2)}) collective-permute-start(bf16[256,768]{1,0:T(8,128)(2,1)S(1)} %add_convert_fusion.2.held), channel_id=1, source_target_pairs={{128,1},{129,0},{130,3},{131,2},{132,5},{133,4},{134,7},{135,6},{1... | collective-permute-start | bytes 1179656 | tf_op jit(solution)/shard_map/ppermute | solution.py:301
  112.4 1.9 copy-start.17
  112.4 22.5 %collective-permute-start.11 = (bf16[256,768]{1,0:T(8,128)(2,1)S(1)}, bf16[256,768]{1,0:T(8,128)(2,1)S(1)}, u32[]{:S(2)}, u32[]{:S(2)}) collective-permute-start(bf16[256,768]{1,0:T(8,128)(2,1)S(1)} %collective-permute-done.9.sent), channel_id=1, source_target_pairs={{0,1},{1,0},{2,3},{3,2},{4,5},{5,4},{6,7},{7,6},{8,9},{9,8},{10,11... | collective-permute-start | bytes 1179656 | tf_op jit(solution)/shard_map/ppermute | solution.py:302
  121.6 3.5 %copy-start.18 = (bf16[256,768]{1,0:T(8,128)(2,1)}, bf16[256,768]{1,0:T(8,128)(2,1)S(1)}, u32[]{:S(2)}) copy-start(bf16[256,768]{1,0:T(8,128)(2,1)S(1)} %collective-permute-done.8.sent) | copy-start | bytes 1179652
  121.6 11.4 %copy-start.8 = (bf16[256,768]{1,0:T(8,128)(2,1)S(1)}, bf16[256,768]{1,0:T(8,128)(2,1)}, u32[]{:S(2)}) copy-start(bf16[256,768]{1,0:T(8,128)(2,1)} %get-tuple-element.93.q0) | copy-start | bytes 1179652
  121.6 12.7 %copy-start.22 = (s32[4]{0:T(128)S(1)}, s32[4]{0:T(128)}, u32[]{:S(2)}) copy-start(s32[4]{0:T(128)} %constant.64.clone) | copy-start | bytes 52
  121.6 21.2 %collective-permute-start.10 = (bf16[256,768]{1,0:T(8,128)(2,1)S(1)}, bf16[256,768]{1,0:T(8,128)(2,1)S(1)}, u32[]{:S(2)}, u32[]{:S(2)}) collective-permute-start(bf16[256,768]{1,0:T(8,128)(2,1)S(1)} %collective-permute-done.8.sent), channel_id=1, source_target_pairs={{0,1},{1,0},{2,3},{3,2},{4,5},{5,4},{6,7},{7,6},{8,9},{9,8},{10,11... | collective-permute-start | bytes 1179656 | tf_op jit(solution)/shard_map/ppermute | solution.py:302
  132.3 18.4 %collective-permute-start.13 = (bf16[256,768]{1,0:T(8,128)(2,1)}, bf16[256,768]{1,0:T(8,128)(2,1)S(1)}, u32[]{:S(2)}, u32[]{:S(2)}) collective-permute-start(bf16[256,768]{1,0:T(8,128)(2,1)} %get-tuple-element.94.q1), channel_id=1, source_target_pairs={{128,129},{129,128},{130,131},{131,130},{132,133},{133,132},{134,1... | collective-permute-start | bytes 1179656 | tf_op jit(solution)/shard_map/ppermute | solution.py:319
  133.0 17.7 %collective-permute-start.12 = (bf16[256,768]{1,0:T(8,128)(2,1)S(1)}, bf16[256,768]{1,0:T(8,128)(2,1)S(1)}, u32[]{:S(2)}, u32[]{:S(2)}) collective-permute-start(bf16[256,768]{1,0:T(8,128)(2,1)S(1)} %copy-done.8), channel_id=1, source_target_pairs={{128,129},{129,128},{130,131},{131,130},{132,133},{133,132},{134,1... | collective-permute-start | bytes 1179656 | tf_op jit(solution)/shard_map/ppermute | solution.py:319
  134.9 0.7 copy-start.19
  142.8 0.7 copy-start.20
  150.7 0.8 copy-start.9
  150.7 0.9 copy-start.10
  160.1 7.6 %collective-permute-start.14 = (bf16[4,512,384]{2,1,0:T(8,128)(2,1)}, bf16[4,512,384]{2,1,0:T(8,128)(2,1)S(1)}, u32[]{:S(2)}, u32[]{:S(2)}) collective-permute-start(bf16[4,512,384]{2,1,0:T(8,128)(2,1)} %shard_map.73), channel_id=1, source_target_pairs={{0,16},{16,0},{32,48},{48,32},{64,80},{80,64},{96,112},{112,96},{1... | collective-permute-start | bytes 4718600 | tf_op jit(solution)/shard_map/ppermute | solution.py:329
  167.7 1.1 copy-start.7
  186.8 22.0 %copy-start.15 = (f32[512,384]{1,0:T(8,128)S(1)}, f32[512,384]{1,0:T(8,128)}, u32[]{:S(2)}) copy-start(f32[512,384]{1,0:T(8,128)} %get-tuple-element.103) | copy-start | bytes 2359300
  186.8 5.7 %collective-permute-start.15 = (bf16[4,512,384]{2,1,0:T(8,128)(2,1)}, bf16[4,512,384]{2,1,0:T(8,128)(2,1)S(1)}, u32[]{:S(2)}, u32[]{:S(2)}) collective-permute-start(bf16[4,512,384]{2,1,0:T(8,128)(2,1)} %shard_map.75), channel_id=1, source_target_pairs={{0,16},{16,0},{32,48},{48,32},{64,80},{80,64},{96,112},{112,96},{1... | collective-permute-start | bytes 4718600 | tf_op jit(solution)/shard_map/ppermute | solution.py:329
  187.1 16.9 %collective-permute-start.19 = (bf16[512,384]{1,0:T(8,128)(2,1)}, bf16[512,384]{1,0:T(8,128)(2,1)S(1)}, u32[]{:S(2)}, u32[]{:S(2)}) collective-permute-start(bf16[512,384]{1,0:T(8,128)(2,1)} %get-tuple-element.104), channel_id=1, source_target_pairs={{0,64},{16,80},{32,96},{48,112},{64,0},{80,16},{96,32},{112,48},{1... | collective-permute-start | bytes 1179656 | tf_op jit(solution)/shard_map/ppermute | solution.py:335
  189.8 19.0 %collective-permute-start.20 = (bf16[512,384]{1,0:T(8,128)(2,1)}, bf16[512,384]{1,0:T(8,128)(2,1)S(1)}, u32[]{:S(2)}, u32[]{:S(2)}) collective-permute-start(bf16[512,384]{1,0:T(8,128)(2,1)} %get-tuple-element.105), channel_id=1, source_target_pairs={{0,32},{16,48},{32,64},{48,80},{64,96},{80,112},{96,0},{112,16},{1... | collective-permute-start | bytes 1179656 | tf_op jit(solution)/shard_map/ppermute | solution.py:335
  190.1 18.7 %collective-permute-start.21 = (bf16[512,384]{1,0:T(8,128)(2,1)}, bf16[512,384]{1,0:T(8,128)(2,1)S(1)}, u32[]{:S(2)}, u32[]{:S(2)}) collective-permute-start(bf16[512,384]{1,0:T(8,128)(2,1)} %get-tuple-element.106), channel_id=1, source_target_pairs={{0,96},{16,112},{32,0},{48,16},{64,32},{80,48},{96,64},{112,80},{1... | collective-permute-start | bytes 1179656 | tf_op jit(solution)/shard_map/ppermute | solution.py:335
  192.5 1.1 copy-start.6
  203.2 22.0 %copy-start.16 = (f32[512,384]{1,0:T(8,128)S(1)}, f32[512,384]{1,0:T(8,128)}, u32[]{:S(2)}) copy-start(f32[512,384]{1,0:T(8,128)} %get-tuple-element.99) | copy-start | bytes 2359300
  203.2 13.2 %collective-permute-start.16 = (bf16[512,384]{1,0:T(8,128)(2,1)}, bf16[512,384]{1,0:T(8,128)(2,1)S(1)}, u32[]{:S(2)}, u32[]{:S(2)}) collective-permute-start(bf16[512,384]{1,0:T(8,128)(2,1)} %get-tuple-element.100), channel_id=1, source_target_pairs={{0,64},{16,80},{32,96},{48,112},{64,0},{80,16},{96,32},{112,48},{1... | collective-permute-start | bytes 1179656 | tf_op jit(solution)/shard_map/ppermute | solution.py:335
  203.7 21.4 %collective-permute-start.17 = (bf16[512,384]{1,0:T(8,128)(2,1)}, bf16[512,384]{1,0:T(8,128)(2,1)S(1)}, u32[]{:S(2)}, u32[]{:S(2)}) collective-permute-start(bf16[512,384]{1,0:T(8,128)(2,1)} %get-tuple-element.101), channel_id=1, source_target_pairs={{0,32},{16,48},{32,64},{48,80},{64,96},{80,112},{96,0},{112,16},{1... | collective-permute-start | bytes 1179656 | tf_op jit(solution)/shard_map/ppermute | solution.py:335
  204.0 21.2 %collective-permute-start.18 = (bf16[512,384]{1,0:T(8,128)(2,1)}, bf16[512,384]{1,0:T(8,128)(2,1)}, u32[]{:S(2)}, u32[]{:S(2)}) collective-permute-start(bf16[512,384]{1,0:T(8,128)(2,1)} %get-tuple-element.102), channel_id=1, source_target_pairs={{0,96},{16,112},{32,0},{48,16},{64,32},{80,48},{96,64},{112,80},{1... | collective-permute-start | bytes 1179656 | tf_op jit(solution)/shard_map/ppermute | solution.py:335
  209.7 16.6 %collective-permute-start.22 = (bf16[512,384]{1,0:T(8,128)(2,1)}, bf16[512,384]{1,0:T(8,128)(2,1)S(1)}, u32[]{:S(2)}, u32[]{:S(2)}) collective-permute-start(bf16[512,384]{1,0:T(8,128)(2,1)} %add_convert_fusion), channel_id=1, source_target_pairs={{0,1},{1,0},{2,3},{3,2},{4,5},{5,4},{6,7},{7,6},{8,9},{9,8},{10,11... | collective-permute-start | bytes 1179656 | tf_op jit(solution)/shard_map/ppermute | solution.py:341
Sparse Core Ops, SparseCore 0:
  9.1 63.2 all-gather.4
  74.7 59.3 all-gather.6

commit v2 on v1

--- a/solution.py
+++ b/solution.py
@@ -54,7 +54,7 @@
     )(columns, source)
 
 
-def far_kernel(core, came, twin, weight, out, acc):
+def far_kernel(core, came, twin, weight, low, high, acc):
     step = pl.program_id(0)
 
     @pl.when(step == 0)
@@ -66,24 +66,27 @@
 
     @pl.when(step == pl.num_programs(0) - 1)
     def _():
-        out[...] = acc[...].astype(BF16)
-
-
-def far_partial(core, came, twin, weight, micro, seq_length):
+        rows = low.shape[0]
+        low[...] = acc[:rows].astype(BF16)
+        high[...] = acc[rows:].astype(BF16)
+
+
+def far_partial(core, came, twin, weight):
+    row_count = came.shape[0]
     depth, width = weight.shape
     piece = depth // 4
-    rows = pl.BlockSpec((seq_length, piece), lambda j, core: (micro, j % 2))
+    rows = pl.BlockSpec((row_count, piece), lambda j, core: (0, j % 2))
     return pl.pallas_call(
         far_kernel,
         grid_spec=pltpu.PrefetchScalarGridSpec(
             num_scalar_prefetch=1,
             grid=(4,),
             in_specs=[rows, rows, pl.BlockSpec((piece, width), lambda j, core: (j, 0))],
-            out_specs=pl.BlockSpec((seq_length, width), lambda j, core: (0, 0)),
-            scratch_shapes=[pltpu.VMEM((seq_length, width), F32)],
-        ),
-        out_shape=jax.ShapeDtypeStruct((seq_length, width), BF16),
-        cost_estimate=cost(2 * seq_length * depth * width, 2 * depth * width),
+            out_specs=[pl.BlockSpec((row_count // 2, width), lambda j, core: (0, 0))] * 2,
+            scratch_shapes=[pltpu.VMEM((row_count, width), F32)],
+        ),
+        out_shape=[jax.ShapeDtypeStruct((row_count // 2, width), BF16)] * 2,
+        cost_estimate=cost(2 * row_count * depth * width, 2 * depth * width),
         name="far",
     )(core, came, twin, weight)
 
@@ -127,29 +130,30 @@
 
 def attend_kernel(heads, flags, held, sent, query, key, value, mask, dq, dk, dv):
     scale = HDIM ** (-0.5)
-    here = mask[0] > 0
-
-    @pl.when(flags[0] + flags[1] > 0)
-    def _():
-        for head in range(heads):
-            cut = slice(head * HDIM, (head + 1) * HDIM)
-            grad = jnp.where(flags[2] > 0, held[:, cut], sent[:, cut])
-            q, k, v = query[:, cut], key[:, cut], value[:, cut]
-            scores = jnp.where(here, mm(q, k, NT) * scale, -jnp.inf)
-            raised = jnp.exp(scores - jnp.max(scores, axis=-1, keepdims=True))
-            probs = raised * (1.0 / jnp.sum(raised, axis=-1, keepdims=True))
-            prob_grad = mm(grad, v, NT)
-            center = jnp.sum(probs * prob_grad, axis=-1, keepdims=True)
-            score_grad = (probs * (prob_grad - center)).astype(BF16)
-
-            @pl.when(flags[0] > 0)
-            def _():
-                dq[:, cut] = (mm(score_grad, k, NN) * scale).astype(BF16)
-
-            @pl.when(flags[1] > 0)
-            def _():
-                dk[:, cut] = (mm(score_grad, q, TN) * scale).astype(BF16)
-                dv[:, cut] = mm(probs.astype(BF16), grad, TN).astype(BF16)
+    cuts = [slice(head * HDIM, (head + 1) * HDIM) for head in range(heads)]
+
+    def grads_of(cut):
+        grad = jnp.where(flags[2] > 0, held[:, cut], sent[:, cut])
+        q, k, v = query[:, cut], key[:, cut], value[:, cut]
+        scores = jnp.where(mask[...] > 0, mm(k, q, NT) * scale, -jnp.inf)
+        raised = jnp.exp(scores - jnp.max(scores, axis=0, keepdims=True))
+        probs = raised * (1.0 / jnp.sum(raised, axis=0, keepdims=True))
+        prob_grad = mm(v, grad, NT)
+        center = jnp.sum(probs * prob_grad, axis=0, keepdims=True)
+        return grad, q, k, probs, (probs * (prob_grad - center)).astype(BF16)
+
+    @pl.when(flags[0] > 0)
+    def _():
+        for cut in cuts:
+            _, _, k, _, score_grad = grads_of(cut)
+            dq[:, cut] = (mm(score_grad, k, TN) * scale).astype(BF16)
+
+    @pl.when(flags[1] > 0)
+    def _():
+        for cut in cuts:
+            grad, q, _, probs, score_grad = grads_of(cut)
+            dk[:, cut] = (mm(score_grad, q, NN) * scale).astype(BF16)
+            dv[:, cut] = mm(probs.astype(BF16), grad, NN).astype(BF16)
 
 
 def attend(flags, held, sent, query, key, value, mask, micro):
@@ -170,7 +174,7 @@
                 row,
                 row,
                 row,
-                pl.BlockSpec((1, 1, seq_length), lambda h, flags: (micro, 0, 0)),
+                pl.BlockSpec((None, seq_length, 1), lambda h, flags: (micro, 0, 0)),
             ],
             out_specs=[one, one, one],
         ),
@@ -183,38 +187,32 @@
 
 
 def products(flags, grads, first, second, put):
-    dq, dk, dv = grads
-    for micro in range(2):
-
-        @pl.when(flags[0] > 0)
-        def _():
-            put(micro, mm(dq[micro][...], second[...], NT))
-
-        @pl.when(flags[0] == 0)
-        def _():
-            put(micro, mm(dk[micro][...], first[...], NT) + mm(dv[micro][...], second[...], NT))
+    dq, dk, dv = [lambda pair=pair: jnp.concatenate([x[...] for x in pair]) for pair in grads]
+
+    @pl.when(flags[0] > 0)
+    def _():
+        put(mm(dq(), second[...], NT))
+
+    @pl.when(flags[0] == 0)
+    def _():
+        put(mm(dk(), first[...], NT) + mm(dv(), second[...], NT))
 
 
 def give_kernel(at, flags, q0, q1, k0, k1, v0, v1, first, second, out):
-    rows = q0.shape[0]
-
-    def put(micro, value):
-        out[micro * rows : (micro + 1) * rows, :] = value.astype(BF16)
+    def put(value):
+        out[...] = value.astype(BF16)
 
     products(flags, ((q0, q1), (k0, k1), (v0, v1)), first, second, put)
 
 
 def keep_kernel(at, flags, q0, q1, k0, k1, v0, v1, first, second, other, *outs):
-    rows = q0.shape[0]
-
-    def put(micro, value):
-        cut = slice(micro * rows, (micro + 1) * rows)
-        total = value + other[cut, :].astype(F32)
+    def put(value):
+        total = value + other[...].astype(F32)
         for i, out in enumerate(outs):
 
             @pl.when(pl.program_id(0) == i)
             def _():
-                out[cut, :] = total.astype(out.dtype)
+                out[...] = total.astype(out.dtype)
 
     products(flags, ((q0, q1), (k0, k1), (v0, v1)), first, second, put)
 
@@ -283,13 +281,13 @@
     )
     second = gathered(second_shard)
     near = [jnp.where(decoder, mine, other) for mine, other in zip(own, came_near)]
+    near[3] = near[3].reshape(micro_count, seq_length, 1)
+    own = (*own[:3], own[3].reshape(micro_count, seq_length, 1))
 
     first_rows = first.reshape(8 * shard_rows, local_width)
     far = [
-        lax.ppermute(
-            far_partial(core[None], came, twin, first_rows, micro, seq_length), BOTH, DEC_SWAP
-        )
-        for micro in micros
+        lax.ppermute(partial, BOTH, DEC_SWAP)
+        for partial in far_partial(core[None], came, twin, first_rows)
     ]
     own_partial = near_partial(half[None], grads, first_rows)
     ctx, ctx_near, ctx_own = [], [], []
@@ -321,8 +319,6 @@
 
     places = 2 * ((chip + jnp.array(STEPS, jnp.int32)) % 4)
     keep_at, give_at = places + core, places + 1 - core
-
-    second, own_dk, own_dv = lax.optimization_barrier((second, own_dk, own_dv))
 
     def chip_sums(grads):
         give = projected(give_at, dec[None], grads, first, second)

time: 235 us -> 238 us (1.013)
  waiting for transfers between devices: 73.4 us -> 86.4 us
  Pallas kernels: 87.3 us -> 76.8 us
    ppermute x2, waiting for transfers between devices: 8.72 us -> 15.4 us  [per_device(): ctx_near.append(lax.ppermute(ctx[micro], BOTH, DEC_TO_ENC))]
    ppermute x2, waiting for transfers between devices: 0.01 us -> 6.65 us  [per_device(): ctx_own.append(lax.ppermute(ctx_near[micro], BOTH, ENC_SWAP))]
    pallas_call x4, Pallas kernels: 28.7 us -> 24.3 us  [attend(): pl.pallas_call(functools.partial(attend_kernel, heads), grid_spec=pltpu.P...]
    pallas_call x2 -> x1, Pallas kernels: 11.1 us -> 7.19 us  [far_partial(): pl.pallas_call(far_kernel, grid_spec=pltpu.PrefetchScalarGridSpec(num_sca...]
    ppermute x2, starting transfers between devices: 4.75 us -> 1.72 us  [chip_sums(): other = lax.ppermute(give, 'segment', CORE_SWAP)]
    all_gather x2, waiting for transfers between devices: 0.01 us -> 2.92 us  [gathered(): return lax.all_gather(shard, 'fsdp', axis=0, axis_index_groups=Z_LINES)]
    ppermute x2, waiting for transfers between devices: 2.67 us -> 0.01 us  [chip_sums(): other = lax.ppermute(give, 'segment', CORE_SWAP)]
    unnamed x46 -> x50, local copies, waits for them, and re-layouts: 6.48 us -> 7.09 us
  transfers between devices with their start and end apart: 25 -> 25, of which waited for: 6 -> 9; matrix products, arithmetic and copies ran while one was open for 4% -> 5% of each run, Pallas kernels for 26% -> 22%
where the time goes in v2:
time: 238 us; the launch traced here: 237 us
  waiting for transfers between devices  86.4 us (36%)
  Pallas kernels  76.8 us (32%)
  starting transfers between devices  37.7 us (16%)
  between operations  13.8 us (6%)
  local copies, waits for them, and re-layouts  11.1 us (5%)
  other arithmetic  11 us (5%)
    ppermute x4, waiting for transfers between devices, per_device(): came_near = tuple((lax.ppermute(value, BOTH, ENC_SWAP) for value in own))  44.1 us
    pallas_call x4, Pallas kernels, projected(): pl.pallas_call(kernel, grid_spec=pltpu.PrefetchScalarGridSpec(num_scalar_...  33.7 us
    pallas_call x4, Pallas kernels, attend(): pl.pallas_call(functools.partial(attend_kernel, heads), grid_spec=pltpu.P...  24.3 us
    ppermute x6, waiting for transfers between devices, reduced(): other = lax.ppermute(block, 'segment', pairs)  17.3 us
    ppermute x2, waiting for transfers between devices, per_device(): ctx_near.append(lax.ppermute(ctx[micro], BOTH, DEC_TO_ENC))  15.4 us
    ppermute x4, starting transfers between devices, per_device(): came_near = tuple((lax.ppermute(value, BOTH, ENC_SWAP) for value in own))  10.6 us
    ppermute x6, starting transfers between devices, reduced(): other = lax.ppermute(block, 'segment', pairs)  8.65 us
    pallas_call x1, Pallas kernels, far_partial(): pl.pallas_call(far_kernel, grid_spec=pltpu.PrefetchScalarGridSpec(num_sca...  7.19 us
  transfers between devices with their start and end apart: 25, of which 9 were waited for; matrix products, arithmetic and copies ran while one was open for 5% of the time, Pallas kernels for 22%

profile of v2, /device:TPU:1, one launch (start us, length us, event | category | flops | bytes accessed | tf_op | source)
XLA Modules:
  0.0 236.7 jit_solution(6125125891822637928)
XLA Ops:
  6.5 2.3 slice_bitcast_fusion
  9.5 4.5 %pick.1 = bf16[512,1536]{1,0:T(8,128)(2,1)} custom-call(s32[4]{0:T(128)} %add_subtract_fusion.1.where, bf16[512,6144]{1,0:T(8,128)(2,1)} %bitcast.32), custom_call_target="tpu_custom_call" | custom-call | bytes 3145728 | tf_op jit(solution)/shard_map/pick/pallas_call | solution.py:43
  14.8 3.3 %collective-permute-start.5 = (bf16[512,1536]{1,0:T(8,128)(2,1)S(1)}, bf16[512,1536]{1,0:T(8,128)(2,1)}, u32[]{:S(2)}, u32[]{:S(2)}) collective-permute-start(bf16[512,1536]{1,0:T(8,128)(2,1)S(1)} %collective-permute-done.4.came), channel_id=1, source_target_pairs={{0,16},{16,0},{32,48},{48,32},{64,80},{80,64},{96,112},{112,96},{1... | collective-permute-start | bytes 4718600 | tf_op jit(solution)/shard_map/ppermute | solution.py:268
  18.1 1.9 collective-permute-start
  20.0 3.4 %collective-permute-start.1 = (bf16[2,256,768]{2,1,0:T(8,128)(2,1)S(1)}, bf16[2,256,768]{2,1,0:T(8,128)(2,1)S(1)}, u32[]{:S(2)}, u32[]{:S(2)}) collective-permute-start(bf16[2,256,768]{2,1,0:T(8,128)(2,1)S(1)} %bitcast.43), channel_id=1, source_target_pairs={{0,1},{1,0},{2,3},{3,2},{4,5},{5,4},{6,7},{7,6},{8,9},{9,8},{10,11... | collective-permute-start | bytes 2359304 | tf_op jit(solution)/shard_map/ppermute | solution.py:276
  23.4 1.9 collective-permute-start.2
  25.3 3.4 %collective-permute-start.3 = (s32[2,1,256]{2,1,0:T(1,128)S(1)}, s32[2,1,256]{2,1,0:T(1,128)S(1)}, u32[]{:S(2)}, u32[]{:S(2)}) collective-permute-start(s32[2,1,256]{2,1,0:T(1,128)S(1)} %copy-done.22), channel_id=1, source_target_pairs={{0,1},{1,0},{2,3},{3,2},{4,5},{5,4},{6,7},{7,6},{8,9},{9,8},{10,11... | collective-permute-start | bytes 6152 | tf_op jit(solution)/shard_map/ppermute | solution.py:276
  28.7 44.1 %collective-permute-done.3 = s32[2,1,256]{2,1,0:T(1,128)S(1)} collective-permute-done((s32[2,1,256]{2,1,0:T(1,128)S(1)}, s32[2,1,256]{2,1,0:T(1,128)S(1)}, u32[]{:S(2)}, u32[]{:S(2)}) %collective-permute-start.3) | collective-permute-done | bytes 2080 | tf_op jit(solution)/shard_map/ppermute | solution.py:276
  72.8 0.9 copy-done.12
  73.7 0.9 copy-done.10
  75.3 7.2 %far.1 = (bf16[256,768]{1,0:T(8,128)(2,1)}, bf16[256,768]{1,0:T(8,128)(2,1)}) custom-call(s32[1]{0:T(128)} %bitcast.9.core, bf16[512,1536]{1,0:T(8,128)(2,1)} %copy-done.24, bf16[512,1536]{1,0:T(8,128)(2,1)} %collective-permute-done.5.twin, bf16[3072,768]{1,0:T(8,128)(2,1)} %bitcast.22), custom_call_target="tpu_custom_call" | custom-call | flops 2415919104 | bytes 4718592 | tf_op jit(solution)/shard_map/far/pallas_call | solution.py:79
  83.1 1.4 collective-permute-start.7
  84.5 2.1 broadcast_select_fusion.2.query
  86.6 7.1 %near.1 = (f32[256,768]{1,0:T(8,128)}, f32[256,768]{1,0:T(8,128)}) custom-call(s32[1]{0:T(128)} %bitcast.1.half, bf16[512,6144]{1,0:T(8,128)(2,1)} %bitcast.33, bf16[512,6144]{1,0:T(8,128)(2,1)} %bitcast.34, bf16[3072,768]{1,0:T(8,128)(2,1)} %bitcast.23), custom_call_target="tpu_custom_call" | custom-call | flops 2415919104 | bytes 4718592 | tf_op jit(solution)/shard_map/near/pallas_call | solution.py:113
  93.7 1.4 add_convert_fusion.3.held
  95.2 1.3 collective-permute-start.9
  96.6 1.3 collective-permute-start.8
  97.9 0.8 reshape.86.mask
  98.7 1.3 broadcast_select_fusion
  100.0 13.8 %collective-permute-done.9.sent = bf16[256,768]{1,0:T(8,128)(2,1)S(1)} collective-permute-done((bf16[256,768]{1,0:T(8,128)(2,1)S(1)}, bf16[256,768]{1,0:T(8,128)(2,1)S(1)}, u32[]{:S(2)}, u32[]{:S(2)}) %collective-permute-start.9) | collective-permute-done | bytes 393248 | tf_op jit(solution)/shard_map/ppermute | solution.py:299
  114.6 6.1 %attend.4 = (bf16[256,768]{1,0:T(8,128)(2,1)}, bf16[256,768]{1,0:T(8,128)(2,1)}, bf16[256,768]{1,0:T(8,128)(2,1)}) custom-call(s32[3]{0:T(128)} %pad_add_fusion.flags, bf16[256,768]{1,0:T(8,128)(2,1)} %copy-done.3, bf16[256,768]{1,0:T(8,128)(2,1)} %copy-done.16, bf16[2,256,768]{2,1,0:T(8,128)(2,1)} %broadcast_select_fusion.2.query, ...), custom_call_target="tpu_custom_call" | custom-call | flops 503316480 | bytes 3145728 | tf_op jit(solution)/shard_map/attend/pallas_call | solution.py:166
  120.7 1.6 collective-permute-done.8.sent
  123.0 6.2 %attend.5 = (bf16[256,768]{1,0:T(8,128)(2,1)}, bf16[256,768]{1,0:T(8,128)(2,1)}, bf16[256,768]{1,0:T(8,128)(2,1)}) custom-call(s32[3]{0:T(128)} %pad_add_fusion.flags, bf16[256,768]{1,0:T(8,128)(2,1)} %copy-done.4, bf16[256,768]{1,0:T(8,128)(2,1)} %copy-done.18, bf16[2,256,768]{2,1,0:T(8,128)(2,1)} %broadcast_select_fusion.2.query, ...), custom_call_target="tpu_custom_call" | custom-call | flops 503316480 | bytes 3145728 | tf_op jit(solution)/shard_map/attend/pallas_call | solution.py:166
  131.2 2.9 %all-gather.7.cloned.1.call-done = bf16[3072,768]{1,0:T(8,128)(2,1)} async-done(((bf16[384,768]{1,0:T(8,128)(2,1)}), bf16[3072,768]{1,0:T(8,128)(2,1)}) %all-gather.7.cloned.1.call-update) | async-done | bytes 4718608 | tf_op jit(solution)/shard_map/all_gather | solution.py:263
  134.1 8.1 %shard_map.73 = bf16[4,512,384]{2,1,0:T(8,128)(2,1)} custom-call(s32[4]{0:T(128)} %get-tuple-element.103.at, s32[1]{0:T(128)} %bitcast.flags, bf16[256,768]{1,0:T(8,128)(2,1)} %copy-done.9, bf16[256,768]{1,0:T(8,128)(2,1)} %copy-done.8, bf16[256,768]{1,0:T(8,128)(2,1)} %get-tuple-element.79.k0, bf16[256,768]{1,0:T(8,128)(2,1)} %get-tuple-element.80.k1, ...), custom_call_target="tpu_custom_call" | custom-call | flops 2415919104 | bytes 4718592 | tf_op jit(solution)/shard_map/pallas_call | solution.py:235
  142.2 0.9 collective-permute-start.14
  143.0 3.1 %collective-permute-start.11 = (bf16[256,768]{1,0:T(8,128)(2,1)S(1)}, bf16[256,768]{1,0:T(8,128)(2,1)S(1)}, u32[]{:S(2)}, u32[]{:S(2)}) collective-permute-start(bf16[256,768]{1,0:T(8,128)(2,1)S(1)} %copy-done.17), channel_id=1, source_target_pairs={{0,1},{1,0},{2,3},{3,2},{4,5},{5,4},{6,7},{7,6},{8,9},{9,8},{10,11... | collective-permute-start | bytes 1179656 | tf_op jit(solution)/shard_map/ppermute | solution.py:300
  146.2 2.4 collective-permute-start.10
  150.6 5.0 %collective-permute-done.11.sent = bf16[256,768]{1,0:T(8,128)(2,1)S(1)} collective-permute-done((bf16[256,768]{1,0:T(8,128)(2,1)S(1)}, bf16[256,768]{1,0:T(8,128)(2,1)S(1)}, u32[]{:S(2)}, u32[]{:S(2)}) %collective-permute-start.11) | collective-permute-done | bytes 393248 | tf_op jit(solution)/shard_map/ppermute | solution.py:300
  156.3 6.0 %attend.6 = (bf16[256,768]{1,0:T(8,128)(2,1)}, bf16[256,768]{1,0:T(8,128)(2,1)}, bf16[256,768]{1,0:T(8,128)(2,1)}) custom-call(s32[3]{0:T(128)} %pad_add_fusion.1.flags, bf16[256,768]{1,0:T(8,128)(2,1)} %copy-done.3, bf16[256,768]{1,0:T(8,128)(2,1)} %copy-done.21, bf16[2,256,768]{2,1,0:T(8,128)(2,1)} %bitcast.35, bf16[2,256,768]{2,1,0:T(8,128)(2,1)} %bitcast.41, ...), custom_call_target="tpu_custom_call" | custom-call | flops 503316480 | bytes 3145728 | tf_op jit(solution)/shard_map/attend/pallas_call | solution.py:166
  162.3 1.7 collective-permute-done.10.sent
  164.8 6.0 %attend.7 = (bf16[256,768]{1,0:T(8,128)(2,1)}, bf16[256,768]{1,0:T(8,128)(2,1)}, bf16[256,768]{1,0:T(8,128)(2,1)}) custom-call(s32[3]{0:T(128)} %pad_add_fusion.1.flags, bf16[256,768]{1,0:T(8,128)(2,1)} %copy-done.4, bf16[256,768]{1,0:T(8,128)(2,1)} %copy-done.20, bf16[2,256,768]{2,1,0:T(8,128)(2,1)} %bitcast.36, bf16[2,256,768]{2,1,0:T(8,128)(2,1)} %bitcast.42, ...), custom_call_target="tpu_custom_call" | custom-call | flops 503316480 | bytes 3145728 | tf_op jit(solution)/shard_map/attend/pallas_call | solution.py:166
  170.8 1.1 copy-done.5
  171.9 8.9 %shard_map.74 = (bf16[512,384]{1,0:T(8,128)(2,1)}, bf16[512,384]{1,0:T(8,128)(2,1)}, bf16[512,384]{1,0:T(8,128)(2,1)}, f32[512,384]{1,0:T(8,128)}) custom-call(s32[4]{0:T(128)} %broadcast_add_fusion.at, s32[1]{0:T(128)} %bitcast.flags, bf16[256,768]{1,0:T(8,128)(2,1)} %copy-done.9, bf16[256,768]{1,0:T(8,128)(2,1)} %copy-done.8, ...), custom_call_target="tpu_custom_call" | custom-call | flops 2415919104 | bytes 4718592 | tf_op jit(solution)/shard_map/pallas_call | solution.py:235
  180.8 7.9 %shard_map.75 = bf16[4,512,384]{2,1,0:T(8,128)(2,1)} custom-call(s32[4]{0:T(128)} %get-tuple-element.103.at, s32[1]{0:T(128)} %bitcast.flags, bf16[256,768]{1,0:T(8,128)(2,1)} %get-tuple-element.87.q0, bf16[256,768]{1,0:T(8,128)(2,1)} %get-tuple-element.88.q1, bf16[256,768]{1,0:T(8,128)(2,1)} %get-tuple-element.89.k0, ...), custom_call_target="tpu_custom_call" | custom-call | flops 2415919104 | bytes 4718592 | tf_op jit(solution)/shard_map/pallas_call | solution.py:235
  188.7 0.9 collective-permute-start.15
  189.6 2.7 %collective-permute-start.19 = (bf16[512,384]{1,0:T(8,128)(2,1)}, bf16[512,384]{1,0:T(8,128)(2,1)S(1)}, u32[]{:S(2)}, u32[]{:S(2)}) collective-permute-start(bf16[512,384]{1,0:T(8,128)(2,1)} %get-tuple-element.98), channel_id=1, source_target_pairs={{0,64},{16,80},{32,96},{48,112},{64,0},{80,16},{96,32},{112,48},{1... | collective-permute-start | bytes 1179656 | tf_op jit(solution)/shard_map/ppermute | solution.py:331
  192.6 2.4 %collective-permute-start.21 = (bf16[512,384]{1,0:T(8,128)(2,1)}, bf16[512,384]{1,0:T(8,128)(2,1)S(1)}, u32[]{:S(2)}, u32[]{:S(2)}) collective-permute-start(bf16[512,384]{1,0:T(8,128)(2,1)} %get-tuple-element.100), channel_id=1, source_target_pairs={{0,96},{16,112},{32,0},{48,16},{64,32},{80,48},{96,64},{112,80},{1... | collective-permute-start | bytes 1179656 | tf_op jit(solution)/shard_map/ppermute | solution.py:331
  195.0 1.1 copy-done.6
  196.1 8.9 %shard_map.76 = (bf16[512,384]{1,0:T(8,128)(2,1)}, bf16[512,384]{1,0:T(8,128)(2,1)}, bf16[512,384]{1,0:T(8,128)(2,1)}, f32[512,384]{1,0:T(8,128)}) custom-call(s32[4]{0:T(128)} %broadcast_add_fusion.at, s32[1]{0:T(128)} %bitcast.flags, bf16[256,768]{1,0:T(8,128)(2,1)} %get-tuple-element.87.q0, bf16[256,768]{1,0:T(8,128)(2,1)} %get-tuple-element.88.q1, ...), custom_call_target="tpu_custom_call" | custom-call | flops 2415919104 | bytes 4718592 | tf_op jit(solution)/shard_map/pallas_call | solution.py:235
  205.9 2.4 %collective-permute-start.18 = (bf16[512,384]{1,0:T(8,128)(2,1)}, bf16[512,384]{1,0:T(8,128)(2,1)}, u32[]{:S(2)}, u32[]{:S(2)}) collective-permute-start(bf16[512,384]{1,0:T(8,128)(2,1)} %get-tuple-element.96), channel_id=1, source_target_pairs={{0,96},{16,112},{32,0},{48,16},{64,32},{80,48},{96,64},{112,80},{1... | collective-permute-start | bytes 1179656 | tf_op jit(solution)/shard_map/ppermute | solution.py:331
  208.3 3.0 %collective-permute-done.20 = bf16[512,384]{1,0:T(8,128)(2,1)S(1)} collective-permute-done((bf16[512,384]{1,0:T(8,128)(2,1)}, bf16[512,384]{1,0:T(8,128)(2,1)S(1)}, u32[]{:S(2)}, u32[]{:S(2)}) %collective-permute-start.20) | collective-permute-done | bytes 393248 | tf_op jit(solution)/shard_map/ppermute | solution.py:331
  211.2 0.9 add_convert_fusion
  212.1 1.2 collective-permute-start.22
  213.3 5.5 %collective-permute-done.16 = bf16[512,384]{1,0:T(8,128)(2,1)S(1)} collective-permute-done((bf16[512,384]{1,0:T(8,128)(2,1)}, bf16[512,384]{1,0:T(8,128)(2,1)S(1)}, u32[]{:S(2)}, u32[]{:S(2)}) %collective-permute-start.16) | collective-permute-done | bytes 393248 | tf_op jit(solution)/shard_map/ppermute | solution.py:331
  218.8 8.8 %collective-permute-done.17 = bf16[512,384]{1,0:T(8,128)(2,1)S(1)} collective-permute-done((bf16[512,384]{1,0:T(8,128)(2,1)}, bf16[512,384]{1,0:T(8,128)(2,1)S(1)}, u32[]{:S(2)}, u32[]{:S(2)}) %collective-permute-start.17) | collective-permute-done | bytes 393248 | tf_op jit(solution)/shard_map/ppermute | solution.py:331
  227.6 1.2 add_convert_fusion.1
  228.8 1.1 maximum_select_fusion
  (81 shorter events, 11.0 us)
Async XLA Ops:
  6.5 68.0 %all-gather.5.cloned.1.call-start = ((), (), s32[]{:S(2)}) async-start(), calls=%async_computation | async-start | bytes 5308416 | tf_op jit(solution)/shard_map/all_gather | solution.py:263
  8.9 125.2 %all-gather.7.cloned.1.call-start = ((), (), s32[]{:S(2)}) async-start(), calls=%async_computation.1 | async-start | bytes 5308416 | tf_op jit(solution)/shard_map/all_gather | solution.py:263
  9.5 8.6 %copy-start = (bf16[2,1,256,768]{3,2,1,0:T(8,128)(2,1)S(1)}, bf16[2,1,256,768]{3,2,1,0:T(8,128)(2,1)}, u32[]{:S(2)}) copy-start(bf16[2,1,256,768]{3,2,1,0:T(8,128)(2,1)} %param.8) | copy-start | bytes 2359300
  9.5 10.5 %copy-start.2 = (bf16[2,1,256,768]{3,2,1,0:T(8,128)(2,1)S(1)}, bf16[2,1,256,768]{3,2,1,0:T(8,128)(2,1)}, u32[]{:S(2)}) copy-start(bf16[2,1,256,768]{3,2,1,0:T(8,128)(2,1)} %param.9) | copy-start | bytes 2359300
  9.5 13.9 %copy-start.1 = (bf16[2,1,256,768]{3,2,1,0:T(8,128)(2,1)S(1)}, bf16[2,1,256,768]{3,2,1,0:T(8,128)(2,1)}, u32[]{:S(2)}) copy-start(bf16[2,1,256,768]{3,2,1,0:T(8,128)(2,1)} %param.10) | copy-start | bytes 2359300
  9.5 15.8 %copy-start.22 = (s32[2,1,256]{2,1,0:T(1,128)S(1)}, s32[2,1,256]{2,1,0:T(1,128)}, u32[]{:S(2)}) copy-start(s32[2,1,256]{2,1,0:T(1,128)} %param.11) | copy-start | bytes 6148
  14.0 0.8 collective-permute-start.4
  14.8 58.0 %copy-start.24 = (bf16[512,1536]{1,0:T(8,128)(2,1)}, bf16[512,1536]{1,0:T(8,128)(2,1)S(1)}, u32[]{:S(2)}) copy-start(bf16[512,1536]{1,0:T(8,128)(2,1)S(1)} %collective-permute-done.4.came) | copy-start | bytes 4718596
  14.8 59.8 %collective-permute-start.5 = (bf16[512,1536]{1,0:T(8,128)(2,1)S(1)}, bf16[512,1536]{1,0:T(8,128)(2,1)}, u32[]{:S(2)}, u32[]{:S(2)}) collective-permute-start(bf16[512,1536]{1,0:T(8,128)(2,1)S(1)} %collective-permute-done.4.came), channel_id=1, source_target_pairs={{0,16},{16,0},{32,48},{48,32},{64,80},{80,64},{96,112},{112,96},{1... | collective-permute-start | bytes 4718600 | tf_op jit(solution)/shard_map/ppermute | solution.py:268
  18.1 54.7 %collective-permute-start = (bf16[2,256,768]{2,1,0:T(8,128)(2,1)S(1)}, bf16[2,256,768]{2,1,0:T(8,128)(2,1)S(1)}, u32[]{:S(2)}, u32[]{:S(2)}) collective-permute-start(bf16[2,256,768]{2,1,0:T(8,128)(2,1)S(1)} %bitcast.37), channel_id=1, source_target_pairs={{0,1},{1,0},{2,3},{3,2},{4,5},{5,4},{6,7},{7,6},{8,9},{9,8},{10,11... | collective-permute-start | bytes 2359304 | tf_op jit(solution)/shard_map/ppermute | solution.py:276
  20.0 52.8 %collective-permute-start.1 = (bf16[2,256,768]{2,1,0:T(8,128)(2,1)S(1)}, bf16[2,256,768]{2,1,0:T(8,128)(2,1)S(1)}, u32[]{:S(2)}, u32[]{:S(2)}) collective-permute-start(bf16[2,256,768]{2,1,0:T(8,128)(2,1)S(1)} %bitcast.43), channel_id=1, source_target_pairs={{0,1},{1,0},{2,3},{3,2},{4,5},{5,4},{6,7},{7,6},{8,9},{9,8},{10,11... | collective-permute-start | bytes 2359304 | tf_op jit(solution)/shard_map/ppermute | solution.py:276
  23.4 49.4 %collective-permute-start.2 = (bf16[2,256,768]{2,1,0:T(8,128)(2,1)S(1)}, bf16[2,256,768]{2,1,0:T(8,128)(2,1)S(1)}, u32[]{:S(2)}, u32[]{:S(2)}) collective-permute-start(bf16[2,256,768]{2,1,0:T(8,128)(2,1)S(1)} %bitcast.40), channel_id=1, source_target_pairs={{0,1},{1,0},{2,3},{3,2},{4,5},{5,4},{6,7},{7,6},{8,9},{9,8},{10,11... | collective-permute-start | bytes 2359304 | tf_op jit(solution)/shard_map/ppermute | solution.py:276
  25.3 47.5 %collective-permute-start.3 = (s32[2,1,256]{2,1,0:T(1,128)S(1)}, s32[2,1,256]{2,1,0:T(1,128)S(1)}, u32[]{:S(2)}, u32[]{:S(2)}) collective-permute-start(s32[2,1,256]{2,1,0:T(1,128)S(1)} %copy-done.22), channel_id=1, source_target_pairs={{0,1},{1,0},{2,3},{3,2},{4,5},{5,4},{6,7},{7,6},{8,9},{9,8},{10,11... | collective-permute-start | bytes 6152 | tf_op jit(solution)/shard_map/ppermute | solution.py:276
  72.8 0.9 copy-start.12
  73.7 0.9 copy-start.10
  82.4 14.0 %collective-permute-start.6 = (bf16[256,768]{1,0:T(8,128)(2,1)}, bf16[256,768]{1,0:T(8,128)(2,1)S(1)}, u32[]{:S(2)}, u32[]{:S(2)}) collective-permute-start(bf16[256,768]{1,0:T(8,128)(2,1)} %get-tuple-element.57), channel_id=1, source_target_pairs={{128,129},{129,128},{130,131},{131,130},{132,133},{133,132},{134,1... | collective-permute-start | bytes 1179656 | tf_op jit(solution)/shard_map/ppermute | solution.py:289
  83.1 10.6 %collective-permute-start.7 = (bf16[256,768]{1,0:T(8,128)(2,1)}, bf16[256,768]{1,0:T(8,128)(2,1)}, u32[]{:S(2)}, u32[]{:S(2)}) collective-permute-start(bf16[256,768]{1,0:T(8,128)(2,1)} %get-tuple-element.59), channel_id=1, source_target_pairs={{128,129},{129,128},{130,131},{131,130},{132,133},{133,132},{134,1... | collective-permute-start | bytes 1179656 | tf_op jit(solution)/shard_map/ppermute | solution.py:289
  93.7 2.8 %copy-start.13 = (f32[256,768]{1,0:T(8,128)S(1)}, f32[256,768]{1,0:T(8,128)}, u32[]{:S(2)}) copy-start(f32[256,768]{1,0:T(8,128)} %get-tuple-element.54) | copy-start | bytes 2359300
  93.7 5.0 %copy-start.11 = (bf16[2,256,768]{2,1,0:T(8,128)(2,1)S(1)}, bf16[2,256,768]{2,1,0:T(8,128)(2,1)}, u32[]{:S(2)}) copy-start(bf16[2,256,768]{2,1,0:T(8,128)(2,1)} %copy-done.10) | copy-start | bytes 2359300
  95.2 4.9 %copy-start.3 = (bf16[256,768]{1,0:T(8,128)(2,1)}, bf16[256,768]{1,0:T(8,128)(2,1)S(1)}, u32[]{:S(2)}) copy-start(bf16[256,768]{1,0:T(8,128)(2,1)S(1)} %add_convert_fusion.3.held) | copy-start | bytes 1179652
  95.2 18.7 %collective-permute-start.9 = (bf16[256,768]{1,0:T(8,128)(2,1)S(1)}, bf16[256,768]{1,0:T(8,128)(2,1)S(1)}, u32[]{:S(2)}, u32[]{:S(2)}) collective-permute-start(bf16[256,768]{1,0:T(8,128)(2,1)S(1)} %add_convert_fusion.3.held), channel_id=1, source_target_pairs={{128,1},{129,0},{130,3},{131,2},{132,5},{133,4},{134,7},{135,6},{1... | collective-permute-start | bytes 1179656 | tf_op jit(solution)/shard_map/ppermute | solution.py:299
  96.6 3.5 %copy-start.4 = (bf16[256,768]{1,0:T(8,128)(2,1)}, bf16[256,768]{1,0:T(8,128)(2,1)S(1)}, u32[]{:S(2)}) copy-start(bf16[256,768]{1,0:T(8,128)(2,1)S(1)} %add_convert_fusion.2.held) | copy-start | bytes 1179652
  96.6 25.7 %collective-permute-start.8 = (bf16[256,768]{1,0:T(8,128)(2,1)S(1)}, bf16[256,768]{1,0:T(8,128)(2,1)S(1)}, u32[]{:S(2)}, u32[]{:S(2)}) collective-permute-start(bf16[256,768]{1,0:T(8,128)(2,1)S(1)} %add_convert_fusion.2.held), channel_id=1, source_target_pairs={{128,1},{129,0},{130,3},{131,2},{132,5},{133,4},{134,7},{135,6},{1... | collective-permute-start | bytes 1179656 | tf_op jit(solution)/shard_map/ppermute | solution.py:299
  113.8 0.7 copy-start.16
  122.3 0.8 copy-start.18
  123.0 6.9 %copy-start.7 = (bf16[256,768]{1,0:T(8,128)(2,1)S(1)}, bf16[256,768]{1,0:T(8,128)(2,1)}, u32[]{:S(2)}) copy-start(bf16[256,768]{1,0:T(8,128)(2,1)} %get-tuple-element.87.q0) | copy-start | bytes 1179652
  123.0 7.6 %copy-start.23 = (s32[4]{0:T(128)S(1)}, s32[4]{0:T(128)}, u32[]{:S(2)}) copy-start(s32[4]{0:T(128)} %constant.64.clone) | copy-start | bytes 52
  129.2 2.0 collective-permute-start.13
  129.9 1.3 collective-permute-start.12
  131.2 2.9 %copy-start.8 = (bf16[256,768]{1,0:T(8,128)(2,1)}, bf16[256,768]{1,0:T(8,128)(2,1)S(1)}, u32[]{:S(2)}) copy-start(bf16[256,768]{1,0:T(8,128)(2,1)S(1)} %collective-permute-done.13.q1) | copy-start | bytes 1179652
  131.2 2.9 %copy-start.9 = (bf16[256,768]{1,0:T(8,128)(2,1)}, bf16[256,768]{1,0:T(8,128)(2,1)S(1)}, u32[]{:S(2)}) copy-start(bf16[256,768]{1,0:T(8,128)(2,1)S(1)} %collective-permute-done.12.q0) | copy-start | bytes 1179652
  134.1 8.9 %copy-start.17 = (bf16[256,768]{1,0:T(8,128)(2,1)S(1)}, bf16[256,768]{1,0:T(8,128)(2,1)}, u32[]{:S(2)}) copy-start(bf16[256,768]{1,0:T(8,128)(2,1)} %copy-done.16) | copy-start | bytes 1179652
  134.1 12.0 %copy-start.19 = (bf16[256,768]{1,0:T(8,128)(2,1)S(1)}, bf16[256,768]{1,0:T(8,128)(2,1)}, u32[]{:S(2)}) copy-start(bf16[256,768]{1,0:T(8,128)(2,1)} %copy-done.18) | copy-start | bytes 1179652
  142.2 28.6 %collective-permute-start.14 = (bf16[4,512,384]{2,1,0:T(8,128)(2,1)}, bf16[4,512,384]{2,1,0:T(8,128)(2,1)S(1)}, u32[]{:S(2)}, u32[]{:S(2)}) collective-permute-start(bf16[4,512,384]{2,1,0:T(8,128)(2,1)} %shard_map.73), channel_id=1, source_target_pairs={{0,16},{16,0},{32,48},{48,32},{64,80},{80,64},{96,112},{112,96},{1... | collective-permute-start | bytes 4718600 | tf_op jit(solution)/shard_map/ppermute | solution.py:325
  143.0 12.5 %collective-permute-start.11 = (bf16[256,768]{1,0:T(8,128)(2,1)S(1)}, bf16[256,768]{1,0:T(8,128)(2,1)S(1)}, u32[]{:S(2)}, u32[]{:S(2)}) collective-permute-start(bf16[256,768]{1,0:T(8,128)(2,1)S(1)} %copy-done.17), channel_id=1, source_target_pairs={{0,1},{1,0},{2,3},{3,2},{4,5},{5,4},{6,7},{7,6},{8,9},{9,8},{10,11... | collective-permute-start | bytes 1179656 | tf_op jit(solution)/shard_map/ppermute | solution.py:300
  146.2 17.8 %collective-permute-start.10 = (bf16[256,768]{1,0:T(8,128)(2,1)S(1)}, bf16[256,768]{1,0:T(8,128)(2,1)S(1)}, u32[]{:S(2)}, u32[]{:S(2)}) collective-permute-start(bf16[256,768]{1,0:T(8,128)(2,1)S(1)} %copy-done.19), channel_id=1, source_target_pairs={{0,1},{1,0},{2,3},{3,2},{4,5},{5,4},{6,7},{7,6},{8,9},{9,8},{10,11... | collective-permute-start | bytes 1179656 | tf_op jit(solution)/shard_map/ppermute | solution.py:300
  170.8 1.1 copy-start.5
  188.7 22.5 %copy-start.14 = (f32[512,384]{1,0:T(8,128)S(1)}, f32[512,384]{1,0:T(8,128)}, u32[]{:S(2)}) copy-start(f32[512,384]{1,0:T(8,128)} %get-tuple-element.97) | copy-start | bytes 2359300
  188.7 6.2 %collective-permute-start.15 = (bf16[4,512,384]{2,1,0:T(8,128)(2,1)}, bf16[4,512,384]{2,1,0:T(8,128)(2,1)S(1)}, u32[]{:S(2)}, u32[]{:S(2)}) collective-permute-start(bf16[4,512,384]{2,1,0:T(8,128)(2,1)} %shard_map.75), channel_id=1, source_target_pairs={{0,16},{16,0},{32,48},{48,32},{64,80},{80,64},{96,112},{112,96},{1... | collective-permute-start | bytes 4718600 | tf_op jit(solution)/shard_map/ppermute | solution.py:325
  189.6 16.3 %collective-permute-start.19 = (bf16[512,384]{1,0:T(8,128)(2,1)}, bf16[512,384]{1,0:T(8,128)(2,1)S(1)}, u32[]{:S(2)}, u32[]{:S(2)}) collective-permute-start(bf16[512,384]{1,0:T(8,128)(2,1)} %get-tuple-element.98), channel_id=1, source_target_pairs={{0,64},{16,80},{32,96},{48,112},{64,0},{80,16},{96,32},{112,48},{1... | collective-permute-start | bytes 1179656 | tf_op jit(solution)/shard_map/ppermute | solution.py:331
  192.3 18.9 %collective-permute-start.20 = (bf16[512,384]{1,0:T(8,128)(2,1)}, bf16[512,384]{1,0:T(8,128)(2,1)S(1)}, u32[]{:S(2)}, u32[]{:S(2)}) collective-permute-start(bf16[512,384]{1,0:T(8,128)(2,1)} %get-tuple-element.99), channel_id=1, source_target_pairs={{0,32},{16,48},{32,64},{48,80},{64,96},{80,112},{96,0},{112,16},{1... | collective-permute-start | bytes 1179656 | tf_op jit(solution)/shard_map/ppermute | solution.py:331
  192.6 18.6 %collective-permute-start.21 = (bf16[512,384]{1,0:T(8,128)(2,1)}, bf16[512,384]{1,0:T(8,128)(2,1)S(1)}, u32[]{:S(2)}, u32[]{:S(2)}) collective-permute-start(bf16[512,384]{1,0:T(8,128)(2,1)} %get-tuple-element.100), channel_id=1, source_target_pairs={{0,96},{16,112},{32,0},{48,16},{64,32},{80,48},{96,64},{112,80},{1... | collective-permute-start | bytes 1179656 | tf_op jit(solution)/shard_map/ppermute | solution.py:331
  195.0 1.1 copy-start.6
  205.0 22.7 %copy-start.15 = (f32[512,384]{1,0:T(8,128)S(1)}, f32[512,384]{1,0:T(8,128)}, u32[]{:S(2)}) copy-start(f32[512,384]{1,0:T(8,128)} %get-tuple-element.93) | copy-start | bytes 2359300
  205.0 13.8 %collective-permute-start.16 = (bf16[512,384]{1,0:T(8,128)(2,1)}, bf16[512,384]{1,0:T(8,128)(2,1)S(1)}, u32[]{:S(2)}, u32[]{:S(2)}) collective-permute-start(bf16[512,384]{1,0:T(8,128)(2,1)} %get-tuple-element.94), channel_id=1, source_target_pairs={{0,64},{16,80},{32,96},{48,112},{64,0},{80,16},{96,32},{112,48},{1... | collective-permute-start | bytes 1179656 | tf_op jit(solution)/shard_map/ppermute | solution.py:331
  205.6 22.1 %collective-permute-start.17 = (bf16[512,384]{1,0:T(8,128)(2,1)}, bf16[512,384]{1,0:T(8,128)(2,1)S(1)}, u32[]{:S(2)}, u32[]{:S(2)}) collective-permute-start(bf16[512,384]{1,0:T(8,128)(2,1)} %get-tuple-element.95), channel_id=1, source_target_pairs={{0,32},{16,48},{32,64},{48,80},{64,96},{80,112},{96,0},{112,16},{1... | collective-permute-start | bytes 1179656 | tf_op jit(solution)/shard_map/ppermute | solution.py:331
  205.9 21.8 %collective-permute-start.18 = (bf16[512,384]{1,0:T(8,128)(2,1)}, bf16[512,384]{1,0:T(8,128)(2,1)}, u32[]{:S(2)}, u32[]{:S(2)}) collective-permute-start(bf16[512,384]{1,0:T(8,128)(2,1)} %get-tuple-element.96), channel_id=1, source_target_pairs={{0,96},{16,112},{32,0},{48,16},{64,32},{80,48},{96,64},{112,80},{1... | collective-permute-start | bytes 1179656 | tf_op jit(solution)/shard_map/ppermute | solution.py:331
  212.1 16.7 %collective-permute-start.22 = (bf16[512,384]{1,0:T(8,128)(2,1)}, bf16[512,384]{1,0:T(8,128)(2,1)S(1)}, u32[]{:S(2)}, u32[]{:S(2)}) collective-permute-start(bf16[512,384]{1,0:T(8,128)(2,1)} %add_convert_fusion), channel_id=1, source_target_pairs={{0,1},{1,0},{2,3},{3,2},{4,5},{5,4},{6,7},{7,6},{8,9},{9,8},{10,11... | collective-permute-start | bytes 1179656 | tf_op jit(solution)/shard_map/ppermute | solution.py:337
  (2 other events, 1.5 us)
Sparse Core Ops, SparseCore 0:
  9.1 63.2 all-gather.4
  74.7 59.3 all-gather.6

commit v3 on v2

v3 whole, which is shorter than its diff:
```python
import functools

import jax
import jax.numpy as jnp
from jax import lax
from jax.experimental import pallas as pl
from jax.experimental.pallas import tpu as pltpu
from jax.sharding import PartitionSpec as P


HDIM = 128

FAR_FIRST = (4, 3, 5, 2, 6, 1, 7)
DEC_SWAP = [(16 + f, 16 + (f ^ 1)) for f in range(16)]
ENC_SWAP = [(f, f ^ 1) for f in range(16)]
DEC_TO_ENC = [(16 + f, f ^ 1) for f in range(16)]
HALF_SWAP = [(f, f ^ 1) for f in range(16)]
CORE_SWAP = [(g, g ^ 1) for g in range(8)]
BOTH = ("section", "fsdp")
STEPS = (2, 1, 3, 0)
F32 = jnp.float32
SMALL = pltpu.CompilerParams(vmem_limit_bytes=20 * 2**20)
ANY = pl.BlockSpec(memory_space=pl.ANY)
BF16 = jnp.bfloat16
NT = (((1,), (1,)), ((), ()))
TN = (((0,), (0,)), ((), ()))
NN = (((1,), (0,)), ((), ()))


def mm(left, right, dims):
    return lax.dot_general(left, right, dims, preferred_element_type=F32)


def cost(flops, bytes_accessed):
    return pl.CostEstimate(flops=flops, bytes_accessed=bytes_accessed, transcendentals=0)


def pick_kernel(where, source, target):
    target[...] = source[...]


def picked(source, columns, width):
    rows = source.shape[0]
    count = columns.shape[0]
    return pl.pallas_call(
        pick_kernel,
        grid_spec=pltpu.PrefetchScalarGridSpec(
            num_scalar_prefetch=1,
            grid=(count,),
            in_specs=[pl.BlockSpec((rows, width), lambda i, at: (0, at[i]))],
            out_specs=pl.BlockSpec((rows, width), lambda i, at: (0, i)),
        ),
        out_shape=jax.ShapeDtypeStruct((rows, count * width), source.dtype),
        cost_estimate=cost(0, 2 * rows * count * width * 2),
        compiler_params=SMALL,
        name="pick",
    )(columns, source)


def fetched(step, weights, buffer, sems):
    rows = weights[0].shape[0]
    copies = [
        pltpu.make_async_copy(weight, buffer.at[pl.ds(d * rows, rows)], sems.at[d])
        for d, weight in enumerate(weights)
    ]

    @pl.when(step == 0)
    def _():
        for copy in copies:
            copy.start()

    for j in range(4):

        @pl.when(step == j)
        def _():
            copies[2 * j].wait()
            copies[2 * j + 1].wait()

    return buffer[pl.ds(pl.multiple_of(step * 2 * rows, 2 * rows), 2 * rows), :]


def added(step, acc, part):
    @pl.when(step == 0)
    def _():
        acc[...] = part

    @pl.when(step > 0)
    def _():
        acc[...] += part


def far_kernel(core, came, twin, *refs):
    weights, (low, high, acc, buffer, sems) = refs[:8], refs[8:]
    step = pl.program_id(0)
    rows = jnp.where(core[0] == step // 2, came[...], twin[...])
    added(step, acc, mm(rows, fetched(step, weights, buffer, sems), NN))

    @pl.when(step == pl.num_programs(0) - 1)
    def _():
        rows = low.shape[0]
        low[...] = acc[:rows].astype(BF16)
        high[...] = acc[rows:].astype(BF16)


def near_kernel(columns, first, second, *refs):
    weights, (low, high, buffer, sems) = refs[:8], refs[8:]
    step = pl.program_id(0)
    rows = jnp.concatenate([first[...], second[...]], axis=1)
    part = mm(rows, fetched(step, weights, buffer, sems), NN)
    half = low.shape[0]
    added(step, low, part[:half])
    added(step, high, part[half:])


def partial_products(scalars, operands, specs, weights, out_dtype, kernel):
    row_count = operands[0].shape[0]
    shard, width = weights[0].shape
    extra = [pltpu.VMEM((row_count, width), F32)] if out_dtype == BF16 else []
    return pl.pallas_call(
        kernel,
        grid_spec=pltpu.PrefetchScalarGridSpec(
            num_scalar_prefetch=1,
            grid=(4,),
            in_specs=specs + [ANY] * 8,
            out_specs=[pl.BlockSpec((row_count // 2, width), lambda j, at: (0, 0))] * 2,
            scratch_shapes=extra
            + [pltpu.VMEM((8 * shard, width), BF16), pltpu.SemaphoreType.DMA((8,))],
        ),
        out_shape=[jax.ShapeDtypeStruct((row_count // 2, width), out_dtype)] * 2,
        cost_estimate=cost(2 * row_count * 8 * shard * width, 2 * 8 * shard * width),
        compiler_params=SMALL,
    )(scalars, *operands, *weights)


def attend_kernel(heads, flags, *refs):
    *sent, query, key, value, mask, dq, dk, dv = refs if len(refs) > 8 else (*refs[:5], None, *refs[5:])
    scale = HDIM ** (-0.5)
    cuts = [slice(head * HDIM, (head + 1) * HDIM) for head in range(heads)]

    def grads_of(cut):
        grad = sent[0][:, cut]
        if len(sent) > 1:
            grad = jnp.where(flags[0] > 0, sent[1][:, cut], grad)
        q, k, v = query[:, cut], key[:, cut], value[:, cut]
        scores = jnp.where(mask[...] > 0, mm(k, q, NT) * scale, -jnp.inf)
        raised = jnp.exp(scores - jnp.max(scores, axis=0, keepdims=True))
        probs = raised * (1.0 / jnp.sum(raised, axis=0, keepdims=True))
        prob_grad = mm(v, grad, NT)
        center = jnp.sum(probs * prob_grad, axis=0, keepdims=True)
        return grad, q, k, probs, (probs * (prob_grad - center)).astype(BF16)

    def query_grads():
        for cut in cuts:
            _, _, k, _, score_grad = grads_of(cut)
            dq[:, cut] = (mm(score_grad, k, TN) * scale).astype(BF16)

    def key_value_grads():
        for cut in cuts:
            grad, q, _, probs, score_grad = grads_of(cut)
            dk[:, cut] = (mm(score_grad, q, NN) * scale).astype(BF16)
            dv[:, cut] = mm(probs.astype(BF16), grad, NN).astype(BF16)

    if len(sent) > 1:
        pl.when(flags[0] > 0)(query_grads)
    pl.when(flags[1] > 0)(key_value_grads)


def attend(flags, sent, query, key, value, mask, micro):
    seq_length, width = sent[0].shape
    heads = 2
    wide = heads * HDIM
    one = pl.BlockSpec((seq_length, wide), lambda h, flags: (0, h))
    row = pl.BlockSpec((None, seq_length, wide), lambda h, flags: (micro, 0, h))
    out = jax.ShapeDtypeStruct((seq_length, width), BF16)
    outs = 1 + len(sent)
    return pl.pallas_call(
        functools.partial(attend_kernel, heads),
        grid_spec=pltpu.PrefetchScalarGridSpec(
            num_scalar_prefetch=1,
            grid=(width // wide,),
            in_specs=[one] * len(sent)
            + [
                row,
                row,
                row,
                pl.BlockSpec((None, seq_length, 1), lambda h, flags: (micro, 0, 0)),
            ],
            out_specs=[one] * outs,
        ),
        out_shape=[out] * outs,
        cost_estimate=cost(
            10 * seq_length * seq_length * width, 16 * seq_length * width
        ),
        compiler_params=SMALL,
        name="attend",
    )(flags, *sent, query, key, value, mask)


def products(at, flags, refs):
    q0, q1, k0, k1, v0, v1 = refs[:6]
    weights = refs[6:14], refs[14:22]
    total, buffer, sems = refs[-3:]
    step = pl.program_id(0)

    def copy(which, place, d):
        return pltpu.make_async_copy(
            weights[which][d], buffer.at[which, place], sems.at[which, place]
        )

    @pl.when(step == 0)
    def _():
        for place in range(4):
            for d in range(8):

                @pl.when(at[place] == d)
                def _():
                    copy(1, place, d).start()

                    @pl.when(flags[0] == 0)
                    def _():
                        copy(0, place, d).start()

    copy(1, step, 0).wait()
    rows = jnp.where(
        flags[0] > 0,
        jnp.concatenate([q0[...], q1[...]]),
        jnp.concatenate([v0[...], v1[...]]),
    )
    total[...] = mm(rows, buffer[1, step], NT)

    @pl.when(flags[0] == 0)
    def _():
        copy(0, step, 0).wait()
        total[...] += mm(jnp.concatenate([k0[...], k1[...]]), buffer[0, step], NT)

    return total[...]


def give_kernel(at, flags, *refs):
    refs[22][...] = products(at, flags, refs).astype(BF16)


def keep_kernel(at, flags, *refs):
    other, outs = refs[22], refs[23:27]
    total = products(at, flags, refs) + other[...].astype(F32)
    for i, out in enumerate(outs):

        @pl.when(pl.program_id(0) == i)
        def _():
            out[...] = total.astype(out.dtype)


def projected(at, flags, grads, first, second, other=None):
    rows, width = grads[0].shape
    shard = first[0].shape[0]
    whole = pl.BlockSpec((rows, width), lambda i, at, flags: (0, 0))
    moving = pl.BlockSpec((None, 2 * rows, shard), lambda i, at, flags: (i, 0, 0))
    fixed = pl.BlockSpec((2 * rows, shard), lambda i, at, flags: (0, 0))
    if other is None:
        kernel, extra = give_kernel, ()
        out_specs = moving
        out_shape = jax.ShapeDtypeStruct((4, 2 * rows, shard), BF16)
    else:
        kernel, extra = keep_kernel, (other,)
        out_specs = [fixed] * 4
        out_shape = [jax.ShapeDtypeStruct((2 * rows, shard), t) for t in (BF16, BF16, BF16, F32)]
    return pl.pallas_call(
        kernel,
        grid_spec=pltpu.PrefetchScalarGridSpec(
            num_scalar_prefetch=2,
            grid=(4,),
            in_specs=[whole] * 6 + [ANY] * 16 + [moving] * len(extra),
            out_specs=out_specs,
            scratch_shapes=[
                pltpu.VMEM((2 * rows, shard), F32),
                pltpu.VMEM((2, 4, shard, width), BF16),
                pltpu.SemaphoreType.DMA((2, 4)),
            ],
        ),
        out_shape=out_shape,
        cost_estimate=cost(2 * 2 * rows * 2 * width * 4 * shard, 2 * 2 * 4 * shard * width),
        compiler_params=SMALL,
    )(at, flags, *grads, *first, *second, *extra)


def per_device(out_grad, queries, enc_keys, enc_values, key_mask, weights):
    decoder = lax.axis_index("section") == 1
    half = lax.axis_index("fsdp") % 2
    line = lax.axis_index("fsdp") // 2
    segment = lax.axis_index("segment")
    core = segment % 2
    chip = segment // 2
    micro_count, reaction_count, seq_length, feature_width = out_grad.shape
    local_width = queries.shape[3]
    shard_rows = weights.shape[2]
    row_count = micro_count * reaction_count * seq_length
    flat = (micro_count, seq_length, local_width)
    micros = range(micro_count)
    dec = decoder.astype(jnp.int32)

    def gathered(shard):
        found = {0: shard}
        for d in FAR_FIRST:
            pairs = [(f, (f + 2 * d) % 16) for f in range(16)]
            found[d] = lax.ppermute(shard, "fsdp", pairs)
        return [found[d] for d in range(8)]

    grads = out_grad.reshape(row_count, feature_width)
    sources = (line - jnp.arange(8, dtype=jnp.int32)) % 8
    columns = 2 * ((line - 4 * core - jnp.arange(4, dtype=jnp.int32)) % 8) + 1 - half
    came = lax.ppermute(picked(grads, columns, shard_rows), BOTH, DEC_SWAP)
    twin = lax.ppermute(came, "segment", CORE_SWAP)

    own = (
        queries.reshape(flat),
        enc_keys.reshape(flat),
        enc_values.reshape(flat),
        key_mask.reshape(micro_count, 1, seq_length),
    )
    came_near = []
    for value in own:
        came_near.append(lax.ppermute(value, BOTH, ENC_SWAP))

    first = gathered(weights[0, 0])
    second_shard, *first[3:6] = lax.optimization_barrier((weights[0, 1], *first[3:6]))
    second = gathered(second_shard)
    near = [jnp.where(decoder, mine, other) for mine, other in zip(own, came_near)]
    near[3] = near[3].reshape(micro_count, seq_length, 1)
    own = (*own[:3], own[3].reshape(micro_count, seq_length, 1))

    piece = 2 * shard_rows
    moved = pl.BlockSpec((row_count, piece), lambda j, at: (0, j % 2))
    far = []
    for partial in partial_products(core[None], (came, twin), [moved] * 2, first, BF16, far_kernel):
        far.append(lax.ppermute(partial, BOTH, DEC_SWAP))
    own_partial = partial_products(
        2 * sources + half,
        (grads, grads),
        [
            pl.BlockSpec((row_count, shard_rows), lambda j, at: (0, at[2 * j])),
            pl.BlockSpec((row_count, shard_rows), lambda j, at: (0, at[2 * j + 1])),
        ],
        first,
        F32,
        near_kernel,
    )
    ctx, ctx_near, ctx_own = [], [], []
    for micro in micros:
        part = far[micro]
        if micro > 0:
            part, ctx[-1] = lax.optimization_barrier((part, ctx[-1]))
        ctx.append((own_partial[micro] + part.astype(F32)).astype(BF16))
        ctx_near.append(lax.ppermute(ctx[micro], BOTH, DEC_TO_ENC))
        ctx_own.append(lax.ppermute(ctx_near[micro], BOTH, ENC_SWAP))

    near_flags = jnp.stack([dec, 1 - dec])
    own_flags = jnp.stack([0 * dec, 1 - dec])

    def attended(flags, sent, held, operands):
        grads = []
        for micro in micros:
            came = sent[micro]
            if micro > 0:
                came, grads[-1] = lax.optimization_barrier((came, grads[-1]))
            grads.append(attend(flags, (came, *held[micro : micro + 1]), *operands, micro))
        return zip(*grads)

    dq, dk, dv = attended(near_flags, ctx_near, ctx, near)
    far_dq = []
    for micro in micros:
        far_dq.append(lax.ppermute(dq[micro], BOTH, DEC_SWAP))
    own_dk, own_dv = attended(own_flags, ctx_own, (), own)

    places = 2 * ((chip + jnp.array(STEPS, jnp.int32)) % 4)
    keep_at, give_at = (line - places - core) % 8, (line - places - 1 + core) % 8

    def chip_sums(grads):
        give = projected(give_at, dec[None], grads, first, second)
        other = lax.ppermute(give, "segment", CORE_SWAP)
        return projected(keep_at, dec[None], grads, first, second, other)

    def reduced(blocks, result):
        for step, block in zip(STEPS, blocks):
            pairs = [(2 * x + k, 2 * ((x + step) % 4) + k) for x in range(4) for k in range(2)]
            other = lax.ppermute(block, "segment", pairs)
            result = result + other.astype(F32)
        return result.astype(BF16)

    *blocks, block = chip_sums((*far_dq, *dk, *dv))
    own_grads, blocks = lax.optimization_barrier(((*dq, *own_dk, *own_dv), blocks))
    from_partner = lax.ppermute(reduced(blocks, block), "fsdp", HALF_SWAP)
    *blocks, block = chip_sums(own_grads)
    own_out = reduced(blocks, block)
    result = jnp.where(
        half == 0,
        jnp.concatenate([own_out, from_partner], axis=1),
        jnp.concatenate([from_partner, own_out], axis=1),
    )
    return result.reshape(1, micro_count, reaction_count, seq_length, 2 * shard_rows)


def solution(mesh):
    return jax.shard_map(
        per_device,
        mesh=mesh,
        in_specs=(
            P(None, "fsdp", None, None),
            P(None, "fsdp", None, "segment"),
            P(None, "fsdp", None, "segment"),
            P(None, "fsdp", None, "segment"),
            P(None, "fsdp", None),
            P("section", None, "fsdp", "segment"),
        ),
        out_specs=P("section", None, "fsdp", None, "segment"),
        check_vma=False,
    )
```

time: 238 us -> 382 us (1.61)
  waiting for transfers between devices: 86.4 us -> 206 us
  starting transfers between devices: 37.7 us -> 89.8 us
  Pallas kernels: 76.8 us -> 62.3 us
  between operations: 13.8 us -> 0.61 us
  local copies, waits for them, and re-layouts: 11.1 us -> 19.7 us
  other arithmetic: 11 us -> 3.27 us
    ppermute x6 -> x20, waiting for transfers between devices: 44.1 us -> 176 us  [the longest x14 158 us: gathered(): found[d] = lax.ppermute(shard, 'fsdp', pairs)]
    ppermute x6 -> x20, starting transfers between devices: 12.6 us -> 56.2 us  [the longest x14 43.1 us: gathered(): found[d] = lax.ppermute(shard, 'fsdp', pairs)]
    ppermute x2, waiting for transfers between devices: 15.4 us -> 0.01 us  [per_device(): ctx_near.append(lax.ppermute(ctx[micro], BOTH, DEC_TO_ENC))]
    unnamed x50 -> x90, local copies, waits for them, and re-layouts: 7.09 us -> 18.6 us
    pallas_call x4, Pallas kernels: 24.3 us -> 15.4 us  [attend(): pl.pallas_call(functools.partial(attend_kernel, heads), grid_spec=pltpu.P...]
    ppermute x2, waiting for transfers between devices: 6.65 us -> 11.5 us  [per_device(): ctx_own.append(lax.ppermute(ctx_near[micro], BOTH, ENC_SWAP))]
    ppermute x2, starting transfers between devices: 1.72 us -> 6.1 us  [chip_sums(): other = lax.ppermute(give, 'segment', CORE_SWAP)]
  transfers between devices with their start and end apart: 25 -> 37, of which waited for: 9 -> 16; matrix products, arithmetic and copies ran while one was open for 5% -> 1% of each run, Pallas kernels for 22% -> 10%
where the time goes in v3:
time: 382 us; the launch traced here: 381 us
  waiting for transfers between devices  206 us (54%)
  starting transfers between devices  89.8 us (24%)
  Pallas kernels  62.3 us (16%)
  local copies, waits for them, and re-layouts  19.7 us (5%)
    ppermute x14, waiting for transfers between devices, gathered(): found[d] = lax.ppermute(shard, 'fsdp', pairs)  158 us
    ppermute x14, starting transfers between devices, gathered(): found[d] = lax.ppermute(shard, 'fsdp', pairs)  43.1 us
    pallas_call x4, Pallas kernels, projected(): pl.pallas_call(kernel, grid_spec=pltpu.PrefetchScalarGridSpec(num_scalar_...  31.6 us
    unnamed x90, local copies, waits for them, and re-layouts  18.6 us
    ppermute x6, waiting for transfers between devices, reduced(): other = lax.ppermute(block, 'segment', pairs)  18.4 us
    ppermute x4, waiting for transfers between devices, per_device(): came_near.append(lax.ppermute(value, BOTH, ENC_SWAP))  17.5 us
    pallas_call x4, Pallas kernels, attend(): pl.pallas_call(functools.partial(attend_kernel, heads), grid_spec=pltpu.P...  15.4 us
    pallas_call x2, Pallas kernels, partial_products(): pl.pallas_call(kernel, grid_spec=pltpu.PrefetchScalarGridSpec(num_scalar_...  14.2 us
  transfers between devices with their start and end apart: 37, of which 16 were waited for; matrix products, arithmetic and copies ran while one was open for 1% of the time, Pallas kernels for 10%

profile of v3, /device:TPU:1, one launch (start us, length us, event | category | flops | bytes accessed | tf_op | source)
XLA Modules:
  0.0 381.3 jit_solution(7465070127564564975)
XLA Ops:
  0.0 2.8 copy-done
  3.9 1.8 collective-permute-start.7
  5.7 3.2 collective-permute-start.8
  9.8 2.6 collective-permute-start.2
  12.5 4.2 %collective-permute-start.3 = (bf16[384,768]{1,0:T(8,128)(2,1)S(1)}, bf16[384,768]{1,0:T(8,128)(2,1)S(1)}, u32[]{:S(2)}, u32[]{:S(2)}) collective-permute-start(bf16[384,768]{1,0:T(8,128)(2,1)S(1)} %get-tuple-element.98.refs_0_.refs_6_), channel_id=1, source_target_pairs={{0,8},{1,9},{2,10},{3,11},{4,12},{5,13},{6,14},{7,15},{8,0},{9,1},... | collective-permute-start | bytes 1769480 | tf_op jit(solution)/shard_map/ppermute | solution.py:305
  16.7 2.8 collective-permute-start.4
  20.2 31.2 %collective-permute-done.2.refs_3_.refs_9_ = bf16[384,768]{1,0:T(8,128)(2,1)S(1)} collective-permute-done((bf16[384,768]{1,0:T(8,128)(2,1)S(1)}, bf16[384,768]{1,0:T(8,128)(2,1)S(1)}, u32[]{:S(2)}, u32[]{:S(2)}) %collective-permute-start.2) | collective-permute-done | bytes 589856 | tf_op jit(solution)/shard_map/ppermute | solution.py:305
  52.2 24.3 %collective-permute-done.3.refs_4_.refs_10_ = bf16[384,768]{1,0:T(8,128)(2,1)S(1)} collective-permute-done((bf16[384,768]{1,0:T(8,128)(2,1)S(1)}, bf16[384,768]{1,0:T(8,128)(2,1)S(1)}, u32[]{:S(2)}, u32[]{:S(2)}) %collective-permute-start.3) | collective-permute-done | bytes 589856 | tf_op jit(solution)/shard_map/ppermute | solution.py:305
  77.3 5.7 %collective-permute-start.5 = (bf16[384,768]{1,0:T(8,128)(2,1)S(1)}, bf16[384,768]{1,0:T(8,128)(2,1)}, u32[]{:S(2)}, u32[]{:S(2)}) collective-permute-start(bf16[384,768]{1,0:T(8,128)(2,1)S(1)} %get-tuple-element.98.refs_0_.refs_6_), channel_id=1, source_target_pairs={{0,12},{1,13},{2,14},{3,15},{4,0},{5,1},{6,2},{7,3},{8,4},{9,5},{1... | collective-permute-start | bytes 1769480 | tf_op jit(solution)/shard_map/ppermute | solution.py:305
  83.8 4.5 %collective-permute-start.6 = (bf16[384,768]{1,0:T(8,128)(2,1)S(1)}, bf16[384,768]{1,0:T(8,128)(2,1)}, u32[]{:S(2)}, u32[]{:S(2)}) collective-permute-start(bf16[384,768]{1,0:T(8,128)(2,1)S(1)} %get-tuple-element.98.refs_0_.refs_6_), channel_id=1, source_target_pairs={{0,14},{1,15},{2,0},{3,1},{4,2},{5,3},{6,4},{7,5},{8,6},{9,7},{10,... | collective-permute-start | bytes 1769480 | tf_op jit(solution)/shard_map/ppermute | solution.py:305
  88.3 2.4 collective-permute-done.refs_1_.refs_7_
  90.7 3.2 collective-permute-start.15
  93.9 17.4 %collective-permute-done.1.refs_2_.refs_8_ = bf16[384,768]{1,0:T(8,128)(2,1)} collective-permute-done((bf16[384,768]{1,0:T(8,128)(2,1)S(1)}, bf16[384,768]{1,0:T(8,128)(2,1)}, u32[]{:S(2)}, u32[]{:S(2)}) %collective-permute-start.1) | collective-permute-done | bytes 589856 | tf_op jit(solution)/shard_map/ppermute | solution.py:305
  111.3 3.2 collective-permute-start.14
  114.5 2.1 collective-permute-start.13
  117.1 3.2 collective-permute-start.16
  122.5 8.0 %shard_map.74 = (bf16[256,768]{1,0:T(8,128)(2,1)S(1)}, bf16[256,768]{1,0:T(8,128)(2,1)S(1)}) custom-call(s32[1]{0:T(128)} %bitcast.4.core, bf16[512,1536]{1,0:T(8,128)(2,1)} %collective-permute-done.7.came, bf16[512,1536]{1,0:T(8,128)(2,1)} %collective-permute-done.8.twin, bf16[384,768]{1,0:T(8,128)(2,1)S(1)} %get-tuple-element.98.refs_0_.refs_6_, ...), custom_call_target="tpu_custom_call" | custom-call | flops 2415919104 | bytes 4718592 | tf_op jit(solution)/shard_map/pallas_call | solution.py:119
  131.3 17.5 %collective-permute-done.16 = s32[2,1,256]{2,1,0:T(1,128)S(1)} collective-permute-done((s32[2,1,256]{2,1,0:T(1,128)S(1)}, s32[2,1,256]{2,1,0:T(1,128)S(1)}, u32[]{:S(2)}, u32[]{:S(2)}) %collective-permute-start.16) | collective-permute-done | bytes 2080 | tf_op jit(solution)/shard_map/ppermute | solution.py:322
  149.6 6.2 %shard_map.73 = (f32[256,768]{1,0:T(8,128)S(1)}, f32[256,768]{1,0:T(8,128)S(1)}) custom-call(s32[8]{0:T(128)S(1)} %fusion.5.columns, bf16[512,6144]{1,0:T(8,128)(2,1)S(1)} %bitcast.23, bf16[512,6144]{1,0:T(8,128)(2,1)S(1)} %bitcast.24, bf16[384,768]{1,0:T(8,128)(2,1)S(1)} %get-tuple-element.98.refs_0_.refs_6_, ...), custom_call_target="tpu_custom_call" | custom-call | flops 2415919104 | bytes 4718592 | tf_op jit(solution)/shard_map/pallas_call | solution.py:119
  155.8 5.9 %collective-permute-start.21 = (bf16[384,768]{1,0:T(8,128)(2,1)}, bf16[384,768]{1,0:T(8,128)(2,1)S(1)}, u32[]{:S(2)}, u32[]{:S(2)}) collective-permute-start(bf16[384,768]{1,0:T(8,128)(2,1)} %get-tuple-element.75.refs_14_), channel_id=1, source_target_pairs={{0,2},{1,3},{2,4},{3,5},{4,6},{5,7},{6,8},{7,9},{8,10},{9,11},{10,... | collective-permute-start | bytes 1769480 | tf_op jit(solution)/shard_map/ppermute | solution.py:305
  166.0 3.5 collective-permute-start.23
  169.5 5.2 %collective-permute-done.21.refs_15_ = bf16[384,768]{1,0:T(8,128)(2,1)S(1)} collective-permute-done((bf16[384,768]{1,0:T(8,128)(2,1)}, bf16[384,768]{1,0:T(8,128)(2,1)S(1)}, u32[]{:S(2)}, u32[]{:S(2)}) %collective-permute-start.21) | collective-permute-done | bytes 589856 | tf_op jit(solution)/shard_map/ppermute | solution.py:305
  174.6 3.3 collective-permute-start.24
  178.1 23.3 %collective-permute-done.22.refs_16_ = bf16[384,768]{1,0:T(8,128)(2,1)S(1)} collective-permute-done((bf16[384,768]{1,0:T(8,128)(2,1)}, bf16[384,768]{1,0:T(8,128)(2,1)S(1)}, u32[]{:S(2)}, u32[]{:S(2)}) %collective-permute-start.22) | collective-permute-done | bytes 589856 | tf_op jit(solution)/shard_map/ppermute | solution.py:305
  202.2 3.4 collective-permute-start.26
  205.6 4.5 %collective-permute-start.27 = (bf16[384,768]{1,0:T(8,128)(2,1)}, bf16[384,768]{1,0:T(8,128)(2,1)}, u32[]{:S(2)}, u32[]{:S(2)}) collective-permute-start(bf16[384,768]{1,0:T(8,128)(2,1)} %get-tuple-element.75.refs_14_), channel_id=1, source_target_pairs={{0,14},{1,15},{2,0},{3,1},{4,2},{5,3},{6,4},{7,5},{8,6},{9,7},{10,... | collective-permute-start | bytes 1769480 | tf_op jit(solution)/shard_map/ppermute | solution.py:305
  210.2 3.7 attend.4
  214.8 4.4 %attend.5 = (bf16[256,768]{1,0:T(8,128)(2,1)}, bf16[256,768]{1,0:T(8,128)(2,1)S(1)}, bf16[256,768]{1,0:T(8,128)(2,1)S(1)}) custom-call(s32[2]{0:T(128)S(1)} %pad_add_fusion.flags, bf16[256,768]{1,0:T(8,128)(2,1)S(1)} %collective-permute-done.11.refs_0_, bf16[256,768]{1,0:T(8,128)(2,1)S(1)} %add_convert_fusion.2.refs_1_, ...), custom_call_target="tpu_custom_call" | custom-call | flops 503316480 | bytes 3145728 | tf_op jit(solution)/shard_map/attend/pallas_call | solution.py:176
  220.7 14.6 %collective-permute-done.23.refs_17_ = bf16[384,768]{1,0:T(8,128)(2,1)S(1)} collective-permute-done((bf16[384,768]{1,0:T(8,128)(2,1)}, bf16[384,768]{1,0:T(8,128)(2,1)S(1)}, u32[]{:S(2)}, u32[]{:S(2)}) %collective-permute-start.23) | collective-permute-done | bytes 589856 | tf_op jit(solution)/shard_map/ppermute | solution.py:305
  237.6 29.0 %collective-permute-done.24.refs_18_ = bf16[384,768]{1,0:T(8,128)(2,1)S(1)} collective-permute-done((bf16[384,768]{1,0:T(8,128)(2,1)}, bf16[384,768]{1,0:T(8,128)(2,1)S(1)}, u32[]{:S(2)}, u32[]{:S(2)}) %collective-permute-start.24) | collective-permute-done | bytes 589856 | tf_op jit(solution)/shard_map/ppermute | solution.py:305
  268.8 10.5 %collective-permute-done.27.refs_21_ = bf16[384,768]{1,0:T(8,128)(2,1)} collective-permute-done((bf16[384,768]{1,0:T(8,128)(2,1)}, bf16[384,768]{1,0:T(8,128)(2,1)}, u32[]{:S(2)}, u32[]{:S(2)}) %collective-permute-start.27) | collective-permute-done | bytes 589856 | tf_op jit(solution)/shard_map/ppermute | solution.py:305
  286.5 7.7 %shard_map.75 = bf16[4,512,384]{2,1,0:T(8,128)(2,1)S(1)} custom-call(s32[4]{0:T(128)S(1)} %get-tuple-element.95.at, s32[1]{0:T(128)} %bitcast.flags, bf16[256,768]{1,0:T(8,128)(2,1)} %collective-permute-done.19.refs_0_, bf16[256,768]{1,0:T(8,128)(2,1)} %collective-permute-done.20.refs_1_, bf16[256,768]{1,0:T(8,128)(2,1)S(1)} %copy-done.24, ...), custom_call_target="tpu_custom_call" | custom-call | flops 2415919104 | bytes 4718592 | tf_op jit(solution)/shard_map/pallas_call | solution.py:267
  294.3 5.1 %collective-permute-start.28 = (bf16[4,512,384]{2,1,0:T(8,128)(2,1)S(1)}, bf16[4,512,384]{2,1,0:T(8,128)(2,1)S(1)}, u32[]{:S(2)}, u32[]{:S(2)}) collective-permute-start(bf16[4,512,384]{2,1,0:T(8,128)(2,1)S(1)} %shard_map.75), channel_id=1, source_target_pairs={{0,16},{16,0},{32,48},{48,32},{64,80},{80,64},{96,112},{112,96},{1... | collective-permute-start | bytes 4718600 | tf_op jit(solution)/shard_map/ppermute | solution.py:379
  299.4 3.2 collective-permute-start.18
  302.6 2.3 collective-permute-start.17
  305.1 6.8 %collective-permute-done.18.refs_0_ = bf16[256,768]{1,0:T(8,128)(2,1)S(1)} collective-permute-done((bf16[256,768]{1,0:T(8,128)(2,1)S(1)}, bf16[256,768]{1,0:T(8,128)(2,1)S(1)}, u32[]{:S(2)}, u32[]{:S(2)}) %collective-permute-start.18) | collective-permute-done | bytes 393248 | tf_op jit(solution)/shard_map/ppermute | solution.py:354
  311.9 3.6 attend.6
  315.6 4.7 %collective-permute-done.17.refs_0_ = bf16[256,768]{1,0:T(8,128)(2,1)S(1)} collective-permute-done((bf16[256,768]{1,0:T(8,128)(2,1)S(1)}, bf16[256,768]{1,0:T(8,128)(2,1)S(1)}, u32[]{:S(2)}, u32[]{:S(2)}) %collective-permute-start.17) | collective-permute-done | bytes 393248 | tf_op jit(solution)/shard_map/ppermute | solution.py:354
  320.3 3.6 attend.7
  324.1 7.8 %shard_map.76 = (bf16[512,384]{1,0:T(8,128)(2,1)S(1)}, bf16[512,384]{1,0:T(8,128)(2,1)S(1)}, bf16[512,384]{1,0:T(8,128)(2,1)S(1)}, f32[512,384]{1,0:T(8,128)S(1)}) custom-call(s32[4]{0:T(128)S(1)} %and_select_fusion.3.at, s32[1]{0:T(128)} %bitcast.flags, bf16[256,768]{1,0:T(8,128)(2,1)} %collective-permute-done.19.refs_0_, ...), custom_call_target="tpu_custom_call" | custom-call | flops 2415919104 | bytes 4718592 | tf_op jit(solution)/shard_map/pallas_call | solution.py:267
  331.9 7.3 %shard_map.77 = bf16[4,512,384]{2,1,0:T(8,128)(2,1)S(1)} custom-call(s32[4]{0:T(128)S(1)} %get-tuple-element.95.at, s32[1]{0:T(128)} %bitcast.flags, bf16[256,768]{1,0:T(8,128)(2,1)S(1)} %get-tuple-element.79.refs_0_, bf16[256,768]{1,0:T(8,128)(2,1)} %get-tuple-element.80.refs_1_, bf16[256,768]{1,0:T(8,128)(2,1)S(1)} %get-tuple-element.81.refs_2_, ...), custom_call_target="tpu_custom_call" | custom-call | flops 2415919104 | bytes 4718592 | tf_op jit(solution)/shard_map/pallas_call | solution.py:267
  340.2 3.9 %collective-permute-start.33 = (bf16[512,384]{1,0:T(8,128)(2,1)S(1)}, bf16[512,384]{1,0:T(8,128)(2,1)S(1)}, u32[]{:S(2)}, u32[]{:S(2)}) collective-permute-start(bf16[512,384]{1,0:T(8,128)(2,1)S(1)} %get-tuple-element.90), channel_id=1, source_target_pairs={{0,64},{16,80},{32,96},{48,112},{64,0},{80,16},{96,32},{112,48},{1... | collective-permute-start | bytes 1179656 | tf_op jit(solution)/shard_map/ppermute | solution.py:385
  344.4 2.4 collective-permute-start.35
  346.8 8.7 %shard_map.78 = (bf16[512,384]{1,0:T(8,128)(2,1)}, bf16[512,384]{1,0:T(8,128)(2,1)}, bf16[512,384]{1,0:T(8,128)(2,1)}, f32[512,384]{1,0:T(8,128)S(1)}) custom-call(s32[4]{0:T(128)S(1)} %and_select_fusion.3.at, s32[1]{0:T(128)} %bitcast.flags, bf16[256,768]{1,0:T(8,128)(2,1)S(1)} %get-tuple-element.79.refs_0_, bf16[256,768]{1,0:T(8,128)(2,1)} %get-tuple-element.80.refs_1_, ...), custom_call_target="tpu_custom_call" | custom-call | flops 2415919104 | bytes 4718592 | tf_op jit(solution)/shard_map/pallas_call | solution.py:267
  356.7 2.4 collective-permute-start.32
  359.0 3.2 collective-permute-done.34
  363.8 6.6 %collective-permute-done.30 = bf16[512,384]{1,0:T(8,128)(2,1)S(1)} collective-permute-done((bf16[512,384]{1,0:T(8,128)(2,1)}, bf16[512,384]{1,0:T(8,128)(2,1)S(1)}, u32[]{:S(2)}, u32[]{:S(2)}) %collective-permute-start.30) | collective-permute-done | bytes 393248 | tf_op jit(solution)/shard_map/ppermute | solution.py:385
  370.4 8.5 %collective-permute-done.31 = bf16[512,384]{1,0:T(8,128)(2,1)S(1)} collective-permute-done((bf16[512,384]{1,0:T(8,128)(2,1)}, bf16[512,384]{1,0:T(8,128)(2,1)S(1)}, u32[]{:S(2)}, u32[]{:S(2)}) %collective-permute-start.31) | collective-permute-done | bytes 393248 | tf_op jit(solution)/shard_map/ppermute | solution.py:385
  (146 shorter events, 35.2 us)
Async XLA Ops:
  3.9 113.2 %copy-start.41 = (s32[2,1,256]{2,1,0:T(1,128)S(1)}, s32[2,1,256]{2,1,0:T(1,128)}, u32[]{:S(2)}) copy-start(s32[2,1,256]{2,1,0:T(1,128)} %param.11) | copy-start | bytes 6148
  3.9 1.8 collective-permute-start.7
  5.7 114.6 %collective-permute-start.8 = (bf16[512,1536]{1,0:T(8,128)(2,1)}, bf16[512,1536]{1,0:T(8,128)(2,1)}, u32[]{:S(2)}, u32[]{:S(2)}) collective-permute-start(bf16[512,1536]{1,0:T(8,128)(2,1)} %collective-permute-done.7.came), channel_id=1, source_target_pairs={{0,16},{16,0},{32,48},{48,32},{64,80},{80,64},{96,112},{112,96},{1... | collective-permute-start | bytes 4718600 | tf_op jit(solution)/shard_map/ppermute | solution.py:312
  8.9 140.7 %slice-start = ((s8[6291456]{0:T(1024)(128)(4,1)}), s8[2097152]{0:T(1024)(128)(4,1)S(1)}, s32[]{:S(2)}) async-start(s8[6291456]{0:T(1024)(128)(4,1)} %bitcast.21), calls=%async_computation | async-start | bytes 4194304
  9.8 41.6 %collective-permute-start.2 = (bf16[384,768]{1,0:T(8,128)(2,1)S(1)}, bf16[384,768]{1,0:T(8,128)(2,1)S(1)}, u32[]{:S(2)}, u32[]{:S(2)}) collective-permute-start(bf16[384,768]{1,0:T(8,128)(2,1)S(1)} %get-tuple-element.98.refs_0_.refs_6_), channel_id=1, source_target_pairs={{0,6},{1,7},{2,8},{3,9},{4,10},{5,11},{6,12},{7,13},{8,14},{9,15},... | collective-permute-start | bytes 1769480 | tf_op jit(solution)/shard_map/ppermute | solution.py:305
  12.5 64.0 %collective-permute-start.3 = (bf16[384,768]{1,0:T(8,128)(2,1)S(1)}, bf16[384,768]{1,0:T(8,128)(2,1)S(1)}, u32[]{:S(2)}, u32[]{:S(2)}) collective-permute-start(bf16[384,768]{1,0:T(8,128)(2,1)S(1)} %get-tuple-element.98.refs_0_.refs_6_), channel_id=1, source_target_pairs={{0,8},{1,9},{2,10},{3,11},{4,12},{5,13},{6,14},{7,15},{8,0},{9,1},... | collective-permute-start | bytes 1769480 | tf_op jit(solution)/shard_map/ppermute | solution.py:305
  16.7 66.3 %collective-permute-start.4 = (bf16[384,768]{1,0:T(8,128)(2,1)S(1)}, bf16[384,768]{1,0:T(8,128)(2,1)S(1)}, u32[]{:S(2)}, u32[]{:S(2)}) collective-permute-start(bf16[384,768]{1,0:T(8,128)(2,1)S(1)} %get-tuple-element.98.refs_0_.refs_6_), channel_id=1, source_target_pairs={{0,10},{1,11},{2,12},{3,13},{4,14},{5,15},{6,0},{7,1},{8,2},{9,3},... | collective-permute-start | bytes 1769480 | tf_op jit(solution)/shard_map/ppermute | solution.py:305
  19.5 71.2 %collective-permute-start = (bf16[384,768]{1,0:T(8,128)(2,1)S(1)}, bf16[384,768]{1,0:T(8,128)(2,1)}, u32[]{:S(2)}, u32[]{:S(2)}) collective-permute-start(bf16[384,768]{1,0:T(8,128)(2,1)S(1)} %get-tuple-element.98.refs_0_.refs_6_), channel_id=1, source_target_pairs={{0,2},{1,3},{2,4},{3,5},{4,6},{5,7},{6,8},{7,9},{8,10},{9,11},{10,... | collective-permute-start | bytes 1769480 | tf_op jit(solution)/shard_map/ppermute | solution.py:305
  51.4 59.9 %collective-permute-start.1 = (bf16[384,768]{1,0:T(8,128)(2,1)S(1)}, bf16[384,768]{1,0:T(8,128)(2,1)}, u32[]{:S(2)}, u32[]{:S(2)}) collective-permute-start(bf16[384,768]{1,0:T(8,128)(2,1)S(1)} %get-tuple-element.98.refs_0_.refs_6_), channel_id=1, source_target_pairs={{0,4},{1,5},{2,6},{3,7},{4,8},{5,9},{6,10},{7,11},{8,12},{9,13},{1... | collective-permute-start | bytes 1769480 | tf_op jit(solution)/shard_map/ppermute | solution.py:305
  77.3 37.2 %collective-permute-start.5 = (bf16[384,768]{1,0:T(8,128)(2,1)S(1)}, bf16[384,768]{1,0:T(8,128)(2,1)}, u32[]{:S(2)}, u32[]{:S(2)}) collective-permute-start(bf16[384,768]{1,0:T(8,128)(2,1)S(1)} %get-tuple-element.98.refs_0_.refs_6_), channel_id=1, source_target_pairs={{0,12},{1,13},{2,14},{3,15},{4,0},{5,1},{6,2},{7,3},{8,4},{9,5},{1... | collective-permute-start | bytes 1769480 | tf_op jit(solution)/shard_map/ppermute | solution.py:305
  83.8 33.3 %collective-permute-start.6 = (bf16[384,768]{1,0:T(8,128)(2,1)S(1)}, bf16[384,768]{1,0:T(8,128)(2,1)}, u32[]{:S(2)}, u32[]{:S(2)}) collective-permute-start(bf16[384,768]{1,0:T(8,128)(2,1)S(1)} %get-tuple-element.98.refs_0_.refs_6_), channel_id=1, source_target_pairs={{0,14},{1,15},{2,0},{3,1},{4,2},{5,3},{6,4},{7,5},{8,6},{9,7},{10,... | collective-permute-start | bytes 1769480 | tf_op jit(solution)/shard_map/ppermute | solution.py:305
  90.7 72.4 %collective-permute-start.15 = (bf16[2,256,768]{2,1,0:T(8,128)(2,1)}, bf16[2,256,768]{2,1,0:T(8,128)(2,1)S(1)}, u32[]{:S(2)}, u32[]{:S(2)}) collective-permute-start(bf16[2,256,768]{2,1,0:T(8,128)(2,1)} %bitcast.31), channel_id=1, source_target_pairs={{0,1},{1,0},{2,3},{3,2},{4,5},{5,4},{6,7},{7,6},{8,9},{9,8},{10,11... | collective-permute-start | bytes 2359304 | tf_op jit(solution)/shard_map/ppermute | solution.py:322
  111.3 53.2 %collective-permute-start.14 = (bf16[2,256,768]{2,1,0:T(8,128)(2,1)}, bf16[2,256,768]{2,1,0:T(8,128)(2,1)S(1)}, u32[]{:S(2)}, u32[]{:S(2)}) collective-permute-start(bf16[2,256,768]{2,1,0:T(8,128)(2,1)} %bitcast.28), channel_id=1, source_target_pairs={{0,1},{1,0},{2,3},{3,2},{4,5},{5,4},{6,7},{7,6},{8,9},{9,8},{10,11... | collective-permute-start | bytes 2359304 | tf_op jit(solution)/shard_map/ppermute | solution.py:322
  114.5 51.5 %collective-permute-start.13 = (bf16[2,256,768]{2,1,0:T(8,128)(2,1)}, bf16[2,256,768]{2,1,0:T(8,128)(2,1)S(1)}, u32[]{:S(2)}, u32[]{:S(2)}) collective-permute-start(bf16[2,256,768]{2,1,0:T(8,128)(2,1)} %bitcast.25), channel_id=1, source_target_pairs={{0,1},{1,0},{2,3},{3,2},{4,5},{5,4},{6,7},{7,6},{8,9},{9,8},{10,11... | collective-permute-start | bytes 2359304 | tf_op jit(solution)/shard_map/ppermute | solution.py:322
  117.1 31.6 %collective-permute-start.16 = (s32[2,1,256]{2,1,0:T(1,128)S(1)}, s32[2,1,256]{2,1,0:T(1,128)S(1)}, u32[]{:S(2)}, u32[]{:S(2)}) collective-permute-start(s32[2,1,256]{2,1,0:T(1,128)S(1)} %copy-done.41), channel_id=1, source_target_pairs={{0,1},{1,0},{2,3},{3,2},{4,5},{5,4},{6,7},{7,6},{8,9},{9,8},{10,11... | collective-permute-start | bytes 6152 | tf_op jit(solution)/shard_map/ppermute | solution.py:322
  122.5 27.2 %slice-start.1 = ((s8[6291456]{0:T(1024)(128)(4,1)}), s8[4194304]{0:T(1024)(128)(4,1)S(1)}, s32[]{:S(2)}) async-start(s8[6291456]{0:T(1024)(128)(4,1)} %bitcast.21), calls=%async_computation.1 | async-start | bytes 8388608
  122.5 27.2 %copy-start.3 = (bf16[384,768]{1,0:T(8,128)(2,1)S(1)}, bf16[384,768]{1,0:T(8,128)(2,1)}, u32[]{:S(2)}) copy-start(bf16[384,768]{1,0:T(8,128)(2,1)} %copy-done.1) | copy-start | bytes 1769476
  130.5 25.3 %collective-permute-start.10 = (bf16[256,768]{1,0:T(8,128)(2,1)S(1)}, bf16[256,768]{1,0:T(8,128)(2,1)S(1)}, u32[]{:S(2)}, u32[]{:S(2)}) collective-permute-start(bf16[256,768]{1,0:T(8,128)(2,1)S(1)} %get-tuple-element.55), channel_id=1, source_target_pairs={{128,129},{129,128},{130,131},{131,130},{132,133},{133,132},{134,1... | collective-permute-start | bytes 1179656 | tf_op jit(solution)/shard_map/ppermute | solution.py:335
  148.9 12.9 %collective-permute-start.9 = (bf16[256,768]{1,0:T(8,128)(2,1)S(1)}, bf16[256,768]{1,0:T(8,128)(2,1)S(1)}, u32[]{:S(2)}, u32[]{:S(2)}) collective-permute-start(bf16[256,768]{1,0:T(8,128)(2,1)S(1)} %get-tuple-element.53), channel_id=1, source_target_pairs={{128,129},{129,128},{130,131},{131,130},{132,133},{133,132},{134,1... | collective-permute-start | bytes 1179656 | tf_op jit(solution)/shard_map/ppermute | solution.py:335
  155.8 18.8 %collective-permute-start.21 = (bf16[384,768]{1,0:T(8,128)(2,1)}, bf16[384,768]{1,0:T(8,128)(2,1)S(1)}, u32[]{:S(2)}, u32[]{:S(2)}) collective-permute-start(bf16[384,768]{1,0:T(8,128)(2,1)} %get-tuple-element.75.refs_14_), channel_id=1, source_target_pairs={{0,2},{1,3},{2,4},{3,5},{4,6},{5,7},{6,8},{7,9},{8,10},{9,11},{10,... | collective-permute-start | bytes 1769480 | tf_op jit(solution)/shard_map/ppermute | solution.py:305
  161.9 39.5 %collective-permute-start.22 = (bf16[384,768]{1,0:T(8,128)(2,1)}, bf16[384,768]{1,0:T(8,128)(2,1)S(1)}, u32[]{:S(2)}, u32[]{:S(2)}) collective-permute-start(bf16[384,768]{1,0:T(8,128)(2,1)} %get-tuple-element.75.refs_14_), channel_id=1, source_target_pairs={{0,4},{1,5},{2,6},{3,7},{4,8},{5,9},{6,10},{7,11},{8,12},{9,13},{1... | collective-permute-start | bytes 1769480 | tf_op jit(solution)/shard_map/ppermute | solution.py:305
  163.1 39.1 %collective-permute-start.12 = (bf16[256,768]{1,0:T(8,128)(2,1)S(1)}, bf16[256,768]{1,0:T(8,128)(2,1)S(1)}, u32[]{:S(2)}, u32[]{:S(2)}) collective-permute-start(bf16[256,768]{1,0:T(8,128)(2,1)S(1)} %add_convert_fusion.3.refs_1_), channel_id=1, source_target_pairs={{128,1},{129,0},{130,3},{131,2},{132,5},{133,4},{134,7},{135,6},{1... | collective-permute-start | bytes 1179656 | tf_op jit(solution)/shard_map/ppermute | solution.py:353
  164.5 41.0 %collective-permute-start.11 = (bf16[256,768]{1,0:T(8,128)(2,1)S(1)}, bf16[256,768]{1,0:T(8,128)(2,1)S(1)}, u32[]{:S(2)}, u32[]{:S(2)}) collective-permute-start(bf16[256,768]{1,0:T(8,128)(2,1)S(1)} %add_convert_fusion.2.refs_1_), channel_id=1, source_target_pairs={{128,1},{129,0},{130,3},{131,2},{132,5},{133,4},{134,7},{135,6},{1... | collective-permute-start | bytes 1179656 | tf_op jit(solution)/shard_map/ppermute | solution.py:353
  166.0 44.2 %copy-start.17 = (bf16[2,1,256,768]{3,2,1,0:T(8,128)(2,1)S(1)}, bf16[2,1,256,768]{3,2,1,0:T(8,128)(2,1)}, u32[]{:S(2)}) copy-start(bf16[2,1,256,768]{3,2,1,0:T(8,128)(2,1)} %param.8) | copy-start | bytes 2359300
  166.0 69.3 %collective-permute-start.23 = (bf16[384,768]{1,0:T(8,128)(2,1)}, bf16[384,768]{1,0:T(8,128)(2,1)S(1)}, u32[]{:S(2)}, u32[]{:S(2)}) collective-permute-start(bf16[384,768]{1,0:T(8,128)(2,1)} %get-tuple-element.75.refs_14_), channel_id=1, source_target_pairs={{0,6},{1,7},{2,8},{3,9},{4,10},{5,11},{6,12},{7,13},{8,14},{9,15},... | collective-permute-start | bytes 1769480 | tf_op jit(solution)/shard_map/ppermute | solution.py:305
  174.6 91.9 %collective-permute-start.24 = (bf16[384,768]{1,0:T(8,128)(2,1)}, bf16[384,768]{1,0:T(8,128)(2,1)S(1)}, u32[]{:S(2)}, u32[]{:S(2)}) collective-permute-start(bf16[384,768]{1,0:T(8,128)(2,1)} %get-tuple-element.75.refs_14_), channel_id=1, source_target_pairs={{0,8},{1,9},{2,10},{3,11},{4,12},{5,13},{6,14},{7,15},{8,0},{9,1},... | collective-permute-start | bytes 1769480 | tf_op jit(solution)/shard_map/ppermute | solution.py:305
  202.2 66.7 %collective-permute-start.25 = (bf16[384,768]{1,0:T(8,128)(2,1)}, bf16[384,768]{1,0:T(8,128)(2,1)}, u32[]{:S(2)}, u32[]{:S(2)}) collective-permute-start(bf16[384,768]{1,0:T(8,128)(2,1)} %get-tuple-element.75.refs_14_), channel_id=1, source_target_pairs={{0,10},{1,11},{2,12},{3,13},{4,14},{5,15},{6,0},{7,1},{8,2},{9,3},... | collective-permute-start | bytes 1769480 | tf_op jit(solution)/shard_map/ppermute | solution.py:305
  202.2 66.7 %collective-permute-start.26 = (bf16[384,768]{1,0:T(8,128)(2,1)}, bf16[384,768]{1,0:T(8,128)(2,1)}, u32[]{:S(2)}, u32[]{:S(2)}) collective-permute-start(bf16[384,768]{1,0:T(8,128)(2,1)} %get-tuple-element.75.refs_14_), channel_id=1, source_target_pairs={{0,12},{1,13},{2,14},{3,15},{4,0},{5,1},{6,2},{7,3},{8,4},{9,5},{1... | collective-permute-start | bytes 1769480 | tf_op jit(solution)/shard_map/ppermute | solution.py:305
  205.6 73.7 %collective-permute-start.27 = (bf16[384,768]{1,0:T(8,128)(2,1)}, bf16[384,768]{1,0:T(8,128)(2,1)}, u32[]{:S(2)}, u32[]{:S(2)}) collective-permute-start(bf16[384,768]{1,0:T(8,128)(2,1)} %get-tuple-element.75.refs_14_), channel_id=1, source_target_pairs={{0,14},{1,15},{2,0},{3,1},{4,2},{5,3},{6,4},{7,5},{8,6},{9,7},{10,... | collective-permute-start | bytes 1769480 | tf_op jit(solution)/shard_map/ppermute | solution.py:305
  214.7 54.1 %copy-start.42 = (s32[4]{0:T(128)S(1)}, s32[4]{0:T(128)}, u32[]{:S(2)}) copy-start(s32[4]{0:T(128)} %constant.102.clone) | copy-start | bytes 52
  214.7 64.6 %copy-start.4 = (bf16[384,768]{1,0:T(8,128)(2,1)S(1)}, bf16[384,768]{1,0:T(8,128)(2,1)}, u32[]{:S(2)}) copy-start(bf16[384,768]{1,0:T(8,128)(2,1)} %copy-done.1) | copy-start | bytes 1769476
  214.7 64.6 %copy-start.7 = (bf16[384,768]{1,0:T(8,128)(2,1)S(1)}, bf16[384,768]{1,0:T(8,128)(2,1)}, u32[]{:S(2)}) copy-start(bf16[384,768]{1,0:T(8,128)(2,1)} %copy-done.5) | copy-start | bytes 1769476
  236.2 43.2 %collective-permute-start.20 = (bf16[256,768]{1,0:T(8,128)(2,1)}, bf16[256,768]{1,0:T(8,128)(2,1)}, u32[]{:S(2)}, u32[]{:S(2)}) collective-permute-start(bf16[256,768]{1,0:T(8,128)(2,1)} %get-tuple-element.80.refs_1_), channel_id=1, source_target_pairs={{128,129},{129,128},{130,131},{131,130},{132,133},{133,132},{134,1... | collective-permute-start | bytes 1179656 | tf_op jit(solution)/shard_map/ppermute | solution.py:371
  267.4 11.9 %collective-permute-start.19 = (bf16[256,768]{1,0:T(8,128)(2,1)S(1)}, bf16[256,768]{1,0:T(8,128)(2,1)}, u32[]{:S(2)}, u32[]{:S(2)}) collective-permute-start(bf16[256,768]{1,0:T(8,128)(2,1)S(1)} %get-tuple-element.79.refs_0_), channel_id=1, source_target_pairs={{128,129},{129,128},{130,131},{131,130},{132,133},{133,132},{134,1... | collective-permute-start | bytes 1179656 | tf_op jit(solution)/shard_map/ppermute | solution.py:371
  286.5 25.4 %copy-start.18 = (bf16[2,1,256,768]{3,2,1,0:T(8,128)(2,1)S(1)}, bf16[2,1,256,768]{3,2,1,0:T(8,128)(2,1)}, u32[]{:S(2)}) copy-start(bf16[2,1,256,768]{3,2,1,0:T(8,128)(2,1)} %param.8) | copy-start | bytes 2359300
  286.5 25.4 %copy-start.20 = (bf16[2,1,256,768]{3,2,1,0:T(8,128)(2,1)S(1)}, bf16[2,1,256,768]{3,2,1,0:T(8,128)(2,1)}, u32[]{:S(2)}) copy-start(bf16[2,1,256,768]{3,2,1,0:T(8,128)(2,1)} %param.9) | copy-start | bytes 2359300
  286.5 25.4 %copy-start.22 = (bf16[2,1,256,768]{3,2,1,0:T(8,128)(2,1)S(1)}, bf16[2,1,256,768]{3,2,1,0:T(8,128)(2,1)}, u32[]{:S(2)}) copy-start(bf16[2,1,256,768]{3,2,1,0:T(8,128)(2,1)} %param.10) | copy-start | bytes 2359300
  294.3 29.7 %collective-permute-start.28 = (bf16[4,512,384]{2,1,0:T(8,128)(2,1)S(1)}, bf16[4,512,384]{2,1,0:T(8,128)(2,1)S(1)}, u32[]{:S(2)}, u32[]{:S(2)}) collective-permute-start(bf16[4,512,384]{2,1,0:T(8,128)(2,1)S(1)} %shard_map.75), channel_id=1, source_target_pairs={{0,16},{16,0},{32,48},{48,32},{64,80},{80,64},{96,112},{112,96},{1... | collective-permute-start | bytes 4718600 | tf_op jit(solution)/shard_map/ppermute | solution.py:379
  299.4 12.5 %collective-permute-start.18 = (bf16[256,768]{1,0:T(8,128)(2,1)S(1)}, bf16[256,768]{1,0:T(8,128)(2,1)S(1)}, u32[]{:S(2)}, u32[]{:S(2)}) collective-permute-start(bf16[256,768]{1,0:T(8,128)(2,1)S(1)} %copy-done.39), channel_id=1, source_target_pairs={{0,1},{1,0},{2,3},{3,2},{4,5},{5,4},{6,7},{7,6},{8,9},{9,8},{10,11... | collective-permute-start | bytes 1179656 | tf_op jit(solution)/shard_map/ppermute | solution.py:354
  302.6 17.8 %collective-permute-start.17 = (bf16[256,768]{1,0:T(8,128)(2,1)S(1)}, bf16[256,768]{1,0:T(8,128)(2,1)S(1)}, u32[]{:S(2)}, u32[]{:S(2)}) collective-permute-start(bf16[256,768]{1,0:T(8,128)(2,1)S(1)} %copy-done.37), channel_id=1, source_target_pairs={{0,1},{1,0},{2,3},{3,2},{4,5},{5,4},{6,7},{7,6},{8,9},{9,8},{10,11... | collective-permute-start | bytes 1179656 | tf_op jit(solution)/shard_map/ppermute | solution.py:354
  339.2 7.6 %collective-permute-start.29 = (bf16[4,512,384]{2,1,0:T(8,128)(2,1)S(1)}, bf16[4,512,384]{2,1,0:T(8,128)(2,1)S(1)}, u32[]{:S(2)}, u32[]{:S(2)}) collective-permute-start(bf16[4,512,384]{2,1,0:T(8,128)(2,1)S(1)} %shard_map.77), channel_id=1, source_target_pairs={{0,16},{16,0},{32,48},{48,32},{64,80},{80,64},{96,112},{112,96},{1... | collective-permute-start | bytes 4718600 | tf_op jit(solution)/shard_map/ppermute | solution.py:379
  340.2 16.5 %collective-permute-start.33 = (bf16[512,384]{1,0:T(8,128)(2,1)S(1)}, bf16[512,384]{1,0:T(8,128)(2,1)S(1)}, u32[]{:S(2)}, u32[]{:S(2)}) collective-permute-start(bf16[512,384]{1,0:T(8,128)(2,1)S(1)} %get-tuple-element.90), channel_id=1, source_target_pairs={{0,64},{16,80},{32,96},{48,112},{64,0},{80,16},{96,32},{112,48},{1... | collective-permute-start | bytes 1179656 | tf_op jit(solution)/shard_map/ppermute | solution.py:385
  344.1 18.2 %collective-permute-start.34 = (bf16[512,384]{1,0:T(8,128)(2,1)S(1)}, bf16[512,384]{1,0:T(8,128)(2,1)S(1)}, u32[]{:S(2)}, u32[]{:S(2)}) collective-permute-start(bf16[512,384]{1,0:T(8,128)(2,1)S(1)} %get-tuple-element.91), channel_id=1, source_target_pairs={{0,32},{16,48},{32,64},{48,80},{64,96},{80,112},{96,0},{112,16},{1... | collective-permute-start | bytes 1179656 | tf_op jit(solution)/shard_map/ppermute | solution.py:385
  344.4 17.9 %collective-permute-start.35 = (bf16[512,384]{1,0:T(8,128)(2,1)S(1)}, bf16[512,384]{1,0:T(8,128)(2,1)S(1)}, u32[]{:S(2)}, u32[]{:S(2)}) collective-permute-start(bf16[512,384]{1,0:T(8,128)(2,1)S(1)} %get-tuple-element.92), channel_id=1, source_target_pairs={{0,96},{16,112},{32,0},{48,16},{64,32},{80,48},{96,64},{112,80},{1... | collective-permute-start | bytes 1179656 | tf_op jit(solution)/shard_map/ppermute | solution.py:385
  355.5 14.9 %collective-permute-start.30 = (bf16[512,384]{1,0:T(8,128)(2,1)}, bf16[512,384]{1,0:T(8,128)(2,1)S(1)}, u32[]{:S(2)}, u32[]{:S(2)}) collective-permute-start(bf16[512,384]{1,0:T(8,128)(2,1)} %get-tuple-element.86), channel_id=1, source_target_pairs={{0,64},{16,80},{32,96},{48,112},{64,0},{80,16},{96,32},{112,48},{1... | collective-permute-start | bytes 1179656 | tf_op jit(solution)/shard_map/ppermute | solution.py:385
  356.4 22.6 %collective-permute-start.31 = (bf16[512,384]{1,0:T(8,128)(2,1)}, bf16[512,384]{1,0:T(8,128)(2,1)S(1)}, u32[]{:S(2)}, u32[]{:S(2)}) collective-permute-start(bf16[512,384]{1,0:T(8,128)(2,1)} %get-tuple-element.87), channel_id=1, source_target_pairs={{0,32},{16,48},{32,64},{48,80},{64,96},{80,112},{96,0},{112,16},{1... | collective-permute-start | bytes 1179656 | tf_op jit(solution)/shard_map/ppermute | solution.py:385
  356.7 22.3 %collective-permute-start.32 = (bf16[512,384]{1,0:T(8,128)(2,1)}, bf16[512,384]{1,0:T(8,128)(2,1)S(1)}, u32[]{:S(2)}, u32[]{:S(2)}) collective-permute-start(bf16[512,384]{1,0:T(8,128)(2,1)} %get-tuple-element.88), channel_id=1, source_target_pairs={{0,96},{16,112},{32,0},{48,16},{64,32},{80,48},{96,64},{112,80},{1... | collective-permute-start | bytes 1179656 | tf_op jit(solution)/shard_map/ppermute | solution.py:385
  362.5 17.8 %collective-permute-start.36 = (bf16[512,384]{1,0:T(8,128)(2,1)S(1)}, bf16[512,384]{1,0:T(8,128)(2,1)S(1)}, u32[]{:S(2)}, u32[]{:S(2)}) collective-permute-start(bf16[512,384]{1,0:T(8,128)(2,1)S(1)} %add_convert_fusion), channel_id=1, source_target_pairs={{0,1},{1,0},{2,3},{3,2},{4,5},{5,4},{6,7},{7,6},{8,9},{9,8},{10,11... | collective-permute-start | bytes 1179656 | tf_op jit(solution)/shard_map/ppermute | solution.py:391
  (34 other events, 167.5 us)

commit v4 on v3

--- a/solution.py
+++ b/solution.py
@@ -10,7 +10,7 @@
 
 HDIM = 128
 
-FAR_FIRST = (4, 3, 5, 2, 6, 1, 7)
+Z_LINES = [[2 * z + half for z in range(8)] for half in range(2)]
 DEC_SWAP = [(16 + f, 16 + (f ^ 1)) for f in range(16)]
 ENC_SWAP = [(f, f ^ 1) for f in range(16)]
 DEC_TO_ENC = [(16 + f, f ^ 1) for f in range(16)]
@@ -19,8 +19,7 @@
 BOTH = ("section", "fsdp")
 STEPS = (2, 1, 3, 0)
 F32 = jnp.float32
-SMALL = pltpu.CompilerParams(vmem_limit_bytes=20 * 2**20)
-ANY = pl.BlockSpec(memory_space=pl.ANY)
+HBM = pl.BlockSpec(memory_space=pltpu.HBM)
 BF16 = jnp.bfloat16
 NT = (((1,), (1,)), ((), ()))
 TN = (((0,), (0,)), ((), ()))
@@ -52,16 +51,15 @@
         ),
         out_shape=jax.ShapeDtypeStruct((rows, count * width), source.dtype),
         cost_estimate=cost(0, 2 * rows * count * width * 2),
-        compiler_params=SMALL,
         name="pick",
     )(columns, source)
 
 
-def fetched(step, weights, buffer, sems):
-    rows = weights[0].shape[0]
+def fetched(step, weight, buffer, sems):
+    rows = weight.shape[1]
     copies = [
-        pltpu.make_async_copy(weight, buffer.at[pl.ds(d * rows, rows)], sems.at[d])
-        for d, weight in enumerate(weights)
+        pltpu.make_async_copy(weight.at[z], buffer.at[pl.ds(z * rows, rows)], sems.at[z])
+        for z in range(8)
     ]
 
     @pl.when(step == 0)
@@ -89,11 +87,10 @@
         acc[...] += part
 
 
-def far_kernel(core, came, twin, *refs):
-    weights, (low, high, acc, buffer, sems) = refs[:8], refs[8:]
+def far_kernel(core, came, twin, weight, low, high, acc, buffer, sems):
     step = pl.program_id(0)
     rows = jnp.where(core[0] == step // 2, came[...], twin[...])
-    added(step, acc, mm(rows, fetched(step, weights, buffer, sems), NN))
+    added(step, acc, mm(rows, fetched(step, weight, buffer, sems), NN))
 
     @pl.when(step == pl.num_programs(0) - 1)
     def _():
@@ -102,34 +99,32 @@
         high[...] = acc[rows:].astype(BF16)
 
 
-def near_kernel(columns, first, second, *refs):
-    weights, (low, high, buffer, sems) = refs[:8], refs[8:]
+def near_kernel(half, first, second, weight, low, high, buffer, sems):
     step = pl.program_id(0)
     rows = jnp.concatenate([first[...], second[...]], axis=1)
-    part = mm(rows, fetched(step, weights, buffer, sems), NN)
-    half = low.shape[0]
-    added(step, low, part[:half])
-    added(step, high, part[half:])
-
-
-def partial_products(scalars, operands, specs, weights, out_dtype, kernel):
+    part = mm(rows, fetched(step, weight, buffer, sems), NN)
+    count = low.shape[0]
+    added(step, low, part[:count])
+    added(step, high, part[count:])
+
+
+def partial_products(scalars, operands, specs, weight, out_dtype, kernel):
     row_count = operands[0].shape[0]
-    shard, width = weights[0].shape
+    _, shard, width = weight.shape
     extra = [pltpu.VMEM((row_count, width), F32)] if out_dtype == BF16 else []
     return pl.pallas_call(
         kernel,
         grid_spec=pltpu.PrefetchScalarGridSpec(
             num_scalar_prefetch=1,
             grid=(4,),
-            in_specs=specs + [ANY] * 8,
+            in_specs=specs + [HBM],
             out_specs=[pl.BlockSpec((row_count // 2, width), lambda j, at: (0, 0))] * 2,
             scratch_shapes=extra
             + [pltpu.VMEM((8 * shard, width), BF16), pltpu.SemaphoreType.DMA((8,))],
         ),
         out_shape=[jax.ShapeDtypeStruct((row_count // 2, width), out_dtype)] * 2,
         cost_estimate=cost(2 * row_count * 8 * shard * width, 2 * 8 * shard * width),
-        compiler_params=SMALL,
-    )(scalars, *operands, *weights)
+    )(scalars, *operands, weight)
 
 
 def attend_kernel(heads, flags, *refs):
@@ -191,70 +186,88 @@
         cost_estimate=cost(
             10 * seq_length * seq_length * width, 16 * seq_length * width
         ),
-        compiler_params=SMALL,
         name="attend",
     )(flags, *sent, query, key, value, mask)
 
 
 def products(at, flags, refs):
     q0, q1, k0, k1, v0, v1 = refs[:6]
-    weights = refs[6:14], refs[14:22]
-    total, buffer, sems = refs[-3:]
+    weights = refs[6:8]
+    buffer, sems = refs[-2:]
     step = pl.program_id(0)
-
-    def copy(which, place, d):
+    encoder = flags[0] == 0
+
+    def copy(which, place):
         return pltpu.make_async_copy(
-            weights[which][d], buffer.at[which, place], sems.at[which, place]
+            weights[which].at[at[place]], buffer.at[which, place], sems.at[which, place]
         )
 
+    def wide(which):
+        pair = buffer[which, pl.ds(2 * step, 2)]
+        return pair.reshape(pair.shape[0] * pair.shape[1], pair.shape[2])
+
     @pl.when(step == 0)
     def _():
         for place in range(4):
-            for d in range(8):
-
-                @pl.when(at[place] == d)
-                def _():
-                    copy(1, place, d).start()
-
-                    @pl.when(flags[0] == 0)
-                    def _():
-                        copy(0, place, d).start()
-
-    copy(1, step, 0).wait()
-    rows = jnp.where(
-        flags[0] > 0,
-        jnp.concatenate([q0[...], q1[...]]),
-        jnp.concatenate([v0[...], v1[...]]),
-    )
-    total[...] = mm(rows, buffer[1, step], NT)
-
-    @pl.when(flags[0] == 0)
-    def _():
-        copy(0, step, 0).wait()
-        total[...] += mm(jnp.concatenate([k0[...], k1[...]]), buffer[0, step], NT)
-
-    return total[...]
+            copy(1, place).start()
+
+            @pl.when(encoder)
+            def _():
+                copy(0, place).start()
+
+    for place in range(2):
+        copy(1, 2 * step + place).wait()
+
+        @pl.when(encoder)
+        def _():
+            copy(0, 2 * step + place).wait()
+
+    return (q0, q1), (k0, k1), (v0, v1), wide, encoder
+
+
+def whole(pair):
+    return jnp.concatenate([x[...] for x in pair])
 
 
 def give_kernel(at, flags, *refs):
-    refs[22][...] = products(at, flags, refs).astype(BF16)
+    out, total = refs[8], refs[-3]
+    dq, dk, dv, wide, encoder = products(at, flags, refs)
+    rows = jnp.where(encoder, whole(dv), whole(dq))
+    total[...] = mm(rows, wide(1), NT)
+
+    @pl.when(encoder)
+    def _():
+        total[...] += mm(whole(dk), wide(0), NT)
+
+    shard = out.shape[2]
+    for place in range(2):
+        out[place] = total[:, place * shard : (place + 1) * shard].astype(BF16)
 
 
 def keep_kernel(at, flags, *refs):
-    other, outs = refs[22], refs[23:27]
-    total = products(at, flags, refs) + other[...].astype(F32)
+    other, outs, total = refs[8], refs[9:13], refs[-3]
+    dq, dk, dv, wide, encoder = products(at, flags, refs)
+    rows = jnp.where(encoder, whole(dv), whole(dq))
+    total[...] = mm(rows, wide(1), NT)
+
+    @pl.when(encoder)
+    def _():
+        total[...] += mm(whole(dk), wide(0), NT)
+
+    shard = outs[0].shape[1]
     for i, out in enumerate(outs):
 
-        @pl.when(pl.program_id(0) == i)
+        @pl.when(pl.program_id(0) == i // 2)
         def _():
-            out[...] = total.astype(out.dtype)
+            cut = slice(i % 2 * shard, (i % 2 + 1) * shard)
+            out[...] = (total[:, cut] + other[i % 2].astype(F32)).astype(out.dtype)
 
 
 def projected(at, flags, grads, first, second, other=None):
     rows, width = grads[0].shape
-    shard = first[0].shape[0]
-    whole = pl.BlockSpec((rows, width), lambda i, at, flags: (0, 0))
-    moving = pl.BlockSpec((None, 2 * rows, shard), lambda i, at, flags: (i, 0, 0))
+    shard = first.shape[1]
+    operand = pl.BlockSpec((rows, width), lambda i, at, flags: (0, 0))
+    moving = pl.BlockSpec((2, 2 * rows, shard), lambda i, at, flags: (i, 0, 0))
     fixed = pl.BlockSpec((2 * rows, shard), lambda i, at, flags: (0, 0))
     if other is None:
         kernel, extra = give_kernel, ()
@@ -268,25 +281,23 @@
         kernel,
         grid_spec=pltpu.PrefetchScalarGridSpec(
             num_scalar_prefetch=2,
-            grid=(4,),
-            in_specs=[whole] * 6 + [ANY] * 16 + [moving] * len(extra),
+            grid=(2,),
+            in_specs=[operand] * 6 + [HBM] * 2 + [moving] * len(extra),
             out_specs=out_specs,
             scratch_shapes=[
-                pltpu.VMEM((2 * rows, shard), F32),
+                pltpu.VMEM((2 * rows, 2 * shard), F32),
                 pltpu.VMEM((2, 4, shard, width), BF16),
                 pltpu.SemaphoreType.DMA((2, 4)),
             ],
         ),
         out_shape=out_shape,
         cost_estimate=cost(2 * 2 * rows * 2 * width * 4 * shard, 2 * 2 * 4 * shard * width),
-        compiler_params=SMALL,
-    )(at, flags, *grads, *first, *second, *extra)
+    )(at, flags, *grads, first, second, *extra)
 
 
 def per_device(out_grad, queries, enc_keys, enc_values, key_mask, weights):
     decoder = lax.axis_index("section") == 1
     half = lax.axis_index("fsdp") % 2
-    line = lax.axis_index("fsdp") // 2
     segment = lax.axis_index("segment")
     core = segment % 2
     chip = segment // 2
@@ -299,15 +310,10 @@
     dec = decoder.astype(jnp.int32)
 
     def gathered(shard):
-        found = {0: shard}
-        for d in FAR_FIRST:
-            pairs = [(f, (f + 2 * d) % 16) for f in range(16)]
-            found[d] = lax.ppermute(shard, "fsdp", pairs)
-        return [found[d] for d in range(8)]
+        return lax.all_gather(shard, "fsdp", axis=0, axis_index_groups=Z_LINES)
 
     grads = out_grad.reshape(row_count, feature_width)
-    sources = (line - jnp.arange(8, dtype=jnp.int32)) % 8
-    columns = 2 * ((line - 4 * core - jnp.arange(4, dtype=jnp.int32)) % 8) + 1 - half
+    columns = 2 * (4 * core + jnp.arange(4, dtype=jnp.int32)) + 1 - half
     came = lax.ppermute(picked(grads, columns, shard_rows), BOTH, DEC_SWAP)
     twin = lax.ppermute(came, "segment", CORE_SWAP)
 
@@ -322,7 +328,9 @@
         came_near.append(lax.ppermute(value, BOTH, ENC_SWAP))
 
     first = gathered(weights[0, 0])
-    second_shard, *first[3:6] = lax.optimization_barrier((weights[0, 1], *first[3:6]))
+    first, second_shard, came, twin = lax.optimization_barrier(
+        (first, weights[0, 1], came, twin)
+    )
     second = gathered(second_shard)
     near = [jnp.where(decoder, mine, other) for mine, other in zip(own, came_near)]
     near[3] = near[3].reshape(micro_count, seq_length, 1)
@@ -334,11 +342,11 @@
     for partial in partial_products(core[None], (came, twin), [moved] * 2, first, BF16, far_kernel):
         far.append(lax.ppermute(partial, BOTH, DEC_SWAP))
     own_partial = partial_products(
-        2 * sources + half,
+        half[None],
         (grads, grads),
         [
-            pl.BlockSpec((row_count, shard_rows), lambda j, at: (0, at[2 * j])),
-            pl.BlockSpec((row_count, shard_rows), lambda j, at: (0, at[2 * j + 1])),
+            pl.BlockSpec((row_count, shard_rows), lambda j, half: (0, 4 * j + half[0])),
+            pl.BlockSpec((row_count, shard_rows), lambda j, half: (0, 4 * j + 2 + half[0])),
         ],
         first,
         F32,
@@ -372,7 +380,7 @@
     own_dk, own_dv = attended(own_flags, ctx_own, (), own)
 
     places = 2 * ((chip + jnp.array(STEPS, jnp.int32)) % 4)
-    keep_at, give_at = (line - places - core) % 8, (line - places - 1 + core) % 8
+    keep_at, give_at = places + core, places + 1 - core
 
     def chip_sums(grads):
         give = projected(give_at, dec[None], grads, first, second)

time: 382 us -> 285 us (0.75)
  waiting for transfers between devices: 206 us -> 129 us
  starting transfers between devices: 89.8 us -> 37.9 us
  Pallas kernels: 62.3 us -> 79.1 us
  between operations: 0.61 us -> 13.8 us
  other arithmetic: 3.27 us -> 12.6 us
  local copies, waits for them, and re-layouts: 19.7 us -> 11.4 us
    ppermute x14 -> x0, waiting for transfers between devices: 158 us -> none  [gathered(): found[d] = lax.ppermute(shard, 'fsdp', pairs)]
    all_gather x0 -> x2, waiting for transfers between devices: none -> 50.2 us  [gathered(): return lax.all_gather(shard, 'fsdp', axis=0, axis_index_groups=Z_LINES)]
    ppermute x14 -> x0, starting transfers between devices: 43.1 us -> none  [gathered(): found[d] = lax.ppermute(shard, 'fsdp', pairs)]
    ppermute x4, waiting for transfers between devices: 17.5 us -> 42.8 us  [per_device(): came_near.append(lax.ppermute(value, BOTH, ENC_SWAP))]
    unnamed x90 -> x44, local copies, waits for them, and re-layouts: 18.6 us -> 7.34 us
    pallas_call x4, Pallas kernels: 15.4 us -> 23.7 us  [attend(): pl.pallas_call(functools.partial(attend_kernel, heads), grid_spec=pltpu.P...]
    ppermute x2, waiting for transfers between devices: 0.01 us -> 8.05 us  [per_device(): ctx_near.append(lax.ppermute(ctx[micro], BOTH, DEC_TO_ENC))]
    select_n x3, other arithmetic: 0.3 us -> 5.22 us  [per_device(): jnp.where(decoder, mine, other)]
  transfers between devices with their start and end apart: 37 -> 25, of which waited for: 16 -> 10; matrix products, arithmetic and copies ran while one was open for 1% -> 5% of each run, Pallas kernels for 10% -> 19%
where the time goes in v4:
time: 285 us; the launch traced here: 284 us
  waiting for transfers between devices  129 us (45%)
  Pallas kernels  79.1 us (28%)
  starting transfers between devices  37.9 us (13%)
  between operations  13.8 us (5%)
  other arithmetic  12.6 us (4%)
  local copies, waits for them, and re-layouts  11.4 us (4%)
    all_gather x2, waiting for transfers between devices, gathered(): return lax.all_gather(shard, 'fsdp', axis=0, axis_index_groups=Z_LINES)  50.2 us
    ppermute x4, waiting for transfers between devices, per_device(): came_near.append(lax.ppermute(value, BOTH, ENC_SWAP))  42.8 us
    pallas_call x4, Pallas kernels, projected(): pl.pallas_call(kernel, grid_spec=pltpu.PrefetchScalarGridSpec(num_scalar_...  35 us
    pallas_call x4, Pallas kernels, attend(): pl.pallas_call(functools.partial(attend_kernel, heads), grid_spec=pltpu.P...  23.7 us
    ppermute x6, waiting for transfers between devices, reduced(): other = lax.ppermute(block, 'segment', pairs)  18.1 us
    pallas_call x2, Pallas kernels, partial_products(): pl.pallas_call(kernel, grid_spec=pltpu.PrefetchScalarGridSpec(num_scalar_...  15.9 us
    ppermute x4, starting transfers between devices, per_device(): came_near.append(lax.ppermute(value, BOTH, ENC_SWAP))  10.6 us
    ppermute x6, starting transfers between devices, reduced(): other = lax.ppermute(block, 'segment', pairs)  8.7 us
  transfers between devices with their start and end apart: 25, of which 10 were waited for; matrix products, arithmetic and copies ran while one was open for 5% of the time, Pallas kernels for 19%

profile of v4, /device:TPU:1, one launch (start us, length us, event | category | flops | bytes accessed | tf_op | source)
XLA Modules:
  0.0 284.1 jit_solution(13009267581630684691)
XLA Ops:
  6.5 2.3 slice_bitcast_fusion
  9.5 4.5 %pick.1 = bf16[512,1536]{1,0:T(8,128)(2,1)} custom-call(s32[4]{0:T(128)} %add_subtract_fusion.1.where, bf16[512,6144]{1,0:T(8,128)(2,1)} %bitcast.31), custom_call_target="tpu_custom_call" | custom-call | bytes 3145728 | tf_op jit(solution)/shard_map/pick/pallas_call | solution.py:44
  14.8 1.1 copy-done.21
  15.9 3.2 %collective-permute-start.1 = (bf16[512,1536]{1,0:T(8,128)(2,1)S(1)}, bf16[512,1536]{1,0:T(8,128)(2,1)}, u32[]{:S(2)}, u32[]{:S(2)}) collective-permute-start(bf16[512,1536]{1,0:T(8,128)(2,1)S(1)} %collective-permute-done.came), channel_id=1, source_target_pairs={{0,16},{16,0},{32,48},{48,32},{64,80},{80,64},{96,112},{112,96},{1... | collective-permute-start | bytes 4718600 | tf_op jit(solution)/shard_map/ppermute | solution.py:318
  19.1 3.2 %collective-permute-done.1.twin = bf16[512,1536]{1,0:T(8,128)(2,1)} collective-permute-done((bf16[512,1536]{1,0:T(8,128)(2,1)S(1)}, bf16[512,1536]{1,0:T(8,128)(2,1)}, u32[]{:S(2)}, u32[]{:S(2)}) %collective-permute-start.1) | collective-permute-done | bytes 1572896 | tf_op jit(solution)/shard_map/ppermute | solution.py:318
  22.3 50.1 %all-gather.5.cloned.1.call-done = bf16[8,1,384,768]{3,2,1,0:T(8,128)(2,1)} async-done(((bf16[1,1,384,768]{3,2,1,0:T(8,128)(2,1)}), bf16[8,1,384,768]{3,2,1,0:T(8,128)(2,1)}) %all-gather.5.cloned.1.call-update) | async-done | bytes 4718608 | tf_op jit(solution)/shard_map/all_gather | solution.py:313
  72.5 3.1 %collective-permute-start.8 = (bf16[2,256,768]{2,1,0:T(8,128)(2,1)S(1)}, bf16[2,256,768]{2,1,0:T(8,128)(2,1)}, u32[]{:S(2)}, u32[]{:S(2)}) collective-permute-start(bf16[2,256,768]{2,1,0:T(8,128)(2,1)S(1)} %bitcast.42), channel_id=1, source_target_pairs={{0,1},{1,0},{2,3},{3,2},{4,5},{5,4},{6,7},{7,6},{8,9},{9,8},{10,11... | collective-permute-start | bytes 2359304 | tf_op jit(solution)/shard_map/ppermute | solution.py:328
  75.6 2.2 collective-permute-start.7
  77.8 3.1 %collective-permute-start.6 = (bf16[2,256,768]{2,1,0:T(8,128)(2,1)S(1)}, bf16[2,256,768]{2,1,0:T(8,128)(2,1)S(1)}, u32[]{:S(2)}, u32[]{:S(2)}) collective-permute-start(bf16[2,256,768]{2,1,0:T(8,128)(2,1)S(1)} %bitcast.36), channel_id=1, source_target_pairs={{0,1},{1,0},{2,3},{3,2},{4,5},{5,4},{6,7},{7,6},{8,9},{9,8},{10,11... | collective-permute-start | bytes 2359304 | tf_op jit(solution)/shard_map/ppermute | solution.py:328
  80.9 2.2 collective-permute-start.9
  83.7 42.8 %collective-permute-done.9 = s32[2,1,256]{2,1,0:T(1,128)S(1)} collective-permute-done((s32[2,1,256]{2,1,0:T(1,128)S(1)}, s32[2,1,256]{2,1,0:T(1,128)S(1)}, u32[]{:S(2)}, u32[]{:S(2)}) %collective-permute-start.9) | collective-permute-done | bytes 2080 | tf_op jit(solution)/shard_map/ppermute | solution.py:328
  126.5 0.8 reshape.82.refs_5_
  127.4 8.2 %shard_map.74 = (bf16[256,768]{1,0:T(8,128)(2,1)}, bf16[256,768]{1,0:T(8,128)(2,1)}) custom-call(s32[1]{0:T(128)} %bitcast.5.core, bf16[512,1536]{1,0:T(8,128)(2,1)} %copy-done.21, bf16[512,1536]{1,0:T(8,128)(2,1)} %collective-permute-done.1.twin, bf16[8,384,768]{2,1,0:T(8,128)(2,1)} %bitcast.21), custom_call_target="tpu_custom_call" | custom-call | flops 2415919104 | bytes 4718592 | tf_op jit(solution)/shard_map/pallas_call | solution.py:115
  136.2 2.1 broadcast_select_fusion.refs_4_
  139.0 7.7 %shard_map.73 = (f32[256,768]{1,0:T(8,128)}, f32[256,768]{1,0:T(8,128)}) custom-call(s32[1]{0:T(128)} %bitcast.1.half, bf16[512,6144]{1,0:T(8,128)(2,1)} %bitcast.32, bf16[512,6144]{1,0:T(8,128)(2,1)} %bitcast.33, bf16[8,384,768]{2,1,0:T(8,128)(2,1)} %bitcast.22), custom_call_target="tpu_custom_call" | custom-call | flops 2415919104 | bytes 4718592 | tf_op jit(solution)/shard_map/pallas_call | solution.py:115
  146.8 1.3 add_convert_fusion.3.refs_1_
  148.1 1.3 collective-permute-start.5
  149.5 1.3 collective-permute-start.4
  150.8 2.1 broadcast_select_fusion.1.refs_3_
  152.9 1.0 broadcast_select_fusion.2.refs_2_
  153.9 6.4 %collective-permute-done.5.refs_0_ = bf16[256,768]{1,0:T(8,128)(2,1)S(1)} collective-permute-done((bf16[256,768]{1,0:T(8,128)(2,1)S(1)}, bf16[256,768]{1,0:T(8,128)(2,1)S(1)}, u32[]{:S(2)}, u32[]{:S(2)}) %collective-permute-start.5) | collective-permute-done | bytes 393248 | tf_op jit(solution)/shard_map/ppermute | solution.py:361
  161.0 6.0 %attend.4 = (bf16[256,768]{1,0:T(8,128)(2,1)}, bf16[256,768]{1,0:T(8,128)(2,1)}, bf16[256,768]{1,0:T(8,128)(2,1)}) custom-call(s32[2]{0:T(128)} %pad_add_fusion.flags, bf16[256,768]{1,0:T(8,128)(2,1)} %copy-done.15, bf16[256,768]{1,0:T(8,128)(2,1)} %copy-done.3, bf16[2,256,768]{2,1,0:T(8,128)(2,1)} %broadcast_select_fusion.2.refs_2_, ...), custom_call_target="tpu_custom_call" | custom-call | flops 503316480 | bytes 3145728 | tf_op jit(solution)/shard_map/attend/pallas_call | solution.py:171
  167.0 1.7 collective-permute-done.4.refs_0_
  169.5 6.2 %attend.5 = (bf16[256,768]{1,0:T(8,128)(2,1)}, bf16[256,768]{1,0:T(8,128)(2,1)}, bf16[256,768]{1,0:T(8,128)(2,1)}) custom-call(s32[2]{0:T(128)} %pad_add_fusion.flags, bf16[256,768]{1,0:T(8,128)(2,1)} %copy-done.17, bf16[256,768]{1,0:T(8,128)(2,1)} %copy-done.4, bf16[2,256,768]{2,1,0:T(8,128)(2,1)} %broadcast_select_fusion.2.refs_2_, ...), custom_call_target="tpu_custom_call" | custom-call | flops 503316480 | bytes 3145728 | tf_op jit(solution)/shard_map/attend/pallas_call | solution.py:171
  178.5 8.4 %shard_map.75 = bf16[4,512,384]{2,1,0:T(8,128)(2,1)} custom-call(s32[4]{0:T(128)} %get-tuple-element.95.at, s32[1]{0:T(128)} %bitcast.flags, bf16[256,768]{1,0:T(8,128)(2,1)} %copy-done.9, bf16[256,768]{1,0:T(8,128)(2,1)} %copy-done.8, bf16[256,768]{1,0:T(8,128)(2,1)} %get-tuple-element.71.refs_2_, bf16[256,768]{1,0:T(8,128)(2,1)} %get-tuple-element.72.refs_3_, ...), custom_call_target="tpu_custom_call" | custom-call | flops 2415919104 | bytes 4718592 | tf_op jit(solution)/shard_map/pallas_call | solution.py:280
  187.0 2.9 %collective-permute-start.14 = (bf16[4,512,384]{2,1,0:T(8,128)(2,1)}, bf16[4,512,384]{2,1,0:T(8,128)(2,1)S(1)}, u32[]{:S(2)}, u32[]{:S(2)}) collective-permute-start(bf16[4,512,384]{2,1,0:T(8,128)(2,1)} %shard_map.75), channel_id=1, source_target_pairs={{0,16},{16,0},{32,48},{48,32},{64,80},{80,64},{96,112},{112,96},{1... | collective-permute-start | bytes 4718600 | tf_op jit(solution)/shard_map/ppermute | solution.py:387
  189.9 1.9 collective-permute-start.11
  191.8 3.5 %collective-permute-start.10 = (bf16[256,768]{1,0:T(8,128)(2,1)S(1)}, bf16[256,768]{1,0:T(8,128)(2,1)S(1)}, u32[]{:S(2)}, u32[]{:S(2)}) collective-permute-start(bf16[256,768]{1,0:T(8,128)(2,1)S(1)} %copy-done.18), channel_id=1, source_target_pairs={{0,1},{1,0},{2,3},{3,2},{4,5},{5,4},{6,7},{7,6},{8,9},{9,8},{10,11... | collective-permute-start | bytes 1179656 | tf_op jit(solution)/shard_map/ppermute | solution.py:362
  196.5 0.8 reshape.83.refs_4_
  197.4 5.1 %collective-permute-done.11.refs_0_ = bf16[256,768]{1,0:T(8,128)(2,1)S(1)} collective-permute-done((bf16[256,768]{1,0:T(8,128)(2,1)S(1)}, bf16[256,768]{1,0:T(8,128)(2,1)S(1)}, u32[]{:S(2)}, u32[]{:S(2)}) %collective-permute-start.11) | collective-permute-done | bytes 393248 | tf_op jit(solution)/shard_map/ppermute | solution.py:362
  203.2 5.8 %attend.6 = (bf16[256,768]{1,0:T(8,128)(2,1)}, bf16[256,768]{1,0:T(8,128)(2,1)}) custom-call(s32[2]{0:T(128)} %pad_add_fusion.1.flags, bf16[256,768]{1,0:T(8,128)(2,1)} %copy-done.14, bf16[2,256,768]{2,1,0:T(8,128)(2,1)} %bitcast.34, bf16[2,256,768]{2,1,0:T(8,128)(2,1)} %bitcast.37, bf16[2,256,768]{2,1,0:T(8,128)(2,1)} %bitcast.40, s32[2,256,1]{2,1,0:T(8,128)} %reshape.83.refs_4_), custom_call_target="tpu_custom_call" | custom-call | flops 503316480 | bytes 3145728 | tf_op jit(solution)/shard_map/attend/pallas_call | solution.py:171
  209.0 1.9 collective-permute-done.10.refs_0_
  211.6 5.8 %attend.7 = (bf16[256,768]{1,0:T(8,128)(2,1)}, bf16[256,768]{1,0:T(8,128)(2,1)}) custom-call(s32[2]{0:T(128)} %pad_add_fusion.1.flags, bf16[256,768]{1,0:T(8,128)(2,1)} %copy-done.13, bf16[2,256,768]{2,1,0:T(8,128)(2,1)} %bitcast.35, bf16[2,256,768]{2,1,0:T(8,128)(2,1)} %bitcast.38, bf16[2,256,768]{2,1,0:T(8,128)(2,1)} %bitcast.41, s32[2,256,1]{2,1,0:T(8,128)} %reshape.83.refs_4_), custom_call_target="tpu_custom_call" | custom-call | flops 503316480 | bytes 3145728 | tf_op jit(solution)/shard_map/attend/pallas_call | solution.py:171
  217.4 1.1 copy-done.5
  218.5 9.1 %shard_map.76 = (bf16[512,384]{1,0:T(8,128)(2,1)}, bf16[512,384]{1,0:T(8,128)(2,1)}, bf16[512,384]{1,0:T(8,128)(2,1)}, f32[512,384]{1,0:T(8,128)}) custom-call(s32[4]{0:T(128)} %broadcast_add_fusion.at, s32[1]{0:T(128)} %bitcast.flags, bf16[256,768]{1,0:T(8,128)(2,1)} %copy-done.9, bf16[256,768]{1,0:T(8,128)(2,1)} %copy-done.8, ...), custom_call_target="tpu_custom_call" | custom-call | flops 2415919104 | bytes 4718592 | tf_op jit(solution)/shard_map/pallas_call | solution.py:280
  227.6 8.3 %shard_map.77 = bf16[4,512,384]{2,1,0:T(8,128)(2,1)} custom-call(s32[4]{0:T(128)} %get-tuple-element.95.at, s32[1]{0:T(128)} %bitcast.flags, bf16[256,768]{1,0:T(8,128)(2,1)} %get-tuple-element.79.refs_0_, bf16[256,768]{1,0:T(8,128)(2,1)} %get-tuple-element.80.refs_1_, bf16[256,768]{1,0:T(8,128)(2,1)} %get-tuple-element.81.refs_2_, ...), custom_call_target="tpu_custom_call" | custom-call | flops 2415919104 | bytes 4718592 | tf_op jit(solution)/shard_map/pallas_call | solution.py:280
  236.0 1.0 collective-permute-start.15
  237.0 2.7 collective-permute-start.19
  239.9 2.4 collective-permute-start.21
  242.3 1.1 copy-done.6
  243.5 9.1 %shard_map.78 = (bf16[512,384]{1,0:T(8,128)(2,1)}, bf16[512,384]{1,0:T(8,128)(2,1)}, bf16[512,384]{1,0:T(8,128)(2,1)}, f32[512,384]{1,0:T(8,128)}) custom-call(s32[4]{0:T(128)} %broadcast_add_fusion.at, s32[1]{0:T(128)} %bitcast.flags, bf16[256,768]{1,0:T(8,128)(2,1)} %get-tuple-element.79.refs_0_, bf16[256,768]{1,0:T(8,128)(2,1)} %get-tuple-element.80.refs_1_, ...), custom_call_target="tpu_custom_call" | custom-call | flops 2415919104 | bytes 4718592 | tf_op jit(solution)/shard_map/pallas_call | solution.py:280
  253.6 2.4 collective-permute-start.18
  256.0 2.6 collective-permute-done.20
  258.6 0.9 add_convert_fusion
  259.5 6.7 %collective-permute-done.16 = bf16[512,384]{1,0:T(8,128)(2,1)S(1)} collective-permute-done((bf16[512,384]{1,0:T(8,128)(2,1)}, bf16[512,384]{1,0:T(8,128)(2,1)S(1)}, u32[]{:S(2)}, u32[]{:S(2)}) %collective-permute-start.16) | collective-permute-done | bytes 393248 | tf_op jit(solution)/shard_map/ppermute | solution.py:393
  266.2 8.8 %collective-permute-done.17 = bf16[512,384]{1,0:T(8,128)(2,1)S(1)} collective-permute-done((bf16[512,384]{1,0:T(8,128)(2,1)}, bf16[512,384]{1,0:T(8,128)(2,1)S(1)}, u32[]{:S(2)}, u32[]{:S(2)}) %collective-permute-start.17) | collective-permute-done | bytes 393248 | tf_op jit(solution)/shard_map/ppermute | solution.py:393
  275.0 1.2 add_convert_fusion.1
  276.2 1.1 maximum_select_fusion
  (76 shorter events, 11.7 us)
Async XLA Ops:
  6.5 65.9 %all-gather.5.cloned.1.call-start = ((), (), s32[]{:S(2)}) async-start(), calls=%async_computation | async-start | bytes 5308416 | tf_op jit(solution)/shard_map/all_gather | solution.py:313
  8.9 168.8 %all-gather.7.cloned.1.call-start = ((), (), s32[]{:S(2)}) async-start(), calls=%async_computation.1 | async-start | bytes 5308416 | tf_op jit(solution)/shard_map/all_gather | solution.py:313
  9.5 63.0 %copy-start.2 = (bf16[2,1,256,768]{3,2,1,0:T(8,128)(2,1)S(1)}, bf16[2,1,256,768]{3,2,1,0:T(8,128)(2,1)}, u32[]{:S(2)}) copy-start(bf16[2,1,256,768]{3,2,1,0:T(8,128)(2,1)} %param.10) | copy-start | bytes 2359300
  9.5 66.1 %copy-start.1 = (bf16[2,1,256,768]{3,2,1,0:T(8,128)(2,1)S(1)}, bf16[2,1,256,768]{3,2,1,0:T(8,128)(2,1)}, u32[]{:S(2)}) copy-start(bf16[2,1,256,768]{3,2,1,0:T(8,128)(2,1)} %param.9) | copy-start | bytes 2359300
  9.5 68.3 %copy-start = (bf16[2,1,256,768]{3,2,1,0:T(8,128)(2,1)S(1)}, bf16[2,1,256,768]{3,2,1,0:T(8,128)(2,1)}, u32[]{:S(2)}) copy-start(bf16[2,1,256,768]{3,2,1,0:T(8,128)(2,1)} %param.8) | copy-start | bytes 2359300
  9.5 71.4 %copy-start.19 = (s32[2,1,256]{2,1,0:T(1,128)S(1)}, s32[2,1,256]{2,1,0:T(1,128)}, u32[]{:S(2)}) copy-start(s32[2,1,256]{2,1,0:T(1,128)} %param.11) | copy-start | bytes 6148
  14.0 0.8 collective-permute-start
  14.8 1.1 copy-start.21
  15.9 6.4 %collective-permute-start.1 = (bf16[512,1536]{1,0:T(8,128)(2,1)S(1)}, bf16[512,1536]{1,0:T(8,128)(2,1)}, u32[]{:S(2)}, u32[]{:S(2)}) collective-permute-start(bf16[512,1536]{1,0:T(8,128)(2,1)S(1)} %collective-permute-done.came), channel_id=1, source_target_pairs={{0,16},{16,0},{32,48},{48,32},{64,80},{80,64},{96,112},{112,96},{1... | collective-permute-start | bytes 4718600 | tf_op jit(solution)/shard_map/ppermute | solution.py:318
  72.5 63.7 %collective-permute-start.8 = (bf16[2,256,768]{2,1,0:T(8,128)(2,1)S(1)}, bf16[2,256,768]{2,1,0:T(8,128)(2,1)}, u32[]{:S(2)}, u32[]{:S(2)}) collective-permute-start(bf16[2,256,768]{2,1,0:T(8,128)(2,1)S(1)} %bitcast.42), channel_id=1, source_target_pairs={{0,1},{1,0},{2,3},{3,2},{4,5},{5,4},{6,7},{7,6},{8,9},{9,8},{10,11... | collective-permute-start | bytes 2359304 | tf_op jit(solution)/shard_map/ppermute | solution.py:328
  75.6 75.2 %collective-permute-start.7 = (bf16[2,256,768]{2,1,0:T(8,128)(2,1)S(1)}, bf16[2,256,768]{2,1,0:T(8,128)(2,1)}, u32[]{:S(2)}, u32[]{:S(2)}) collective-permute-start(bf16[2,256,768]{2,1,0:T(8,128)(2,1)S(1)} %bitcast.39), channel_id=1, source_target_pairs={{0,1},{1,0},{2,3},{3,2},{4,5},{5,4},{6,7},{7,6},{8,9},{9,8},{10,11... | collective-permute-start | bytes 2359304 | tf_op jit(solution)/shard_map/ppermute | solution.py:328
  77.8 75.1 %collective-permute-start.6 = (bf16[2,256,768]{2,1,0:T(8,128)(2,1)S(1)}, bf16[2,256,768]{2,1,0:T(8,128)(2,1)S(1)}, u32[]{:S(2)}, u32[]{:S(2)}) collective-permute-start(bf16[2,256,768]{2,1,0:T(8,128)(2,1)S(1)} %bitcast.36), channel_id=1, source_target_pairs={{0,1},{1,0},{2,3},{3,2},{4,5},{5,4},{6,7},{7,6},{8,9},{9,8},{10,11... | collective-permute-start | bytes 2359304 | tf_op jit(solution)/shard_map/ppermute | solution.py:328
  80.9 45.6 %collective-permute-start.9 = (s32[2,1,256]{2,1,0:T(1,128)S(1)}, s32[2,1,256]{2,1,0:T(1,128)S(1)}, u32[]{:S(2)}, u32[]{:S(2)}) collective-permute-start(s32[2,1,256]{2,1,0:T(1,128)S(1)} %copy-done.19), channel_id=1, source_target_pairs={{0,1},{1,0},{2,3},{3,2},{4,5},{5,4},{6,7},{7,6},{8,9},{9,8},{10,11... | collective-permute-start | bytes 6152 | tf_op jit(solution)/shard_map/ppermute | solution.py:328
  135.5 11.3 %collective-permute-start.3 = (bf16[256,768]{1,0:T(8,128)(2,1)}, bf16[256,768]{1,0:T(8,128)(2,1)S(1)}, u32[]{:S(2)}, u32[]{:S(2)}) collective-permute-start(bf16[256,768]{1,0:T(8,128)(2,1)} %get-tuple-element.55), channel_id=1, source_target_pairs={{128,129},{129,128},{130,131},{131,130},{132,133},{133,132},{134,1... | collective-permute-start | bytes 1179656 | tf_op jit(solution)/shard_map/ppermute | solution.py:343
  138.4 11.0 %collective-permute-start.2 = (bf16[256,768]{1,0:T(8,128)(2,1)}, bf16[256,768]{1,0:T(8,128)(2,1)S(1)}, u32[]{:S(2)}, u32[]{:S(2)}) collective-permute-start(bf16[256,768]{1,0:T(8,128)(2,1)} %get-tuple-element.53), channel_id=1, source_target_pairs={{128,129},{129,128},{130,131},{131,130},{132,133},{133,132},{134,1... | collective-permute-start | bytes 1179656 | tf_op jit(solution)/shard_map/ppermute | solution.py:343
  146.8 2.6 copy-start.10
  148.1 4.8 %copy-start.3 = (bf16[256,768]{1,0:T(8,128)(2,1)}, bf16[256,768]{1,0:T(8,128)(2,1)S(1)}, u32[]{:S(2)}) copy-start(bf16[256,768]{1,0:T(8,128)(2,1)S(1)} %add_convert_fusion.3.refs_1_) | copy-start | bytes 1179652
  148.1 12.2 %collective-permute-start.5 = (bf16[256,768]{1,0:T(8,128)(2,1)S(1)}, bf16[256,768]{1,0:T(8,128)(2,1)S(1)}, u32[]{:S(2)}, u32[]{:S(2)}) collective-permute-start(bf16[256,768]{1,0:T(8,128)(2,1)S(1)} %add_convert_fusion.3.refs_1_), channel_id=1, source_target_pairs={{128,1},{129,0},{130,3},{131,2},{132,5},{133,4},{134,7},{135,6},{1... | collective-permute-start | bytes 1179656 | tf_op jit(solution)/shard_map/ppermute | solution.py:361
  149.5 4.4 %copy-start.4 = (bf16[256,768]{1,0:T(8,128)(2,1)}, bf16[256,768]{1,0:T(8,128)(2,1)S(1)}, u32[]{:S(2)}) copy-start(bf16[256,768]{1,0:T(8,128)(2,1)S(1)} %add_convert_fusion.2.refs_1_) | copy-start | bytes 1179652
  149.5 19.2 %collective-permute-start.4 = (bf16[256,768]{1,0:T(8,128)(2,1)S(1)}, bf16[256,768]{1,0:T(8,128)(2,1)S(1)}, u32[]{:S(2)}, u32[]{:S(2)}) collective-permute-start(bf16[256,768]{1,0:T(8,128)(2,1)S(1)} %add_convert_fusion.2.refs_1_), channel_id=1, source_target_pairs={{128,1},{129,0},{130,3},{131,2},{132,5},{133,4},{134,7},{135,6},{1... | collective-permute-start | bytes 1179656 | tf_op jit(solution)/shard_map/ppermute | solution.py:361
  160.3 0.8 copy-start.15
  168.7 0.8 copy-start.17
  169.5 6.9 %copy-start.7 = (bf16[256,768]{1,0:T(8,128)(2,1)S(1)}, bf16[256,768]{1,0:T(8,128)(2,1)}, u32[]{:S(2)}) copy-start(bf16[256,768]{1,0:T(8,128)(2,1)} %get-tuple-element.79.refs_0_) | copy-start | bytes 1179652
  169.5 7.6 %copy-start.20 = (s32[4]{0:T(128)S(1)}, s32[4]{0:T(128)}, u32[]{:S(2)}) copy-start(s32[4]{0:T(128)} %constant.64.clone) | copy-start | bytes 52
  175.7 2.0 collective-permute-start.13
  176.3 1.3 collective-permute-start.12
  177.7 0.8 copy-start.8
  177.7 0.9 copy-start.9
  178.5 11.4 %copy-start.16 = (bf16[256,768]{1,0:T(8,128)(2,1)S(1)}, bf16[256,768]{1,0:T(8,128)(2,1)}, u32[]{:S(2)}) copy-start(bf16[256,768]{1,0:T(8,128)(2,1)} %copy-done.15) | copy-start | bytes 1179652
  178.5 13.3 %copy-start.18 = (bf16[256,768]{1,0:T(8,128)(2,1)S(1)}, bf16[256,768]{1,0:T(8,128)(2,1)}, u32[]{:S(2)}) copy-start(bf16[256,768]{1,0:T(8,128)(2,1)} %copy-done.17) | copy-start | bytes 1179652
  187.0 30.4 %collective-permute-start.14 = (bf16[4,512,384]{2,1,0:T(8,128)(2,1)}, bf16[4,512,384]{2,1,0:T(8,128)(2,1)S(1)}, u32[]{:S(2)}, u32[]{:S(2)}) collective-permute-start(bf16[4,512,384]{2,1,0:T(8,128)(2,1)} %shard_map.75), channel_id=1, source_target_pairs={{0,16},{16,0},{32,48},{48,32},{64,80},{80,64},{96,112},{112,96},{1... | collective-permute-start | bytes 4718600 | tf_op jit(solution)/shard_map/ppermute | solution.py:387
  189.9 12.5 %collective-permute-start.11 = (bf16[256,768]{1,0:T(8,128)(2,1)S(1)}, bf16[256,768]{1,0:T(8,128)(2,1)S(1)}, u32[]{:S(2)}, u32[]{:S(2)}) collective-permute-start(bf16[256,768]{1,0:T(8,128)(2,1)S(1)} %copy-done.16), channel_id=1, source_target_pairs={{0,1},{1,0},{2,3},{3,2},{4,5},{5,4},{6,7},{7,6},{8,9},{9,8},{10,11... | collective-permute-start | bytes 1179656 | tf_op jit(solution)/shard_map/ppermute | solution.py:362
  191.8 19.0 %collective-permute-start.10 = (bf16[256,768]{1,0:T(8,128)(2,1)S(1)}, bf16[256,768]{1,0:T(8,128)(2,1)S(1)}, u32[]{:S(2)}, u32[]{:S(2)}) collective-permute-start(bf16[256,768]{1,0:T(8,128)(2,1)S(1)} %copy-done.18), channel_id=1, source_target_pairs={{0,1},{1,0},{2,3},{3,2},{4,5},{5,4},{6,7},{7,6},{8,9},{9,8},{10,11... | collective-permute-start | bytes 1179656 | tf_op jit(solution)/shard_map/ppermute | solution.py:362
  202.4 0.7 copy-start.14
  210.9 0.7 copy-start.13
  217.4 1.1 copy-start.5
  236.0 22.6 %copy-start.11 = (f32[512,384]{1,0:T(8,128)S(1)}, f32[512,384]{1,0:T(8,128)}, u32[]{:S(2)}) copy-start(f32[512,384]{1,0:T(8,128)} %get-tuple-element.89) | copy-start | bytes 2359300
  236.0 6.4 %collective-permute-start.15 = (bf16[4,512,384]{2,1,0:T(8,128)(2,1)}, bf16[4,512,384]{2,1,0:T(8,128)(2,1)S(1)}, u32[]{:S(2)}, u32[]{:S(2)}) collective-permute-start(bf16[4,512,384]{2,1,0:T(8,128)(2,1)} %shard_map.77), channel_id=1, source_target_pairs={{0,16},{16,0},{32,48},{48,32},{64,80},{80,64},{96,112},{112,96},{1... | collective-permute-start | bytes 4718600 | tf_op jit(solution)/shard_map/ppermute | solution.py:387
  237.0 16.6 %collective-permute-start.19 = (bf16[512,384]{1,0:T(8,128)(2,1)}, bf16[512,384]{1,0:T(8,128)(2,1)S(1)}, u32[]{:S(2)}, u32[]{:S(2)}) collective-permute-start(bf16[512,384]{1,0:T(8,128)(2,1)} %get-tuple-element.90), channel_id=1, source_target_pairs={{0,64},{16,80},{32,96},{48,112},{64,0},{80,16},{96,32},{112,48},{1... | collective-permute-start | bytes 1179656 | tf_op jit(solution)/shard_map/ppermute | solution.py:393
  239.7 18.9 %collective-permute-start.20 = (bf16[512,384]{1,0:T(8,128)(2,1)}, bf16[512,384]{1,0:T(8,128)(2,1)S(1)}, u32[]{:S(2)}, u32[]{:S(2)}) collective-permute-start(bf16[512,384]{1,0:T(8,128)(2,1)} %get-tuple-element.91), channel_id=1, source_target_pairs={{0,32},{16,48},{32,64},{48,80},{64,96},{80,112},{96,0},{112,16},{1... | collective-permute-start | bytes 1179656 | tf_op jit(solution)/shard_map/ppermute | solution.py:393
  239.9 18.6 %collective-permute-start.21 = (bf16[512,384]{1,0:T(8,128)(2,1)}, bf16[512,384]{1,0:T(8,128)(2,1)S(1)}, u32[]{:S(2)}, u32[]{:S(2)}) collective-permute-start(bf16[512,384]{1,0:T(8,128)(2,1)} %get-tuple-element.92), channel_id=1, source_target_pairs={{0,96},{16,112},{32,0},{48,16},{64,32},{80,48},{96,64},{112,80},{1... | collective-permute-start | bytes 1179656 | tf_op jit(solution)/shard_map/ppermute | solution.py:393
  242.3 1.1 copy-start.6
  252.6 22.4 %copy-start.12 = (f32[512,384]{1,0:T(8,128)S(1)}, f32[512,384]{1,0:T(8,128)}, u32[]{:S(2)}) copy-start(f32[512,384]{1,0:T(8,128)} %get-tuple-element.85) | copy-start | bytes 2359300
  252.6 13.6 %collective-permute-start.16 = (bf16[512,384]{1,0:T(8,128)(2,1)}, bf16[512,384]{1,0:T(8,128)(2,1)S(1)}, u32[]{:S(2)}, u32[]{:S(2)}) collective-permute-start(bf16[512,384]{1,0:T(8,128)(2,1)} %get-tuple-element.86), channel_id=1, source_target_pairs={{0,64},{16,80},{32,96},{48,112},{64,0},{80,16},{96,32},{112,48},{1... | collective-permute-start | bytes 1179656 | tf_op jit(solution)/shard_map/ppermute | solution.py:393
  253.3 21.7 %collective-permute-start.17 = (bf16[512,384]{1,0:T(8,128)(2,1)}, bf16[512,384]{1,0:T(8,128)(2,1)S(1)}, u32[]{:S(2)}, u32[]{:S(2)}) collective-permute-start(bf16[512,384]{1,0:T(8,128)(2,1)} %get-tuple-element.87), channel_id=1, source_target_pairs={{0,32},{16,48},{32,64},{48,80},{64,96},{80,112},{96,0},{112,16},{1... | collective-permute-start | bytes 1179656 | tf_op jit(solution)/shard_map/ppermute | solution.py:393
  253.6 21.4 %collective-permute-start.18 = (bf16[512,384]{1,0:T(8,128)(2,1)}, bf16[512,384]{1,0:T(8,128)(2,1)}, u32[]{:S(2)}, u32[]{:S(2)}) collective-permute-start(bf16[512,384]{1,0:T(8,128)(2,1)} %get-tuple-element.88), channel_id=1, source_target_pairs={{0,96},{16,112},{32,0},{48,16},{64,32},{80,48},{96,64},{112,80},{1... | collective-permute-start | bytes 1179656 | tf_op jit(solution)/shard_map/ppermute | solution.py:393
  259.5 16.7 %collective-permute-start.22 = (bf16[512,384]{1,0:T(8,128)(2,1)}, bf16[512,384]{1,0:T(8,128)(2,1)S(1)}, u32[]{:S(2)}, u32[]{:S(2)}) collective-permute-start(bf16[512,384]{1,0:T(8,128)(2,1)} %add_convert_fusion), channel_id=1, source_target_pairs={{0,1},{1,0},{2,3},{3,2},{4,5},{5,4},{6,7},{7,6},{8,9},{9,8},{10,11... | collective-permute-start | bytes 1179656 | tf_op jit(solution)/shard_map/ppermute | solution.py:399
Sparse Core Ops, SparseCore 0:
  9.1 63.2 all-gather.4
  74.2 58.2 all-gather.6

commit v5 on v4

--- a/solution.py
+++ b/solution.py
@@ -137,7 +137,7 @@
         if len(sent) > 1:
             grad = jnp.where(flags[0] > 0, sent[1][:, cut], grad)
         q, k, v = query[:, cut], key[:, cut], value[:, cut]
-        scores = jnp.where(mask[...] > 0, mm(k, q, NT) * scale, -jnp.inf)
+        scores = jnp.where(mask[:, :1] > 0, mm(k, q, NT) * scale, -jnp.inf)
         raised = jnp.exp(scores - jnp.max(scores, axis=0, keepdims=True))
         probs = raised * (1.0 / jnp.sum(raised, axis=0, keepdims=True))
         prob_grad = mm(v, grad, NT)
@@ -178,7 +178,7 @@
                 row,
                 row,
                 row,
-                pl.BlockSpec((None, seq_length, 1), lambda h, flags: (micro, 0, 0)),
+                pl.BlockSpec((None, seq_length, HDIM), lambda h, flags: (micro, 0, 0)),
             ],
             out_specs=[one] * outs,
         ),
@@ -312,11 +312,6 @@
     def gathered(shard):
         return lax.all_gather(shard, "fsdp", axis=0, axis_index_groups=Z_LINES)
 
-    grads = out_grad.reshape(row_count, feature_width)
-    columns = 2 * (4 * core + jnp.arange(4, dtype=jnp.int32)) + 1 - half
-    came = lax.ppermute(picked(grads, columns, shard_rows), BOTH, DEC_SWAP)
-    twin = lax.ppermute(came, "segment", CORE_SWAP)
-
     own = (
         queries.reshape(flat),
         enc_keys.reshape(flat),
@@ -326,15 +321,30 @@
     came_near = []
     for value in own:
         came_near.append(lax.ppermute(value, BOTH, ENC_SWAP))
-
+    near = [jnp.where(decoder, mine, other) for mine, other in zip(own, came_near)]
+    near[3], own_mask = [
+        jnp.broadcast_to(mask.reshape(micro_count, seq_length, 1), (micro_count, seq_length, HDIM))
+        for mask in (near[3], own[3])
+    ]
+
+    near_flags = jnp.stack([dec, 1 - dec])
+    own_flags = jnp.stack([0 * dec, 1 - dec])
+    places = 2 * ((chip + jnp.array(STEPS, jnp.int32)) % 4)
+    keep_at, give_at = places + core, places + 1 - core
+
+    grads = out_grad.reshape(row_count, feature_width)
+    columns = 2 * (4 * core + jnp.arange(4, dtype=jnp.int32)) + 1 - half
     first = gathered(weights[0, 0])
-    first, second_shard, came, twin = lax.optimization_barrier(
-        (first, weights[0, 1], came, twin)
-    )
+    part = picked(grads, columns, shard_rows)
+    part, later_weights = lax.optimization_barrier((part, weights))
+    came = lax.ppermute(part, BOTH, DEC_SWAP)
+    twin = lax.ppermute(came, "segment", CORE_SWAP)
+
+    ready = (came, twin, later_weights[0, 1], near, own_mask, near_flags, own_flags, keep_at, give_at)
+    first, ready = lax.optimization_barrier((first, ready))
+    came, twin, second_shard, near, own_mask, near_flags, own_flags, keep_at, give_at = ready
+    own = (*own[:3], own_mask)
     second = gathered(second_shard)
-    near = [jnp.where(decoder, mine, other) for mine, other in zip(own, came_near)]
-    near[3] = near[3].reshape(micro_count, seq_length, 1)
-    own = (*own[:3], own[3].reshape(micro_count, seq_length, 1))
 
     piece = 2 * shard_rows
     moved = pl.BlockSpec((row_count, piece), lambda j, at: (0, j % 2))
@@ -361,9 +371,6 @@
         ctx_near.append(lax.ppermute(ctx[micro], BOTH, DEC_TO_ENC))
         ctx_own.append(lax.ppermute(ctx_near[micro], BOTH, ENC_SWAP))
 
-    near_flags = jnp.stack([dec, 1 - dec])
-    own_flags = jnp.stack([0 * dec, 1 - dec])
-
     def attended(flags, sent, held, operands):
         grads = []
         for micro in micros:
@@ -379,9 +386,6 @@
         far_dq.append(lax.ppermute(dq[micro], BOTH, DEC_SWAP))
     own_dk, own_dv = attended(own_flags, ctx_own, (), own)
 
-    places = 2 * ((chip + jnp.array(STEPS, jnp.int32)) % 4)
-    keep_at, give_at = places + core, places + 1 - core
-
     def chip_sums(grads):
         give = projected(give_at, dec[None], grads, first, second)
         other = lax.ppermute(give, "segment", CORE_SWAP)
@@ -395,7 +399,7 @@
         return result.astype(BF16)
 
     *blocks, block = chip_sums((*far_dq, *dk, *dv))
-    own_grads, blocks = lax.optimization_barrier(((*dq, *own_dk, *own_dv), blocks))
+    own_grads = (*dq, *own_dk, *own_dv)
     from_partner = lax.ppermute(reduced(blocks, block), "fsdp", HALF_SWAP)
     *blocks, block = chip_sums(own_grads)
     own_out = reduced(blocks, block)

time: 285 us -> 229 us (0.80)
  waiting for transfers between devices: 129 us -> 74.3 us
    all_gather x2, waiting for transfers between devices: 50.2 us -> 10.4 us  [gathered(): return lax.all_gather(shard, 'fsdp', axis=0, axis_index_groups=Z_LINES)]
    ppermute x2, waiting for transfers between devices: 7 us -> 0.01 us  [per_device(): ctx_own.append(lax.ppermute(ctx_near[micro], BOTH, ENC_SWAP))]
    ppermute x4, waiting for transfers between devices: 42.8 us -> 36.2 us  [per_device(): came_near.append(lax.ppermute(value, BOTH, ENC_SWAP))]
    ppermute x1, waiting for transfers between devices: 3.17 us -> 0.01 us  [per_device(): twin = lax.ppermute(came, 'segment', CORE_SWAP)]
    select_n x3 -> x4, other arithmetic: 5.22 us -> 6.32 us  [per_device(): jnp.where(decoder, mine, other)]
  transfers between devices with their start and end apart: 25 -> 25, of which waited for: 10 -> 7; matrix products, arithmetic and copies ran while one was open for 5% -> 5% of each run, Pallas kernels for 19% -> 35%
where the time goes in v5:
time: 229 us; the launch traced here: 228 us
  Pallas kernels  79.3 us (35%)
  waiting for transfers between devices  74.3 us (32%)
  starting transfers between devices  38.2 us (17%)
  between operations  13.8 us (6%)
  other arithmetic  12.5 us (5%)
  local copies, waits for them, and re-layouts  9.94 us (4%)
    ppermute x4, waiting for transfers between devices, per_device(): came_near.append(lax.ppermute(value, BOTH, ENC_SWAP))  36.2 us
    pallas_call x4, Pallas kernels, projected(): pl.pallas_call(kernel, grid_spec=pltpu.PrefetchScalarGridSpec(num_scalar_...  34.9 us
    pallas_call x4, Pallas kernels, attend(): pl.pallas_call(functools.partial(attend_kernel, heads), grid_spec=pltpu.P...  23.8 us
    ppermute x6, waiting for transfers between devices, reduced(): other = lax.ppermute(block, 'segment', pairs)  16.9 us
    pallas_call x2, Pallas kernels, partial_products(): pl.pallas_call(kernel, grid_spec=pltpu.PrefetchScalarGridSpec(num_scalar_...  15.9 us
    ppermute x4, starting transfers between devices, per_device(): came_near.append(lax.ppermute(value, BOTH, ENC_SWAP))  11.2 us
    ppermute x2, waiting for transfers between devices, per_device(): ctx_near.append(lax.ppermute(ctx[micro], BOTH, DEC_TO_ENC))  10.7 us
    all_gather x2, waiting for transfers between devices, gathered(): return lax.all_gather(shard, 'fsdp', axis=0, axis_index_groups=Z_LINES)  10.4 us
  transfers between devices with their start and end apart: 25, of which 7 were waited for; matrix products, arithmetic and copies ran while one was open for 5% of the time, Pallas kernels for 35%

profile of v5, /device:TPU:1, one launch (start us, length us, event | category | flops | bytes accessed | tf_op | source)
XLA Modules:
  0.0 228.0 jit_solution(13854564841038496648)
XLA Ops:
  6.5 1.9 slice.6
  9.1 4.7 %pick.1 = bf16[512,1536]{1,0:T(8,128)(2,1)} custom-call(s32[4]{0:T(128)} %add_subtract_fusion.1.where, bf16[512,6144]{1,0:T(8,128)(2,1)} %bitcast.37), custom_call_target="tpu_custom_call" | custom-call | bytes 3145728 | tf_op jit(solution)/shard_map/pick/pallas_call | solution.py:44
  13.8 1.8 collective-permute-start
  15.6 4.0 %collective-permute-start.4 = (bf16[2,256,768]{2,1,0:T(8,128)(2,1)S(1)}, bf16[2,256,768]{2,1,0:T(8,128)(2,1)}, u32[]{:S(2)}, u32[]{:S(2)}) collective-permute-start(bf16[2,256,768]{2,1,0:T(8,128)(2,1)S(1)} %bitcast.48), channel_id=1, source_target_pairs={{0,1},{1,0},{2,3},{3,2},{4,5},{5,4},{6,7},{7,6},{8,9},{9,8},{10,11... | collective-permute-start | bytes 2359304 | tf_op jit(solution)/shard_map/ppermute | solution.py:323
  19.7 1.9 collective-permute-start.3
  21.6 3.4 %collective-permute-start.2 = (bf16[2,256,768]{2,1,0:T(8,128)(2,1)S(1)}, bf16[2,256,768]{2,1,0:T(8,128)(2,1)}, u32[]{:S(2)}, u32[]{:S(2)}) collective-permute-start(bf16[2,256,768]{2,1,0:T(8,128)(2,1)S(1)} %bitcast.42), channel_id=1, source_target_pairs={{0,1},{1,0},{2,3},{3,2},{4,5},{5,4},{6,7},{7,6},{8,9},{9,8},{10,11... | collective-permute-start | bytes 2359304 | tf_op jit(solution)/shard_map/ppermute | solution.py:323
  25.0 1.9 collective-permute-start.5
  26.9 0.9 slice_bitcast_fusion
  27.8 3.7 %collective-permute-start.1 = (bf16[512,1536]{1,0:T(8,128)(2,1)}, bf16[512,1536]{1,0:T(8,128)(2,1)}, u32[]{:S(2)}, u32[]{:S(2)}) collective-permute-start(bf16[512,1536]{1,0:T(8,128)(2,1)} %collective-permute-done.came), channel_id=1, source_target_pairs={{0,16},{16,0},{32,48},{48,32},{64,80},{80,64},{96,112},{112,96},{1... | collective-permute-start | bytes 4718600 | tf_op jit(solution)/shard_map/ppermute | solution.py:341
  33.3 36.2 %collective-permute-done.5 = s32[2,1,256]{2,1,0:T(1,128)S(1)} collective-permute-done((s32[2,1,256]{2,1,0:T(1,128)S(1)}, s32[2,1,256]{2,1,0:T(1,128)S(1)}, u32[]{:S(2)}, u32[]{:S(2)}) %collective-permute-start.5) | collective-permute-done | bytes 2080 | tf_op jit(solution)/shard_map/ppermute | solution.py:323
  69.5 2.1 broadcast_select_fusion.refs_4_
  71.6 2.1 broadcast_select_fusion.1.refs_3_
  73.7 2.1 broadcast_select_fusion.2.refs_2_
  75.8 0.8 broadcast_in_dim.25.refs_5_
  76.7 0.8 broadcast_in_dim.27.refs_4_
  77.5 8.2 %shard_map.74 = (bf16[256,768]{1,0:T(8,128)(2,1)}, bf16[256,768]{1,0:T(8,128)(2,1)}) custom-call(s32[1]{0:T(128)} %bitcast.9.core, bf16[512,1536]{1,0:T(8,128)(2,1)} %collective-permute-done.came, bf16[512,1536]{1,0:T(8,128)(2,1)} %collective-permute-done.1.twin, bf16[8,384,768]{2,1,0:T(8,128)(2,1)} %bitcast.27), custom_call_target="tpu_custom_call" | custom-call | flops 2415919104 | bytes 4718592 | tf_op jit(solution)/shard_map/pallas_call | solution.py:115
  87.1 7.7 %shard_map.73 = (f32[256,768]{1,0:T(8,128)}, f32[256,768]{1,0:T(8,128)}) custom-call(s32[1]{0:T(128)} %bitcast.8.half, bf16[512,6144]{1,0:T(8,128)(2,1)} %bitcast.38, bf16[512,6144]{1,0:T(8,128)(2,1)} %bitcast.39, bf16[8,384,768]{2,1,0:T(8,128)(2,1)} %bitcast.28), custom_call_target="tpu_custom_call" | custom-call | flops 2415919104 | bytes 4718592 | tf_op jit(solution)/shard_map/pallas_call | solution.py:115
  94.8 1.3 add_convert_fusion.3.refs_1_
  96.1 1.3 collective-permute-start.9
  97.5 1.3 collective-permute-start.8
  98.8 8.6 %collective-permute-done.9.refs_0_ = bf16[256,768]{1,0:T(8,128)(2,1)S(1)} collective-permute-done((bf16[256,768]{1,0:T(8,128)(2,1)S(1)}, bf16[256,768]{1,0:T(8,128)(2,1)S(1)}, u32[]{:S(2)}, u32[]{:S(2)}) %collective-permute-start.9) | collective-permute-done | bytes 393248 | tf_op jit(solution)/shard_map/ppermute | solution.py:371
  107.4 0.7 copy-done.16
  108.2 6.1 %attend.4 = (bf16[256,768]{1,0:T(8,128)(2,1)}, bf16[256,768]{1,0:T(8,128)(2,1)}, bf16[256,768]{1,0:T(8,128)(2,1)}) custom-call(s32[2]{0:T(128)} %get-tuple-element.62.flags, bf16[256,768]{1,0:T(8,128)(2,1)} %copy-done.16, bf16[256,768]{1,0:T(8,128)(2,1)} %copy-done.4, bf16[2,256,768]{2,1,0:T(8,128)(2,1)} %broadcast_select_fusion.2.refs_2_, ...), custom_call_target="tpu_custom_call" | custom-call | flops 503316480 | bytes 3145728 | tf_op jit(solution)/shard_map/attend/pallas_call | solution.py:171
  114.3 2.1 collective-permute-done.8.refs_0_
  116.4 0.8 copy-done.18
  117.2 6.2 %attend.5 = (bf16[256,768]{1,0:T(8,128)(2,1)}, bf16[256,768]{1,0:T(8,128)(2,1)}, bf16[256,768]{1,0:T(8,128)(2,1)}) custom-call(s32[2]{0:T(128)} %get-tuple-element.62.flags, bf16[256,768]{1,0:T(8,128)(2,1)} %copy-done.18, bf16[256,768]{1,0:T(8,128)(2,1)} %copy-done.3, bf16[2,256,768]{2,1,0:T(8,128)(2,1)} %broadcast_select_fusion.2.refs_2_, ...), custom_call_target="tpu_custom_call" | custom-call | flops 503316480 | bytes 3145728 | tf_op jit(solution)/shard_map/attend/pallas_call | solution.py:171
  124.7 3.4 %collective-permute-start.11 = (bf16[256,768]{1,0:T(8,128)(2,1)S(1)}, bf16[256,768]{1,0:T(8,128)(2,1)S(1)}, u32[]{:S(2)}, u32[]{:S(2)}) collective-permute-start(bf16[256,768]{1,0:T(8,128)(2,1)S(1)} %copy-done.17), channel_id=1, source_target_pairs={{0,1},{1,0},{2,3},{3,2},{4,5},{5,4},{6,7},{7,6},{8,9},{9,8},{10,11... | collective-permute-start | bytes 1179656 | tf_op jit(solution)/shard_map/ppermute | solution.py:372
  128.2 1.9 collective-permute-start.10
  130.1 10.4 %all-gather.7.cloned.1.call-done = bf16[3072,768]{1,0:T(8,128)(2,1)} async-done(((bf16[384,768]{1,0:T(8,128)(2,1)}), bf16[3072,768]{1,0:T(8,128)(2,1)}) %all-gather.7.cloned.1.call-update) | async-done | bytes 4718608 | tf_op jit(solution)/shard_map/all_gather | solution.py:313
  140.5 8.4 %shard_map.77 = bf16[4,512,384]{2,1,0:T(8,128)(2,1)} custom-call(s32[4]{0:T(128)} %get-tuple-element.84.at, s32[1]{0:T(128)} %bitcast.6.flags, bf16[256,768]{1,0:T(8,128)(2,1)} %copy-done.9, bf16[256,768]{1,0:T(8,128)(2,1)} %copy-done.8, bf16[256,768]{1,0:T(8,128)(2,1)} %get-tuple-element.89.refs_2_, bf16[256,768]{1,0:T(8,128)(2,1)} %get-tuple-element.90.refs_3_, ...), custom_call_target="tpu_custom_call" | custom-call | flops 2415919104 | bytes 4718592 | tf_op jit(solution)/shard_map/pallas_call | solution.py:280
  148.9 1.1 collective-permute-start.18
  150.0 0.7 copy-done.15
  150.8 5.8 %attend.6 = (bf16[256,768]{1,0:T(8,128)(2,1)}, bf16[256,768]{1,0:T(8,128)(2,1)}) custom-call(s32[2]{0:T(128)} %get-tuple-element.74.flags, bf16[256,768]{1,0:T(8,128)(2,1)} %copy-done.15, bf16[2,256,768]{2,1,0:T(8,128)(2,1)} %bitcast.40, bf16[2,256,768]{2,1,0:T(8,128)(2,1)} %bitcast.43, bf16[2,256,768]{2,1,0:T(8,128)(2,1)} %bitcast.46, ...), custom_call_target="tpu_custom_call" | custom-call | flops 503316480 | bytes 3145728 | tf_op jit(solution)/shard_map/attend/pallas_call | solution.py:171
  157.3 5.8 %attend.7 = (bf16[256,768]{1,0:T(8,128)(2,1)}, bf16[256,768]{1,0:T(8,128)(2,1)}) custom-call(s32[2]{0:T(128)} %get-tuple-element.74.flags, bf16[256,768]{1,0:T(8,128)(2,1)} %copy-done.14, bf16[2,256,768]{2,1,0:T(8,128)(2,1)} %bitcast.41, bf16[2,256,768]{2,1,0:T(8,128)(2,1)} %bitcast.44, bf16[2,256,768]{2,1,0:T(8,128)(2,1)} %bitcast.47, ...), custom_call_target="tpu_custom_call" | custom-call | flops 503316480 | bytes 3145728 | tf_op jit(solution)/shard_map/attend/pallas_call | solution.py:171
  163.1 8.3 %shard_map.75 = bf16[4,512,384]{2,1,0:T(8,128)(2,1)} custom-call(s32[4]{0:T(128)} %get-tuple-element.84.at, s32[1]{0:T(128)} %bitcast.6.flags, bf16[256,768]{1,0:T(8,128)(2,1)} %get-tuple-element.71.refs_0_, bf16[256,768]{1,0:T(8,128)(2,1)} %get-tuple-element.73.refs_1_, bf16[256,768]{1,0:T(8,128)(2,1)} %get-tuple-element.78.refs_2_, ...), custom_call_target="tpu_custom_call" | custom-call | flops 2415919104 | bytes 4718592 | tf_op jit(solution)/shard_map/pallas_call | solution.py:280
  171.5 1.2 copy-done.6
  172.7 9.1 %shard_map.78 = (bf16[512,384]{1,0:T(8,128)(2,1)}, bf16[512,384]{1,0:T(8,128)(2,1)}, bf16[512,384]{1,0:T(8,128)(2,1)}, f32[512,384]{1,0:T(8,128)}) custom-call(s32[4]{0:T(128)} %broadcast_add_fusion.at, s32[1]{0:T(128)} %bitcast.6.flags, bf16[256,768]{1,0:T(8,128)(2,1)} %copy-done.9, bf16[256,768]{1,0:T(8,128)(2,1)} %copy-done.8, ...), custom_call_target="tpu_custom_call" | custom-call | flops 2415919104 | bytes 4718592 | tf_op jit(solution)/shard_map/pallas_call | solution.py:280
  181.8 2.8 %collective-permute-start.19 = (bf16[512,384]{1,0:T(8,128)(2,1)}, bf16[512,384]{1,0:T(8,128)(2,1)S(1)}, u32[]{:S(2)}, u32[]{:S(2)}) collective-permute-start(bf16[512,384]{1,0:T(8,128)(2,1)} %get-tuple-element.94), channel_id=1, source_target_pairs={{0,64},{16,80},{32,96},{48,112},{64,0},{80,16},{96,32},{112,48},{1... | collective-permute-start | bytes 1179656 | tf_op jit(solution)/shard_map/ppermute | solution.py:397
  184.9 2.4 %collective-permute-start.21 = (bf16[512,384]{1,0:T(8,128)(2,1)}, bf16[512,384]{1,0:T(8,128)(2,1)}, u32[]{:S(2)}, u32[]{:S(2)}) collective-permute-start(bf16[512,384]{1,0:T(8,128)(2,1)} %get-tuple-element.96), channel_id=1, source_target_pairs={{0,96},{16,112},{32,0},{48,16},{64,32},{80,48},{96,64},{112,80},{1... | collective-permute-start | bytes 1179656 | tf_op jit(solution)/shard_map/ppermute | solution.py:397
  187.3 1.1 copy-done.5
  188.4 9.2 %shard_map.76 = (bf16[512,384]{1,0:T(8,128)(2,1)}, bf16[512,384]{1,0:T(8,128)(2,1)}, bf16[512,384]{1,0:T(8,128)(2,1)}, f32[512,384]{1,0:T(8,128)}) custom-call(s32[4]{0:T(128)} %broadcast_add_fusion.at, s32[1]{0:T(128)} %bitcast.6.flags, bf16[256,768]{1,0:T(8,128)(2,1)} %get-tuple-element.71.refs_0_, bf16[256,768]{1,0:T(8,128)(2,1)} %get-tuple-element.73.refs_1_, ...), custom_call_target="tpu_custom_call" | custom-call | flops 2415919104 | bytes 4718592 | tf_op jit(solution)/shard_map/pallas_call | solution.py:280
  198.3 2.2 collective-permute-start.15
  200.5 3.5 %collective-permute-done.20 = bf16[512,384]{1,0:T(8,128)(2,1)} collective-permute-done((bf16[512,384]{1,0:T(8,128)(2,1)}, bf16[512,384]{1,0:T(8,128)(2,1)}, u32[]{:S(2)}, u32[]{:S(2)}) %collective-permute-start.20) | collective-permute-done | bytes 393248 | tf_op jit(solution)/shard_map/ppermute | solution.py:397
  204.0 1.3 add_convert_fusion
  205.3 1.3 collective-permute-start.22
  206.6 4.2 %collective-permute-done.13 = bf16[512,384]{1,0:T(8,128)(2,1)S(1)} collective-permute-done((bf16[512,384]{1,0:T(8,128)(2,1)}, bf16[512,384]{1,0:T(8,128)(2,1)S(1)}, u32[]{:S(2)}, u32[]{:S(2)}) %collective-permute-start.13) | collective-permute-done | bytes 393248 | tf_op jit(solution)/shard_map/ppermute | solution.py:397
  210.7 9.2 %collective-permute-done.14 = bf16[512,384]{1,0:T(8,128)(2,1)S(1)} collective-permute-done((bf16[512,384]{1,0:T(8,128)(2,1)}, bf16[512,384]{1,0:T(8,128)(2,1)S(1)}, u32[]{:S(2)}, u32[]{:S(2)}) %collective-permute-start.14) | collective-permute-done | bytes 393248 | tf_op jit(solution)/shard_map/ppermute | solution.py:397
  220.1 1.1 maximum_select_fusion
  (76 shorter events, 7.3 us)
Async XLA Ops:
  6.5 69.3 %all-gather.5.cloned.1.call-start = ((), (), s32[]{:S(2)}) async-start(), calls=%async_computation | async-start | bytes 5308416 | tf_op jit(solution)/shard_map/all_gather | solution.py:313
  8.5 132.1 %all-gather.7.cloned.1.call-start = ((), (), s32[]{:S(2)}) async-start(), calls=%async_computation.1 | async-start | bytes 5308416 | tf_op jit(solution)/shard_map/all_gather | solution.py:313
  9.1 6.6 %copy-start.2 = (bf16[2,1,256,768]{3,2,1,0:T(8,128)(2,1)S(1)}, bf16[2,1,256,768]{3,2,1,0:T(8,128)(2,1)}, u32[]{:S(2)}) copy-start(bf16[2,1,256,768]{3,2,1,0:T(8,128)(2,1)} %param.10) | copy-start | bytes 2359300
  9.1 10.6 %copy-start.1 = (bf16[2,1,256,768]{3,2,1,0:T(8,128)(2,1)S(1)}, bf16[2,1,256,768]{3,2,1,0:T(8,128)(2,1)}, u32[]{:S(2)}) copy-start(bf16[2,1,256,768]{3,2,1,0:T(8,128)(2,1)} %param.9) | copy-start | bytes 2359300
  9.1 12.5 %copy-start = (bf16[2,1,256,768]{3,2,1,0:T(8,128)(2,1)S(1)}, bf16[2,1,256,768]{3,2,1,0:T(8,128)(2,1)}, u32[]{:S(2)}) copy-start(bf16[2,1,256,768]{3,2,1,0:T(8,128)(2,1)} %param.8) | copy-start | bytes 2359300
  9.1 15.9 %copy-start.19 = (s32[2,1,256]{2,1,0:T(1,128)S(1)}, s32[2,1,256]{2,1,0:T(1,128)}, u32[]{:S(2)}) copy-start(s32[2,1,256]{2,1,0:T(1,128)} %param.11) | copy-start | bytes 6148
  9.1 17.9 %copy-start.10 = (bf16[1,2,384,768]{3,2,1,0:T(8,128)(2,1)S(1)}, bf16[1,2,384,768]{3,2,1,0:T(8,128)(2,1)}, u32[]{:S(2)}) copy-start(bf16[1,2,384,768]{3,2,1,0:T(8,128)(2,1)} %param.12) | copy-start | bytes 3538948
  9.1 22.4 %copy-start.20 = (s32[4]{0:T(128)S(1)}, s32[4]{0:T(128)}, u32[]{:S(2)}) copy-start(s32[4]{0:T(128)} %constant.64.clone) | copy-start | bytes 52
  13.8 14.0 %collective-permute-start = (bf16[512,1536]{1,0:T(8,128)(2,1)}, bf16[512,1536]{1,0:T(8,128)(2,1)}, u32[]{:S(2)}, u32[]{:S(2)}) collective-permute-start(bf16[512,1536]{1,0:T(8,128)(2,1)} %pick.1), channel_id=1, source_target_pairs={{128,129},{129,128},{130,131},{131,130},{132,133},{133,132},{134,1... | collective-permute-start | bytes 4718600 | tf_op jit(solution)/shard_map/ppermute | solution.py:340
  15.6 53.8 %collective-permute-start.4 = (bf16[2,256,768]{2,1,0:T(8,128)(2,1)S(1)}, bf16[2,256,768]{2,1,0:T(8,128)(2,1)}, u32[]{:S(2)}, u32[]{:S(2)}) collective-permute-start(bf16[2,256,768]{2,1,0:T(8,128)(2,1)S(1)} %bitcast.48), channel_id=1, source_target_pairs={{0,1},{1,0},{2,3},{3,2},{4,5},{5,4},{6,7},{7,6},{8,9},{9,8},{10,11... | collective-permute-start | bytes 2359304 | tf_op jit(solution)/shard_map/ppermute | solution.py:323
  19.7 51.9 %collective-permute-start.3 = (bf16[2,256,768]{2,1,0:T(8,128)(2,1)S(1)}, bf16[2,256,768]{2,1,0:T(8,128)(2,1)}, u32[]{:S(2)}, u32[]{:S(2)}) collective-permute-start(bf16[2,256,768]{2,1,0:T(8,128)(2,1)S(1)} %bitcast.45), channel_id=1, source_target_pairs={{0,1},{1,0},{2,3},{3,2},{4,5},{5,4},{6,7},{7,6},{8,9},{9,8},{10,11... | collective-permute-start | bytes 2359304 | tf_op jit(solution)/shard_map/ppermute | solution.py:323
  21.6 52.1 %collective-permute-start.2 = (bf16[2,256,768]{2,1,0:T(8,128)(2,1)S(1)}, bf16[2,256,768]{2,1,0:T(8,128)(2,1)}, u32[]{:S(2)}, u32[]{:S(2)}) collective-permute-start(bf16[2,256,768]{2,1,0:T(8,128)(2,1)S(1)} %bitcast.42), channel_id=1, source_target_pairs={{0,1},{1,0},{2,3},{3,2},{4,5},{5,4},{6,7},{7,6},{8,9},{9,8},{10,11... | collective-permute-start | bytes 2359304 | tf_op jit(solution)/shard_map/ppermute | solution.py:323
  25.0 44.5 %collective-permute-start.5 = (s32[2,1,256]{2,1,0:T(1,128)S(1)}, s32[2,1,256]{2,1,0:T(1,128)S(1)}, u32[]{:S(2)}, u32[]{:S(2)}) collective-permute-start(s32[2,1,256]{2,1,0:T(1,128)S(1)} %copy-done.19), channel_id=1, source_target_pairs={{0,1},{1,0},{2,3},{3,2},{4,5},{5,4},{6,7},{7,6},{8,9},{9,8},{10,11... | collective-permute-start | bytes 6152 | tf_op jit(solution)/shard_map/ppermute | solution.py:323
  27.8 48.0 %collective-permute-start.1 = (bf16[512,1536]{1,0:T(8,128)(2,1)}, bf16[512,1536]{1,0:T(8,128)(2,1)}, u32[]{:S(2)}, u32[]{:S(2)}) collective-permute-start(bf16[512,1536]{1,0:T(8,128)(2,1)} %collective-permute-done.came), channel_id=1, source_target_pairs={{0,16},{16,0},{32,48},{48,32},{64,80},{80,64},{96,112},{112,96},{1... | collective-permute-start | bytes 4718600 | tf_op jit(solution)/shard_map/ppermute | solution.py:341
  85.7 9.1 %collective-permute-start.7 = (bf16[256,768]{1,0:T(8,128)(2,1)}, bf16[256,768]{1,0:T(8,128)(2,1)S(1)}, u32[]{:S(2)}, u32[]{:S(2)}) collective-permute-start(bf16[256,768]{1,0:T(8,128)(2,1)} %get-tuple-element.60), channel_id=1, source_target_pairs={{128,129},{129,128},{130,131},{131,130},{132,133},{133,132},{134,1... | collective-permute-start | bytes 1179656 | tf_op jit(solution)/shard_map/ppermute | solution.py:353
  86.4 11.0 %collective-permute-start.6 = (bf16[256,768]{1,0:T(8,128)(2,1)}, bf16[256,768]{1,0:T(8,128)(2,1)S(1)}, u32[]{:S(2)}, u32[]{:S(2)}) collective-permute-start(bf16[256,768]{1,0:T(8,128)(2,1)} %get-tuple-element.58), channel_id=1, source_target_pairs={{128,129},{129,128},{130,131},{131,130},{132,133},{133,132},{134,1... | collective-permute-start | bytes 1179656 | tf_op jit(solution)/shard_map/ppermute | solution.py:353
  94.8 2.6 %copy-start.11 = (f32[256,768]{1,0:T(8,128)S(1)}, f32[256,768]{1,0:T(8,128)}, u32[]{:S(2)}) copy-start(f32[256,768]{1,0:T(8,128)} %get-tuple-element.55) | copy-start | bytes 2359300
  96.1 11.3 %copy-start.4 = (bf16[256,768]{1,0:T(8,128)(2,1)}, bf16[256,768]{1,0:T(8,128)(2,1)S(1)}, u32[]{:S(2)}) copy-start(bf16[256,768]{1,0:T(8,128)(2,1)S(1)} %add_convert_fusion.3.refs_1_) | copy-start | bytes 1179652
  96.1 11.3 %collective-permute-start.9 = (bf16[256,768]{1,0:T(8,128)(2,1)S(1)}, bf16[256,768]{1,0:T(8,128)(2,1)S(1)}, u32[]{:S(2)}, u32[]{:S(2)}) collective-permute-start(bf16[256,768]{1,0:T(8,128)(2,1)S(1)} %add_convert_fusion.3.refs_1_), channel_id=1, source_target_pairs={{128,1},{129,0},{130,3},{131,2},{132,5},{133,4},{134,7},{135,6},{1... | collective-permute-start | bytes 1179656 | tf_op jit(solution)/shard_map/ppermute | solution.py:371
  97.5 16.7 %copy-start.3 = (bf16[256,768]{1,0:T(8,128)(2,1)}, bf16[256,768]{1,0:T(8,128)(2,1)S(1)}, u32[]{:S(2)}) copy-start(bf16[256,768]{1,0:T(8,128)(2,1)S(1)} %add_convert_fusion.2.refs_1_) | copy-start | bytes 1179652
  97.5 18.9 %collective-permute-start.8 = (bf16[256,768]{1,0:T(8,128)(2,1)S(1)}, bf16[256,768]{1,0:T(8,128)(2,1)S(1)}, u32[]{:S(2)}, u32[]{:S(2)}) collective-permute-start(bf16[256,768]{1,0:T(8,128)(2,1)S(1)} %add_convert_fusion.2.refs_1_), channel_id=1, source_target_pairs={{128,1},{129,0},{130,3},{131,2},{132,5},{133,4},{134,7},{135,6},{1... | collective-permute-start | bytes 1179656 | tf_op jit(solution)/shard_map/ppermute | solution.py:371
  107.4 0.7 copy-start.16
  116.4 0.8 copy-start.18
  117.2 6.9 %copy-start.7 = (bf16[256,768]{1,0:T(8,128)(2,1)S(1)}, bf16[256,768]{1,0:T(8,128)(2,1)}, u32[]{:S(2)}) copy-start(bf16[256,768]{1,0:T(8,128)(2,1)} %get-tuple-element.71.refs_0_) | copy-start | bytes 1179652
  117.2 7.6 %copy-start.17 = (bf16[256,768]{1,0:T(8,128)(2,1)S(1)}, bf16[256,768]{1,0:T(8,128)(2,1)}, u32[]{:S(2)}) copy-start(bf16[256,768]{1,0:T(8,128)(2,1)} %copy-done.16) | copy-start | bytes 1179652
  123.3 6.8 %collective-permute-start.17 = (bf16[256,768]{1,0:T(8,128)(2,1)}, bf16[256,768]{1,0:T(8,128)(2,1)S(1)}, u32[]{:S(2)}, u32[]{:S(2)}) collective-permute-start(bf16[256,768]{1,0:T(8,128)(2,1)} %get-tuple-element.73.refs_1_), channel_id=1, source_target_pairs={{128,129},{129,128},{130,131},{131,130},{132,133},{133,132},{134,1... | collective-permute-start | bytes 1179656 | tf_op jit(solution)/shard_map/ppermute | solution.py:386
  124.0 6.1 %collective-permute-start.16 = (bf16[256,768]{1,0:T(8,128)(2,1)S(1)}, bf16[256,768]{1,0:T(8,128)(2,1)S(1)}, u32[]{:S(2)}, u32[]{:S(2)}) collective-permute-start(bf16[256,768]{1,0:T(8,128)(2,1)S(1)} %copy-done.7), channel_id=1, source_target_pairs={{128,129},{129,128},{130,131},{131,130},{132,133},{133,132},{134,1... | collective-permute-start | bytes 1179656 | tf_op jit(solution)/shard_map/ppermute | solution.py:386
  124.7 25.3 %collective-permute-start.11 = (bf16[256,768]{1,0:T(8,128)(2,1)S(1)}, bf16[256,768]{1,0:T(8,128)(2,1)S(1)}, u32[]{:S(2)}, u32[]{:S(2)}) collective-permute-start(bf16[256,768]{1,0:T(8,128)(2,1)S(1)} %copy-done.17), channel_id=1, source_target_pairs={{0,1},{1,0},{2,3},{3,2},{4,5},{5,4},{6,7},{7,6},{8,9},{9,8},{10,11... | collective-permute-start | bytes 1179656 | tf_op jit(solution)/shard_map/ppermute | solution.py:372
  128.2 28.4 %collective-permute-start.10 = (bf16[256,768]{1,0:T(8,128)(2,1)}, bf16[256,768]{1,0:T(8,128)(2,1)S(1)}, u32[]{:S(2)}, u32[]{:S(2)}) collective-permute-start(bf16[256,768]{1,0:T(8,128)(2,1)} %copy-done.18), channel_id=1, source_target_pairs={{0,1},{1,0},{2,3},{3,2},{4,5},{5,4},{6,7},{7,6},{8,9},{9,8},{10,11... | collective-permute-start | bytes 1179656 | tf_op jit(solution)/shard_map/ppermute | solution.py:372
  130.1 10.4 %copy-start.8 = (bf16[256,768]{1,0:T(8,128)(2,1)}, bf16[256,768]{1,0:T(8,128)(2,1)S(1)}, u32[]{:S(2)}) copy-start(bf16[256,768]{1,0:T(8,128)(2,1)S(1)} %collective-permute-done.17.refs_1_) | copy-start | bytes 1179652
  130.1 10.4 %copy-start.9 = (bf16[256,768]{1,0:T(8,128)(2,1)}, bf16[256,768]{1,0:T(8,128)(2,1)S(1)}, u32[]{:S(2)}) copy-start(bf16[256,768]{1,0:T(8,128)(2,1)S(1)} %collective-permute-done.16.refs_0_) | copy-start | bytes 1179652
  148.9 22.6 %collective-permute-start.18 = (bf16[4,512,384]{2,1,0:T(8,128)(2,1)}, bf16[4,512,384]{2,1,0:T(8,128)(2,1)S(1)}, u32[]{:S(2)}, u32[]{:S(2)}) collective-permute-start(bf16[4,512,384]{2,1,0:T(8,128)(2,1)} %shard_map.77), channel_id=1, source_target_pairs={{0,16},{16,0},{32,48},{48,32},{64,80},{80,64},{96,112},{112,96},{1... | collective-permute-start | bytes 4718600 | tf_op jit(solution)/shard_map/ppermute | solution.py:391
  150.0 0.7 copy-start.15
  156.5 0.7 copy-start.14
  171.4 15.9 %collective-permute-start.12 = (bf16[4,512,384]{2,1,0:T(8,128)(2,1)}, bf16[4,512,384]{2,1,0:T(8,128)(2,1)S(1)}, u32[]{:S(2)}, u32[]{:S(2)}) collective-permute-start(bf16[4,512,384]{2,1,0:T(8,128)(2,1)} %shard_map.75), channel_id=1, source_target_pairs={{0,16},{16,0},{32,48},{48,32},{64,80},{80,64},{96,112},{112,96},{1... | collective-permute-start | bytes 4718600 | tf_op jit(solution)/shard_map/ppermute | solution.py:391
  171.5 1.2 copy-start.6
  181.8 16.5 %collective-permute-start.19 = (bf16[512,384]{1,0:T(8,128)(2,1)}, bf16[512,384]{1,0:T(8,128)(2,1)S(1)}, u32[]{:S(2)}, u32[]{:S(2)}) collective-permute-start(bf16[512,384]{1,0:T(8,128)(2,1)} %get-tuple-element.94), channel_id=1, source_target_pairs={{0,64},{16,80},{32,96},{48,112},{64,0},{80,16},{96,32},{112,48},{1... | collective-permute-start | bytes 1179656 | tf_op jit(solution)/shard_map/ppermute | solution.py:397
  184.6 19.4 %collective-permute-start.20 = (bf16[512,384]{1,0:T(8,128)(2,1)}, bf16[512,384]{1,0:T(8,128)(2,1)}, u32[]{:S(2)}, u32[]{:S(2)}) collective-permute-start(bf16[512,384]{1,0:T(8,128)(2,1)} %get-tuple-element.95), channel_id=1, source_target_pairs={{0,32},{16,48},{32,64},{48,80},{64,96},{80,112},{96,0},{112,16},{1... | collective-permute-start | bytes 1179656 | tf_op jit(solution)/shard_map/ppermute | solution.py:397
  184.9 19.1 %copy-start.12 = (f32[512,384]{1,0:T(8,128)S(1)}, f32[512,384]{1,0:T(8,128)}, u32[]{:S(2)}) copy-start(f32[512,384]{1,0:T(8,128)} %get-tuple-element.93) | copy-start | bytes 2359300
  184.9 19.1 %collective-permute-start.21 = (bf16[512,384]{1,0:T(8,128)(2,1)}, bf16[512,384]{1,0:T(8,128)(2,1)}, u32[]{:S(2)}, u32[]{:S(2)}) collective-permute-start(bf16[512,384]{1,0:T(8,128)(2,1)} %get-tuple-element.96), channel_id=1, source_target_pairs={{0,96},{16,112},{32,0},{48,16},{64,32},{80,48},{96,64},{112,80},{1... | collective-permute-start | bytes 1179656 | tf_op jit(solution)/shard_map/ppermute | solution.py:397
  187.3 1.2 copy-start.5
  197.6 22.3 %copy-start.13 = (f32[512,384]{1,0:T(8,128)S(1)}, f32[512,384]{1,0:T(8,128)}, u32[]{:S(2)}) copy-start(f32[512,384]{1,0:T(8,128)} %get-tuple-element.85) | copy-start | bytes 2359300
  197.6 13.1 %collective-permute-start.13 = (bf16[512,384]{1,0:T(8,128)(2,1)}, bf16[512,384]{1,0:T(8,128)(2,1)S(1)}, u32[]{:S(2)}, u32[]{:S(2)}) collective-permute-start(bf16[512,384]{1,0:T(8,128)(2,1)} %get-tuple-element.86), channel_id=1, source_target_pairs={{0,64},{16,80},{32,96},{48,112},{64,0},{80,16},{96,32},{112,48},{1... | collective-permute-start | bytes 1179656 | tf_op jit(solution)/shard_map/ppermute | solution.py:397
  197.7 22.2 %collective-permute-start.14 = (bf16[512,384]{1,0:T(8,128)(2,1)}, bf16[512,384]{1,0:T(8,128)(2,1)S(1)}, u32[]{:S(2)}, u32[]{:S(2)}) collective-permute-start(bf16[512,384]{1,0:T(8,128)(2,1)} %get-tuple-element.87), channel_id=1, source_target_pairs={{0,32},{16,48},{32,64},{48,80},{64,96},{80,112},{96,0},{112,16},{1... | collective-permute-start | bytes 1179656 | tf_op jit(solution)/shard_map/ppermute | solution.py:397
  198.3 21.6 %collective-permute-start.15 = (bf16[512,384]{1,0:T(8,128)(2,1)}, bf16[512,384]{1,0:T(8,128)(2,1)S(1)}, u32[]{:S(2)}, u32[]{:S(2)}) collective-permute-start(bf16[512,384]{1,0:T(8,128)(2,1)} %get-tuple-element.88), channel_id=1, source_target_pairs={{0,96},{16,112},{32,0},{48,16},{64,32},{80,48},{96,64},{112,80},{1... | collective-permute-start | bytes 1179656 | tf_op jit(solution)/shard_map/ppermute | solution.py:397
  205.3 14.8 %collective-permute-start.22 = (bf16[512,384]{1,0:T(8,128)(2,1)S(1)}, bf16[512,384]{1,0:T(8,128)(2,1)S(1)}, u32[]{:S(2)}, u32[]{:S(2)}) collective-permute-start(bf16[512,384]{1,0:T(8,128)(2,1)S(1)} %add_convert_fusion), channel_id=1, source_target_pairs={{0,1},{1,0},{2,3},{3,2},{4,5},{5,4},{6,7},{7,6},{8,9},{9,8},{10,11... | collective-permute-start | bytes 1179656 | tf_op jit(solution)/shard_map/ppermute | solution.py:403
Sparse Core Ops, SparseCore 0:
  9.1 63.2 all-gather.4
  77.7 62.8 all-gather.6

commit v6 on v5

--- a/solution.py
+++ b/solution.py
@@ -190,12 +190,14 @@
     )(flags, *sent, query, key, value, mask)
 
 
-def products(at, flags, refs):
-    q0, q1, k0, k1, v0, v1 = refs[:6]
-    weights = refs[6:8]
-    buffer, sems = refs[-2:]
+def products(count, at, flags, refs):
+    weights = refs[3 * count : 3 * count + 2]
+    total, buffer, sems = refs[-3:]
     step = pl.program_id(0)
     encoder = flags[0] == 0
+
+    def rows(kind):
+        return jnp.concatenate([x[...] for x in refs[kind * count : (kind + 1) * count]])
 
     def copy(which, place):
         return pltpu.make_async_copy(
@@ -215,45 +217,30 @@
             def _():
                 copy(0, place).start()
 
-    for place in range(2):
-        copy(1, 2 * step + place).wait()
-
-        @pl.when(encoder)
-        def _():
-            copy(0, 2 * step + place).wait()
-
-    return (q0, q1), (k0, k1), (v0, v1), wide, encoder
-
-
-def whole(pair):
-    return jnp.concatenate([x[...] for x in pair])
-
-
-def give_kernel(at, flags, *refs):
-    out, total = refs[8], refs[-3]
-    dq, dk, dv, wide, encoder = products(at, flags, refs)
-    rows = jnp.where(encoder, whole(dv), whole(dq))
-    total[...] = mm(rows, wide(1), NT)
+    copy(1, 2 * step).wait()
+    copy(1, 2 * step + 1).wait()
+    total[...] = mm(jnp.where(encoder, rows(2), rows(0)), wide(1), NT)
 
     @pl.when(encoder)
     def _():
-        total[...] += mm(whole(dk), wide(0), NT)
-
+        copy(0, 2 * step).wait()
+        copy(0, 2 * step + 1).wait()
+        total[...] += mm(rows(1), wide(0), NT)
+
+    return total
+
+
+def give_kernel(count, at, flags, *refs):
+    out = refs[3 * count + 2]
+    total = products(count, at, flags, refs)
     shard = out.shape[2]
     for place in range(2):
         out[place] = total[:, place * shard : (place + 1) * shard].astype(BF16)
 
 
-def keep_kernel(at, flags, *refs):
-    other, outs, total = refs[8], refs[9:13], refs[-3]
-    dq, dk, dv, wide, encoder = products(at, flags, refs)
-    rows = jnp.where(encoder, whole(dv), whole(dq))
-    total[...] = mm(rows, wide(1), NT)
-
-    @pl.when(encoder)
-    def _():
-        total[...] += mm(whole(dk), wide(0), NT)
-
+def keep_kernel(count, at, flags, *refs):
+    other, outs = refs[3 * count + 2], refs[3 * count + 3 : 3 * count + 7]
+    total = products(count, at, flags, refs)
     shard = outs[0].shape[1]
     for i, out in enumerate(outs):
 
@@ -264,34 +251,39 @@
 
 
 def projected(at, flags, grads, first, second, other=None):
+    count = len(grads) // 3
     rows, width = grads[0].shape
     shard = first.shape[1]
     operand = pl.BlockSpec((rows, width), lambda i, at, flags: (0, 0))
-    moving = pl.BlockSpec((2, 2 * rows, shard), lambda i, at, flags: (i, 0, 0))
-    fixed = pl.BlockSpec((2 * rows, shard), lambda i, at, flags: (0, 0))
+    moving = pl.BlockSpec((2, count * rows, shard), lambda i, at, flags: (i, 0, 0))
+    fixed = pl.BlockSpec((count * rows, shard), lambda i, at, flags: (0, 0))
     if other is None:
         kernel, extra = give_kernel, ()
         out_specs = moving
-        out_shape = jax.ShapeDtypeStruct((4, 2 * rows, shard), BF16)
+        out_shape = jax.ShapeDtypeStruct((4, count * rows, shard), BF16)
     else:
         kernel, extra = keep_kernel, (other,)
         out_specs = [fixed] * 4
-        out_shape = [jax.ShapeDtypeStruct((2 * rows, shard), t) for t in (BF16, BF16, BF16, F32)]
+        out_shape = [
+            jax.ShapeDtypeStruct((count * rows, shard), t) for t in (BF16, BF16, BF16, F32)
+        ]
     return pl.pallas_call(
-        kernel,
+        functools.partial(kernel, count),
         grid_spec=pltpu.PrefetchScalarGridSpec(
             num_scalar_prefetch=2,
             grid=(2,),
-            in_specs=[operand] * 6 + [HBM] * 2 + [moving] * len(extra),
+            in_specs=[operand] * len(grads) + [HBM] * 2 + [moving] * len(extra),
             out_specs=out_specs,
             scratch_shapes=[
-                pltpu.VMEM((2 * rows, 2 * shard), F32),
+                pltpu.VMEM((count * rows, 2 * shard), F32),
                 pltpu.VMEM((2, 4, shard, width), BF16),
                 pltpu.SemaphoreType.DMA((2, 4)),
             ],
         ),
         out_shape=out_shape,
-        cost_estimate=cost(2 * 2 * rows * 2 * width * 4 * shard, 2 * 2 * 4 * shard * width),
+        cost_estimate=cost(
+            2 * count * rows * 2 * width * 4 * shard, 2 * 2 * 4 * shard * width
+        ),
     )(at, flags, *grads, first, second, *extra)
 
 
@@ -337,14 +329,14 @@
     first = gathered(weights[0, 0])
     part = picked(grads, columns, shard_rows)
     part, later_weights = lax.optimization_barrier((part, weights))
+    second = gathered(later_weights[0, 1])
     came = lax.ppermute(part, BOTH, DEC_SWAP)
     twin = lax.ppermute(came, "segment", CORE_SWAP)
 
-    ready = (came, twin, later_weights[0, 1], near, own_mask, near_flags, own_flags, keep_at, give_at)
+    ready = (came, twin, near, own_mask, near_flags, own_flags, keep_at, give_at)
     first, ready = lax.optimization_barrier((first, ready))
-    came, twin, second_shard, near, own_mask, near_flags, own_flags, keep_at, give_at = ready
+    came, twin, near, own_mask, near_flags, own_flags, keep_at, give_at = ready
     own = (*own[:3], own_mask)
-    second = gathered(second_shard)
 
     piece = 2 * shard_rows
     moved = pl.BlockSpec((row_count, piece), lambda j, at: (0, j % 2))
@@ -398,11 +390,11 @@
             result = result + other.astype(F32)
         return result.astype(BF16)
 
-    *blocks, block = chip_sums((*far_dq, *dk, *dv))
-    own_grads = (*dq, *own_dk, *own_dv)
-    from_partner = lax.ppermute(reduced(blocks, block), "fsdp", HALF_SWAP)
-    *blocks, block = chip_sums(own_grads)
-    own_out = reduced(blocks, block)
+    *blocks, block = chip_sums((*far_dq, dq[0], *dk, own_dk[0], *dv, own_dv[0]))
+    early = reduced(blocks, block)
+    from_partner = lax.ppermute(early[:row_count], "fsdp", HALF_SWAP)
+    *blocks, block = chip_sums((dq[1], own_dk[1], own_dv[1]))
+    own_out = jnp.concatenate([early[row_count:], reduced(blocks, block)])
     result = jnp.where(
         half == 0,
         jnp.concatenate([own_out, from_partner], axis=1),

time: 229 us -> 227 us (level)
  waiting for transfers between devices: 74.3 us -> 71.2 us
  starting transfers between devices: 38.2 us -> 41 us
    all_gather x2, waiting for transfers between devices: 10.4 us -> 0.05 us  [gathered(): return lax.all_gather(shard, 'fsdp', axis=0, axis_index_groups=Z_LINES)]
    ppermute x1, waiting for transfers between devices: 0.01 us -> 4.74 us  [per_device(): from_partner = lax.ppermute(early[:row_count], 'fsdp', HALF_SWAP)]
    ppermute x2, starting transfers between devices: 1.22 us -> 5.18 us  [chip_sums(): other = lax.ppermute(give, 'segment', CORE_SWAP)]
    ppermute x6, waiting for transfers between devices: 16.9 us -> 19.4 us  [reduced(): other = lax.ppermute(block, 'segment', pairs)]
    ppermute x2, waiting for transfers between devices: 10.7 us -> 13.1 us  [per_device(): ctx_near.append(lax.ppermute(ctx[micro], BOTH, DEC_TO_ENC))]
    ppermute x4, waiting for transfers between devices: 36.2 us -> 33.9 us  [per_device(): came_near.append(lax.ppermute(value, BOTH, ENC_SWAP))]
  transfers between devices with their start and end apart: 25 -> 25, of which waited for: 7 -> 9; matrix products, arithmetic and copies ran while one was open for 5% -> 6% of each run, Pallas kernels for 35% -> 30%
where the time goes in v6:
time: 227 us; the launch traced here: 226 us
  Pallas kernels  78.4 us (35%)
  waiting for transfers between devices  71.2 us (31%)
  starting transfers between devices  41 us (18%)
  between operations  13.9 us (6%)
  other arithmetic  11.7 us (5%)
  local copies, waits for them, and re-layouts  9.33 us (4%)
    pallas_call x4, Pallas kernels, projected(): pl.pallas_call(functools.partial(kernel, count), grid_spec=pltpu.Prefetch...  34.3 us
    ppermute x4, waiting for transfers between devices, per_device(): came_near.append(lax.ppermute(value, BOTH, ENC_SWAP))  33.9 us
    pallas_call x4, Pallas kernels, attend(): pl.pallas_call(functools.partial(attend_kernel, heads), grid_spec=pltpu.P...  23.7 us
    ppermute x6, waiting for transfers between devices, reduced(): other = lax.ppermute(block, 'segment', pairs)  19.4 us
    pallas_call x2, Pallas kernels, partial_products(): pl.pallas_call(kernel, grid_spec=pltpu.PrefetchScalarGridSpec(num_scalar_...  16 us
    ppermute x2, waiting for transfers between devices, per_device(): ctx_near.append(lax.ppermute(ctx[micro], BOTH, DEC_TO_ENC))  13.1 us
    ppermute x4, starting transfers between devices, per_device(): came_near.append(lax.ppermute(value, BOTH, ENC_SWAP))  11.2 us
    ppermute x6, starting transfers between devices, reduced(): other = lax.ppermute(block, 'segment', pairs)  8.53 us
  transfers between devices with their start and end apart: 25, of which 9 were waited for; matrix products, arithmetic and copies ran while one was open for 6% of the time, Pallas kernels for 30%

profile of v6, /device:TPU:1, one launch (start us, length us, event | category | flops | bytes accessed | tf_op | source)
XLA Modules:
  0.0 225.6 jit_solution(15288555323955509966)
XLA Ops:
  6.5 1.9 slice.12
  9.1 4.5 %pick.1 = bf16[512,1536]{1,0:T(8,128)(2,1)} custom-call(s32[4]{0:T(128)} %add_subtract_fusion.1.where, bf16[512,6144]{1,0:T(8,128)(2,1)} %bitcast.35), custom_call_target="tpu_custom_call" | custom-call | bytes 3145728 | tf_op jit(solution)/shard_map/pick/pallas_call | solution.py:44
  13.6 0.9 slice.13
  14.5 1.9 collective-permute-start
  16.4 4.0 %collective-permute-start.2 = (bf16[2,256,768]{2,1,0:T(8,128)(2,1)S(1)}, bf16[2,256,768]{2,1,0:T(8,128)(2,1)S(1)}, u32[]{:S(2)}, u32[]{:S(2)}) collective-permute-start(bf16[2,256,768]{2,1,0:T(8,128)(2,1)S(1)} %bitcast.40), channel_id=1, source_target_pairs={{0,1},{1,0},{2,3},{3,2},{4,5},{5,4},{6,7},{7,6},{8,9},{9,8},{10,11... | collective-permute-start | bytes 2359304 | tf_op jit(solution)/shard_map/ppermute | solution.py:315
  20.5 1.9 collective-permute-start.5
  22.4 3.4 %collective-permute-start.3 = (bf16[2,256,768]{2,1,0:T(8,128)(2,1)S(1)}, bf16[2,256,768]{2,1,0:T(8,128)(2,1)}, u32[]{:S(2)}, u32[]{:S(2)}) collective-permute-start(bf16[2,256,768]{2,1,0:T(8,128)(2,1)S(1)} %bitcast.43), channel_id=1, source_target_pairs={{0,1},{1,0},{2,3},{3,2},{4,5},{5,4},{6,7},{7,6},{8,9},{9,8},{10,11... | collective-permute-start | bytes 2359304 | tf_op jit(solution)/shard_map/ppermute | solution.py:315
  25.8 1.9 collective-permute-start.4
  27.8 3.7 %collective-permute-start.1 = (bf16[512,1536]{1,0:T(8,128)(2,1)}, bf16[512,1536]{1,0:T(8,128)(2,1)}, u32[]{:S(2)}, u32[]{:S(2)}) collective-permute-start(bf16[512,1536]{1,0:T(8,128)(2,1)} %collective-permute-done.came), channel_id=1, source_target_pairs={{0,16},{16,0},{32,48},{48,32},{64,80},{80,64},{96,112},{112,96},{1... | collective-permute-start | bytes 4718600 | tf_op jit(solution)/shard_map/ppermute | solution.py:334
  33.3 3.3 %collective-permute-done.5 = s32[2,1,256]{2,1,0:T(1,128)S(1)} collective-permute-done((s32[2,1,256]{2,1,0:T(1,128)S(1)}, s32[2,1,256]{2,1,0:T(1,128)S(1)}, u32[]{:S(2)}, u32[]{:S(2)}) %collective-permute-start.5) | collective-permute-done | bytes 2080 | tf_op jit(solution)/shard_map/ppermute | solution.py:315
  36.6 0.9 broadcast_select_fusion.2.refs_2_
  37.5 15.9 %collective-permute-done.3 = bf16[2,256,768]{2,1,0:T(8,128)(2,1)} collective-permute-done((bf16[2,256,768]{2,1,0:T(8,128)(2,1)S(1)}, bf16[2,256,768]{2,1,0:T(8,128)(2,1)}, u32[]{:S(2)}, u32[]{:S(2)}) %collective-permute-start.3) | collective-permute-done | bytes 786464 | tf_op jit(solution)/shard_map/ppermute | solution.py:315
  53.4 2.1 broadcast_select_fusion.1.refs_3_
  55.5 14.7 %collective-permute-done.4 = bf16[2,256,768]{2,1,0:T(8,128)(2,1)} collective-permute-done((bf16[2,256,768]{2,1,0:T(8,128)(2,1)S(1)}, bf16[2,256,768]{2,1,0:T(8,128)(2,1)}, u32[]{:S(2)}, u32[]{:S(2)}) %collective-permute-start.4) | collective-permute-done | bytes 786464 | tf_op jit(solution)/shard_map/ppermute | solution.py:315
  70.3 2.1 broadcast_select_fusion.refs_4_
  72.4 0.8 broadcast_in_dim.25.refs_5_
  73.3 0.8 broadcast_in_dim.27.refs_4_
  74.1 8.2 %shard_map.74 = (bf16[256,768]{1,0:T(8,128)(2,1)}, bf16[256,768]{1,0:T(8,128)(2,1)}) custom-call(s32[1]{0:T(128)} %bitcast.8.core, bf16[512,1536]{1,0:T(8,128)(2,1)} %collective-permute-done.came, bf16[512,1536]{1,0:T(8,128)(2,1)} %collective-permute-done.1.twin, bf16[8,384,768]{2,1,0:T(8,128)(2,1)} %bitcast.25), custom_call_target="tpu_custom_call" | custom-call | flops 2415919104 | bytes 4718592 | tf_op jit(solution)/shard_map/pallas_call | solution.py:115
  83.6 7.8 %shard_map.73 = (f32[256,768]{1,0:T(8,128)}, f32[256,768]{1,0:T(8,128)}) custom-call(s32[1]{0:T(128)} %bitcast.7.half, bf16[512,6144]{1,0:T(8,128)(2,1)} %bitcast.36, bf16[512,6144]{1,0:T(8,128)(2,1)} %bitcast.37, bf16[8,384,768]{2,1,0:T(8,128)(2,1)} %bitcast.26), custom_call_target="tpu_custom_call" | custom-call | flops 2415919104 | bytes 4718592 | tf_op jit(solution)/shard_map/pallas_call | solution.py:115
  91.5 1.3 add_convert_fusion.2.refs_1_
  92.8 1.3 collective-permute-start.9
  94.2 1.3 collective-permute-start.8
  95.5 12.6 %collective-permute-done.9.refs_0_ = bf16[256,768]{1,0:T(8,128)(2,1)S(1)} collective-permute-done((bf16[256,768]{1,0:T(8,128)(2,1)S(1)}, bf16[256,768]{1,0:T(8,128)(2,1)S(1)}, u32[]{:S(2)}, u32[]{:S(2)}) %collective-permute-start.9) | collective-permute-done | bytes 393248 | tf_op jit(solution)/shard_map/ppermute | solution.py:363
  108.1 1.9 collective-permute-start.13
  110.1 6.1 %attend.4 = (bf16[256,768]{1,0:T(8,128)(2,1)}, bf16[256,768]{1,0:T(8,128)(2,1)}, bf16[256,768]{1,0:T(8,128)(2,1)}) custom-call(s32[2]{0:T(128)} %get-tuple-element.60.flags, bf16[256,768]{1,0:T(8,128)(2,1)} %copy-done.17, bf16[256,768]{1,0:T(8,128)(2,1)} %copy-done.5, bf16[2,256,768]{2,1,0:T(8,128)(2,1)} %broadcast_select_fusion.2.refs_2_, ...), custom_call_target="tpu_custom_call" | custom-call | flops 503316480 | bytes 3145728 | tf_op jit(solution)/shard_map/attend/pallas_call | solution.py:171
  116.6 3.1 %collective-permute-start.12 = (bf16[256,768]{1,0:T(8,128)(2,1)S(1)}, bf16[256,768]{1,0:T(8,128)(2,1)S(1)}, u32[]{:S(2)}, u32[]{:S(2)}) collective-permute-start(bf16[256,768]{1,0:T(8,128)(2,1)S(1)} %collective-permute-done.8.refs_0_), channel_id=1, source_target_pairs={{0,1},{1,0},{2,3},{3,2},{4,5},{5,4},{6,7},{7,6},{8,9},{9,8},{10,11... | collective-permute-start | bytes 1179656 | tf_op jit(solution)/shard_map/ppermute | solution.py:364
  119.7 6.1 %attend.5 = (bf16[256,768]{1,0:T(8,128)(2,1)}, bf16[256,768]{1,0:T(8,128)(2,1)}, bf16[256,768]{1,0:T(8,128)(2,1)}) custom-call(s32[2]{0:T(128)} %get-tuple-element.60.flags, bf16[256,768]{1,0:T(8,128)(2,1)} %copy-done.18, bf16[256,768]{1,0:T(8,128)(2,1)} %copy-done.4, bf16[2,256,768]{2,1,0:T(8,128)(2,1)} %broadcast_select_fusion.2.refs_2_, ...), custom_call_target="tpu_custom_call" | custom-call | flops 503316480 | bytes 3145728 | tf_op jit(solution)/shard_map/attend/pallas_call | solution.py:171
  126.4 0.7 collective-permute-start.10
  127.2 0.7 copy-done.15
  127.9 5.8 %attend.6 = (bf16[256,768]{1,0:T(8,128)(2,1)}, bf16[256,768]{1,0:T(8,128)(2,1)}) custom-call(s32[2]{0:T(128)} %get-tuple-element.74.flags, bf16[256,768]{1,0:T(8,128)(2,1)} %copy-done.15, bf16[2,256,768]{2,1,0:T(8,128)(2,1)} %bitcast.38, bf16[2,256,768]{2,1,0:T(8,128)(2,1)} %bitcast.41, bf16[2,256,768]{2,1,0:T(8,128)(2,1)} %bitcast.44, ...), custom_call_target="tpu_custom_call" | custom-call | flops 503316480 | bytes 3145728 | tf_op jit(solution)/shard_map/attend/pallas_call | solution.py:171
  134.7 10.0 %shard_map.75 = bf16[4,768,384]{2,1,0:T(8,128)(2,1)} custom-call(s32[4]{0:T(128)} %get-tuple-element.83.at, s32[1]{0:T(128)} %bitcast.5.flags, bf16[256,768]{1,0:T(8,128)(2,1)} %copy-done.8, bf16[256,768]{1,0:T(8,128)(2,1)} %copy-done.7, bf16[256,768]{1,0:T(8,128)(2,1)} %get-tuple-element.69.refs_2_, bf16[256,768]{1,0:T(8,128)(2,1)} %get-tuple-element.72.refs_3_, ...), custom_call_target="tpu_custom_call" | custom-call | flops 3623878656 | bytes 4718592 | tf_op jit(solution)/shard_map/pallas_call | solution.py:270
  144.7 5.1 %collective-permute-start.14 = (bf16[4,768,384]{2,1,0:T(8,128)(2,1)}, bf16[4,768,384]{2,1,0:T(8,128)(2,1)S(1)}, u32[]{:S(2)}, u32[]{:S(2)}) collective-permute-start(bf16[4,768,384]{2,1,0:T(8,128)(2,1)} %shard_map.75), channel_id=1, source_target_pairs={{0,16},{16,0},{32,48},{48,32},{64,80},{80,64},{96,112},{112,96},{1... | collective-permute-start | bytes 7077896 | tf_op jit(solution)/shard_map/ppermute | solution.py:383
  149.8 5.8 %attend.7 = (bf16[256,768]{1,0:T(8,128)(2,1)}, bf16[256,768]{1,0:T(8,128)(2,1)}) custom-call(s32[2]{0:T(128)} %get-tuple-element.74.flags, bf16[256,768]{1,0:T(8,128)(2,1)} %copy-done.14, bf16[2,256,768]{2,1,0:T(8,128)(2,1)} %bitcast.39, bf16[2,256,768]{2,1,0:T(8,128)(2,1)} %bitcast.42, bf16[2,256,768]{2,1,0:T(8,128)(2,1)} %bitcast.45, ...), custom_call_target="tpu_custom_call" | custom-call | flops 503316480 | bytes 3145728 | tf_op jit(solution)/shard_map/attend/pallas_call | solution.py:171
  155.6 6.3 %shard_map.77 = bf16[4,256,384]{2,1,0:T(8,128)(2,1)} custom-call(s32[4]{0:T(128)} %get-tuple-element.83.at, s32[1]{0:T(128)} %bitcast.5.flags, bf16[256,768]{1,0:T(8,128)(2,1)} %get-tuple-element.71.refs_0_, bf16[256,768]{1,0:T(8,128)(2,1)} %get-tuple-element.89.refs_1_, bf16[256,768]{1,0:T(8,128)(2,1)} %get-tuple-element.90.refs_2_, ...), custom_call_target="tpu_custom_call" | custom-call | flops 1207959552 | bytes 4718592 | tf_op jit(solution)/shard_map/pallas_call | solution.py:270
  162.0 1.4 copy-done.3
  163.4 11.2 %shard_map.76 = (bf16[768,384]{1,0:T(8,128)(2,1)}, bf16[768,384]{1,0:T(8,128)(2,1)}, bf16[768,384]{1,0:T(8,128)(2,1)}, f32[768,384]{1,0:T(8,128)}) custom-call(s32[4]{0:T(128)} %broadcast_add_fusion.at, s32[1]{0:T(128)} %bitcast.5.flags, bf16[256,768]{1,0:T(8,128)(2,1)} %copy-done.8, bf16[256,768]{1,0:T(8,128)(2,1)} %copy-done.7, ...), custom_call_target="tpu_custom_call" | custom-call | flops 3623878656 | bytes 4718592 | tf_op jit(solution)/shard_map/pallas_call | solution.py:270
  174.6 2.8 %collective-permute-start.15 = (bf16[768,384]{1,0:T(8,128)(2,1)}, bf16[768,384]{1,0:T(8,128)(2,1)S(1)}, u32[]{:S(2)}, u32[]{:S(2)}) collective-permute-start(bf16[768,384]{1,0:T(8,128)(2,1)} %get-tuple-element.85), channel_id=1, source_target_pairs={{0,64},{16,80},{32,96},{48,112},{64,0},{80,16},{96,32},{112,48},{1... | collective-permute-start | bytes 1769480 | tf_op jit(solution)/shard_map/ppermute | solution.py:389
  177.7 2.4 %collective-permute-start.17 = (bf16[768,384]{1,0:T(8,128)(2,1)}, bf16[768,384]{1,0:T(8,128)(2,1)S(1)}, u32[]{:S(2)}, u32[]{:S(2)}) collective-permute-start(bf16[768,384]{1,0:T(8,128)(2,1)} %get-tuple-element.87), channel_id=1, source_target_pairs={{0,96},{16,112},{32,0},{48,16},{64,32},{80,48},{96,64},{112,80},{1... | collective-permute-start | bytes 1769480 | tf_op jit(solution)/shard_map/ppermute | solution.py:389
  180.1 0.9 copy-done.11
  181.0 6.8 %shard_map.78 = (bf16[256,384]{1,0:T(8,128)(2,1)}, bf16[256,384]{1,0:T(8,128)(2,1)}, bf16[256,384]{1,0:T(8,128)(2,1)}, f32[256,384]{1,0:T(8,128)}) custom-call(s32[4]{0:T(128)} %broadcast_add_fusion.at, s32[1]{0:T(128)} %bitcast.5.flags, bf16[256,768]{1,0:T(8,128)(2,1)} %get-tuple-element.71.refs_0_, bf16[256,768]{1,0:T(8,128)(2,1)} %get-tuple-element.89.refs_1_, ...), custom_call_target="tpu_custom_call" | custom-call | flops 1207959552 | bytes 4718592 | tf_op jit(solution)/shard_map/pallas_call | solution.py:270
  188.4 2.5 %collective-permute-done.15 = bf16[768,384]{1,0:T(8,128)(2,1)S(1)} collective-permute-done((bf16[768,384]{1,0:T(8,128)(2,1)}, bf16[768,384]{1,0:T(8,128)(2,1)S(1)}, u32[]{:S(2)}, u32[]{:S(2)}) %collective-permute-start.15) | collective-permute-done | bytes 589856 | tf_op jit(solution)/shard_map/ppermute | solution.py:389
  190.9 2.4 %collective-permute-start.21 = (bf16[256,384]{1,0:T(8,128)(2,1)}, bf16[256,384]{1,0:T(8,128)(2,1)S(1)}, u32[]{:S(2)}, u32[]{:S(2)}) collective-permute-start(bf16[256,384]{1,0:T(8,128)(2,1)} %get-tuple-element.94), channel_id=1, source_target_pairs={{0,96},{16,112},{32,0},{48,16},{64,32},{80,48},{96,64},{112,80},{1... | collective-permute-start | bytes 589832 | tf_op jit(solution)/shard_map/ppermute | solution.py:389
  193.3 11.9 %collective-permute-done.16 = bf16[768,384]{1,0:T(8,128)(2,1)} collective-permute-done((bf16[768,384]{1,0:T(8,128)(2,1)}, bf16[768,384]{1,0:T(8,128)(2,1)}, u32[]{:S(2)}, u32[]{:S(2)}) %collective-permute-start.16) | collective-permute-done | bytes 589856 | tf_op jit(solution)/shard_map/ppermute | solution.py:389
  205.2 0.8 copy-done.13
  206.0 1.6 add_convert_fusion
  207.8 5.0 %collective-permute-done.20 = bf16[256,384]{1,0:T(8,128)(2,1)S(1)} collective-permute-done((bf16[256,384]{1,0:T(8,128)(2,1)}, bf16[256,384]{1,0:T(8,128)(2,1)S(1)}, u32[]{:S(2)}, u32[]{:S(2)}) %collective-permute-start.20) | collective-permute-done | bytes 196640 | tf_op jit(solution)/shard_map/ppermute | solution.py:389
  212.9 4.7 %collective-permute-done.22 = bf16[512,384]{1,0:T(8,128)(2,1)S(1)} collective-permute-done((bf16[512,384]{1,0:T(8,128)(2,1)S(1)}, bf16[512,384]{1,0:T(8,128)(2,1)S(1)}, u32[]{:S(2)}, u32[]{:S(2)}) %collective-permute-start.22) | collective-permute-done | bytes 393248 | tf_op jit(solution)/shard_map/ppermute | solution.py:395
  217.7 1.1 maximum_select_fusion
  (79 shorter events, 7.5 us)
Async XLA Ops:
  6.5 65.9 %all-gather.5.cloned.1.call-start = ((), (), s32[]{:S(2)}) async-start(), calls=%async_computation | async-start | bytes 5308416 | tf_op jit(solution)/shard_map/all_gather | solution.py:305
  8.5 125.2 %all-gather.7.cloned.1.call-start = ((), (), s32[]{:S(2)}) async-start(), calls=%async_computation.1 | async-start | bytes 5308416 | tf_op jit(solution)/shard_map/all_gather | solution.py:305
  9.1 4.5 %copy-start.10 = (bf16[1,2,384,768]{3,2,1,0:T(8,128)(2,1)S(1)}, bf16[1,2,384,768]{3,2,1,0:T(8,128)(2,1)}, u32[]{:S(2)}) copy-start(bf16[1,2,384,768]{3,2,1,0:T(8,128)(2,1)} %param.12) | copy-start | bytes 3538948
  9.1 16.6 %copy-start.2 = (bf16[2,1,256,768]{3,2,1,0:T(8,128)(2,1)S(1)}, bf16[2,1,256,768]{3,2,1,0:T(8,128)(2,1)}, u32[]{:S(2)}) copy-start(bf16[2,1,256,768]{3,2,1,0:T(8,128)(2,1)} %param.10) | copy-start | bytes 2359300
  13.6 2.8 %copy-start = (bf16[2,1,256,768]{3,2,1,0:T(8,128)(2,1)S(1)}, bf16[2,1,256,768]{3,2,1,0:T(8,128)(2,1)}, u32[]{:S(2)}) copy-start(bf16[2,1,256,768]{3,2,1,0:T(8,128)(2,1)} %param.8) | copy-start | bytes 2359300
  13.6 6.9 %copy-start.19 = (s32[2,1,256]{2,1,0:T(1,128)S(1)}, s32[2,1,256]{2,1,0:T(1,128)}, u32[]{:S(2)}) copy-start(s32[2,1,256]{2,1,0:T(1,128)} %param.11) | copy-start | bytes 6148
  13.6 8.8 %copy-start.1 = (bf16[2,1,256,768]{3,2,1,0:T(8,128)(2,1)S(1)}, bf16[2,1,256,768]{3,2,1,0:T(8,128)(2,1)}, u32[]{:S(2)}) copy-start(bf16[2,1,256,768]{3,2,1,0:T(8,128)(2,1)} %param.9) | copy-start | bytes 2359300
  13.6 17.9 %copy-start.20 = (s32[4]{0:T(128)S(1)}, s32[4]{0:T(128)}, u32[]{:S(2)}) copy-start(s32[4]{0:T(128)} %constant.64.clone) | copy-start | bytes 52
  14.5 13.2 %collective-permute-start = (bf16[512,1536]{1,0:T(8,128)(2,1)}, bf16[512,1536]{1,0:T(8,128)(2,1)}, u32[]{:S(2)}, u32[]{:S(2)}) collective-permute-start(bf16[512,1536]{1,0:T(8,128)(2,1)} %pick.1), channel_id=1, source_target_pairs={{128,129},{129,128},{130,131},{131,130},{132,133},{133,132},{134,1... | collective-permute-start | bytes 4718600 | tf_op jit(solution)/shard_map/ppermute | solution.py:333
  16.4 20.1 %collective-permute-start.2 = (bf16[2,256,768]{2,1,0:T(8,128)(2,1)S(1)}, bf16[2,256,768]{2,1,0:T(8,128)(2,1)S(1)}, u32[]{:S(2)}, u32[]{:S(2)}) collective-permute-start(bf16[2,256,768]{2,1,0:T(8,128)(2,1)S(1)} %bitcast.40), channel_id=1, source_target_pairs={{0,1},{1,0},{2,3},{3,2},{4,5},{5,4},{6,7},{7,6},{8,9},{9,8},{10,11... | collective-permute-start | bytes 2359304 | tf_op jit(solution)/shard_map/ppermute | solution.py:315
  20.5 16.1 %collective-permute-start.5 = (s32[2,1,256]{2,1,0:T(1,128)S(1)}, s32[2,1,256]{2,1,0:T(1,128)S(1)}, u32[]{:S(2)}, u32[]{:S(2)}) collective-permute-start(s32[2,1,256]{2,1,0:T(1,128)S(1)} %copy-done.19), channel_id=1, source_target_pairs={{0,1},{1,0},{2,3},{3,2},{4,5},{5,4},{6,7},{7,6},{8,9},{9,8},{10,11... | collective-permute-start | bytes 6152 | tf_op jit(solution)/shard_map/ppermute | solution.py:315
  22.4 31.0 %collective-permute-start.3 = (bf16[2,256,768]{2,1,0:T(8,128)(2,1)S(1)}, bf16[2,256,768]{2,1,0:T(8,128)(2,1)}, u32[]{:S(2)}, u32[]{:S(2)}) collective-permute-start(bf16[2,256,768]{2,1,0:T(8,128)(2,1)S(1)} %bitcast.43), channel_id=1, source_target_pairs={{0,1},{1,0},{2,3},{3,2},{4,5},{5,4},{6,7},{7,6},{8,9},{9,8},{10,11... | collective-permute-start | bytes 2359304 | tf_op jit(solution)/shard_map/ppermute | solution.py:315
  25.8 44.5 %collective-permute-start.4 = (bf16[2,256,768]{2,1,0:T(8,128)(2,1)S(1)}, bf16[2,256,768]{2,1,0:T(8,128)(2,1)}, u32[]{:S(2)}, u32[]{:S(2)}) collective-permute-start(bf16[2,256,768]{2,1,0:T(8,128)(2,1)S(1)} %bitcast.46), channel_id=1, source_target_pairs={{0,1},{1,0},{2,3},{3,2},{4,5},{5,4},{6,7},{7,6},{8,9},{9,8},{10,11... | collective-permute-start | bytes 2359304 | tf_op jit(solution)/shard_map/ppermute | solution.py:315
  27.8 44.7 %collective-permute-start.1 = (bf16[512,1536]{1,0:T(8,128)(2,1)}, bf16[512,1536]{1,0:T(8,128)(2,1)}, u32[]{:S(2)}, u32[]{:S(2)}) collective-permute-start(bf16[512,1536]{1,0:T(8,128)(2,1)} %collective-permute-done.came), channel_id=1, source_target_pairs={{0,16},{16,0},{32,48},{48,32},{64,80},{80,64},{96,112},{112,96},{1... | collective-permute-start | bytes 4718600 | tf_op jit(solution)/shard_map/ppermute | solution.py:334
  82.3 9.2 %collective-permute-start.7 = (bf16[256,768]{1,0:T(8,128)(2,1)}, bf16[256,768]{1,0:T(8,128)(2,1)S(1)}, u32[]{:S(2)}, u32[]{:S(2)}) collective-permute-start(bf16[256,768]{1,0:T(8,128)(2,1)} %get-tuple-element.58), channel_id=1, source_target_pairs={{128,129},{129,128},{130,131},{131,130},{132,133},{133,132},{134,1... | collective-permute-start | bytes 1179656 | tf_op jit(solution)/shard_map/ppermute | solution.py:345
  82.9 11.1 %collective-permute-start.6 = (bf16[256,768]{1,0:T(8,128)(2,1)}, bf16[256,768]{1,0:T(8,128)(2,1)S(1)}, u32[]{:S(2)}, u32[]{:S(2)}) collective-permute-start(bf16[256,768]{1,0:T(8,128)(2,1)} %get-tuple-element.56), channel_id=1, source_target_pairs={{128,129},{129,128},{130,131},{131,130},{132,133},{133,132},{134,1... | collective-permute-start | bytes 1179656 | tf_op jit(solution)/shard_map/ppermute | solution.py:345
  91.5 2.6 %copy-start.12 = (f32[256,768]{1,0:T(8,128)S(1)}, f32[256,768]{1,0:T(8,128)}, u32[]{:S(2)}) copy-start(f32[256,768]{1,0:T(8,128)} %get-tuple-element.53) | copy-start | bytes 2359300
  92.8 17.3 %copy-start.5 = (bf16[256,768]{1,0:T(8,128)(2,1)}, bf16[256,768]{1,0:T(8,128)(2,1)S(1)}, u32[]{:S(2)}) copy-start(bf16[256,768]{1,0:T(8,128)(2,1)S(1)} %add_convert_fusion.2.refs_1_) | copy-start | bytes 1179652
  92.8 15.4 %collective-permute-start.9 = (bf16[256,768]{1,0:T(8,128)(2,1)S(1)}, bf16[256,768]{1,0:T(8,128)(2,1)S(1)}, u32[]{:S(2)}, u32[]{:S(2)}) collective-permute-start(bf16[256,768]{1,0:T(8,128)(2,1)S(1)} %add_convert_fusion.2.refs_1_), channel_id=1, source_target_pairs={{128,1},{129,0},{130,3},{131,2},{132,5},{133,4},{134,7},{135,6},{1... | collective-permute-start | bytes 1179656 | tf_op jit(solution)/shard_map/ppermute | solution.py:363
  94.2 22.0 %copy-start.4 = (bf16[256,768]{1,0:T(8,128)(2,1)}, bf16[256,768]{1,0:T(8,128)(2,1)S(1)}, u32[]{:S(2)}) copy-start(bf16[256,768]{1,0:T(8,128)(2,1)S(1)} %add_convert_fusion.1.refs_1_) | copy-start | bytes 1179652
  94.2 22.4 %collective-permute-start.8 = (bf16[256,768]{1,0:T(8,128)(2,1)S(1)}, bf16[256,768]{1,0:T(8,128)(2,1)S(1)}, u32[]{:S(2)}, u32[]{:S(2)}) collective-permute-start(bf16[256,768]{1,0:T(8,128)(2,1)S(1)} %add_convert_fusion.1.refs_1_), channel_id=1, source_target_pairs={{128,1},{129,0},{130,3},{131,2},{132,5},{133,4},{134,7},{135,6},{1... | collective-permute-start | bytes 1179656 | tf_op jit(solution)/shard_map/ppermute | solution.py:363
  108.1 1.9 copy-start.17
  108.1 19.0 %collective-permute-start.13 = (bf16[256,768]{1,0:T(8,128)(2,1)S(1)}, bf16[256,768]{1,0:T(8,128)(2,1)S(1)}, u32[]{:S(2)}, u32[]{:S(2)}) collective-permute-start(bf16[256,768]{1,0:T(8,128)(2,1)S(1)} %collective-permute-done.9.refs_0_), channel_id=1, source_target_pairs={{0,1},{1,0},{2,3},{3,2},{4,5},{5,4},{6,7},{7,6},{8,9},{9,8},{10,11... | collective-permute-start | bytes 1179656 | tf_op jit(solution)/shard_map/ppermute | solution.py:364
  116.6 3.1 %copy-start.18 = (bf16[256,768]{1,0:T(8,128)(2,1)}, bf16[256,768]{1,0:T(8,128)(2,1)S(1)}, u32[]{:S(2)}) copy-start(bf16[256,768]{1,0:T(8,128)(2,1)S(1)} %collective-permute-done.8.refs_0_) | copy-start | bytes 1179652
  116.6 9.9 %copy-start.6 = (bf16[256,768]{1,0:T(8,128)(2,1)S(1)}, bf16[256,768]{1,0:T(8,128)(2,1)}, u32[]{:S(2)}) copy-start(bf16[256,768]{1,0:T(8,128)(2,1)} %get-tuple-element.69.refs_2_) | copy-start | bytes 1179652
  116.6 17.1 %collective-permute-start.12 = (bf16[256,768]{1,0:T(8,128)(2,1)S(1)}, bf16[256,768]{1,0:T(8,128)(2,1)S(1)}, u32[]{:S(2)}, u32[]{:S(2)}) collective-permute-start(bf16[256,768]{1,0:T(8,128)(2,1)S(1)} %collective-permute-done.8.refs_0_), channel_id=1, source_target_pairs={{0,1},{1,0},{2,3},{3,2},{4,5},{5,4},{6,7},{7,6},{8,9},{9,8},{10,11... | collective-permute-start | bytes 1179656 | tf_op jit(solution)/shard_map/ppermute | solution.py:364
  125.8 8.0 %collective-permute-start.11 = (bf16[256,768]{1,0:T(8,128)(2,1)}, bf16[256,768]{1,0:T(8,128)(2,1)S(1)}, u32[]{:S(2)}, u32[]{:S(2)}) collective-permute-start(bf16[256,768]{1,0:T(8,128)(2,1)} %get-tuple-element.71.refs_0_), channel_id=1, source_target_pairs={{128,129},{129,128},{130,131},{131,130},{132,133},{133,132},{134,1... | collective-permute-start | bytes 1179656 | tf_op jit(solution)/shard_map/ppermute | solution.py:378
  126.4 7.3 %collective-permute-start.10 = (bf16[256,768]{1,0:T(8,128)(2,1)S(1)}, bf16[256,768]{1,0:T(8,128)(2,1)S(1)}, u32[]{:S(2)}, u32[]{:S(2)}) collective-permute-start(bf16[256,768]{1,0:T(8,128)(2,1)S(1)} %copy-done.6), channel_id=1, source_target_pairs={{128,129},{129,128},{130,131},{131,130},{132,133},{133,132},{134,1... | collective-permute-start | bytes 1179656 | tf_op jit(solution)/shard_map/ppermute | solution.py:378
  127.1 0.7 copy-start.15
  133.7 0.7 copy-start.14
  133.7 0.8 copy-start.7
  133.7 1.0 copy-start.8
  144.7 17.3 %collective-permute-start.14 = (bf16[4,768,384]{2,1,0:T(8,128)(2,1)}, bf16[4,768,384]{2,1,0:T(8,128)(2,1)S(1)}, u32[]{:S(2)}, u32[]{:S(2)}) collective-permute-start(bf16[4,768,384]{2,1,0:T(8,128)(2,1)} %shard_map.75), channel_id=1, source_target_pairs={{0,16},{16,0},{32,48},{48,32},{64,80},{80,64},{96,112},{112,96},{1... | collective-permute-start | bytes 7077896 | tf_op jit(solution)/shard_map/ppermute | solution.py:383
  161.9 18.2 %collective-permute-start.18 = (bf16[4,256,384]{2,1,0:T(8,128)(2,1)}, bf16[4,256,384]{2,1,0:T(8,128)(2,1)S(1)}, u32[]{:S(2)}, u32[]{:S(2)}) collective-permute-start(bf16[4,256,384]{2,1,0:T(8,128)(2,1)} %shard_map.77), channel_id=1, source_target_pairs={{0,16},{16,0},{32,48},{48,32},{64,80},{80,64},{96,112},{112,96},{1... | collective-permute-start | bytes 2359304 | tf_op jit(solution)/shard_map/ppermute | solution.py:383
  162.0 1.4 copy-start.3
  174.6 16.2 %collective-permute-start.15 = (bf16[768,384]{1,0:T(8,128)(2,1)}, bf16[768,384]{1,0:T(8,128)(2,1)S(1)}, u32[]{:S(2)}, u32[]{:S(2)}) collective-permute-start(bf16[768,384]{1,0:T(8,128)(2,1)} %get-tuple-element.85), channel_id=1, source_target_pairs={{0,64},{16,80},{32,96},{48,112},{64,0},{80,16},{96,32},{112,48},{1... | collective-permute-start | bytes 1769480 | tf_op jit(solution)/shard_map/ppermute | solution.py:389
  177.4 27.8 %collective-permute-start.16 = (bf16[768,384]{1,0:T(8,128)(2,1)}, bf16[768,384]{1,0:T(8,128)(2,1)}, u32[]{:S(2)}, u32[]{:S(2)}) collective-permute-start(bf16[768,384]{1,0:T(8,128)(2,1)} %get-tuple-element.86), channel_id=1, source_target_pairs={{0,32},{16,48},{32,64},{48,80},{64,96},{80,112},{96,0},{112,16},{1... | collective-permute-start | bytes 1769480 | tf_op jit(solution)/shard_map/ppermute | solution.py:389
  177.7 28.3 %copy-start.9 = (f32[768,384]{1,0:T(8,128)S(1)}, f32[768,384]{1,0:T(8,128)}, u32[]{:S(2)}) copy-start(f32[768,384]{1,0:T(8,128)} %get-tuple-element.84) | copy-start | bytes 3538948
  177.7 27.5 %collective-permute-start.17 = (bf16[768,384]{1,0:T(8,128)(2,1)}, bf16[768,384]{1,0:T(8,128)(2,1)S(1)}, u32[]{:S(2)}, u32[]{:S(2)}) collective-permute-start(bf16[768,384]{1,0:T(8,128)(2,1)} %get-tuple-element.87), channel_id=1, source_target_pairs={{0,96},{16,112},{32,0},{48,16},{64,32},{80,48},{96,64},{112,80},{1... | collective-permute-start | bytes 1769480 | tf_op jit(solution)/shard_map/ppermute | solution.py:389
  180.1 0.9 copy-start.11
  187.7 20.0 %collective-permute-start.19 = (bf16[256,384]{1,0:T(8,128)(2,1)}, bf16[256,384]{1,0:T(8,128)(2,1)S(1)}, u32[]{:S(2)}, u32[]{:S(2)}) collective-permute-start(bf16[256,384]{1,0:T(8,128)(2,1)} %get-tuple-element.92), channel_id=1, source_target_pairs={{0,64},{16,80},{32,96},{48,112},{64,0},{80,16},{96,32},{112,48},{1... | collective-permute-start | bytes 589832 | tf_op jit(solution)/shard_map/ppermute | solution.py:389
  187.8 24.9 %collective-permute-start.20 = (bf16[256,384]{1,0:T(8,128)(2,1)}, bf16[256,384]{1,0:T(8,128)(2,1)S(1)}, u32[]{:S(2)}, u32[]{:S(2)}) collective-permute-start(bf16[256,384]{1,0:T(8,128)(2,1)} %get-tuple-element.93), channel_id=1, source_target_pairs={{0,32},{16,48},{32,64},{48,80},{64,96},{80,112},{96,0},{112,16},{1... | collective-permute-start | bytes 589832 | tf_op jit(solution)/shard_map/ppermute | solution.py:389
  190.9 21.9 %collective-permute-start.21 = (bf16[256,384]{1,0:T(8,128)(2,1)}, bf16[256,384]{1,0:T(8,128)(2,1)S(1)}, u32[]{:S(2)}, u32[]{:S(2)}) collective-permute-start(bf16[256,384]{1,0:T(8,128)(2,1)} %get-tuple-element.94), channel_id=1, source_target_pairs={{0,96},{16,112},{32,0},{48,16},{64,32},{80,48},{96,64},{112,80},{1... | collective-permute-start | bytes 589832 | tf_op jit(solution)/shard_map/ppermute | solution.py:389
  205.2 0.8 copy-start.13
  206.0 6.7 %copy-start.16 = (f32[256,384]{1,0:T(8,128)S(1)}, f32[256,384]{1,0:T(8,128)}, u32[]{:S(2)}) copy-start(f32[256,384]{1,0:T(8,128)} %get-tuple-element.91) | copy-start | bytes 1179652
  207.7 10.0 %collective-permute-start.22 = (bf16[512,384]{1,0:T(8,128)(2,1)S(1)}, bf16[512,384]{1,0:T(8,128)(2,1)S(1)}, u32[]{:S(2)}, u32[]{:S(2)}) collective-permute-start(bf16[512,384]{1,0:T(8,128)(2,1)S(1)} %slice.17), channel_id=1, source_target_pairs={{0,1},{1,0},{2,3},{3,2},{4,5},{5,4},{6,7},{7,6},{8,9},{9,8},{10,11... | collective-permute-start | bytes 1179656 | tf_op jit(solution)/shard_map/ppermute | solution.py:395
Sparse Core Ops, SparseCore 0:
  9.1 63.2 all-gather.4
  74.2 58.2 all-gather.6

commit v7 on v6

--- a/solution.py
+++ b/solution.py
@@ -128,7 +128,7 @@
 
 
 def attend_kernel(heads, flags, *refs):
-    *sent, query, key, value, mask, dq, dk, dv = refs if len(refs) > 8 else (*refs[:5], None, *refs[5:])
+    *sent, query, key, value, hidden, first_out, second_out = refs
     scale = HDIM ** (-0.5)
     cuts = [slice(head * HDIM, (head + 1) * HDIM) for head in range(heads)]
 
@@ -137,23 +137,24 @@
         if len(sent) > 1:
             grad = jnp.where(flags[0] > 0, sent[1][:, cut], grad)
         q, k, v = query[:, cut], key[:, cut], value[:, cut]
-        scores = jnp.where(mask[:, :1] > 0, mm(k, q, NT) * scale, -jnp.inf)
+        scores = mm(k, q, NT) * scale + jnp.concatenate([hidden[...]] * 2, axis=1)
+        prob_grad = mm(v, grad, NT)
         raised = jnp.exp(scores - jnp.max(scores, axis=0, keepdims=True))
-        probs = raised * (1.0 / jnp.sum(raised, axis=0, keepdims=True))
-        prob_grad = mm(v, grad, NT)
-        center = jnp.sum(probs * prob_grad, axis=0, keepdims=True)
+        share = 1.0 / jnp.sum(raised, axis=0, keepdims=True)
+        center = jnp.sum(raised * prob_grad, axis=0, keepdims=True) * share
+        probs = raised * share
         return grad, q, k, probs, (probs * (prob_grad - center)).astype(BF16)
 
     def query_grads():
         for cut in cuts:
             _, _, k, _, score_grad = grads_of(cut)
-            dq[:, cut] = (mm(score_grad, k, TN) * scale).astype(BF16)
+            second_out[:, cut] = (mm(score_grad, k, TN) * scale).astype(BF16)
 
     def key_value_grads():
         for cut in cuts:
             grad, q, _, probs, score_grad = grads_of(cut)
-            dk[:, cut] = (mm(score_grad, q, NN) * scale).astype(BF16)
-            dv[:, cut] = mm(probs.astype(BF16), grad, NN).astype(BF16)
+            first_out[:, cut] = (mm(score_grad, q, NN) * scale).astype(BF16)
+            second_out[:, cut] = mm(probs.astype(BF16), grad, NN).astype(BF16)
 
     if len(sent) > 1:
         pl.when(flags[0] > 0)(query_grads)
@@ -167,7 +168,6 @@
     one = pl.BlockSpec((seq_length, wide), lambda h, flags: (0, h))
     row = pl.BlockSpec((None, seq_length, wide), lambda h, flags: (micro, 0, h))
     out = jax.ShapeDtypeStruct((seq_length, width), BF16)
-    outs = 1 + len(sent)
     return pl.pallas_call(
         functools.partial(attend_kernel, heads),
         grid_spec=pltpu.PrefetchScalarGridSpec(
@@ -180,9 +180,9 @@
                 row,
                 pl.BlockSpec((None, seq_length, HDIM), lambda h, flags: (micro, 0, 0)),
             ],
-            out_specs=[one] * outs,
-        ),
-        out_shape=[out] * outs,
+            out_specs=[one] * 2,
+        ),
+        out_shape=[out] * 2,
         cost_estimate=cost(
             10 * seq_length * seq_length * width, 16 * seq_length * width
         ),
@@ -191,13 +191,17 @@
 
 
 def products(count, at, flags, refs):
+    kinds = [refs[kind * count : (kind + 1) * count] for kind in range(3)]
     weights = refs[3 * count : 3 * count + 2]
-    total, buffer, sems = refs[-3:]
+    total, rows, row_sems, buffer, sems = refs[-5:]
+    each = rows.shape[1] // count
     step = pl.program_id(0)
     encoder = flags[0] == 0
 
-    def rows(kind):
-        return jnp.concatenate([x[...] for x in refs[kind * count : (kind + 1) * count]])
+    def row_copy(kind, which, i):
+        return pltpu.make_async_copy(
+            kinds[kind][i], rows.at[which, pl.ds(i * each, each)], row_sems.at[which, i]
+        )
 
     def copy(which, place):
         return pltpu.make_async_copy(
@@ -208,24 +212,40 @@
         pair = buffer[which, pl.ds(2 * step, 2)]
         return pair.reshape(pair.shape[0] * pair.shape[1], pair.shape[2])
 
-    @pl.when(step == 0)
-    def _():
+    @pl.when((step == 0) & encoder)
+    def _():
+        for turn in range(2):
+            for which, kind in ((1, 2), (0, 1)):
+                for i in range(count if turn == 0 else 0):
+                    row_copy(kind, which, i).start()
+                copy(which, 2 * turn).start()
+                copy(which, 2 * turn + 1).start()
+        for i in range(count):
+            row_copy(2, 1, i).wait()
+
+    @pl.when((step == 0) & (flags[0] > 0))
+    def _():
+        for i in range(count):
+            row_copy(0, 1, i).start()
         for place in range(4):
             copy(1, place).start()
-
-            @pl.when(encoder)
-            def _():
-                copy(0, place).start()
+        for i in range(count):
+            row_copy(0, 1, i).wait()
 
     copy(1, 2 * step).wait()
     copy(1, 2 * step + 1).wait()
-    total[...] = mm(jnp.where(encoder, rows(2), rows(0)), wide(1), NT)
+    total[...] = mm(rows[1], wide(1), NT)
+
+    @pl.when((step == 0) & encoder)
+    def _():
+        for i in range(count):
+            row_copy(1, 0, i).wait()
 
     @pl.when(encoder)
     def _():
         copy(0, 2 * step).wait()
         copy(0, 2 * step + 1).wait()
-        total[...] += mm(rows(1), wide(0), NT)
+        total[...] += mm(rows[0], wide(0), NT)
 
     return total
 
@@ -254,7 +274,6 @@
     count = len(grads) // 3
     rows, width = grads[0].shape
     shard = first.shape[1]
-    operand = pl.BlockSpec((rows, width), lambda i, at, flags: (0, 0))
     moving = pl.BlockSpec((2, count * rows, shard), lambda i, at, flags: (i, 0, 0))
     fixed = pl.BlockSpec((count * rows, shard), lambda i, at, flags: (0, 0))
     if other is None:
@@ -272,10 +291,12 @@
         grid_spec=pltpu.PrefetchScalarGridSpec(
             num_scalar_prefetch=2,
             grid=(2,),
-            in_specs=[operand] * len(grads) + [HBM] * 2 + [moving] * len(extra),
+            in_specs=[HBM] * (len(grads) + 2) + [moving] * len(extra),
             out_specs=out_specs,
             scratch_shapes=[
                 pltpu.VMEM((count * rows, 2 * shard), F32),
+                pltpu.VMEM((2, count * rows, width), BF16),
+                pltpu.SemaphoreType.DMA((2, count)),
                 pltpu.VMEM((2, 4, shard, width), BF16),
                 pltpu.SemaphoreType.DMA((2, 4)),
             ],
@@ -308,17 +329,15 @@
         queries.reshape(flat),
         enc_keys.reshape(flat),
         enc_values.reshape(flat),
-        key_mask.reshape(micro_count, 1, seq_length),
+        jnp.broadcast_to(
+            jnp.where(key_mask > 0, 0.0, -jnp.inf).astype(F32).reshape(micro_count, seq_length, 1),
+            (micro_count, seq_length, HDIM),
+        ),
     )
     came_near = []
     for value in own:
         came_near.append(lax.ppermute(value, BOTH, ENC_SWAP))
     near = [jnp.where(decoder, mine, other) for mine, other in zip(own, came_near)]
-    near[3], own_mask = [
-        jnp.broadcast_to(mask.reshape(micro_count, seq_length, 1), (micro_count, seq_length, HDIM))
-        for mask in (near[3], own[3])
-    ]
-
     near_flags = jnp.stack([dec, 1 - dec])
     own_flags = jnp.stack([0 * dec, 1 - dec])
     places = 2 * ((chip + jnp.array(STEPS, jnp.int32)) % 4)
@@ -333,7 +352,7 @@
     came = lax.ppermute(part, BOTH, DEC_SWAP)
     twin = lax.ppermute(came, "segment", CORE_SWAP)
 
-    ready = (came, twin, near, own_mask, near_flags, own_flags, keep_at, give_at)
+    ready = (came, twin, near, own[3], near_flags, own_flags, keep_at, give_at)
     first, ready = lax.optimization_barrier((first, ready))
     came, twin, near, own_mask, near_flags, own_flags, keep_at, give_at = ready
     own = (*own[:3], own_mask)
@@ -372,10 +391,10 @@
             grads.append(attend(flags, (came, *held[micro : micro + 1]), *operands, micro))
         return zip(*grads)
 
-    dq, dk, dv = attended(near_flags, ctx_near, ctx, near)
+    dk, dv = attended(near_flags, ctx_near, ctx, near)
     far_dq = []
     for micro in micros:
-        far_dq.append(lax.ppermute(dq[micro], BOTH, DEC_SWAP))
+        far_dq.append(lax.ppermute(dv[micro], BOTH, DEC_SWAP))
     own_dk, own_dv = attended(own_flags, ctx_own, (), own)
 
     def chip_sums(grads):
@@ -390,10 +409,10 @@
             result = result + other.astype(F32)
         return result.astype(BF16)
 
-    *blocks, block = chip_sums((*far_dq, dq[0], *dk, own_dk[0], *dv, own_dv[0]))
+    *blocks, block = chip_sums((*far_dq, dv[0], *dk, own_dk[0], *dv, own_dv[0]))
     early = reduced(blocks, block)
     from_partner = lax.ppermute(early[:row_count], "fsdp", HALF_SWAP)
-    *blocks, block = chip_sums((dq[1], own_dk[1], own_dv[1]))
+    *blocks, block = chip_sums((dv[1], own_dk[1], own_dv[1]))
     own_out = jnp.concatenate([early[row_count:], reduced(blocks, block)])
     result = jnp.where(
         half == 0,

time: 227 us -> 225 us (level)
  starting transfers between devices: 41 us -> 44.1 us
  Pallas kernels: 78.4 us -> 75.6 us
  waiting for transfers between devices: 71.2 us -> 68.6 us
    ppermute x2, waiting for transfers between devices: 13.1 us -> 8.51 us  [per_device(): ctx_near.append(lax.ppermute(ctx[micro], BOTH, DEC_TO_ENC))]
    ppermute x4, waiting for transfers between devices: 33.9 us -> 36.5 us  [per_device(): came_near.append(lax.ppermute(value, BOTH, ENC_SWAP))]
    unnamed x44 -> x45, local copies, waits for them, and re-layouts: 4.82 us -> 4.87 us
  transfers between devices with their start and end apart: 25 -> 25, of which waited for: 9 -> 8; matrix products, arithmetic and copies ran while one was open for 6% -> 6% of each run, Pallas kernels for 30% -> 30%
where the time goes in v7:
time: 225 us; the launch traced here: 224 us
  Pallas kernels  75.6 us (34%)
  waiting for transfers between devices  68.6 us (30%)
  starting transfers between devices  44.1 us (20%)
  between operations  13.9 us (6%)
  other arithmetic  13.5 us (6%)
  local copies, waits for them, and re-layouts  7.85 us (3%)
    ppermute x4, waiting for transfers between devices, per_device(): came_near.append(lax.ppermute(value, BOTH, ENC_SWAP))  36.5 us
    pallas_call x4, Pallas kernels, projected(): pl.pallas_call(functools.partial(kernel, count), grid_spec=pltpu.Prefetch...  32.2 us
    pallas_call x4, Pallas kernels, attend(): pl.pallas_call(functools.partial(attend_kernel, heads), grid_spec=pltpu.P...  23 us
    ppermute x6, waiting for transfers between devices, reduced(): other = lax.ppermute(block, 'segment', pairs)  18.7 us
    pallas_call x2, Pallas kernels, partial_products(): pl.pallas_call(kernel, grid_spec=pltpu.PrefetchScalarGridSpec(num_scalar_...  15.9 us
    ppermute x4, starting transfers between devices, per_device(): came_near.append(lax.ppermute(value, BOTH, ENC_SWAP))  11.2 us
    ppermute x6, starting transfers between devices, reduced(): other = lax.ppermute(block, 'segment', pairs)  8.77 us
    ppermute x2, waiting for transfers between devices, per_device(): ctx_near.append(lax.ppermute(ctx[micro], BOTH, DEC_TO_ENC))  8.51 us
  transfers between devices with their start and end apart: 25, of which 8 were waited for; matrix products, arithmetic and copies ran while one was open for 6% of the time, Pallas kernels for 30%

profile of v7, /device:TPU:1, one launch (start us, length us, event | category | flops | bytes accessed | tf_op | source)
XLA Modules:
  0.0 223.5 jit_solution(17629409491312224595)
XLA Ops:
  6.5 1.9 slice.12
  9.2 4.5 %pick.1 = bf16[512,1536]{1,0:T(8,128)(2,1)} custom-call(s32[4]{0:T(128)} %add_subtract_fusion.1.where, bf16[512,6144]{1,0:T(8,128)(2,1)} %bitcast.32), custom_call_target="tpu_custom_call" | custom-call | bytes 3145728 | tf_op jit(solution)/shard_map/pick/pallas_call | solution.py:44
  13.7 0.9 slice.13
  14.6 1.8 collective-permute-start
  16.5 4.0 %collective-permute-start.5 = (f32[2,256,128]{2,1,0:T(8,128)S(1)}, f32[2,256,128]{2,1,0:T(8,128)}, u32[]{:S(2)}, u32[]{:S(2)}) collective-permute-start(f32[2,256,128]{2,1,0:T(8,128)S(1)} %broadcast_in_dim.28.refs_4_), channel_id=1, source_target_pairs={{0,1},{1,0},{2,3},{3,2},{4,5},{5,4},{6,7},{7,6},{8,9},{9,8},{10,11... | collective-permute-start | bytes 786440 | tf_op jit(solution)/shard_map/ppermute | solution.py:339
  20.6 1.9 collective-permute-start.2
  22.5 3.4 %collective-permute-start.3 = (bf16[2,256,768]{2,1,0:T(8,128)(2,1)S(1)}, bf16[2,256,768]{2,1,0:T(8,128)(2,1)}, u32[]{:S(2)}, u32[]{:S(2)}) collective-permute-start(bf16[2,256,768]{2,1,0:T(8,128)(2,1)S(1)} %bitcast.40), channel_id=1, source_target_pairs={{0,1},{1,0},{2,3},{3,2},{4,5},{5,4},{6,7},{7,6},{8,9},{9,8},{10,11... | collective-permute-start | bytes 2359304 | tf_op jit(solution)/shard_map/ppermute | solution.py:339
  25.9 1.9 collective-permute-start.4
  27.9 3.7 %collective-permute-start.1 = (bf16[512,1536]{1,0:T(8,128)(2,1)}, bf16[512,1536]{1,0:T(8,128)(2,1)}, u32[]{:S(2)}, u32[]{:S(2)}) collective-permute-start(bf16[512,1536]{1,0:T(8,128)(2,1)} %collective-permute-done.came), channel_id=1, source_target_pairs={{0,16},{16,0},{32,48},{48,32},{64,80},{80,64},{96,112},{112,96},{1... | collective-permute-start | bytes 4718600 | tf_op jit(solution)/shard_map/ppermute | solution.py:353
  33.4 1.8 broadcast_select_fusion.3.refs_5_
  35.2 7.0 %collective-permute-done.2 = bf16[2,256,768]{2,1,0:T(8,128)(2,1)} collective-permute-done((bf16[2,256,768]{2,1,0:T(8,128)(2,1)S(1)}, bf16[2,256,768]{2,1,0:T(8,128)(2,1)}, u32[]{:S(2)}, u32[]{:S(2)}) %collective-permute-start.2) | collective-permute-done | bytes 786464 | tf_op jit(solution)/shard_map/ppermute | solution.py:339
  42.2 2.1 broadcast_select_fusion.2.refs_2_
  44.4 14.7 %collective-permute-done.3 = bf16[2,256,768]{2,1,0:T(8,128)(2,1)} collective-permute-done((bf16[2,256,768]{2,1,0:T(8,128)(2,1)S(1)}, bf16[2,256,768]{2,1,0:T(8,128)(2,1)}, u32[]{:S(2)}, u32[]{:S(2)}) %collective-permute-start.3) | collective-permute-done | bytes 786464 | tf_op jit(solution)/shard_map/ppermute | solution.py:339
  59.1 2.1 broadcast_select_fusion.1.refs_3_
  61.2 14.7 %collective-permute-done.4 = bf16[2,256,768]{2,1,0:T(8,128)(2,1)S(1)} collective-permute-done((bf16[2,256,768]{2,1,0:T(8,128)(2,1)S(1)}, bf16[2,256,768]{2,1,0:T(8,128)(2,1)S(1)}, u32[]{:S(2)}, u32[]{:S(2)}) %collective-permute-start.4) | collective-permute-done | bytes 786464 | tf_op jit(solution)/shard_map/ppermute | solution.py:339
  75.9 1.0 broadcast_select_fusion.refs_4_
  76.9 8.2 %shard_map.74 = (bf16[256,768]{1,0:T(8,128)(2,1)}, bf16[256,768]{1,0:T(8,128)(2,1)}) custom-call(s32[1]{0:T(128)} %bitcast.8.core, bf16[512,1536]{1,0:T(8,128)(2,1)} %collective-permute-done.came, bf16[512,1536]{1,0:T(8,128)(2,1)} %collective-permute-done.1.twin, bf16[8,384,768]{2,1,0:T(8,128)(2,1)} %bitcast.22), custom_call_target="tpu_custom_call" | custom-call | flops 2415919104 | bytes 4718592 | tf_op jit(solution)/shard_map/pallas_call | solution.py:115
  85.8 0.7 collective-permute-start.6
  86.5 7.7 %shard_map.73 = (f32[256,768]{1,0:T(8,128)}, f32[256,768]{1,0:T(8,128)}) custom-call(s32[1]{0:T(128)} %bitcast.7.half, bf16[512,6144]{1,0:T(8,128)(2,1)} %bitcast.33, bf16[512,6144]{1,0:T(8,128)(2,1)} %bitcast.34, bf16[8,384,768]{2,1,0:T(8,128)(2,1)} %bitcast.23), custom_call_target="tpu_custom_call" | custom-call | flops 2415919104 | bytes 4718592 | tf_op jit(solution)/shard_map/pallas_call | solution.py:115
  94.3 1.3 add_convert_fusion.2.refs_1_
  95.6 1.3 collective-permute-start.9
  97.0 1.3 collective-permute-start.8
  98.3 8.5 %collective-permute-done.9.refs_0_ = bf16[256,768]{1,0:T(8,128)(2,1)S(1)} collective-permute-done((bf16[256,768]{1,0:T(8,128)(2,1)S(1)}, bf16[256,768]{1,0:T(8,128)(2,1)S(1)}, u32[]{:S(2)}, u32[]{:S(2)}) %collective-permute-start.9) | collective-permute-done | bytes 393248 | tf_op jit(solution)/shard_map/ppermute | solution.py:382
  106.8 3.7 %collective-permute-start.13 = (bf16[256,768]{1,0:T(8,128)(2,1)S(1)}, bf16[256,768]{1,0:T(8,128)(2,1)S(1)}, u32[]{:S(2)}, u32[]{:S(2)}) collective-permute-start(bf16[256,768]{1,0:T(8,128)(2,1)S(1)} %collective-permute-done.9.refs_0_), channel_id=1, source_target_pairs={{0,1},{1,0},{2,3},{3,2},{4,5},{5,4},{6,7},{7,6},{8,9},{9,8},{10,11... | collective-permute-start | bytes 1179656 | tf_op jit(solution)/shard_map/ppermute | solution.py:383
  110.5 5.9 %attend.4 = (bf16[256,768]{1,0:T(8,128)(2,1)}, bf16[256,768]{1,0:T(8,128)(2,1)}) custom-call(s32[2]{0:T(128)} %get-tuple-element.57.flags, bf16[256,768]{1,0:T(8,128)(2,1)} %copy-done.18, bf16[256,768]{1,0:T(8,128)(2,1)} %copy-done.7, bf16[2,256,768]{2,1,0:T(8,128)(2,1)} %broadcast_select_fusion.2.refs_2_, ...), custom_call_target="tpu_custom_call" | custom-call | flops 503316480 | bytes 3145728 | tf_op jit(solution)/shard_map/attend/pallas_call | solution.py:171
  116.4 2.6 %collective-permute-start.12 = (bf16[256,768]{1,0:T(8,128)(2,1)S(1)}, bf16[256,768]{1,0:T(8,128)(2,1)S(1)}, u32[]{:S(2)}, u32[]{:S(2)}) collective-permute-start(bf16[256,768]{1,0:T(8,128)(2,1)S(1)} %collective-permute-done.8.refs_0_), channel_id=1, source_target_pairs={{0,1},{1,0},{2,3},{3,2},{4,5},{5,4},{6,7},{7,6},{8,9},{9,8},{10,11... | collective-permute-start | bytes 1179656 | tf_op jit(solution)/shard_map/ppermute | solution.py:383
  119.0 5.9 %attend.5 = (bf16[256,768]{1,0:T(8,128)(2,1)}, bf16[256,768]{1,0:T(8,128)(2,1)}) custom-call(s32[2]{0:T(128)} %get-tuple-element.57.flags, bf16[256,768]{1,0:T(8,128)(2,1)} %copy-done.19, bf16[256,768]{1,0:T(8,128)(2,1)} %copy-done.6, bf16[2,256,768]{2,1,0:T(8,128)(2,1)} %broadcast_select_fusion.2.refs_2_, ...), custom_call_target="tpu_custom_call" | custom-call | flops 503316480 | bytes 3145728 | tf_op jit(solution)/shard_map/attend/pallas_call | solution.py:171
  126.3 0.7 copy-done.16
  127.0 5.7 %attend.6 = (bf16[256,768]{1,0:T(8,128)(2,1)}, bf16[256,768]{1,0:T(8,128)(2,1)}) custom-call(s32[2]{0:T(128)} %get-tuple-element.70.flags, bf16[256,768]{1,0:T(8,128)(2,1)} %copy-done.16, bf16[2,256,768]{2,1,0:T(8,128)(2,1)} %bitcast.35, bf16[2,256,768]{2,1,0:T(8,128)(2,1)} %bitcast.38, bf16[2,256,768]{2,1,0:T(8,128)(2,1)} %bitcast.41, f32[2,256,128]{2,1,0:T(8,128)} %copy-done.4), custom_call_target="tpu_custom_call" | custom-call | flops 503316480 | bytes 3145728 | tf_op jit(solution)/shard_map/attend/pallas_call | solution.py:171
  132.8 0.8 copy-done.8
  133.7 8.6 %shard_map.75 = bf16[4,768,384]{2,1,0:T(8,128)(2,1)} custom-call(s32[4]{0:T(128)} %get-tuple-element.77.at, s32[1]{0:T(128)} %bitcast.5.flags, bf16[256,768]{1,0:T(8,128)(2,1)} %copy-done.9, bf16[256,768]{1,0:T(8,128)(2,1)} %copy-done.8, bf16[256,768]{1,0:T(8,128)(2,1)} %get-tuple-element.65.refs_2_.refs_6_, bf16[256,768]{1,0:T(8,128)(2,1)} %get-tuple-element.68.refs_3_, ...), custom_call_target="tpu_custom_call" | custom-call | flops 3623878656 | bytes 4718592 | tf_op jit(solution)/shard_map/pallas_call | solution.py:289
  142.3 6.5 %collective-permute-start.14 = (bf16[4,768,384]{2,1,0:T(8,128)(2,1)}, bf16[4,768,384]{2,1,0:T(8,128)(2,1)S(1)}, u32[]{:S(2)}, u32[]{:S(2)}) collective-permute-start(bf16[4,768,384]{2,1,0:T(8,128)(2,1)} %shard_map.75), channel_id=1, source_target_pairs={{0,16},{16,0},{32,48},{48,32},{64,80},{80,64},{96,112},{112,96},{1... | collective-permute-start | bytes 7077896 | tf_op jit(solution)/shard_map/ppermute | solution.py:402
  148.8 5.7 %attend.7 = (bf16[256,768]{1,0:T(8,128)(2,1)}, bf16[256,768]{1,0:T(8,128)(2,1)}) custom-call(s32[2]{0:T(128)} %get-tuple-element.70.flags, bf16[256,768]{1,0:T(8,128)(2,1)} %copy-done.15, bf16[2,256,768]{2,1,0:T(8,128)(2,1)} %bitcast.36, bf16[2,256,768]{2,1,0:T(8,128)(2,1)} %bitcast.39, bf16[2,256,768]{2,1,0:T(8,128)(2,1)} %bitcast.42, f32[2,256,128]{2,1,0:T(8,128)} %copy-done.4), custom_call_target="tpu_custom_call" | custom-call | flops 503316480 | bytes 3145728 | tf_op jit(solution)/shard_map/attend/pallas_call | solution.py:171
  154.4 5.9 %shard_map.77 = bf16[4,256,384]{2,1,0:T(8,128)(2,1)} custom-call(s32[4]{0:T(128)} %get-tuple-element.77.at, s32[1]{0:T(128)} %bitcast.5.flags, bf16[256,768]{1,0:T(8,128)(2,1)} %get-tuple-element.67.refs_7_.refs_0_, bf16[256,768]{1,0:T(8,128)(2,1)} %get-tuple-element.83.refs_1_, bf16[256,768]{1,0:T(8,128)(2,1)} %get-tuple-element.84.refs_2_, ...), custom_call_target="tpu_custom_call" | custom-call | flops 1207959552 | bytes 4718592 | tf_op jit(solution)/shard_map/pallas_call | solution.py:289
  160.5 1.4 copy-done.5
  161.9 10.7 %shard_map.76 = (bf16[768,384]{1,0:T(8,128)(2,1)}, bf16[768,384]{1,0:T(8,128)(2,1)}, bf16[768,384]{1,0:T(8,128)(2,1)}, f32[768,384]{1,0:T(8,128)}) custom-call(s32[4]{0:T(128)} %broadcast_add_fusion.at, s32[1]{0:T(128)} %bitcast.5.flags, bf16[256,768]{1,0:T(8,128)(2,1)} %copy-done.9, bf16[256,768]{1,0:T(8,128)(2,1)} %copy-done.8, ...), custom_call_target="tpu_custom_call" | custom-call | flops 3623878656 | bytes 4718592 | tf_op jit(solution)/shard_map/pallas_call | solution.py:289
  172.5 2.9 %collective-permute-start.15 = (bf16[768,384]{1,0:T(8,128)(2,1)}, bf16[768,384]{1,0:T(8,128)(2,1)S(1)}, u32[]{:S(2)}, u32[]{:S(2)}) collective-permute-start(bf16[768,384]{1,0:T(8,128)(2,1)} %get-tuple-element.79), channel_id=1, source_target_pairs={{0,64},{16,80},{32,96},{48,112},{64,0},{80,16},{96,32},{112,48},{1... | collective-permute-start | bytes 1769480 | tf_op jit(solution)/shard_map/ppermute | solution.py:408
  175.7 2.4 %collective-permute-start.17 = (bf16[768,384]{1,0:T(8,128)(2,1)}, bf16[768,384]{1,0:T(8,128)(2,1)S(1)}, u32[]{:S(2)}, u32[]{:S(2)}) collective-permute-start(bf16[768,384]{1,0:T(8,128)(2,1)} %get-tuple-element.81), channel_id=1, source_target_pairs={{0,96},{16,112},{32,0},{48,16},{64,32},{80,48},{96,64},{112,80},{1... | collective-permute-start | bytes 1769480 | tf_op jit(solution)/shard_map/ppermute | solution.py:408
  178.1 0.9 copy-done.12
  179.0 7.0 %shard_map.78 = (bf16[256,384]{1,0:T(8,128)(2,1)}, bf16[256,384]{1,0:T(8,128)(2,1)}, bf16[256,384]{1,0:T(8,128)(2,1)}, f32[256,384]{1,0:T(8,128)}) custom-call(s32[4]{0:T(128)} %broadcast_add_fusion.at, s32[1]{0:T(128)} %bitcast.5.flags, bf16[256,768]{1,0:T(8,128)(2,1)} %get-tuple-element.67.refs_7_.refs_0_, bf16[256,768]{1,0:T(8,128)(2,1)} %get-tuple-element.83.refs_1_, ...), custom_call_target="tpu_custom_call" | custom-call | flops 1207959552 | bytes 4718592 | tf_op jit(solution)/shard_map/pallas_call | solution.py:289
  186.7 2.1 collective-permute-done.15
  188.8 2.5 %collective-permute-start.21 = (bf16[256,384]{1,0:T(8,128)(2,1)}, bf16[256,384]{1,0:T(8,128)(2,1)S(1)}, u32[]{:S(2)}, u32[]{:S(2)}) collective-permute-start(bf16[256,384]{1,0:T(8,128)(2,1)} %get-tuple-element.88), channel_id=1, source_target_pairs={{0,96},{16,112},{32,0},{48,16},{64,32},{80,48},{96,64},{112,80},{1... | collective-permute-start | bytes 589832 | tf_op jit(solution)/shard_map/ppermute | solution.py:408
  191.3 11.8 %collective-permute-done.16 = bf16[768,384]{1,0:T(8,128)(2,1)} collective-permute-done((bf16[768,384]{1,0:T(8,128)(2,1)}, bf16[768,384]{1,0:T(8,128)(2,1)}, u32[]{:S(2)}, u32[]{:S(2)}) %collective-permute-start.16) | collective-permute-done | bytes 589856 | tf_op jit(solution)/shard_map/ppermute | solution.py:408
  203.1 0.8 copy-done.14
  204.0 1.6 add_convert_fusion
  205.8 4.8 %collective-permute-done.20 = bf16[256,384]{1,0:T(8,128)(2,1)S(1)} collective-permute-done((bf16[256,384]{1,0:T(8,128)(2,1)}, bf16[256,384]{1,0:T(8,128)(2,1)S(1)}, u32[]{:S(2)}, u32[]{:S(2)}) %collective-permute-start.20) | collective-permute-done | bytes 196640 | tf_op jit(solution)/shard_map/ppermute | solution.py:408
  210.8 4.8 %collective-permute-done.22 = bf16[512,384]{1,0:T(8,128)(2,1)S(1)} collective-permute-done((bf16[512,384]{1,0:T(8,128)(2,1)S(1)}, bf16[512,384]{1,0:T(8,128)(2,1)S(1)}, u32[]{:S(2)}, u32[]{:S(2)}) %collective-permute-start.22) | collective-permute-done | bytes 393248 | tf_op jit(solution)/shard_map/ppermute | solution.py:414
  215.6 1.1 maximum_select_fusion
  (80 shorter events, 6.6 us)
Async XLA Ops:
  6.5 70.4 %all-gather.5.cloned.1.call-start = ((), (), s32[]{:S(2)}) async-start(), calls=%async_computation | async-start | bytes 5308416 | tf_op jit(solution)/shard_map/all_gather | solution.py:326
  8.5 124.2 %all-gather.7.cloned.1.call-start = ((), (), s32[]{:S(2)}) async-start(), calls=%async_computation.1 | async-start | bytes 5308416 | tf_op jit(solution)/shard_map/all_gather | solution.py:326
  9.1 4.5 %copy-start.11 = (bf16[1,2,384,768]{3,2,1,0:T(8,128)(2,1)S(1)}, bf16[1,2,384,768]{3,2,1,0:T(8,128)(2,1)}, u32[]{:S(2)}) copy-start(bf16[1,2,384,768]{3,2,1,0:T(8,128)(2,1)} %param.12) | copy-start | bytes 3538948
  9.2 16.7 %copy-start.2 = (bf16[2,1,256,768]{3,2,1,0:T(8,128)(2,1)S(1)}, bf16[2,1,256,768]{3,2,1,0:T(8,128)(2,1)}, u32[]{:S(2)}) copy-start(bf16[2,1,256,768]{3,2,1,0:T(8,128)(2,1)} %param.10) | copy-start | bytes 2359300
  13.6 2.8 %copy-start.20 = (s32[2,1,256]{2,1,0:T(1,128)S(1)}, s32[2,1,256]{2,1,0:T(1,128)}, u32[]{:S(2)}) copy-start(s32[2,1,256]{2,1,0:T(1,128)} %param.11) | copy-start | bytes 6148
  13.6 6.9 %copy-start = (bf16[2,1,256,768]{3,2,1,0:T(8,128)(2,1)S(1)}, bf16[2,1,256,768]{3,2,1,0:T(8,128)(2,1)}, u32[]{:S(2)}) copy-start(bf16[2,1,256,768]{3,2,1,0:T(8,128)(2,1)} %param.8) | copy-start | bytes 2359300
  13.6 8.9 %copy-start.1 = (bf16[2,1,256,768]{3,2,1,0:T(8,128)(2,1)S(1)}, bf16[2,1,256,768]{3,2,1,0:T(8,128)(2,1)}, u32[]{:S(2)}) copy-start(bf16[2,1,256,768]{3,2,1,0:T(8,128)(2,1)} %param.9) | copy-start | bytes 2359300
  13.6 18.0 %copy-start.21 = (s32[4]{0:T(128)S(1)}, s32[4]{0:T(128)}, u32[]{:S(2)}) copy-start(s32[4]{0:T(128)} %constant.69.clone) | copy-start | bytes 52
  14.6 13.3 %collective-permute-start = (bf16[512,1536]{1,0:T(8,128)(2,1)}, bf16[512,1536]{1,0:T(8,128)(2,1)}, u32[]{:S(2)}, u32[]{:S(2)}) collective-permute-start(bf16[512,1536]{1,0:T(8,128)(2,1)} %pick.1), channel_id=1, source_target_pairs={{128,129},{129,128},{130,131},{131,130},{132,133},{133,132},{134,1... | collective-permute-start | bytes 4718600 | tf_op jit(solution)/shard_map/ppermute | solution.py:352
  16.5 44.7 %copy-start.4 = (f32[2,256,128]{2,1,0:T(8,128)}, f32[2,256,128]{2,1,0:T(8,128)S(1)}, u32[]{:S(2)}) copy-start(f32[2,256,128]{2,1,0:T(8,128)S(1)} %broadcast_in_dim.28.refs_4_) | copy-start | bytes 786436
  16.5 16.9 %collective-permute-start.5 = (f32[2,256,128]{2,1,0:T(8,128)S(1)}, f32[2,256,128]{2,1,0:T(8,128)}, u32[]{:S(2)}, u32[]{:S(2)}) collective-permute-start(f32[2,256,128]{2,1,0:T(8,128)S(1)} %broadcast_in_dim.28.refs_4_), channel_id=1, source_target_pairs={{0,1},{1,0},{2,3},{3,2},{4,5},{5,4},{6,7},{7,6},{8,9},{9,8},{10,11... | collective-permute-start | bytes 786440 | tf_op jit(solution)/shard_map/ppermute | solution.py:339
  20.6 21.7 %collective-permute-start.2 = (bf16[2,256,768]{2,1,0:T(8,128)(2,1)S(1)}, bf16[2,256,768]{2,1,0:T(8,128)(2,1)}, u32[]{:S(2)}, u32[]{:S(2)}) collective-permute-start(bf16[2,256,768]{2,1,0:T(8,128)(2,1)S(1)} %bitcast.37), channel_id=1, source_target_pairs={{0,1},{1,0},{2,3},{3,2},{4,5},{5,4},{6,7},{7,6},{8,9},{9,8},{10,11... | collective-permute-start | bytes 2359304 | tf_op jit(solution)/shard_map/ppermute | solution.py:339
  22.5 36.6 %collective-permute-start.3 = (bf16[2,256,768]{2,1,0:T(8,128)(2,1)S(1)}, bf16[2,256,768]{2,1,0:T(8,128)(2,1)}, u32[]{:S(2)}, u32[]{:S(2)}) collective-permute-start(bf16[2,256,768]{2,1,0:T(8,128)(2,1)S(1)} %bitcast.40), channel_id=1, source_target_pairs={{0,1},{1,0},{2,3},{3,2},{4,5},{5,4},{6,7},{7,6},{8,9},{9,8},{10,11... | collective-permute-start | bytes 2359304 | tf_op jit(solution)/shard_map/ppermute | solution.py:339
  25.9 50.0 %collective-permute-start.4 = (bf16[2,256,768]{2,1,0:T(8,128)(2,1)S(1)}, bf16[2,256,768]{2,1,0:T(8,128)(2,1)S(1)}, u32[]{:S(2)}, u32[]{:S(2)}) collective-permute-start(bf16[2,256,768]{2,1,0:T(8,128)(2,1)S(1)} %bitcast.43), channel_id=1, source_target_pairs={{0,1},{1,0},{2,3},{3,2},{4,5},{5,4},{6,7},{7,6},{8,9},{9,8},{10,11... | collective-permute-start | bytes 2359304 | tf_op jit(solution)/shard_map/ppermute | solution.py:339
  27.9 49.1 %collective-permute-start.1 = (bf16[512,1536]{1,0:T(8,128)(2,1)}, bf16[512,1536]{1,0:T(8,128)(2,1)}, u32[]{:S(2)}, u32[]{:S(2)}) collective-permute-start(bf16[512,1536]{1,0:T(8,128)(2,1)} %collective-permute-done.came), channel_id=1, source_target_pairs={{0,16},{16,0},{32,48},{48,32},{64,80},{80,64},{96,112},{112,96},{1... | collective-permute-start | bytes 4718600 | tf_op jit(solution)/shard_map/ppermute | solution.py:353
  85.1 9.2 %collective-permute-start.7 = (bf16[256,768]{1,0:T(8,128)(2,1)}, bf16[256,768]{1,0:T(8,128)(2,1)S(1)}, u32[]{:S(2)}, u32[]{:S(2)}) collective-permute-start(bf16[256,768]{1,0:T(8,128)(2,1)} %get-tuple-element.55), channel_id=1, source_target_pairs={{128,129},{129,128},{130,131},{131,130},{132,133},{133,132},{134,1... | collective-permute-start | bytes 1179656 | tf_op jit(solution)/shard_map/ppermute | solution.py:364
  85.8 11.1 %collective-permute-start.6 = (bf16[256,768]{1,0:T(8,128)(2,1)}, bf16[256,768]{1,0:T(8,128)(2,1)S(1)}, u32[]{:S(2)}, u32[]{:S(2)}) collective-permute-start(bf16[256,768]{1,0:T(8,128)(2,1)} %get-tuple-element.53), channel_id=1, source_target_pairs={{128,129},{129,128},{130,131},{131,130},{132,133},{133,132},{134,1... | collective-permute-start | bytes 1179656 | tf_op jit(solution)/shard_map/ppermute | solution.py:364
  94.2 2.6 %copy-start.13 = (f32[256,768]{1,0:T(8,128)S(1)}, f32[256,768]{1,0:T(8,128)}, u32[]{:S(2)}) copy-start(f32[256,768]{1,0:T(8,128)} %get-tuple-element.50) | copy-start | bytes 2359300
  95.6 14.9 %copy-start.7 = (bf16[256,768]{1,0:T(8,128)(2,1)}, bf16[256,768]{1,0:T(8,128)(2,1)S(1)}, u32[]{:S(2)}) copy-start(bf16[256,768]{1,0:T(8,128)(2,1)S(1)} %add_convert_fusion.2.refs_1_) | copy-start | bytes 1179652
  95.6 11.2 %collective-permute-start.9 = (bf16[256,768]{1,0:T(8,128)(2,1)S(1)}, bf16[256,768]{1,0:T(8,128)(2,1)S(1)}, u32[]{:S(2)}, u32[]{:S(2)}) collective-permute-start(bf16[256,768]{1,0:T(8,128)(2,1)S(1)} %add_convert_fusion.2.refs_1_), channel_id=1, source_target_pairs={{128,1},{129,0},{130,3},{131,2},{132,5},{133,4},{134,7},{135,6},{1... | collective-permute-start | bytes 1179656 | tf_op jit(solution)/shard_map/ppermute | solution.py:382
  97.0 19.4 %copy-start.6 = (bf16[256,768]{1,0:T(8,128)(2,1)}, bf16[256,768]{1,0:T(8,128)(2,1)S(1)}, u32[]{:S(2)}) copy-start(bf16[256,768]{1,0:T(8,128)(2,1)S(1)} %add_convert_fusion.1.refs_1_) | copy-start | bytes 1179652
  97.0 19.4 %collective-permute-start.8 = (bf16[256,768]{1,0:T(8,128)(2,1)S(1)}, bf16[256,768]{1,0:T(8,128)(2,1)S(1)}, u32[]{:S(2)}, u32[]{:S(2)}) collective-permute-start(bf16[256,768]{1,0:T(8,128)(2,1)S(1)} %add_convert_fusion.1.refs_1_), channel_id=1, source_target_pairs={{128,1},{129,0},{130,3},{131,2},{132,5},{133,4},{134,7},{135,6},{1... | collective-permute-start | bytes 1179656 | tf_op jit(solution)/shard_map/ppermute | solution.py:382
  106.8 3.7 %copy-start.18 = (bf16[256,768]{1,0:T(8,128)(2,1)}, bf16[256,768]{1,0:T(8,128)(2,1)S(1)}, u32[]{:S(2)}) copy-start(bf16[256,768]{1,0:T(8,128)(2,1)S(1)} %collective-permute-done.9.refs_0_) | copy-start | bytes 1179652
  106.8 19.5 %collective-permute-start.13 = (bf16[256,768]{1,0:T(8,128)(2,1)S(1)}, bf16[256,768]{1,0:T(8,128)(2,1)S(1)}, u32[]{:S(2)}, u32[]{:S(2)}) collective-permute-start(bf16[256,768]{1,0:T(8,128)(2,1)S(1)} %collective-permute-done.9.refs_0_), channel_id=1, source_target_pairs={{0,1},{1,0},{2,3},{3,2},{4,5},{5,4},{6,7},{7,6},{8,9},{9,8},{10,11... | collective-permute-start | bytes 1179656 | tf_op jit(solution)/shard_map/ppermute | solution.py:383
  116.3 2.7 %copy-start.19 = (bf16[256,768]{1,0:T(8,128)(2,1)}, bf16[256,768]{1,0:T(8,128)(2,1)S(1)}, u32[]{:S(2)}) copy-start(bf16[256,768]{1,0:T(8,128)(2,1)S(1)} %collective-permute-done.8.refs_0_) | copy-start | bytes 1179652
  116.3 9.2 %copy-start.3 = (bf16[256,768]{1,0:T(8,128)(2,1)S(1)}, bf16[256,768]{1,0:T(8,128)(2,1)}, u32[]{:S(2)}) copy-start(bf16[256,768]{1,0:T(8,128)(2,1)} %get-tuple-element.65.refs_2_.refs_6_) | copy-start | bytes 1179652
  116.4 16.3 %collective-permute-start.12 = (bf16[256,768]{1,0:T(8,128)(2,1)S(1)}, bf16[256,768]{1,0:T(8,128)(2,1)S(1)}, u32[]{:S(2)}, u32[]{:S(2)}) collective-permute-start(bf16[256,768]{1,0:T(8,128)(2,1)S(1)} %collective-permute-done.8.refs_0_), channel_id=1, source_target_pairs={{0,1},{1,0},{2,3},{3,2},{4,5},{5,4},{6,7},{7,6},{8,9},{9,8},{10,11... | collective-permute-start | bytes 1179656 | tf_op jit(solution)/shard_map/ppermute | solution.py:383
  124.9 7.9 %collective-permute-start.11 = (bf16[256,768]{1,0:T(8,128)(2,1)}, bf16[256,768]{1,0:T(8,128)(2,1)S(1)}, u32[]{:S(2)}, u32[]{:S(2)}) collective-permute-start(bf16[256,768]{1,0:T(8,128)(2,1)} %get-tuple-element.67.refs_7_.refs_0_), channel_id=1, source_target_pairs={{128,129},{129,128},{130,131},{131,130},{132,133},{133,132},{134,1... | collective-permute-start | bytes 1179656 | tf_op jit(solution)/shard_map/ppermute | solution.py:397
  125.6 7.2 %collective-permute-start.10 = (bf16[256,768]{1,0:T(8,128)(2,1)S(1)}, bf16[256,768]{1,0:T(8,128)(2,1)S(1)}, u32[]{:S(2)}, u32[]{:S(2)}) collective-permute-start(bf16[256,768]{1,0:T(8,128)(2,1)S(1)} %copy-done.3), channel_id=1, source_target_pairs={{128,129},{129,128},{130,131},{131,130},{132,133},{133,132},{134,1... | collective-permute-start | bytes 1179656 | tf_op jit(solution)/shard_map/ppermute | solution.py:397
  126.3 0.7 copy-start.16
  132.7 9.6 %copy-start.15 = (bf16[256,768]{1,0:T(8,128)(2,1)}, bf16[256,768]{1,0:T(8,128)(2,1)S(1)}, u32[]{:S(2)}) copy-start(bf16[256,768]{1,0:T(8,128)(2,1)S(1)} %collective-permute-done.12.refs_0_) | copy-start | bytes 1179652
  132.7 0.8 copy-start.8
  132.8 1.0 copy-start.9
  142.3 18.2 %collective-permute-start.14 = (bf16[4,768,384]{2,1,0:T(8,128)(2,1)}, bf16[4,768,384]{2,1,0:T(8,128)(2,1)S(1)}, u32[]{:S(2)}, u32[]{:S(2)}) collective-permute-start(bf16[4,768,384]{2,1,0:T(8,128)(2,1)} %shard_map.75), channel_id=1, source_target_pairs={{0,16},{16,0},{32,48},{48,32},{64,80},{80,64},{96,112},{112,96},{1... | collective-permute-start | bytes 7077896 | tf_op jit(solution)/shard_map/ppermute | solution.py:402
  160.3 17.8 %collective-permute-start.18 = (bf16[4,256,384]{2,1,0:T(8,128)(2,1)}, bf16[4,256,384]{2,1,0:T(8,128)(2,1)S(1)}, u32[]{:S(2)}, u32[]{:S(2)}) collective-permute-start(bf16[4,256,384]{2,1,0:T(8,128)(2,1)} %shard_map.77), channel_id=1, source_target_pairs={{0,16},{16,0},{32,48},{48,32},{64,80},{80,64},{96,112},{112,96},{1... | collective-permute-start | bytes 2359304 | tf_op jit(solution)/shard_map/ppermute | solution.py:402
  160.5 1.4 copy-start.5
  172.5 16.2 %collective-permute-start.15 = (bf16[768,384]{1,0:T(8,128)(2,1)}, bf16[768,384]{1,0:T(8,128)(2,1)S(1)}, u32[]{:S(2)}, u32[]{:S(2)}) collective-permute-start(bf16[768,384]{1,0:T(8,128)(2,1)} %get-tuple-element.79), channel_id=1, source_target_pairs={{0,64},{16,80},{32,96},{48,112},{64,0},{80,16},{96,32},{112,48},{1... | collective-permute-start | bytes 1769480 | tf_op jit(solution)/shard_map/ppermute | solution.py:408
  175.4 27.7 %collective-permute-start.16 = (bf16[768,384]{1,0:T(8,128)(2,1)}, bf16[768,384]{1,0:T(8,128)(2,1)}, u32[]{:S(2)}, u32[]{:S(2)}) collective-permute-start(bf16[768,384]{1,0:T(8,128)(2,1)} %get-tuple-element.80), channel_id=1, source_target_pairs={{0,32},{16,48},{32,64},{48,80},{64,96},{80,112},{96,0},{112,16},{1... | collective-permute-start | bytes 1769480 | tf_op jit(solution)/shard_map/ppermute | solution.py:408
  175.7 28.2 %copy-start.10 = (f32[768,384]{1,0:T(8,128)S(1)}, f32[768,384]{1,0:T(8,128)}, u32[]{:S(2)}) copy-start(f32[768,384]{1,0:T(8,128)} %get-tuple-element.78) | copy-start | bytes 3538948
  175.7 27.4 %collective-permute-start.17 = (bf16[768,384]{1,0:T(8,128)(2,1)}, bf16[768,384]{1,0:T(8,128)(2,1)S(1)}, u32[]{:S(2)}, u32[]{:S(2)}) collective-permute-start(bf16[768,384]{1,0:T(8,128)(2,1)} %get-tuple-element.81), channel_id=1, source_target_pairs={{0,96},{16,112},{32,0},{48,16},{64,32},{80,48},{96,64},{112,80},{1... | collective-permute-start | bytes 1769480 | tf_op jit(solution)/shard_map/ppermute | solution.py:408
  178.1 0.9 copy-start.12
  186.0 19.8 %collective-permute-start.19 = (bf16[256,384]{1,0:T(8,128)(2,1)}, bf16[256,384]{1,0:T(8,128)(2,1)S(1)}, u32[]{:S(2)}, u32[]{:S(2)}) collective-permute-start(bf16[256,384]{1,0:T(8,128)(2,1)} %get-tuple-element.86), channel_id=1, source_target_pairs={{0,64},{16,80},{32,96},{48,112},{64,0},{80,16},{96,32},{112,48},{1... | collective-permute-start | bytes 589832 | tf_op jit(solution)/shard_map/ppermute | solution.py:408
  186.1 24.5 %collective-permute-start.20 = (bf16[256,384]{1,0:T(8,128)(2,1)}, bf16[256,384]{1,0:T(8,128)(2,1)S(1)}, u32[]{:S(2)}, u32[]{:S(2)}) collective-permute-start(bf16[256,384]{1,0:T(8,128)(2,1)} %get-tuple-element.87), channel_id=1, source_target_pairs={{0,32},{16,48},{32,64},{48,80},{64,96},{80,112},{96,0},{112,16},{1... | collective-permute-start | bytes 589832 | tf_op jit(solution)/shard_map/ppermute | solution.py:408
  188.8 21.9 %collective-permute-start.21 = (bf16[256,384]{1,0:T(8,128)(2,1)}, bf16[256,384]{1,0:T(8,128)(2,1)S(1)}, u32[]{:S(2)}, u32[]{:S(2)}) collective-permute-start(bf16[256,384]{1,0:T(8,128)(2,1)} %get-tuple-element.88), channel_id=1, source_target_pairs={{0,96},{16,112},{32,0},{48,16},{64,32},{80,48},{96,64},{112,80},{1... | collective-permute-start | bytes 589832 | tf_op jit(solution)/shard_map/ppermute | solution.py:408
  203.1 0.8 copy-start.14
  204.0 6.7 %copy-start.17 = (f32[256,384]{1,0:T(8,128)S(1)}, f32[256,384]{1,0:T(8,128)}, u32[]{:S(2)}) copy-start(f32[256,384]{1,0:T(8,128)} %get-tuple-element.85) | copy-start | bytes 1179652
  205.6 10.0 %collective-permute-start.22 = (bf16[512,384]{1,0:T(8,128)(2,1)S(1)}, bf16[512,384]{1,0:T(8,128)(2,1)S(1)}, u32[]{:S(2)}, u32[]{:S(2)}) collective-permute-start(bf16[512,384]{1,0:T(8,128)(2,1)S(1)} %slice.17), channel_id=1, source_target_pairs={{0,1},{1,0},{2,3},{3,2},{4,5},{5,4},{6,7},{7,6},{8,9},{9,8},{10,11... | collective-permute-start | bytes 1179656 | tf_op jit(solution)/shard_map/ppermute | solution.py:414
Sparse Core Ops, SparseCore 0:
  9.1 63.2 all-gather.4
  74.2 58.2 all-gather.6

commit v8 on v7

--- a/solution.py
+++ b/solution.py
@@ -87,25 +87,31 @@
         acc[...] += part
 
 
-def far_kernel(core, came, twin, weight, low, high, acc, buffer, sems):
+def far_kernel(scalars, came, twin, weight, low, high, acc, buffer, sems):
     step = pl.program_id(0)
-    rows = jnp.where(core[0] == step // 2, came[...], twin[...])
-    added(step, acc, mm(rows, fetched(step, weight, buffer, sems), NN))
-
-    @pl.when(step == pl.num_programs(0) - 1)
-    def _():
-        rows = low.shape[0]
-        low[...] = acc[:rows].astype(BF16)
-        high[...] = acc[rows:].astype(BF16)
-
-
-def near_kernel(half, first, second, weight, low, high, buffer, sems):
+
+    @pl.when(scalars[1] > 0)
+    def _():
+        rows = jnp.where(scalars[0] == step // 2, came[...], twin[...])
+        added(step, acc, mm(rows, fetched(step, weight, buffer, sems), NN))
+
+        @pl.when(step == pl.num_programs(0) - 1)
+        def _():
+            count = low.shape[0]
+            low[...] = acc[:count].astype(BF16)
+            high[...] = acc[count:].astype(BF16)
+
+
+def near_kernel(scalars, first, second, weight, low, high, buffer, sems):
     step = pl.program_id(0)
-    rows = jnp.concatenate([first[...], second[...]], axis=1)
-    part = mm(rows, fetched(step, weight, buffer, sems), NN)
-    count = low.shape[0]
-    added(step, low, part[:count])
-    added(step, high, part[count:])
+
+    @pl.when(scalars[1] > 0)
+    def _():
+        rows = jnp.concatenate([first[...], second[...]], axis=1)
+        part = mm(rows, fetched(step, weight, buffer, sems), NN)
+        count = low.shape[0]
+        added(step, low, part[:count])
+        added(step, high, part[count:])
 
 
 def partial_products(scalars, operands, specs, weight, out_dtype, kernel):
@@ -340,6 +346,7 @@
     near = [jnp.where(decoder, mine, other) for mine, other in zip(own, came_near)]
     near_flags = jnp.stack([dec, 1 - dec])
     own_flags = jnp.stack([0 * dec, 1 - dec])
+    far_scalars, near_scalars = jnp.stack([core, dec]), jnp.stack([half, dec])
     places = 2 * ((chip + jnp.array(STEPS, jnp.int32)) % 4)
     keep_at, give_at = places + core, places + 1 - core
 
@@ -353,17 +360,19 @@
     twin = lax.ppermute(came, "segment", CORE_SWAP)
 
     ready = (came, twin, near, own[3], near_flags, own_flags, keep_at, give_at)
+    ready = (*ready, far_scalars, near_scalars)
     first, ready = lax.optimization_barrier((first, ready))
-    came, twin, near, own_mask, near_flags, own_flags, keep_at, give_at = ready
+    came, twin, near, own_mask, near_flags, own_flags, keep_at, give_at, *scalars = ready
+    far_scalars, near_scalars = scalars
     own = (*own[:3], own_mask)
 
     piece = 2 * shard_rows
     moved = pl.BlockSpec((row_count, piece), lambda j, at: (0, j % 2))
     far = []
-    for partial in partial_products(core[None], (came, twin), [moved] * 2, first, BF16, far_kernel):
+    for partial in partial_products(far_scalars, (came, twin), [moved] * 2, first, BF16, far_kernel):
         far.append(lax.ppermute(partial, BOTH, DEC_SWAP))
     own_partial = partial_products(
-        half[None],
+        near_scalars,
         (grads, grads),
         [
             pl.BlockSpec((row_count, shard_rows), lambda j, half: (0, 4 * j + half[0])),
@@ -397,6 +406,8 @@
         far_dq.append(lax.ppermute(dv[micro], BOTH, DEC_SWAP))
     own_dk, own_dv = attended(own_flags, ctx_own, (), own)
 
+    second, own_dk, own_dv = lax.optimization_barrier((second, own_dk, own_dv))
+
     def chip_sums(grads):
         give = projected(give_at, dec[None], grads, first, second)
         other = lax.ppermute(give, "segment", CORE_SWAP)
@@ -409,11 +420,10 @@
             result = result + other.astype(F32)
         return result.astype(BF16)
 
-    *blocks, block = chip_sums((*far_dq, dv[0], *dk, own_dk[0], *dv, own_dv[0]))
-    early = reduced(blocks, block)
-    from_partner = lax.ppermute(early[:row_count], "fsdp", HALF_SWAP)
-    *blocks, block = chip_sums((dv[1], own_dk[1], own_dv[1]))
-    own_out = jnp.concatenate([early[row_count:], reduced(blocks, block)])
+    *blocks, block = chip_sums((*far_dq, *dk, *dv))
+    from_partner = lax.ppermute(reduced(blocks, block), "fsdp", HALF_SWAP)
+    *blocks, block = chip_sums((*dv, *own_dk, *own_dv))
+    own_out = reduced(blocks, block)
     result = jnp.where(
         half == 0,
         jnp.concatenate([own_out, from_partner], axis=1),

time: 225 us -> 221 us (0.982)
  waiting for transfers between devices: 68.6 us -> 76.2 us
  Pallas kernels: 75.6 us -> 69.2 us
  starting transfers between devices: 44.1 us -> 38.3 us
    ppermute x2, waiting for transfers between devices: 8.51 us -> 22.8 us  [per_device(): ctx_near.append(lax.ppermute(ctx[micro], BOTH, DEC_TO_ENC))]
    pallas_call x2, Pallas kernels: 15.9 us -> 9.53 us  [partial_products(): pl.pallas_call(kernel, grid_spec=pltpu.PrefetchScalarGridSpec(num_scalar_...]
    ppermute x1, waiting for transfers between devices: 4.75 us -> 0.01 us  [per_device(): from_partner = lax.ppermute(reduced(blocks, block), 'fsdp', HALF_SWAP)]
    ppermute x2, starting transfers between devices: 6.59 us -> 2.49 us  [chip_sums(): other = lax.ppermute(give, 'segment', CORE_SWAP)]
    ppermute x2, starting transfers between devices: 6.32 us -> 3.82 us  [per_device(): ctx_own.append(lax.ppermute(ctx_near[micro], BOTH, ENC_SWAP))]
    unnamed x45 -> x43, local copies, waits for them, and re-layouts: 4.87 us -> 4.74 us
  transfers between devices with their start and end apart: 25 -> 25, of which waited for: 8 -> 8; matrix products, arithmetic and copies ran while one was open for 6% -> 7% of each run, Pallas kernels for 30% -> 28%
where the time goes in v8:
time: 221 us; the launch traced here: 220 us
  waiting for transfers between devices  76.2 us (34%)
  Pallas kernels  69.2 us (31%)
  starting transfers between devices  38.3 us (17%)
  other arithmetic  14.4 us (7%)
  between operations  13.9 us (6%)
  local copies, waits for them, and re-layouts  7.65 us (3%)
    ppermute x4, waiting for transfers between devices, per_device(): came_near.append(lax.ppermute(value, BOTH, ENC_SWAP))  35.9 us
    pallas_call x4, Pallas kernels, projected(): pl.pallas_call(functools.partial(kernel, count), grid_spec=pltpu.Prefetch...  32 us
    pallas_call x4, Pallas kernels, attend(): pl.pallas_call(functools.partial(attend_kernel, heads), grid_spec=pltpu.P...  23.1 us
    ppermute x2, waiting for transfers between devices, per_device(): ctx_near.append(lax.ppermute(ctx[micro], BOTH, DEC_TO_ENC))  22.8 us
    ppermute x6, waiting for transfers between devices, reduced(): other = lax.ppermute(block, 'segment', pairs)  17.4 us
    ppermute x4, starting transfers between devices, per_device(): came_near.append(lax.ppermute(value, BOTH, ENC_SWAP))  11.2 us
    pallas_call x2, Pallas kernels, partial_products(): pl.pallas_call(kernel, grid_spec=pltpu.PrefetchScalarGridSpec(num_scalar_...  9.53 us
    ppermute x6, starting transfers between devices, reduced(): other = lax.ppermute(block, 'segment', pairs)  8.31 us
  transfers between devices with their start and end apart: 25, of which 8 were waited for; matrix products, arithmetic and copies ran while one was open for 7% of the time, Pallas kernels for 28%

profile of v8, /device:TPU:1, one launch (start us, length us, event | category | flops | bytes accessed | tf_op | source)
XLA Modules:
  0.0 219.7 jit_solution(3491523551427545385)
XLA Ops:
  6.5 1.9 slice.6
  9.1 4.5 %pick.1 = bf16[512,1536]{1,0:T(8,128)(2,1)} custom-call(s32[4]{0:T(128)} %add_subtract_fusion.1.where, bf16[512,6144]{1,0:T(8,128)(2,1)} %bitcast.32), custom_call_target="tpu_custom_call" | custom-call | bytes 3145728 | tf_op jit(solution)/shard_map/pick/pallas_call | solution.py:44
  13.6 0.9 slice.7
  14.5 1.9 collective-permute-start
  16.6 4.0 %collective-permute-start.5 = (f32[2,256,128]{2,1,0:T(8,128)S(1)}, f32[2,256,128]{2,1,0:T(8,128)}, u32[]{:S(2)}, u32[]{:S(2)}) collective-permute-start(f32[2,256,128]{2,1,0:T(8,128)S(1)} %broadcast_in_dim.22.refs_4_), channel_id=1, source_target_pairs={{0,1},{1,0},{2,3},{3,2},{4,5},{5,4},{6,7},{7,6},{8,9},{9,8},{10,11... | collective-permute-start | bytes 786440 | tf_op jit(solution)/shard_map/ppermute | solution.py:345
  20.6 1.9 collective-permute-start.4
  22.6 3.4 %collective-permute-start.3 = (bf16[2,256,768]{2,1,0:T(8,128)(2,1)S(1)}, bf16[2,256,768]{2,1,0:T(8,128)(2,1)}, u32[]{:S(2)}, u32[]{:S(2)}) collective-permute-start(bf16[2,256,768]{2,1,0:T(8,128)(2,1)S(1)} %bitcast.40), channel_id=1, source_target_pairs={{0,1},{1,0},{2,3},{3,2},{4,5},{5,4},{6,7},{7,6},{8,9},{9,8},{10,11... | collective-permute-start | bytes 2359304 | tf_op jit(solution)/shard_map/ppermute | solution.py:345
  25.9 1.9 collective-permute-start.2
  27.9 3.7 %collective-permute-start.1 = (bf16[512,1536]{1,0:T(8,128)(2,1)}, bf16[512,1536]{1,0:T(8,128)(2,1)}, u32[]{:S(2)}, u32[]{:S(2)}) collective-permute-start(bf16[512,1536]{1,0:T(8,128)(2,1)} %collective-permute-done.came), channel_id=1, source_target_pairs={{0,16},{16,0},{32,48},{48,32},{64,80},{80,64},{96,112},{112,96},{1... | collective-permute-start | bytes 4718600 | tf_op jit(solution)/shard_map/ppermute | solution.py:360
  34.1 1.8 broadcast_select_fusion.3.refs_5_
  35.9 6.4 %collective-permute-done.4 = bf16[2,256,768]{2,1,0:T(8,128)(2,1)} collective-permute-done((bf16[2,256,768]{2,1,0:T(8,128)(2,1)S(1)}, bf16[2,256,768]{2,1,0:T(8,128)(2,1)}, u32[]{:S(2)}, u32[]{:S(2)}) %collective-permute-start.4) | collective-permute-done | bytes 786464 | tf_op jit(solution)/shard_map/ppermute | solution.py:345
  42.3 2.1 broadcast_select_fusion.refs_4_
  44.4 14.7 %collective-permute-done.3 = bf16[2,256,768]{2,1,0:T(8,128)(2,1)} collective-permute-done((bf16[2,256,768]{2,1,0:T(8,128)(2,1)S(1)}, bf16[2,256,768]{2,1,0:T(8,128)(2,1)}, u32[]{:S(2)}, u32[]{:S(2)}) %collective-permute-start.3) | collective-permute-done | bytes 786464 | tf_op jit(solution)/shard_map/ppermute | solution.py:345
  59.1 2.1 broadcast_select_fusion.1.refs_3_
  61.2 14.8 %collective-permute-done.2 = bf16[2,256,768]{2,1,0:T(8,128)(2,1)S(1)} collective-permute-done((bf16[2,256,768]{2,1,0:T(8,128)(2,1)S(1)}, bf16[2,256,768]{2,1,0:T(8,128)(2,1)S(1)}, u32[]{:S(2)}, u32[]{:S(2)}) %collective-permute-start.2) | collective-permute-done | bytes 786464 | tf_op jit(solution)/shard_map/ppermute | solution.py:345
  76.0 1.0 broadcast_select_fusion.2.refs_2_
  77.0 5.0 %shard_map.74 = (bf16[256,768]{1,0:T(8,128)(2,1)}, bf16[256,768]{1,0:T(8,128)(2,1)}) custom-call(s32[2]{0:T(128)} %get-tuple-element.59.scalars, bf16[512,1536]{1,0:T(8,128)(2,1)} %collective-permute-done.came, bf16[512,1536]{1,0:T(8,128)(2,1)} %collective-permute-done.1.twin, bf16[8,384,768]{2,1,0:T(8,128)(2,1)} %bitcast.22), custom_call_target="tpu_custom_call" | custom-call | flops 2415919104 | bytes 4718592 | tf_op jit(solution)/shard_map/pallas_call | solution.py:121
  83.3 4.6 %shard_map.73 = (f32[256,768]{1,0:T(8,128)}, f32[256,768]{1,0:T(8,128)}) custom-call(s32[2]{0:T(128)} %get-tuple-element.56.scalars, bf16[512,6144]{1,0:T(8,128)(2,1)} %bitcast.33, bf16[512,6144]{1,0:T(8,128)(2,1)} %bitcast.34, bf16[8,384,768]{2,1,0:T(8,128)(2,1)} %bitcast.23), custom_call_target="tpu_custom_call" | custom-call | flops 2415919104 | bytes 4718592 | tf_op jit(solution)/shard_map/pallas_call | solution.py:121
  87.9 1.3 add_convert_fusion.3.refs_1_
  89.2 1.3 collective-permute-start.9
  90.6 1.3 collective-permute-start.8
  91.9 16.3 %collective-permute-done.9.refs_0_ = bf16[256,768]{1,0:T(8,128)(2,1)S(1)} collective-permute-done((bf16[256,768]{1,0:T(8,128)(2,1)S(1)}, bf16[256,768]{1,0:T(8,128)(2,1)S(1)}, u32[]{:S(2)}, u32[]{:S(2)}) %collective-permute-start.9) | collective-permute-done | bytes 393248 | tf_op jit(solution)/shard_map/ppermute | solution.py:391
  108.3 1.9 collective-permute-start.11
  110.2 6.5 %collective-permute-done.8.refs_0_ = bf16[256,768]{1,0:T(8,128)(2,1)S(1)} collective-permute-done((bf16[256,768]{1,0:T(8,128)(2,1)S(1)}, bf16[256,768]{1,0:T(8,128)(2,1)S(1)}, u32[]{:S(2)}, u32[]{:S(2)}) %collective-permute-start.8) | collective-permute-done | bytes 393248 | tf_op jit(solution)/shard_map/ppermute | solution.py:391
  116.7 1.9 collective-permute-start.10
  118.6 5.8 %attend.4 = (bf16[256,768]{1,0:T(8,128)(2,1)}, bf16[256,768]{1,0:T(8,128)(2,1)}) custom-call(s32[2]{0:T(128)} %get-tuple-element.66.flags, bf16[256,768]{1,0:T(8,128)(2,1)} %copy-done.17, bf16[256,768]{1,0:T(8,128)(2,1)} %copy-done.5, bf16[2,256,768]{2,1,0:T(8,128)(2,1)} %broadcast_select_fusion.2.refs_2_, ...), custom_call_target="tpu_custom_call" | custom-call | flops 503316480 | bytes 3145728 | tf_op jit(solution)/shard_map/attend/pallas_call | solution.py:177
  124.5 5.9 %attend.5 = (bf16[256,768]{1,0:T(8,128)(2,1)}, bf16[256,768]{1,0:T(8,128)(2,1)}) custom-call(s32[2]{0:T(128)} %get-tuple-element.66.flags, bf16[256,768]{1,0:T(8,128)(2,1)} %copy-done.18, bf16[256,768]{1,0:T(8,128)(2,1)} %copy-done.6, bf16[2,256,768]{2,1,0:T(8,128)(2,1)} %broadcast_select_fusion.2.refs_2_, ...), custom_call_target="tpu_custom_call" | custom-call | flops 503316480 | bytes 3145728 | tf_op jit(solution)/shard_map/attend/pallas_call | solution.py:177
  131.8 0.7 copy-done.16
  132.6 5.7 %attend.6 = (bf16[256,768]{1,0:T(8,128)(2,1)}, bf16[256,768]{1,0:T(8,128)(2,1)}) custom-call(s32[2]{0:T(128)} %get-tuple-element.78.flags, bf16[256,768]{1,0:T(8,128)(2,1)} %copy-done.16, bf16[2,256,768]{2,1,0:T(8,128)(2,1)} %bitcast.35, bf16[2,256,768]{2,1,0:T(8,128)(2,1)} %bitcast.38, bf16[2,256,768]{2,1,0:T(8,128)(2,1)} %bitcast.41, f32[2,256,128]{2,1,0:T(8,128)} %copy-done.4), custom_call_target="tpu_custom_call" | custom-call | flops 503316480 | bytes 3145728 | tf_op jit(solution)/shard_map/attend/pallas_call | solution.py:177
  138.2 0.7 copy-done.15
  139.0 5.7 %attend.7 = (bf16[256,768]{1,0:T(8,128)(2,1)}, bf16[256,768]{1,0:T(8,128)(2,1)}) custom-call(s32[2]{0:T(128)} %get-tuple-element.78.flags, bf16[256,768]{1,0:T(8,128)(2,1)} %copy-done.15, bf16[2,256,768]{2,1,0:T(8,128)(2,1)} %bitcast.36, bf16[2,256,768]{2,1,0:T(8,128)(2,1)} %bitcast.39, bf16[2,256,768]{2,1,0:T(8,128)(2,1)} %bitcast.42, f32[2,256,128]{2,1,0:T(8,128)} %copy-done.4), custom_call_target="tpu_custom_call" | custom-call | flops 503316480 | bytes 3145728 | tf_op jit(solution)/shard_map/attend/pallas_call | solution.py:177
  145.5 7.2 %shard_map.77 = bf16[4,512,384]{2,1,0:T(8,128)(2,1)} custom-call(s32[4]{0:T(128)} %get-tuple-element.92.at, s32[1]{0:T(128)} %bitcast.5.flags, bf16[256,768]{1,0:T(8,128)(2,1)} %copy-done.10, bf16[256,768]{1,0:T(8,128)(2,1)} %copy-done.9, bf16[256,768]{1,0:T(8,128)(2,1)} %get-tuple-element.97.refs_2_, bf16[256,768]{1,0:T(8,128)(2,1)} %get-tuple-element.98.refs_3_, ...), custom_call_target="tpu_custom_call" | custom-call | flops 2415919104 | bytes 4718592 | tf_op jit(solution)/shard_map/pallas_call | solution.py:295
  152.8 2.4 %collective-permute-start.18 = (bf16[4,512,384]{2,1,0:T(8,128)(2,1)}, bf16[4,512,384]{2,1,0:T(8,128)(2,1)S(1)}, u32[]{:S(2)}, u32[]{:S(2)}) collective-permute-start(bf16[4,512,384]{2,1,0:T(8,128)(2,1)} %shard_map.77), channel_id=1, source_target_pairs={{0,16},{16,0},{32,48},{48,32},{64,80},{80,64},{96,112},{112,96},{1... | collective-permute-start | bytes 4718600 | tf_op jit(solution)/shard_map/ppermute | solution.py:413
  155.1 7.2 %shard_map.75 = bf16[4,512,384]{2,1,0:T(8,128)(2,1)} custom-call(s32[4]{0:T(128)} %get-tuple-element.92.at, s32[1]{0:T(128)} %bitcast.5.flags, bf16[256,768]{1,0:T(8,128)(2,1)} %get-tuple-element.74.refs_0_.refs_4_, bf16[256,768]{1,0:T(8,128)(2,1)} %get-tuple-element.76.refs_1_.refs_5_, bf16[256,768]{1,0:T(8,128)(2,1)} %get-tuple-element.87.refs_2_, ...), custom_call_target="tpu_custom_call" | custom-call | flops 2415919104 | bytes 4718592 | tf_op jit(solution)/shard_map/pallas_call | solution.py:295
  162.4 1.2 copy-done.8
  163.6 8.8 %shard_map.78 = (bf16[512,384]{1,0:T(8,128)(2,1)}, bf16[512,384]{1,0:T(8,128)(2,1)}, bf16[512,384]{1,0:T(8,128)(2,1)}, f32[512,384]{1,0:T(8,128)}) custom-call(s32[4]{0:T(128)} %broadcast_add_fusion.at, s32[1]{0:T(128)} %bitcast.5.flags, bf16[256,768]{1,0:T(8,128)(2,1)} %copy-done.10, bf16[256,768]{1,0:T(8,128)(2,1)} %copy-done.9, ...), custom_call_target="tpu_custom_call" | custom-call | flops 2415919104 | bytes 4718592 | tf_op jit(solution)/shard_map/pallas_call | solution.py:295
  172.5 2.8 %collective-permute-start.19 = (bf16[512,384]{1,0:T(8,128)(2,1)}, bf16[512,384]{1,0:T(8,128)(2,1)S(1)}, u32[]{:S(2)}, u32[]{:S(2)}) collective-permute-start(bf16[512,384]{1,0:T(8,128)(2,1)} %get-tuple-element.100), channel_id=1, source_target_pairs={{0,64},{16,80},{32,96},{48,112},{64,0},{80,16},{96,32},{112,48},{1... | collective-permute-start | bytes 1179656 | tf_op jit(solution)/shard_map/ppermute | solution.py:419
  175.5 2.4 %collective-permute-start.21 = (bf16[512,384]{1,0:T(8,128)(2,1)}, bf16[512,384]{1,0:T(8,128)(2,1)S(1)}, u32[]{:S(2)}, u32[]{:S(2)}) collective-permute-start(bf16[512,384]{1,0:T(8,128)(2,1)} %get-tuple-element.102), channel_id=1, source_target_pairs={{0,96},{16,112},{32,0},{48,16},{64,32},{80,48},{96,64},{112,80},{1... | collective-permute-start | bytes 1179656 | tf_op jit(solution)/shard_map/ppermute | solution.py:419
  177.9 1.1 copy-done.7
  179.1 8.8 %shard_map.76 = (bf16[512,384]{1,0:T(8,128)(2,1)}, bf16[512,384]{1,0:T(8,128)(2,1)}, bf16[512,384]{1,0:T(8,128)(2,1)}, f32[512,384]{1,0:T(8,128)}) custom-call(s32[4]{0:T(128)} %broadcast_add_fusion.at, s32[1]{0:T(128)} %bitcast.5.flags, bf16[256,768]{1,0:T(8,128)(2,1)} %get-tuple-element.74.refs_0_.refs_4_, ...), custom_call_target="tpu_custom_call" | custom-call | flops 2415919104 | bytes 4718592 | tf_op jit(solution)/shard_map/pallas_call | solution.py:295
  188.6 2.2 collective-permute-start.15
  190.8 3.8 %collective-permute-done.20 = bf16[512,384]{1,0:T(8,128)(2,1)S(1)} collective-permute-done((bf16[512,384]{1,0:T(8,128)(2,1)}, bf16[512,384]{1,0:T(8,128)(2,1)S(1)}, u32[]{:S(2)}, u32[]{:S(2)}) %collective-permute-start.20) | collective-permute-done | bytes 393248 | tf_op jit(solution)/shard_map/ppermute | solution.py:419
  194.5 0.9 add_convert_fusion
  195.5 1.5 collective-permute-start.22
  197.0 4.4 %collective-permute-done.13 = bf16[512,384]{1,0:T(8,128)(2,1)S(1)} collective-permute-done((bf16[512,384]{1,0:T(8,128)(2,1)}, bf16[512,384]{1,0:T(8,128)(2,1)S(1)}, u32[]{:S(2)}, u32[]{:S(2)}) %collective-permute-start.13) | collective-permute-done | bytes 393248 | tf_op jit(solution)/shard_map/ppermute | solution.py:419
  201.4 9.2 %collective-permute-done.14 = bf16[512,384]{1,0:T(8,128)(2,1)S(1)} collective-permute-done((bf16[512,384]{1,0:T(8,128)(2,1)}, bf16[512,384]{1,0:T(8,128)(2,1)S(1)}, u32[]{:S(2)}, u32[]{:S(2)}) %collective-permute-start.14) | collective-permute-done | bytes 393248 | tf_op jit(solution)/shard_map/ppermute | solution.py:419
  210.6 1.2 add_convert_fusion.1
  211.8 1.1 maximum_select_fusion
  (76 shorter events, 8.0 us)
Async XLA Ops:
  6.5 70.4 %all-gather.5.cloned.1.call-start = ((), (), s32[]{:S(2)}) async-start(), calls=%async_computation | async-start | bytes 5308416 | tf_op jit(solution)/shard_map/all_gather | solution.py:332
  8.5 136.2 %all-gather.7.cloned.1.call-start = ((), (), s32[]{:S(2)}) async-start(), calls=%async_computation.1 | async-start | bytes 5308416 | tf_op jit(solution)/shard_map/all_gather | solution.py:332
  9.1 4.5 %copy-start.11 = (bf16[1,2,384,768]{3,2,1,0:T(8,128)(2,1)S(1)}, bf16[1,2,384,768]{3,2,1,0:T(8,128)(2,1)}, u32[]{:S(2)}) copy-start(bf16[1,2,384,768]{3,2,1,0:T(8,128)(2,1)} %param.12) | copy-start | bytes 3538948
  9.1 11.5 %copy-start.2 = (bf16[2,1,256,768]{3,2,1,0:T(8,128)(2,1)S(1)}, bf16[2,1,256,768]{3,2,1,0:T(8,128)(2,1)}, u32[]{:S(2)}) copy-start(bf16[2,1,256,768]{3,2,1,0:T(8,128)(2,1)} %param.10) | copy-start | bytes 2359300
  13.6 2.8 %copy-start.19 = (s32[2,1,256]{2,1,0:T(1,128)S(1)}, s32[2,1,256]{2,1,0:T(1,128)}, u32[]{:S(2)}) copy-start(s32[2,1,256]{2,1,0:T(1,128)} %param.11) | copy-start | bytes 6148
  13.6 8.9 %copy-start.1 = (bf16[2,1,256,768]{3,2,1,0:T(8,128)(2,1)S(1)}, bf16[2,1,256,768]{3,2,1,0:T(8,128)(2,1)}, u32[]{:S(2)}) copy-start(bf16[2,1,256,768]{3,2,1,0:T(8,128)(2,1)} %param.9) | copy-start | bytes 2359300
  13.6 12.3 %copy-start = (bf16[2,1,256,768]{3,2,1,0:T(8,128)(2,1)S(1)}, bf16[2,1,256,768]{3,2,1,0:T(8,128)(2,1)}, u32[]{:S(2)}) copy-start(bf16[2,1,256,768]{3,2,1,0:T(8,128)(2,1)} %param.8) | copy-start | bytes 2359300
  13.6 18.0 %copy-start.20 = (s32[4]{0:T(128)S(1)}, s32[4]{0:T(128)}, u32[]{:S(2)}) copy-start(s32[4]{0:T(128)} %constant.69.clone) | copy-start | bytes 52
  14.5 13.3 %collective-permute-start = (bf16[512,1536]{1,0:T(8,128)(2,1)}, bf16[512,1536]{1,0:T(8,128)(2,1)}, u32[]{:S(2)}, u32[]{:S(2)}) collective-permute-start(bf16[512,1536]{1,0:T(8,128)(2,1)} %pick.1), channel_id=1, source_target_pairs={{128,129},{129,128},{130,131},{131,130},{132,133},{133,132},{134,1... | collective-permute-start | bytes 4718600 | tf_op jit(solution)/shard_map/ppermute | solution.py:359
  16.6 44.7 %copy-start.4 = (f32[2,256,128]{2,1,0:T(8,128)}, f32[2,256,128]{2,1,0:T(8,128)S(1)}, u32[]{:S(2)}) copy-start(f32[2,256,128]{2,1,0:T(8,128)S(1)} %broadcast_in_dim.22.refs_4_) | copy-start | bytes 786436
  16.6 17.5 %collective-permute-start.5 = (f32[2,256,128]{2,1,0:T(8,128)S(1)}, f32[2,256,128]{2,1,0:T(8,128)}, u32[]{:S(2)}, u32[]{:S(2)}) collective-permute-start(f32[2,256,128]{2,1,0:T(8,128)S(1)} %broadcast_in_dim.22.refs_4_), channel_id=1, source_target_pairs={{0,1},{1,0},{2,3},{3,2},{4,5},{5,4},{6,7},{7,6},{8,9},{9,8},{10,11... | collective-permute-start | bytes 786440 | tf_op jit(solution)/shard_map/ppermute | solution.py:345
  20.6 21.7 %collective-permute-start.4 = (bf16[2,256,768]{2,1,0:T(8,128)(2,1)S(1)}, bf16[2,256,768]{2,1,0:T(8,128)(2,1)}, u32[]{:S(2)}, u32[]{:S(2)}) collective-permute-start(bf16[2,256,768]{2,1,0:T(8,128)(2,1)S(1)} %bitcast.43), channel_id=1, source_target_pairs={{0,1},{1,0},{2,3},{3,2},{4,5},{5,4},{6,7},{7,6},{8,9},{9,8},{10,11... | collective-permute-start | bytes 2359304 | tf_op jit(solution)/shard_map/ppermute | solution.py:345
  22.6 36.6 %collective-permute-start.3 = (bf16[2,256,768]{2,1,0:T(8,128)(2,1)S(1)}, bf16[2,256,768]{2,1,0:T(8,128)(2,1)}, u32[]{:S(2)}, u32[]{:S(2)}) collective-permute-start(bf16[2,256,768]{2,1,0:T(8,128)(2,1)S(1)} %bitcast.40), channel_id=1, source_target_pairs={{0,1},{1,0},{2,3},{3,2},{4,5},{5,4},{6,7},{7,6},{8,9},{9,8},{10,11... | collective-permute-start | bytes 2359304 | tf_op jit(solution)/shard_map/ppermute | solution.py:345
  25.9 50.0 %collective-permute-start.2 = (bf16[2,256,768]{2,1,0:T(8,128)(2,1)S(1)}, bf16[2,256,768]{2,1,0:T(8,128)(2,1)S(1)}, u32[]{:S(2)}, u32[]{:S(2)}) collective-permute-start(bf16[2,256,768]{2,1,0:T(8,128)(2,1)S(1)} %bitcast.37), channel_id=1, source_target_pairs={{0,1},{1,0},{2,3},{3,2},{4,5},{5,4},{6,7},{7,6},{8,9},{9,8},{10,11... | collective-permute-start | bytes 2359304 | tf_op jit(solution)/shard_map/ppermute | solution.py:345
  27.9 49.1 %collective-permute-start.1 = (bf16[512,1536]{1,0:T(8,128)(2,1)}, bf16[512,1536]{1,0:T(8,128)(2,1)}, u32[]{:S(2)}, u32[]{:S(2)}) collective-permute-start(bf16[512,1536]{1,0:T(8,128)(2,1)} %collective-permute-done.came), channel_id=1, source_target_pairs={{0,16},{16,0},{32,48},{48,32},{64,80},{80,64},{96,112},{112,96},{1... | collective-permute-start | bytes 4718600 | tf_op jit(solution)/shard_map/ppermute | solution.py:360
  81.9 6.0 %collective-permute-start.7 = (bf16[256,768]{1,0:T(8,128)(2,1)}, bf16[256,768]{1,0:T(8,128)(2,1)S(1)}, u32[]{:S(2)}, u32[]{:S(2)}) collective-permute-start(bf16[256,768]{1,0:T(8,128)(2,1)} %get-tuple-element.64), channel_id=1, source_target_pairs={{128,129},{129,128},{130,131},{131,130},{132,133},{133,132},{134,1... | collective-permute-start | bytes 1179656 | tf_op jit(solution)/shard_map/ppermute | solution.py:373
  82.6 7.9 %collective-permute-start.6 = (bf16[256,768]{1,0:T(8,128)(2,1)}, bf16[256,768]{1,0:T(8,128)(2,1)S(1)}, u32[]{:S(2)}, u32[]{:S(2)}) collective-permute-start(bf16[256,768]{1,0:T(8,128)(2,1)} %get-tuple-element.62), channel_id=1, source_target_pairs={{128,129},{129,128},{130,131},{131,130},{132,133},{133,132},{134,1... | collective-permute-start | bytes 1179656 | tf_op jit(solution)/shard_map/ppermute | solution.py:373
  87.9 2.6 %copy-start.12 = (f32[256,768]{1,0:T(8,128)S(1)}, f32[256,768]{1,0:T(8,128)}, u32[]{:S(2)}) copy-start(f32[256,768]{1,0:T(8,128)} %get-tuple-element.58) | copy-start | bytes 2359300
  89.2 29.4 %copy-start.5 = (bf16[256,768]{1,0:T(8,128)(2,1)}, bf16[256,768]{1,0:T(8,128)(2,1)S(1)}, u32[]{:S(2)}) copy-start(bf16[256,768]{1,0:T(8,128)(2,1)S(1)} %add_convert_fusion.3.refs_1_) | copy-start | bytes 1179652
  89.2 19.1 %collective-permute-start.9 = (bf16[256,768]{1,0:T(8,128)(2,1)S(1)}, bf16[256,768]{1,0:T(8,128)(2,1)S(1)}, u32[]{:S(2)}, u32[]{:S(2)}) collective-permute-start(bf16[256,768]{1,0:T(8,128)(2,1)S(1)} %add_convert_fusion.3.refs_1_), channel_id=1, source_target_pairs={{128,1},{129,0},{130,3},{131,2},{132,5},{133,4},{134,7},{135,6},{1... | collective-permute-start | bytes 1179656 | tf_op jit(solution)/shard_map/ppermute | solution.py:391
  90.6 33.9 %copy-start.6 = (bf16[256,768]{1,0:T(8,128)(2,1)}, bf16[256,768]{1,0:T(8,128)(2,1)S(1)}, u32[]{:S(2)}) copy-start(bf16[256,768]{1,0:T(8,128)(2,1)S(1)} %add_convert_fusion.2.refs_1_) | copy-start | bytes 1179652
  90.6 26.1 %collective-permute-start.8 = (bf16[256,768]{1,0:T(8,128)(2,1)S(1)}, bf16[256,768]{1,0:T(8,128)(2,1)S(1)}, u32[]{:S(2)}, u32[]{:S(2)}) collective-permute-start(bf16[256,768]{1,0:T(8,128)(2,1)S(1)} %add_convert_fusion.2.refs_1_), channel_id=1, source_target_pairs={{128,1},{129,0},{130,3},{131,2},{132,5},{133,4},{134,7},{135,6},{1... | collective-permute-start | bytes 1179656 | tf_op jit(solution)/shard_map/ppermute | solution.py:391
  108.3 10.4 %copy-start.17 = (bf16[256,768]{1,0:T(8,128)(2,1)}, bf16[256,768]{1,0:T(8,128)(2,1)S(1)}, u32[]{:S(2)}) copy-start(bf16[256,768]{1,0:T(8,128)(2,1)S(1)} %collective-permute-done.9.refs_0_) | copy-start | bytes 1179652
  108.3 23.5 %collective-permute-start.11 = (bf16[256,768]{1,0:T(8,128)(2,1)S(1)}, bf16[256,768]{1,0:T(8,128)(2,1)S(1)}, u32[]{:S(2)}, u32[]{:S(2)}) collective-permute-start(bf16[256,768]{1,0:T(8,128)(2,1)S(1)} %collective-permute-done.9.refs_0_), channel_id=1, source_target_pairs={{0,1},{1,0},{2,3},{3,2},{4,5},{5,4},{6,7},{7,6},{8,9},{9,8},{10,11... | collective-permute-start | bytes 1179656 | tf_op jit(solution)/shard_map/ppermute | solution.py:392
  116.7 7.8 %copy-start.18 = (bf16[256,768]{1,0:T(8,128)(2,1)}, bf16[256,768]{1,0:T(8,128)(2,1)S(1)}, u32[]{:S(2)}) copy-start(bf16[256,768]{1,0:T(8,128)(2,1)S(1)} %collective-permute-done.8.refs_0_) | copy-start | bytes 1179652
  116.7 21.5 %collective-permute-start.10 = (bf16[256,768]{1,0:T(8,128)(2,1)S(1)}, bf16[256,768]{1,0:T(8,128)(2,1)S(1)}, u32[]{:S(2)}, u32[]{:S(2)}) collective-permute-start(bf16[256,768]{1,0:T(8,128)(2,1)S(1)} %collective-permute-done.8.refs_0_), channel_id=1, source_target_pairs={{0,1},{1,0},{2,3},{3,2},{4,5},{5,4},{6,7},{7,6},{8,9},{9,8},{10,11... | collective-permute-start | bytes 1179656 | tf_op jit(solution)/shard_map/ppermute | solution.py:392
  124.5 6.6 %copy-start.3 = (bf16[256,768]{1,0:T(8,128)(2,1)S(1)}, bf16[256,768]{1,0:T(8,128)(2,1)}, u32[]{:S(2)}) copy-start(bf16[256,768]{1,0:T(8,128)(2,1)} %get-tuple-element.74.refs_0_.refs_4_) | copy-start | bytes 1179652
  130.4 14.2 %collective-permute-start.17 = (bf16[256,768]{1,0:T(8,128)(2,1)}, bf16[256,768]{1,0:T(8,128)(2,1)S(1)}, u32[]{:S(2)}, u32[]{:S(2)}) collective-permute-start(bf16[256,768]{1,0:T(8,128)(2,1)} %get-tuple-element.76.refs_1_.refs_5_), channel_id=1, source_target_pairs={{128,129},{129,128},{130,131},{131,130},{132,133},{133,132},{134,1... | collective-permute-start | bytes 1179656 | tf_op jit(solution)/shard_map/ppermute | solution.py:406
  131.1 13.6 %collective-permute-start.16 = (bf16[256,768]{1,0:T(8,128)(2,1)S(1)}, bf16[256,768]{1,0:T(8,128)(2,1)S(1)}, u32[]{:S(2)}, u32[]{:S(2)}) collective-permute-start(bf16[256,768]{1,0:T(8,128)(2,1)S(1)} %copy-done.3), channel_id=1, source_target_pairs={{128,129},{129,128},{130,131},{131,130},{132,133},{133,132},{134,1... | collective-permute-start | bytes 1179656 | tf_op jit(solution)/shard_map/ppermute | solution.py:406
  131.8 0.7 copy-start.16
  138.2 0.7 copy-start.15
  144.7 0.7 copy-start.9
  144.7 0.9 copy-start.10
  152.8 9.7 %collective-permute-start.18 = (bf16[4,512,384]{2,1,0:T(8,128)(2,1)}, bf16[4,512,384]{2,1,0:T(8,128)(2,1)S(1)}, u32[]{:S(2)}, u32[]{:S(2)}) collective-permute-start(bf16[4,512,384]{2,1,0:T(8,128)(2,1)} %shard_map.77), channel_id=1, source_target_pairs={{0,16},{16,0},{32,48},{48,32},{64,80},{80,64},{96,112},{112,96},{1... | collective-permute-start | bytes 4718600 | tf_op jit(solution)/shard_map/ppermute | solution.py:413
  162.3 15.6 %collective-permute-start.12 = (bf16[4,512,384]{2,1,0:T(8,128)(2,1)}, bf16[4,512,384]{2,1,0:T(8,128)(2,1)S(1)}, u32[]{:S(2)}, u32[]{:S(2)}) collective-permute-start(bf16[4,512,384]{2,1,0:T(8,128)(2,1)} %shard_map.75), channel_id=1, source_target_pairs={{0,16},{16,0},{32,48},{48,32},{64,80},{80,64},{96,112},{112,96},{1... | collective-permute-start | bytes 4718600 | tf_op jit(solution)/shard_map/ppermute | solution.py:413
  162.4 1.2 copy-start.8
  172.5 16.1 %collective-permute-start.19 = (bf16[512,384]{1,0:T(8,128)(2,1)}, bf16[512,384]{1,0:T(8,128)(2,1)S(1)}, u32[]{:S(2)}, u32[]{:S(2)}) collective-permute-start(bf16[512,384]{1,0:T(8,128)(2,1)} %get-tuple-element.100), channel_id=1, source_target_pairs={{0,64},{16,80},{32,96},{48,112},{64,0},{80,16},{96,32},{112,48},{1... | collective-permute-start | bytes 1179656 | tf_op jit(solution)/shard_map/ppermute | solution.py:419
  175.2 19.3 %collective-permute-start.20 = (bf16[512,384]{1,0:T(8,128)(2,1)}, bf16[512,384]{1,0:T(8,128)(2,1)S(1)}, u32[]{:S(2)}, u32[]{:S(2)}) collective-permute-start(bf16[512,384]{1,0:T(8,128)(2,1)} %get-tuple-element.101), channel_id=1, source_target_pairs={{0,32},{16,48},{32,64},{48,80},{64,96},{80,112},{96,0},{112,16},{1... | collective-permute-start | bytes 1179656 | tf_op jit(solution)/shard_map/ppermute | solution.py:419
  175.5 19.0 %copy-start.13 = (f32[512,384]{1,0:T(8,128)S(1)}, f32[512,384]{1,0:T(8,128)}, u32[]{:S(2)}) copy-start(f32[512,384]{1,0:T(8,128)} %get-tuple-element.99) | copy-start | bytes 2359300
  175.5 19.0 %collective-permute-start.21 = (bf16[512,384]{1,0:T(8,128)(2,1)}, bf16[512,384]{1,0:T(8,128)(2,1)S(1)}, u32[]{:S(2)}, u32[]{:S(2)}) collective-permute-start(bf16[512,384]{1,0:T(8,128)(2,1)} %get-tuple-element.102), channel_id=1, source_target_pairs={{0,96},{16,112},{32,0},{48,16},{64,32},{80,48},{96,64},{112,80},{1... | collective-permute-start | bytes 1179656 | tf_op jit(solution)/shard_map/ppermute | solution.py:419
  177.9 1.1 copy-start.7
  187.9 22.7 %copy-start.14 = (f32[512,384]{1,0:T(8,128)S(1)}, f32[512,384]{1,0:T(8,128)}, u32[]{:S(2)}) copy-start(f32[512,384]{1,0:T(8,128)} %get-tuple-element.93) | copy-start | bytes 2359300
  187.9 13.5 %collective-permute-start.13 = (bf16[512,384]{1,0:T(8,128)(2,1)}, bf16[512,384]{1,0:T(8,128)(2,1)S(1)}, u32[]{:S(2)}, u32[]{:S(2)}) collective-permute-start(bf16[512,384]{1,0:T(8,128)(2,1)} %get-tuple-element.94), channel_id=1, source_target_pairs={{0,64},{16,80},{32,96},{48,112},{64,0},{80,16},{96,32},{112,48},{1... | collective-permute-start | bytes 1179656 | tf_op jit(solution)/shard_map/ppermute | solution.py:419
  188.0 22.6 %collective-permute-start.14 = (bf16[512,384]{1,0:T(8,128)(2,1)}, bf16[512,384]{1,0:T(8,128)(2,1)S(1)}, u32[]{:S(2)}, u32[]{:S(2)}) collective-permute-start(bf16[512,384]{1,0:T(8,128)(2,1)} %get-tuple-element.95), channel_id=1, source_target_pairs={{0,32},{16,48},{32,64},{48,80},{64,96},{80,112},{96,0},{112,16},{1... | collective-permute-start | bytes 1179656 | tf_op jit(solution)/shard_map/ppermute | solution.py:419
  188.6 22.0 %collective-permute-start.15 = (bf16[512,384]{1,0:T(8,128)(2,1)}, bf16[512,384]{1,0:T(8,128)(2,1)}, u32[]{:S(2)}, u32[]{:S(2)}) collective-permute-start(bf16[512,384]{1,0:T(8,128)(2,1)} %get-tuple-element.96), channel_id=1, source_target_pairs={{0,96},{16,112},{32,0},{48,16},{64,32},{80,48},{96,64},{112,80},{1... | collective-permute-start | bytes 1179656 | tf_op jit(solution)/shard_map/ppermute | solution.py:419
  195.5 16.3 %collective-permute-start.22 = (bf16[512,384]{1,0:T(8,128)(2,1)}, bf16[512,384]{1,0:T(8,128)(2,1)S(1)}, u32[]{:S(2)}, u32[]{:S(2)}) collective-permute-start(bf16[512,384]{1,0:T(8,128)(2,1)} %add_convert_fusion), channel_id=1, source_target_pairs={{0,1},{1,0},{2,3},{3,2},{4,5},{5,4},{6,7},{7,6},{8,9},{9,8},{10,11... | collective-permute-start | bytes 1179656 | tf_op jit(solution)/shard_map/ppermute | solution.py:424
Sparse Core Ops, SparseCore 0:
  9.1 63.2 all-gather.4
  74.2 58.2 all-gather.6

commit v9 on v8

--- a/solution.py
+++ b/solution.py
@@ -19,6 +19,7 @@
 BOTH = ("section", "fsdp")
 STEPS = (2, 1, 3, 0)
 F32 = jnp.float32
+SMALL = pltpu.CompilerParams(vmem_limit_bytes=20 * 2**20)
 HBM = pl.BlockSpec(memory_space=pltpu.HBM)
 BF16 = jnp.bfloat16
 NT = (((1,), (1,)), ((), ()))
@@ -174,12 +175,18 @@
     one = pl.BlockSpec((seq_length, wide), lambda h, flags: (0, h))
     row = pl.BlockSpec((None, seq_length, wide), lambda h, flags: (micro, 0, h))
     out = jax.ShapeDtypeStruct((seq_length, width), BF16)
+    taken = [one]
+    if len(sent) > 1:
+        taken = [
+            pl.BlockSpec((seq_length, wide), lambda h, flags: (0, h * flags[1])),
+            pl.BlockSpec((seq_length, wide), lambda h, flags: (0, h * flags[0])),
+        ]
     return pl.pallas_call(
         functools.partial(attend_kernel, heads),
         grid_spec=pltpu.PrefetchScalarGridSpec(
             num_scalar_prefetch=1,
             grid=(width // wide,),
-            in_specs=[one] * len(sent)
+            in_specs=taken
             + [
                 row,
                 row,
@@ -192,6 +199,7 @@
         cost_estimate=cost(
             10 * seq_length * seq_length * width, 16 * seq_length * width
         ),
+        compiler_params=SMALL,
         name="attend",
     )(flags, *sent, query, key, value, mask)
 
@@ -290,7 +298,7 @@
         kernel, extra = keep_kernel, (other,)
         out_specs = [fixed] * 4
         out_shape = [
-            jax.ShapeDtypeStruct((count * rows, shard), t) for t in (BF16, BF16, BF16, F32)
+            jax.ShapeDtypeStruct((count * rows, shard), t) for t in (BF16,) * 4
         ]
     return pl.pallas_call(
         functools.partial(kernel, count),
@@ -414,6 +422,7 @@
         return projected(keep_at, dec[None], grads, first, second, other)
 
     def reduced(blocks, result):
+        result = result.astype(F32)
         for step, block in zip(STEPS, blocks):
             pairs = [(2 * x + k, 2 * ((x + step) % 4) + k) for x in range(4) for k in range(2)]
             other = lax.ppermute(block, "segment", pairs)

time: 221 us -> 212 us (0.959)
  Pallas kernels: 69.2 us -> 60.5 us
    pallas_call x4, Pallas kernels: 23.1 us -> 14.7 us  [attend(): pl.pallas_call(functools.partial(attend_kernel, heads), grid_spec=pltpu.P...]
    unnamed x43 -> x45, local copies, waits for them, and re-layouts: 4.74 us -> 4.23 us
  transfers between devices with their start and end apart: 25 -> 25, of which waited for: 8 -> 8; matrix products, arithmetic and copies ran while one was open for 7% -> 6% of each run, Pallas kernels for 28% -> 25%
where the time goes in v9:
time: 212 us; the launch traced here: 211 us
  waiting for transfers between devices  76.6 us (36%)
  Pallas kernels  60.5 us (29%)
  starting transfers between devices  40.4 us (19%)
  between operations  13.9 us (7%)
  other arithmetic  12.9 us (6%)
  local copies, waits for them, and re-layouts  7.16 us (3%)
    ppermute x4, waiting for transfers between devices, per_device(): came_near.append(lax.ppermute(value, BOTH, ENC_SWAP))  37.9 us
    pallas_call x4, Pallas kernels, projected(): pl.pallas_call(functools.partial(kernel, count), grid_spec=pltpu.Prefetch...  31.8 us
    ppermute x2, waiting for transfers between devices, per_device(): ctx_near.append(lax.ppermute(ctx[micro], BOTH, DEC_TO_ENC))  21.2 us
    ppermute x6, waiting for transfers between devices, reduced(): other = lax.ppermute(block, 'segment', pairs)  17.4 us
    pallas_call x4, Pallas kernels, attend(): pl.pallas_call(functools.partial(attend_kernel, heads), grid_spec=pltpu.P...  14.7 us
    ppermute x4, starting transfers between devices, per_device(): came_near.append(lax.ppermute(value, BOTH, ENC_SWAP))  11.2 us
    pallas_call x2, Pallas kernels, partial_products(): pl.pallas_call(kernel, grid_spec=pltpu.PrefetchScalarGridSpec(num_scalar_...  9.39 us
    ppermute x6, starting transfers between devices, reduced(): other = lax.ppermute(block, 'segment', pairs)  8.31 us
  transfers between devices with their start and end apart: 25, of which 8 were waited for; matrix products, arithmetic and copies ran while one was open for 6% of the time, Pallas kernels for 25%

profile of v9, /device:TPU:1, one launch (start us, length us, event | category | flops | bytes accessed | tf_op | source)
XLA Modules:
  0.0 211.4 jit_solution(9417843008909929006)
XLA Ops:
  6.5 1.9 slice.6
  9.1 4.5 %pick.1 = bf16[512,1536]{1,0:T(8,128)(2,1)} custom-call(s32[4]{0:T(128)} %add_subtract_fusion.1.where, bf16[512,6144]{1,0:T(8,128)(2,1)} %bitcast.41), custom_call_target="tpu_custom_call" | custom-call | bytes 3145728 | tf_op jit(solution)/shard_map/pick/pallas_call | solution.py:45
  13.6 0.9 slice.7
  14.5 1.8 collective-permute-start
  16.5 4.0 %collective-permute-start.5 = (f32[2,256,128]{2,1,0:T(8,128)S(1)}, f32[2,256,128]{2,1,0:T(8,128)S(1)}, u32[]{:S(2)}, u32[]{:S(2)}) collective-permute-start(f32[2,256,128]{2,1,0:T(8,128)S(1)} %broadcast_in_dim.22.refs_4_), channel_id=1, source_target_pairs={{0,1},{1,0},{2,3},{3,2},{4,5},{5,4},{6,7},{7,6},{8,9},{9,8},{10,11... | collective-permute-start | bytes 786440 | tf_op jit(solution)/shard_map/ppermute | solution.py:353
  20.5 1.9 collective-permute-start.4
  22.5 3.4 %collective-permute-start.3 = (bf16[2,256,768]{2,1,0:T(8,128)(2,1)S(1)}, bf16[2,256,768]{2,1,0:T(8,128)(2,1)}, u32[]{:S(2)}, u32[]{:S(2)}) collective-permute-start(bf16[2,256,768]{2,1,0:T(8,128)(2,1)S(1)} %bitcast.25), channel_id=1, source_target_pairs={{0,1},{1,0},{2,3},{3,2},{4,5},{5,4},{6,7},{7,6},{8,9},{9,8},{10,11... | collective-permute-start | bytes 2359304 | tf_op jit(solution)/shard_map/ppermute | solution.py:353
  25.9 1.9 collective-permute-start.2
  27.8 3.7 %collective-permute-start.1 = (bf16[512,1536]{1,0:T(8,128)(2,1)}, bf16[512,1536]{1,0:T(8,128)(2,1)}, u32[]{:S(2)}, u32[]{:S(2)}) collective-permute-start(bf16[512,1536]{1,0:T(8,128)(2,1)} %collective-permute-done.came), channel_id=1, source_target_pairs={{0,16},{16,0},{32,48},{48,32},{64,80},{80,64},{96,112},{112,96},{1... | collective-permute-start | bytes 4718600 | tf_op jit(solution)/shard_map/ppermute | solution.py:368
  33.8 0.8 broadcast_select_fusion.3.refs_5_
  34.7 7.5 %collective-permute-done.4 = bf16[2,256,768]{2,1,0:T(8,128)(2,1)} collective-permute-done((bf16[2,256,768]{2,1,0:T(8,128)(2,1)S(1)}, bf16[2,256,768]{2,1,0:T(8,128)(2,1)}, u32[]{:S(2)}, u32[]{:S(2)}) %collective-permute-start.4) | collective-permute-done | bytes 786464 | tf_op jit(solution)/shard_map/ppermute | solution.py:353
  42.2 1.2 broadcast_select_fusion.refs_4_
  43.4 15.6 %collective-permute-done.3 = bf16[2,256,768]{2,1,0:T(8,128)(2,1)} collective-permute-done((bf16[2,256,768]{2,1,0:T(8,128)(2,1)S(1)}, bf16[2,256,768]{2,1,0:T(8,128)(2,1)}, u32[]{:S(2)}, u32[]{:S(2)}) %collective-permute-start.3) | collective-permute-done | bytes 786464 | tf_op jit(solution)/shard_map/ppermute | solution.py:353
  59.1 2.1 broadcast_select_fusion.1.refs_3_
  61.2 14.7 %collective-permute-done.2 = bf16[2,256,768]{2,1,0:T(8,128)(2,1)} collective-permute-done((bf16[2,256,768]{2,1,0:T(8,128)(2,1)S(1)}, bf16[2,256,768]{2,1,0:T(8,128)(2,1)}, u32[]{:S(2)}, u32[]{:S(2)}) %collective-permute-start.2) | collective-permute-done | bytes 786464 | tf_op jit(solution)/shard_map/ppermute | solution.py:353
  75.9 2.1 broadcast_select_fusion.2.refs_2_
  78.0 5.0 %shard_map.74 = (bf16[256,768]{1,0:T(8,128)(2,1)}, bf16[256,768]{1,0:T(8,128)(2,1)}) custom-call(s32[2]{0:T(128)} %get-tuple-element.59.scalars, bf16[512,1536]{1,0:T(8,128)(2,1)} %collective-permute-done.came, bf16[512,1536]{1,0:T(8,128)(2,1)} %collective-permute-done.1.twin, bf16[8,384,768]{2,1,0:T(8,128)(2,1)} %bitcast.31), custom_call_target="tpu_custom_call" | custom-call | flops 2415919104 | bytes 4718592 | tf_op jit(solution)/shard_map/pallas_call | solution.py:122
  83.0 1.4 collective-permute-start.7
  85.1 4.4 %shard_map.73 = (f32[256,768]{1,0:T(8,128)}, f32[256,768]{1,0:T(8,128)}) custom-call(s32[2]{0:T(128)} %get-tuple-element.56.scalars, bf16[512,6144]{1,0:T(8,128)(2,1)} %bitcast.42, bf16[512,6144]{1,0:T(8,128)(2,1)} %bitcast.43, bf16[8,384,768]{2,1,0:T(8,128)(2,1)} %bitcast.32), custom_call_target="tpu_custom_call" | custom-call | flops 2415919104 | bytes 4718592 | tf_op jit(solution)/shard_map/pallas_call | solution.py:122
  89.6 1.5 add_convert_fusion.3.refs_1_
  91.1 1.3 collective-permute-start.9
  92.5 1.3 collective-permute-start.8
  93.8 14.7 %collective-permute-done.9.refs_0_ = bf16[256,768]{1,0:T(8,128)(2,1)S(1)} collective-permute-done((bf16[256,768]{1,0:T(8,128)(2,1)S(1)}, bf16[256,768]{1,0:T(8,128)(2,1)S(1)}, u32[]{:S(2)}, u32[]{:S(2)}) %collective-permute-start.9) | collective-permute-done | bytes 393248 | tf_op jit(solution)/shard_map/ppermute | solution.py:399
  108.4 1.9 collective-permute-start.11
  110.3 6.5 %collective-permute-done.8.refs_0_ = bf16[256,768]{1,0:T(8,128)(2,1)S(1)} collective-permute-done((bf16[256,768]{1,0:T(8,128)(2,1)S(1)}, bf16[256,768]{1,0:T(8,128)(2,1)S(1)}, u32[]{:S(2)}, u32[]{:S(2)}) %collective-permute-start.8) | collective-permute-done | bytes 393248 | tf_op jit(solution)/shard_map/ppermute | solution.py:399
  116.9 1.9 collective-permute-start.10
  118.8 3.6 %attend.4 = (bf16[256,768]{1,0:T(8,128)(2,1)S(1)}, bf16[256,768]{1,0:T(8,128)(2,1)S(1)}) custom-call(s32[2]{0:T(128)S(1)} %get-tuple-element.66.flags, bf16[256,768]{1,0:T(8,128)(2,1)S(1)} %collective-permute-done.9.refs_0_, bf16[256,768]{1,0:T(8,128)(2,1)S(1)} %add_convert_fusion.3.refs_1_, bf16[2,256,768]{2,1,0:T(8,128)(2,1)S(1)} %copy-done.4, ...), custom_call_target="tpu_custom_call" | custom-call | flops 503316480 | bytes 3145728 | tf_op jit(solution)/shard_map/attend/pallas_call | solution.py:184
  123.2 4.2 %attend.5 = (bf16[256,768]{1,0:T(8,128)(2,1)S(1)}, bf16[256,768]{1,0:T(8,128)(2,1)}) custom-call(s32[2]{0:T(128)S(1)} %get-tuple-element.66.flags, bf16[256,768]{1,0:T(8,128)(2,1)S(1)} %collective-permute-done.8.refs_0_, bf16[256,768]{1,0:T(8,128)(2,1)S(1)} %add_convert_fusion.2.refs_1_, bf16[2,256,768]{2,1,0:T(8,128)(2,1)S(1)} %copy-done.4, ...), custom_call_target="tpu_custom_call" | custom-call | flops 503316480 | bytes 3145728 | tf_op jit(solution)/shard_map/attend/pallas_call | solution.py:184
  128.1 1.4 collective-permute-start.17
  129.5 1.4 collective-permute-start.16
  131.0 3.5 %attend.6 = (bf16[256,768]{1,0:T(8,128)(2,1)S(1)}, bf16[256,768]{1,0:T(8,128)(2,1)S(1)}) custom-call(s32[2]{0:T(128)S(1)} %get-tuple-element.78.flags, bf16[256,768]{1,0:T(8,128)(2,1)S(1)} %collective-permute-done.11.refs_0_, bf16[2,256,768]{2,1,0:T(8,128)(2,1)S(1)} %bitcast.23, bf16[2,256,768]{2,1,0:T(8,128)(2,1)S(1)} %bitcast.26, ...), custom_call_target="tpu_custom_call" | custom-call | flops 503316480 | bytes 3145728 | tf_op jit(solution)/shard_map/attend/pallas_call | solution.py:184
  134.5 3.5 %attend.7 = (bf16[256,768]{1,0:T(8,128)(2,1)S(1)}, bf16[256,768]{1,0:T(8,128)(2,1)S(1)}) custom-call(s32[2]{0:T(128)S(1)} %get-tuple-element.78.flags, bf16[256,768]{1,0:T(8,128)(2,1)S(1)} %collective-permute-done.10.refs_0_, bf16[2,256,768]{2,1,0:T(8,128)(2,1)S(1)} %bitcast.24, bf16[2,256,768]{2,1,0:T(8,128)(2,1)S(1)} %bitcast.27, ...), custom_call_target="tpu_custom_call" | custom-call | flops 503316480 | bytes 3145728 | tf_op jit(solution)/shard_map/attend/pallas_call | solution.py:184
  138.0 0.8 copy-done.12
  139.5 7.2 %shard_map.77 = bf16[4,512,384]{2,1,0:T(8,128)(2,1)} custom-call(s32[4]{0:T(128)} %get-tuple-element.92.at, s32[1]{0:T(128)} %bitcast.5.flags, bf16[256,768]{1,0:T(8,128)(2,1)} %collective-permute-done.16.refs_0_, bf16[256,768]{1,0:T(8,128)(2,1)} %collective-permute-done.17.refs_1_, bf16[256,768]{1,0:T(8,128)(2,1)} %copy-done.11, ...), custom_call_target="tpu_custom_call" | custom-call | flops 2415919104 | bytes 4718592 | tf_op jit(solution)/shard_map/pallas_call | solution.py:303
  146.7 2.4 %collective-permute-start.18 = (bf16[4,512,384]{2,1,0:T(8,128)(2,1)}, bf16[4,512,384]{2,1,0:T(8,128)(2,1)}, u32[]{:S(2)}, u32[]{:S(2)}) collective-permute-start(bf16[4,512,384]{2,1,0:T(8,128)(2,1)} %shard_map.77), channel_id=1, source_target_pairs={{0,16},{16,0},{32,48},{48,32},{64,80},{80,64},{96,112},{112,96},{1... | collective-permute-start | bytes 4718600 | tf_op jit(solution)/shard_map/ppermute | solution.py:421
  149.0 7.2 %shard_map.75 = bf16[4,512,384]{2,1,0:T(8,128)(2,1)} custom-call(s32[4]{0:T(128)} %get-tuple-element.92.at, s32[1]{0:T(128)} %bitcast.5.flags, bf16[256,768]{1,0:T(8,128)(2,1)} %copy-done.5, bf16[256,768]{1,0:T(8,128)(2,1)} %get-tuple-element.76.refs_1_.refs_5_, bf16[256,768]{1,0:T(8,128)(2,1)} %copy-done.9, bf16[256,768]{1,0:T(8,128)(2,1)} %copy-done.12, ...), custom_call_target="tpu_custom_call" | custom-call | flops 2415919104 | bytes 4718592 | tf_op jit(solution)/shard_map/pallas_call | solution.py:303
  156.4 8.7 %shard_map.78 = (bf16[512,384]{1,0:T(8,128)(2,1)}, bf16[512,384]{1,0:T(8,128)(2,1)}, bf16[512,384]{1,0:T(8,128)(2,1)}, bf16[512,384]{1,0:T(8,128)(2,1)}) custom-call(s32[4]{0:T(128)} %broadcast_add_fusion.at, s32[1]{0:T(128)} %bitcast.5.flags, bf16[256,768]{1,0:T(8,128)(2,1)} %collective-permute-done.16.refs_0_, ...), custom_call_target="tpu_custom_call" | custom-call | flops 2415919104 | bytes 4718592 | tf_op jit(solution)/shard_map/pallas_call | solution.py:303
  165.1 2.8 %collective-permute-start.19 = (bf16[512,384]{1,0:T(8,128)(2,1)}, bf16[512,384]{1,0:T(8,128)(2,1)S(1)}, u32[]{:S(2)}, u32[]{:S(2)}) collective-permute-start(bf16[512,384]{1,0:T(8,128)(2,1)} %get-tuple-element.100), channel_id=1, source_target_pairs={{0,64},{16,80},{32,96},{48,112},{64,0},{80,16},{96,32},{112,48},{1... | collective-permute-start | bytes 1179656 | tf_op jit(solution)/shard_map/ppermute | solution.py:428
  168.2 2.4 %collective-permute-start.21 = (bf16[512,384]{1,0:T(8,128)(2,1)}, bf16[512,384]{1,0:T(8,128)(2,1)S(1)}, u32[]{:S(2)}, u32[]{:S(2)}) collective-permute-start(bf16[512,384]{1,0:T(8,128)(2,1)} %get-tuple-element.102), channel_id=1, source_target_pairs={{0,96},{16,112},{32,0},{48,16},{64,32},{80,48},{96,64},{112,80},{1... | collective-permute-start | bytes 1179656 | tf_op jit(solution)/shard_map/ppermute | solution.py:428
  170.6 1.1 copy-done.15
  171.7 8.7 %shard_map.76 = (bf16[512,384]{1,0:T(8,128)(2,1)}, bf16[512,384]{1,0:T(8,128)(2,1)}, bf16[512,384]{1,0:T(8,128)(2,1)}, bf16[512,384]{1,0:T(8,128)(2,1)}) custom-call(s32[4]{0:T(128)} %broadcast_add_fusion.at, s32[1]{0:T(128)} %bitcast.5.flags, bf16[256,768]{1,0:T(8,128)(2,1)} %copy-done.5, bf16[256,768]{1,0:T(8,128)(2,1)} %get-tuple-element.76.refs_1_.refs_5_, ...), custom_call_target="tpu_custom_call" | custom-call | flops 2415919104 | bytes 4718592 | tf_op jit(solution)/shard_map/pallas_call | solution.py:303
  181.2 2.2 %collective-permute-start.15 = (bf16[512,384]{1,0:T(8,128)(2,1)}, bf16[512,384]{1,0:T(8,128)(2,1)S(1)}, u32[]{:S(2)}, u32[]{:S(2)}) collective-permute-start(bf16[512,384]{1,0:T(8,128)(2,1)} %get-tuple-element.96), channel_id=1, source_target_pairs={{0,96},{16,112},{32,0},{48,16},{64,32},{80,48},{96,64},{112,80},{1... | collective-permute-start | bytes 1179656 | tf_op jit(solution)/shard_map/ppermute | solution.py:428
  183.3 3.8 %collective-permute-done.20 = bf16[512,384]{1,0:T(8,128)(2,1)S(1)} collective-permute-done((bf16[512,384]{1,0:T(8,128)(2,1)}, bf16[512,384]{1,0:T(8,128)(2,1)S(1)}, u32[]{:S(2)}, u32[]{:S(2)}) %collective-permute-start.20) | collective-permute-done | bytes 393248 | tf_op jit(solution)/shard_map/ppermute | solution.py:428
  187.2 0.9 add_convert_fusion
  188.1 1.5 collective-permute-start.22
  189.6 4.4 %collective-permute-done.13 = bf16[512,384]{1,0:T(8,128)(2,1)S(1)} collective-permute-done((bf16[512,384]{1,0:T(8,128)(2,1)}, bf16[512,384]{1,0:T(8,128)(2,1)S(1)}, u32[]{:S(2)}, u32[]{:S(2)}) %collective-permute-start.13) | collective-permute-done | bytes 393248 | tf_op jit(solution)/shard_map/ppermute | solution.py:428
  194.0 9.2 %collective-permute-done.14 = bf16[512,384]{1,0:T(8,128)(2,1)S(1)} collective-permute-done((bf16[512,384]{1,0:T(8,128)(2,1)}, bf16[512,384]{1,0:T(8,128)(2,1)S(1)}, u32[]{:S(2)}, u32[]{:S(2)}) %collective-permute-start.14) | collective-permute-done | bytes 393248 | tf_op jit(solution)/shard_map/ppermute | solution.py:428
  203.4 1.1 maximum_select_fusion
  (78 shorter events, 7.4 us)
Async XLA Ops:
  6.5 71.5 %all-gather.5.cloned.1.call-start = ((), (), s32[]{:S(2)}) async-start(), calls=%async_computation | async-start | bytes 5308416 | tf_op jit(solution)/shard_map/all_gather | solution.py:340
  8.5 131.0 %all-gather.7.cloned.1.call-start = ((), (), s32[]{:S(2)}) async-start(), calls=%async_computation.1 | async-start | bytes 5308416 | tf_op jit(solution)/shard_map/all_gather | solution.py:340
  9.1 4.5 %copy-start.16 = (bf16[1,2,384,768]{3,2,1,0:T(8,128)(2,1)S(1)}, bf16[1,2,384,768]{3,2,1,0:T(8,128)(2,1)}, u32[]{:S(2)}) copy-start(bf16[1,2,384,768]{3,2,1,0:T(8,128)(2,1)} %param.12) | copy-start | bytes 3538948
  9.1 11.4 %copy-start.2 = (bf16[2,1,256,768]{3,2,1,0:T(8,128)(2,1)S(1)}, bf16[2,1,256,768]{3,2,1,0:T(8,128)(2,1)}, u32[]{:S(2)}) copy-start(bf16[2,1,256,768]{3,2,1,0:T(8,128)(2,1)} %param.10) | copy-start | bytes 2359300
  13.6 2.8 %copy-start.20 = (s32[2,1,256]{2,1,0:T(1,128)S(1)}, s32[2,1,256]{2,1,0:T(1,128)}, u32[]{:S(2)}) copy-start(s32[2,1,256]{2,1,0:T(1,128)} %param.11) | copy-start | bytes 6148
  13.6 8.9 %copy-start.1 = (bf16[2,1,256,768]{3,2,1,0:T(8,128)(2,1)S(1)}, bf16[2,1,256,768]{3,2,1,0:T(8,128)(2,1)}, u32[]{:S(2)}) copy-start(bf16[2,1,256,768]{3,2,1,0:T(8,128)(2,1)} %param.9) | copy-start | bytes 2359300
  13.6 12.3 %copy-start = (bf16[2,1,256,768]{3,2,1,0:T(8,128)(2,1)S(1)}, bf16[2,1,256,768]{3,2,1,0:T(8,128)(2,1)}, u32[]{:S(2)}) copy-start(bf16[2,1,256,768]{3,2,1,0:T(8,128)(2,1)} %param.8) | copy-start | bytes 2359300
  13.6 18.0 %copy-start.21 = (s32[4]{0:T(128)S(1)}, s32[4]{0:T(128)}, u32[]{:S(2)}) copy-start(s32[4]{0:T(128)} %constant.69.clone) | copy-start | bytes 52
  14.5 13.3 %collective-permute-start = (bf16[512,1536]{1,0:T(8,128)(2,1)}, bf16[512,1536]{1,0:T(8,128)(2,1)}, u32[]{:S(2)}, u32[]{:S(2)}) collective-permute-start(bf16[512,1536]{1,0:T(8,128)(2,1)} %pick.1), channel_id=1, source_target_pairs={{128,129},{129,128},{130,131},{131,130},{132,133},{133,132},{134,1... | collective-permute-start | bytes 4718600 | tf_op jit(solution)/shard_map/ppermute | solution.py:367
  16.5 18.2 %copy-start.7 = (f32[2,256,128]{2,1,0:T(8,128)}, f32[2,256,128]{2,1,0:T(8,128)S(1)}, u32[]{:S(2)}) copy-start(f32[2,256,128]{2,1,0:T(8,128)S(1)} %broadcast_in_dim.22.refs_4_) | copy-start | bytes 786436
  16.5 17.3 %collective-permute-start.5 = (f32[2,256,128]{2,1,0:T(8,128)S(1)}, f32[2,256,128]{2,1,0:T(8,128)S(1)}, u32[]{:S(2)}, u32[]{:S(2)}) collective-permute-start(f32[2,256,128]{2,1,0:T(8,128)S(1)} %broadcast_in_dim.22.refs_4_), channel_id=1, source_target_pairs={{0,1},{1,0},{2,3},{3,2},{4,5},{5,4},{6,7},{7,6},{8,9},{9,8},{10,11... | collective-permute-start | bytes 786440 | tf_op jit(solution)/shard_map/ppermute | solution.py:353
  20.5 21.7 %collective-permute-start.4 = (bf16[2,256,768]{2,1,0:T(8,128)(2,1)S(1)}, bf16[2,256,768]{2,1,0:T(8,128)(2,1)}, u32[]{:S(2)}, u32[]{:S(2)}) collective-permute-start(bf16[2,256,768]{2,1,0:T(8,128)(2,1)S(1)} %bitcast.28), channel_id=1, source_target_pairs={{0,1},{1,0},{2,3},{3,2},{4,5},{5,4},{6,7},{7,6},{8,9},{9,8},{10,11... | collective-permute-start | bytes 2359304 | tf_op jit(solution)/shard_map/ppermute | solution.py:353
  22.5 36.6 %collective-permute-start.3 = (bf16[2,256,768]{2,1,0:T(8,128)(2,1)S(1)}, bf16[2,256,768]{2,1,0:T(8,128)(2,1)}, u32[]{:S(2)}, u32[]{:S(2)}) collective-permute-start(bf16[2,256,768]{2,1,0:T(8,128)(2,1)S(1)} %bitcast.25), channel_id=1, source_target_pairs={{0,1},{1,0},{2,3},{3,2},{4,5},{5,4},{6,7},{7,6},{8,9},{9,8},{10,11... | collective-permute-start | bytes 2359304 | tf_op jit(solution)/shard_map/ppermute | solution.py:353
  25.9 50.0 %collective-permute-start.2 = (bf16[2,256,768]{2,1,0:T(8,128)(2,1)S(1)}, bf16[2,256,768]{2,1,0:T(8,128)(2,1)}, u32[]{:S(2)}, u32[]{:S(2)}) collective-permute-start(bf16[2,256,768]{2,1,0:T(8,128)(2,1)S(1)} %bitcast.22), channel_id=1, source_target_pairs={{0,1},{1,0},{2,3},{3,2},{4,5},{5,4},{6,7},{7,6},{8,9},{9,8},{10,11... | collective-permute-start | bytes 2359304 | tf_op jit(solution)/shard_map/ppermute | solution.py:353
  27.8 50.2 %collective-permute-start.1 = (bf16[512,1536]{1,0:T(8,128)(2,1)}, bf16[512,1536]{1,0:T(8,128)(2,1)}, u32[]{:S(2)}, u32[]{:S(2)}) collective-permute-start(bf16[512,1536]{1,0:T(8,128)(2,1)} %collective-permute-done.came), channel_id=1, source_target_pairs={{0,16},{16,0},{32,48},{48,32},{64,80},{80,64},{96,112},{112,96},{1... | collective-permute-start | bytes 4718600 | tf_op jit(solution)/shard_map/ppermute | solution.py:368
  83.0 6.6 %collective-permute-start.7 = (bf16[256,768]{1,0:T(8,128)(2,1)}, bf16[256,768]{1,0:T(8,128)(2,1)}, u32[]{:S(2)}, u32[]{:S(2)}) collective-permute-start(bf16[256,768]{1,0:T(8,128)(2,1)} %get-tuple-element.64), channel_id=1, source_target_pairs={{128,129},{129,128},{130,131},{131,130},{132,133},{133,132},{134,1... | collective-permute-start | bytes 1179656 | tf_op jit(solution)/shard_map/ppermute | solution.py:381
  84.4 8.0 %collective-permute-start.6 = (bf16[256,768]{1,0:T(8,128)(2,1)}, bf16[256,768]{1,0:T(8,128)(2,1)S(1)}, u32[]{:S(2)}, u32[]{:S(2)}) collective-permute-start(bf16[256,768]{1,0:T(8,128)(2,1)} %get-tuple-element.62), channel_id=1, source_target_pairs={{128,129},{129,128},{130,131},{131,130},{132,133},{133,132},{134,1... | collective-permute-start | bytes 1179656 | tf_op jit(solution)/shard_map/ppermute | solution.py:381
  89.5 2.8 %copy-start.17 = (f32[256,768]{1,0:T(8,128)S(1)}, f32[256,768]{1,0:T(8,128)}, u32[]{:S(2)}) copy-start(f32[256,768]{1,0:T(8,128)} %get-tuple-element.58) | copy-start | bytes 2359300
  89.5 29.2 %copy-start.3 = (bf16[2,256,768]{2,1,0:T(8,128)(2,1)S(1)}, bf16[2,256,768]{2,1,0:T(8,128)(2,1)}, u32[]{:S(2)}) copy-start(bf16[2,256,768]{2,1,0:T(8,128)(2,1)} %broadcast_select_fusion.1.refs_3_) | copy-start | bytes 2359300
  89.6 29.2 %copy-start.4 = (bf16[2,256,768]{2,1,0:T(8,128)(2,1)S(1)}, bf16[2,256,768]{2,1,0:T(8,128)(2,1)}, u32[]{:S(2)}) copy-start(bf16[2,256,768]{2,1,0:T(8,128)(2,1)} %broadcast_select_fusion.2.refs_2_) | copy-start | bytes 2359300
  89.6 29.2 %copy-start.6 = (f32[2,256,128]{2,1,0:T(8,128)S(1)}, f32[2,256,128]{2,1,0:T(8,128)}, u32[]{:S(2)}) copy-start(f32[2,256,128]{2,1,0:T(8,128)} %broadcast_select_fusion.3.refs_5_) | copy-start | bytes 786436
  91.1 17.4 %collective-permute-start.9 = (bf16[256,768]{1,0:T(8,128)(2,1)S(1)}, bf16[256,768]{1,0:T(8,128)(2,1)S(1)}, u32[]{:S(2)}, u32[]{:S(2)}) collective-permute-start(bf16[256,768]{1,0:T(8,128)(2,1)S(1)} %add_convert_fusion.3.refs_1_), channel_id=1, source_target_pairs={{128,1},{129,0},{130,3},{131,2},{132,5},{133,4},{134,7},{135,6},{1... | collective-permute-start | bytes 1179656 | tf_op jit(solution)/shard_map/ppermute | solution.py:399
  92.5 24.4 %collective-permute-start.8 = (bf16[256,768]{1,0:T(8,128)(2,1)S(1)}, bf16[256,768]{1,0:T(8,128)(2,1)S(1)}, u32[]{:S(2)}, u32[]{:S(2)}) collective-permute-start(bf16[256,768]{1,0:T(8,128)(2,1)S(1)} %add_convert_fusion.2.refs_1_), channel_id=1, source_target_pairs={{128,1},{129,0},{130,3},{131,2},{132,5},{133,4},{134,7},{135,6},{1... | collective-permute-start | bytes 1179656 | tf_op jit(solution)/shard_map/ppermute | solution.py:399
  108.4 22.5 %collective-permute-start.11 = (bf16[256,768]{1,0:T(8,128)(2,1)S(1)}, bf16[256,768]{1,0:T(8,128)(2,1)S(1)}, u32[]{:S(2)}, u32[]{:S(2)}) collective-permute-start(bf16[256,768]{1,0:T(8,128)(2,1)S(1)} %collective-permute-done.9.refs_0_), channel_id=1, source_target_pairs={{0,1},{1,0},{2,3},{3,2},{4,5},{5,4},{6,7},{7,6},{8,9},{9,8},{10,11... | collective-permute-start | bytes 1179656 | tf_op jit(solution)/shard_map/ppermute | solution.py:400
  116.9 17.6 %collective-permute-start.10 = (bf16[256,768]{1,0:T(8,128)(2,1)S(1)}, bf16[256,768]{1,0:T(8,128)(2,1)S(1)}, u32[]{:S(2)}, u32[]{:S(2)}) collective-permute-start(bf16[256,768]{1,0:T(8,128)(2,1)S(1)} %collective-permute-done.8.refs_0_), channel_id=1, source_target_pairs={{0,1},{1,0},{2,3},{3,2},{4,5},{5,4},{6,7},{7,6},{8,9},{9,8},{10,11... | collective-permute-start | bytes 1179656 | tf_op jit(solution)/shard_map/ppermute | solution.py:400
  122.4 0.8 copy-start.11
  123.2 6.4 %copy-start.5 = (bf16[256,768]{1,0:T(8,128)(2,1)}, bf16[256,768]{1,0:T(8,128)(2,1)S(1)}, u32[]{:S(2)}) copy-start(bf16[256,768]{1,0:T(8,128)(2,1)S(1)} %get-tuple-element.74.refs_0_.refs_4_) | copy-start | bytes 1179652
  123.2 7.8 %copy-start.8 = (f32[2,256,128]{2,1,0:T(8,128)S(1)}, f32[2,256,128]{2,1,0:T(8,128)}, u32[]{:S(2)}) copy-start(f32[2,256,128]{2,1,0:T(8,128)} %copy-done.7) | copy-start | bytes 786436
  127.4 0.7 copy-start.14
  128.1 11.4 %collective-permute-start.17 = (bf16[256,768]{1,0:T(8,128)(2,1)}, bf16[256,768]{1,0:T(8,128)(2,1)}, u32[]{:S(2)}, u32[]{:S(2)}) collective-permute-start(bf16[256,768]{1,0:T(8,128)(2,1)} %get-tuple-element.76.refs_1_.refs_5_), channel_id=1, source_target_pairs={{128,129},{129,128},{130,131},{131,130},{132,133},{133,132},{134,1... | collective-permute-start | bytes 1179656 | tf_op jit(solution)/shard_map/ppermute | solution.py:414
  129.5 10.0 %collective-permute-start.16 = (bf16[256,768]{1,0:T(8,128)(2,1)S(1)}, bf16[256,768]{1,0:T(8,128)(2,1)}, u32[]{:S(2)}, u32[]{:S(2)}) collective-permute-start(bf16[256,768]{1,0:T(8,128)(2,1)S(1)} %get-tuple-element.74.refs_0_.refs_4_), channel_id=1, source_target_pairs={{128,129},{129,128},{130,131},{131,130},{132,133},{133,132},{134,1... | collective-permute-start | bytes 1179656 | tf_op jit(solution)/shard_map/ppermute | solution.py:414
  134.4 12.2 %copy-start.9 = (bf16[256,768]{1,0:T(8,128)(2,1)}, bf16[256,768]{1,0:T(8,128)(2,1)S(1)}, u32[]{:S(2)}) copy-start(bf16[256,768]{1,0:T(8,128)(2,1)S(1)} %get-tuple-element.87.refs_2_) | copy-start | bytes 1179652
  134.5 12.2 %copy-start.10 = (bf16[256,768]{1,0:T(8,128)(2,1)}, bf16[256,768]{1,0:T(8,128)(2,1)S(1)}, u32[]{:S(2)}) copy-start(bf16[256,768]{1,0:T(8,128)(2,1)S(1)} %get-tuple-element.89.refs_4_) | copy-start | bytes 1179652
  138.0 0.8 copy-start.12
  138.7 0.7 copy-start.13
  146.7 9.7 %collective-permute-start.18 = (bf16[4,512,384]{2,1,0:T(8,128)(2,1)}, bf16[4,512,384]{2,1,0:T(8,128)(2,1)}, u32[]{:S(2)}, u32[]{:S(2)}) collective-permute-start(bf16[4,512,384]{2,1,0:T(8,128)(2,1)} %shard_map.77), channel_id=1, source_target_pairs={{0,16},{16,0},{32,48},{48,32},{64,80},{80,64},{96,112},{112,96},{1... | collective-permute-start | bytes 4718600 | tf_op jit(solution)/shard_map/ppermute | solution.py:421
  156.3 14.3 %collective-permute-start.12 = (bf16[4,512,384]{2,1,0:T(8,128)(2,1)}, bf16[4,512,384]{2,1,0:T(8,128)(2,1)S(1)}, u32[]{:S(2)}, u32[]{:S(2)}) collective-permute-start(bf16[4,512,384]{2,1,0:T(8,128)(2,1)} %shard_map.75), channel_id=1, source_target_pairs={{0,16},{16,0},{32,48},{48,32},{64,80},{80,64},{96,112},{112,96},{1... | collective-permute-start | bytes 4718600 | tf_op jit(solution)/shard_map/ppermute | solution.py:421
  165.1 16.0 %collective-permute-start.19 = (bf16[512,384]{1,0:T(8,128)(2,1)}, bf16[512,384]{1,0:T(8,128)(2,1)S(1)}, u32[]{:S(2)}, u32[]{:S(2)}) collective-permute-start(bf16[512,384]{1,0:T(8,128)(2,1)} %get-tuple-element.100), channel_id=1, source_target_pairs={{0,64},{16,80},{32,96},{48,112},{64,0},{80,16},{96,32},{112,48},{1... | collective-permute-start | bytes 1179656 | tf_op jit(solution)/shard_map/ppermute | solution.py:428
  167.9 19.3 %collective-permute-start.20 = (bf16[512,384]{1,0:T(8,128)(2,1)}, bf16[512,384]{1,0:T(8,128)(2,1)S(1)}, u32[]{:S(2)}, u32[]{:S(2)}) collective-permute-start(bf16[512,384]{1,0:T(8,128)(2,1)} %get-tuple-element.101), channel_id=1, source_target_pairs={{0,32},{16,48},{32,64},{48,80},{64,96},{80,112},{96,0},{112,16},{1... | collective-permute-start | bytes 1179656 | tf_op jit(solution)/shard_map/ppermute | solution.py:428
  168.2 19.0 %copy-start.18 = (bf16[512,384]{1,0:T(8,128)(2,1)S(1)}, bf16[512,384]{1,0:T(8,128)(2,1)}, u32[]{:S(2)}) copy-start(bf16[512,384]{1,0:T(8,128)(2,1)} %get-tuple-element.99) | copy-start | bytes 1179652
  168.2 19.0 %collective-permute-start.21 = (bf16[512,384]{1,0:T(8,128)(2,1)}, bf16[512,384]{1,0:T(8,128)(2,1)S(1)}, u32[]{:S(2)}, u32[]{:S(2)}) collective-permute-start(bf16[512,384]{1,0:T(8,128)(2,1)} %get-tuple-element.102), channel_id=1, source_target_pairs={{0,96},{16,112},{32,0},{48,16},{64,32},{80,48},{96,64},{112,80},{1... | collective-permute-start | bytes 1179656 | tf_op jit(solution)/shard_map/ppermute | solution.py:428
  170.6 1.1 copy-start.15
  180.5 22.8 %copy-start.19 = (bf16[512,384]{1,0:T(8,128)(2,1)S(1)}, bf16[512,384]{1,0:T(8,128)(2,1)}, u32[]{:S(2)}) copy-start(bf16[512,384]{1,0:T(8,128)(2,1)} %get-tuple-element.93) | copy-start | bytes 1179652
  180.5 13.6 %collective-permute-start.13 = (bf16[512,384]{1,0:T(8,128)(2,1)}, bf16[512,384]{1,0:T(8,128)(2,1)S(1)}, u32[]{:S(2)}, u32[]{:S(2)}) collective-permute-start(bf16[512,384]{1,0:T(8,128)(2,1)} %get-tuple-element.94), channel_id=1, source_target_pairs={{0,64},{16,80},{32,96},{48,112},{64,0},{80,16},{96,32},{112,48},{1... | collective-permute-start | bytes 1179656 | tf_op jit(solution)/shard_map/ppermute | solution.py:428
  180.6 22.7 %collective-permute-start.14 = (bf16[512,384]{1,0:T(8,128)(2,1)}, bf16[512,384]{1,0:T(8,128)(2,1)S(1)}, u32[]{:S(2)}, u32[]{:S(2)}) collective-permute-start(bf16[512,384]{1,0:T(8,128)(2,1)} %get-tuple-element.95), channel_id=1, source_target_pairs={{0,32},{16,48},{32,64},{48,80},{64,96},{80,112},{96,0},{112,16},{1... | collective-permute-start | bytes 1179656 | tf_op jit(solution)/shard_map/ppermute | solution.py:428
  181.2 22.1 %collective-permute-start.15 = (bf16[512,384]{1,0:T(8,128)(2,1)}, bf16[512,384]{1,0:T(8,128)(2,1)S(1)}, u32[]{:S(2)}, u32[]{:S(2)}) collective-permute-start(bf16[512,384]{1,0:T(8,128)(2,1)} %get-tuple-element.96), channel_id=1, source_target_pairs={{0,96},{16,112},{32,0},{48,16},{64,32},{80,48},{96,64},{112,80},{1... | collective-permute-start | bytes 1179656 | tf_op jit(solution)/shard_map/ppermute | solution.py:428
  188.1 15.3 %collective-permute-start.22 = (bf16[512,384]{1,0:T(8,128)(2,1)}, bf16[512,384]{1,0:T(8,128)(2,1)S(1)}, u32[]{:S(2)}, u32[]{:S(2)}) collective-permute-start(bf16[512,384]{1,0:T(8,128)(2,1)} %add_convert_fusion), channel_id=1, source_target_pairs={{0,1},{1,0},{2,3},{3,2},{4,5},{5,4},{6,7},{7,6},{8,9},{9,8},{10,11... | collective-permute-start | bytes 1179656 | tf_op jit(solution)/shard_map/ppermute | solution.py:433
Sparse Core Ops, SparseCore 0:
  9.1 63.2 all-gather.4
  74.2 58.2 all-gather.6
